TPU v7x, 512 devices: a whole 4x4x16 slice. The times are simulated.
512 devices in a mesh: dp: 32 (over z, y_hi), tensor: 16 (over x, y_lo, core).
Axes of the slice: x: 4, y: 4 (y_hi: 2, y_lo: 2; y = y_hi * 2 + y_lo), z: 16, core: 2. Of those that a mesh axis runs over, the one named last changes fastest.
Arguments:
- residual: bfloat16 [4096, 2048], P(('dp', 'tensor')), may hold values from -6 to 6
- norm_gain: float32 [2048], replicated, may hold values from 0.1 to 1.9
- gate_weight: bfloat16 [2048, 7168], P(None, 'tensor'), may hold values from -0.125 to 0.125
- up_weight: bfloat16 [2048, 7168], P(None, 'tensor'), may hold values from -0.125 to 0.125
- hidden_grad: bfloat16 [4096, 7168], P('dp', 'tensor'), may hold values from -6 to 6
Outputs:
- residual_grad: bfloat16 [4096, 2048], P(('dp', 'tensor'))
- gate_weight_grad: bfloat16 [2048, 7168], P('dp', 'tensor')
- up_weight_grad: bfloat16 [2048, 7168], P('dp', 'tensor')
All inputs are finite; a program needn't handle non-finite values.
Results may differ from a plain program's by a relative error of at most 0.024.
Values may be sent and summed in bfloat16 or wider, within the bound.
No kernel may reach another device: no remote copies, remote signals or barrier semaphores. Data moves between devices by JAX's collectives and lax.ppermute only.
A program may use at most 64 MiB of HBM per device.

v0:
```python
import jax
import jax.numpy as jnp
from jax import lax
from jax.sharding import PartitionSpec as P

EPSILON = 1e-05


def normalize(residual):
    values = residual.astype(jnp.float32)
    inverse = lax.rsqrt(jnp.mean(values * values, axis=-1, keepdims=True) + EPSILON)
    return (values * inverse, inverse)


def contract_last(left, right):
    return lax.dot_general(
        left, right, (((1,), (1,)), ((), ())), preferred_element_type=jnp.float32
    )


def contract_first(left, right):
    return lax.dot_general(
        left, right, (((0,), (0,)), ((), ())), preferred_element_type=jnp.float32
    )


def shards(residual, norm_gain, gate_weight, up_weight, hidden_grad):
    scaled, inverse = normalize(residual)
    gathered = lax.all_gather(residual, "tensor", axis=0, tiled=True)
    whole_scaled = normalize(gathered)[0]
    normed = (whole_scaled * norm_gain).astype(jnp.bfloat16)
    gate_value = jnp.dot(normed, gate_weight, preferred_element_type=jnp.float32)
    up_value = jnp.dot(normed, up_weight, preferred_element_type=jnp.float32)
    sigmoid_gate = jax.nn.sigmoid(gate_value)
    upstream = hidden_grad.astype(jnp.float32)
    up_grad = (upstream * gate_value * sigmoid_gate).astype(jnp.bfloat16)
    gate_grad = (
        upstream * up_value * sigmoid_gate * (1.0 + gate_value * (1.0 - sigmoid_gate))
    ).astype(jnp.bfloat16)
    normed_grad = lax.psum_scatter(
        (contract_last(gate_grad, gate_weight) + contract_last(up_grad, up_weight)).astype(
            jnp.bfloat16
        ),
        "tensor",
        scatter_dimension=0,
        tiled=True,
    ).astype(jnp.float32)
    weighted = normed_grad * norm_gain
    residual_grad = (
        (weighted - scaled * jnp.mean(weighted * scaled, axis=-1, keepdims=True)) * inverse
    ).astype(jnp.bfloat16)
    factor = float(normed.shape[0] * lax.axis_size("dp")) ** (-0.5)
    gate_part = contract_first(normed, gate_grad) * factor
    up_part = contract_first(normed, up_grad) * factor
    gate_total, up_total = (
        lax.psum_scatter(
            gate_part.astype(jnp.bfloat16), "dp", scatter_dimension=0, tiled=True
        ).astype(jnp.float32),
        lax.psum_scatter(
            up_part.astype(jnp.bfloat16), "dp", scatter_dimension=0, tiled=True
        ).astype(jnp.float32),
    )
    return (residual_grad, gate_total.astype(jnp.bfloat16), up_total.astype(jnp.bfloat16))


def solution(mesh):
    return jax.shard_map(
        shards,
        mesh=mesh,
        in_specs=(
            P(("dp", "tensor"), None),
            P(),
            P(None, "tensor"),
            P(None, "tensor"),
            P("dp", "tensor"),
        ),
        out_specs=(P(("dp", "tensor"), None), P("dp", "tensor"), P("dp", "tensor")),
        check_vma=False,
    )
```

profile of v0, /device:TPU:1, one launch (start us, length us, event | category | flops | bytes accessed | tf_op | source)
XLA Modules:
  0.0 1419.8 jit_solution(12643667574390376313)
XLA Ops:
  7.2 0.0 copy-start
  7.2 0.0 copy-start.4
  7.2 0.0 copy-start.3
  7.2 0.0 reduce-scatter.4.cloned.1.call-start
  7.2 0.0 copy-start.1
  7.3 24.6 %all_gather.3 = bf16[128,2048]{1,0:T(8,128)(2,1)S(1)} all-gather(bf16[8,2048]{1,0:T(8,128)(2,1)} %param.5), channel_id=1, replica_groups=mesh['dp'=32,'tensor'=16] {'tensor'}, dimensions={0}, use_global_device_ids=true | all-gather | bytes 557056 | tf_op jit(solution)/shard_map/all_gather | solution.py:29
  31.9 0.2 fusion.4
  32.1 0.0 copy-done
  32.1 1.4 fusion.20
  33.5 0.0 copy-done.4
  33.5 0.0 copy-done.3
  33.5 0.0 copy-done.1
  33.5 0.7 fusion.3
  34.3 0.5 fusion.23
  34.7 1.3 fusion
  36.0 0.0 reduce-scatter.4.cloned.1.call-update
  36.1 0.0 reduce-scatter.8.cloned.1.call-start
  36.1 2.1 multiply_convert_fusion
  38.2 0.0 reduce-scatter.8.cloned.1.call-update
  38.3 0.0 copy-start.2
  38.3 0.0 reduce-scatter.6.cloned.1.call-start
  38.3 2.2 multiply_convert_fusion.1
  40.5 0.0 reduce-scatter.6.cloned.1.call-update
  40.5 0.0 copy-done.2
  40.5 0.1 fusion.15
  40.7 60.8 %reduce-scatter.4.cloned.1.call-done = bf16[8,2048]{1,0:T(8,128)(2,1)} async-done(((bf16[128,2048]{1,0:T(8,128)(2,1)}), bf16[8,2048]{1,0:T(8,128)(2,1)}) %reduce-scatter.4.cloned.1.call-update) | async-done | bytes 32784 | tf_op jit(solution)/shard_map/reduce_scatter | solution.py:40
  101.5 1.0 fusion.11
  102.4 1.5 fusion.14
  103.9 660.3 %reduce-scatter.8.cloned.1.call-done = bf16[64,448]{1,0:T(8,128)(2,1)} async-done(((bf16[2048,448]{1,0:T(8,128)(2,1)}), bf16[64,448]{1,0:T(8,128)(2,1)}) %reduce-scatter.8.cloned.1.call-update) | async-done | bytes 57360 | tf_op jit(solution)/shard_map/reduce_scatter | solution.py:59
  764.1 649.1 %reduce-scatter.6.cloned.1.call-done = bf16[64,448]{1,0:T(8,128)(2,1)} async-done(((bf16[2048,448]{1,0:T(8,128)(2,1)}), bf16[64,448]{1,0:T(8,128)(2,1)}) %reduce-scatter.6.cloned.1.call-update) | async-done | bytes 57360 | tf_op jit(solution)/shard_map/reduce_scatter | solution.py:56
  (3 shorter events, 0.0 us)
Async XLA Ops:
  7.2 24.9 %copy-start = (bf16[2048,448]{0,1:T(8,128)(2,1)S(1)}, bf16[2048,448]{0,1:T(8,128)(2,1)}, u32[]{:S(2)}) copy-start(bf16[2048,448]{0,1:T(8,128)(2,1)} %param.7) | copy-start | bytes 5505028
  7.2 26.3 %copy-start.4 = (f32[2048]{0:T(1024)S(1)}, f32[2048]{0:T(1024)}, u32[]{:S(2)}) copy-start(f32[2048]{0:T(1024)} %param.6) | copy-start | bytes 24580
  7.2 26.3 %copy-start.3 = (bf16[128,448]{0,1:T(8,128)(2,1)S(1)}, bf16[128,448]{0,1:T(8,128)(2,1)}, u32[]{:S(2)}) copy-start(bf16[128,448]{0,1:T(8,128)(2,1)} %param.9) | copy-start | bytes 344068
  7.2 94.3 %reduce-scatter.4.cloned.1.call-start = ((), (), s32[]{:S(2)}) async-start(), calls=%async_computation.3 | async-start | bytes 557056 | tf_op jit(solution)/shard_map/reduce_scatter | solution.py:40
  7.2 26.3 %copy-start.1 = (bf16[2048,448]{0,1:T(8,128)(2,1)S(1)}, bf16[2048,448]{0,1:T(8,128)(2,1)}, u32[]{:S(2)}) copy-start(bf16[2048,448]{0,1:T(8,128)(2,1)} %param.8) | copy-start | bytes 5505028
  36.1 728.1 %reduce-scatter.8.cloned.1.call-start = ((), (), s32[]{:S(2)}) async-start(), calls=%async_computation.5 | async-start | bytes 2162688 | tf_op jit(solution)/shard_map/reduce_scatter | solution.py:59
  38.3 2.3 copy-start.2
  38.3 1375.0 %reduce-scatter.6.cloned.1.call-start = ((), (), s32[]{:S(2)}) async-start(), calls=%async_computation.4 | async-start | bytes 2162688 | tf_op jit(solution)/shard_map/reduce_scatter | solution.py:56
Sparse Core Ops, SparseCore 0:
  36.2 65.2 reduce-scatter.3
  107.1 657.0 reduce-scatter.7
  769.7 643.4 reduce-scatter.5
where the time goes:
time: 1430 us; the launch traced here: 1420 us
  waiting for transfers between devices  1370 us (96%)
  blocking collectives  24.6 us (2%)
    reduce_scatter x1, waiting for transfers between devices, shards(): lax.psum_scatter(up_part.astype(jnp.bfloat16), 'dp', scatter_dimension=0,...  660 us
    reduce_scatter x1, waiting for transfers between devices, shards(): lax.psum_scatter(gate_part.astype(jnp.bfloat16), 'dp', scatter_dimension=...  649 us
    reduce_scatter x1, waiting for transfers between devices, shards(): lax.psum_scatter((contract_last(gate_grad, gate_weight) + contract_last(u...  60.8 us
  transfers between devices with their start and end apart: 3, of which 3 were waited for; matrix products, arithmetic and copies ran while one was open for 0% of the time, Pallas kernels for 0%

commit v1 on v0

v1 whole, which is shorter than its diff:
```python
import jax
import jax.numpy as jnp
from jax import lax
from jax.sharding import Mesh
from jax.sharding import PartitionSpec as P

EPSILON = 1e-05
DP = ("z", "yh")
TENSOR = ("x", "yl", "core")


def normalize(residual):
    values = residual.astype(jnp.float32)
    inverse = lax.rsqrt(jnp.mean(values * values, axis=-1, keepdims=True) + EPSILON)
    return (values * inverse, inverse)


def contract_last(left, right):
    return lax.dot_general(
        left, right, (((1,), (1,)), ((), ())), preferred_element_type=jnp.float32
    )


def contract_first(left, right):
    return lax.dot_general(
        left, right, (((0,), (0,)), ((), ())), preferred_element_type=jnp.float32
    )


def gather_rows(block, axes, count):
    copies = jnp.broadcast_to(block[None], (count,) + block.shape)
    return lax.all_to_all(copies, axes, 0, 0, tiled=True).reshape(
        (count * block.shape[0],) + block.shape[1:]
    )


def scatter_sum(partial, axes, count):
    blocks = partial.reshape((count, partial.shape[0] // count) + partial.shape[1:])
    moved = lax.all_to_all(blocks, axes, 0, 0, tiled=True)
    return jnp.sum(moved.astype(jnp.float32), axis=0)


def shards(residual, norm_gain, gate_weight, up_weight, hidden_grad):
    n_tensor = lax.axis_size(TENSOR)
    scaled, inverse = normalize(residual)
    gathered = gather_rows(residual, TENSOR, n_tensor)
    normed = (normalize(gathered)[0] * norm_gain).astype(jnp.bfloat16)
    gate_value = jnp.dot(normed, gate_weight, preferred_element_type=jnp.float32)
    up_value = jnp.dot(normed, up_weight, preferred_element_type=jnp.float32)
    sigmoid_gate = jax.nn.sigmoid(gate_value)
    upstream = hidden_grad.astype(jnp.float32)
    up_grad = (upstream * gate_value * sigmoid_gate).astype(jnp.bfloat16)
    gate_grad = (
        upstream * up_value * sigmoid_gate * (1.0 + gate_value * (1.0 - sigmoid_gate))
    ).astype(jnp.bfloat16)
    factor = float(normed.shape[0] * lax.axis_size(DP)) ** (-0.5)
    both = jnp.concatenate([gate_grad, up_grad], axis=1)
    part = (contract_first(normed, both) * factor).astype(jnp.bfloat16)
    over_z = lax.psum_scatter(part, "z", scatter_dimension=0, tiled=True)
    total = scatter_sum(over_z, "yh", lax.axis_size("yh")).astype(jnp.bfloat16)
    width = gate_grad.shape[1]
    normed_grad = scatter_sum(
        (contract_last(gate_grad, gate_weight) + contract_last(up_grad, up_weight)).astype(
            jnp.bfloat16
        ),
        TENSOR,
        n_tensor,
    )
    weighted = normed_grad * norm_gain
    residual_grad = (
        (weighted - scaled * jnp.mean(weighted * scaled, axis=-1, keepdims=True)) * inverse
    ).astype(jnp.bfloat16)
    return (residual_grad, total[:, :width], total[:, width:])


def solution(mesh):
    fine = Mesh(mesh.devices.reshape(16, 2, 4, 2, 2), DP + TENSOR)
    return jax.shard_map(
        shards,
        mesh=fine,
        in_specs=(
            P(DP + TENSOR, None),
            P(),
            P(None, TENSOR),
            P(None, TENSOR),
            P(DP, TENSOR),
        ),
        out_specs=(P(DP + TENSOR, None), P(DP, TENSOR), P(DP, TENSOR)),
        check_vma=False,
    )
```

time: 1430 us -> 129 us (0.09)
  the two profiles are of different devices: /device:TPU:1 before, /device:TPU:4 now
where the time goes in v1:
time: 129 us
  waiting for transfers between devices  76.6 us (59%)
  blocking collectives  16.8 us (13%)
  between operations  14.1 us (11%)
  starting transfers between devices  10.4 us (8%)
  matrix products  6.24 us (5%)
  local copies, waits for them, and re-layouts  3.53 us (3%)
  other arithmetic  1.35 us (1%)
    reduce_scatter x1, waiting for transfers between devices, shards(): over_z = lax.psum_scatter(part, 'z', scatter_dimension=0, tiled=True)  62.5 us
    all_to_all x1, blocking collectives, gather_rows(): lax.all_to_all(copies, axes, 0, 0, tiled=True)  16.8 us
    all_to_all x2, waiting for transfers between devices, scatter_sum(): moved = lax.all_to_all(blocks, axes, 0, 0, tiled=True)  14.1 us
    all_to_all x2, starting transfers between devices, scatter_sum(): moved = lax.all_to_all(blocks, axes, 0, 0, tiled=True)  10.3 us
    dot_general x1, matrix products, contract_first(): lax.dot_general(left, right, (((0,), (0,)), ((), ())), preferred_element_...  3.02 us
  transfers between devices with their start and end apart: 3, of which 3 were waited for; matrix products, arithmetic and copies ran while one was open for 2% of the time, Pallas kernels for 0%

profile of v1, /device:TPU:4, one launch (start us, length us, event | category | flops | bytes accessed | tf_op | source)
XLA Modules:
  0.0 129.0 jit_solution(8708259690438918469)
XLA Ops:
  7.2 0.0 copy-start
  7.2 0.0 copy-start.4
  7.2 0.0 copy-start.5
  7.2 0.0 reduce-scatter.2.cloned.1.call-start
  7.2 0.9 broadcast_in_dim.2
  8.2 16.8 %all_to_all.15 = bf16[16,8,2048]{2,1,0:T(8,128)(2,1)S(1)} all-to-all(bf16[16,8,2048]{2,1,0:T(8,128)(2,1)S(1)} %broadcast_in_dim.2), channel_id=1, replica_groups=mesh['z'=16,'yh'=2,'x'=4,'yl'=2,'core'=2] {'x','yl','core'}, dimensions={0} | all-to-all | bytes 1048576 | tf_op jit(solution)/shard_map/all_to_all | solution.py:32
  24.9 0.2 fusion.8
  25.1 0.1 rsqrt.20
  25.2 0.0 copy-done
  25.2 0.0 copy-done.4
  25.2 0.0 copy-done.5
  25.3 0.0 copy-start.1
  25.3 0.7 fusion.10
  26.0 0.7 copy-done.1
  26.8 0.7 fusion.4
  27.5 3.0 %multiply_convert_fusion = bf16[2048,896]{1,0:T(8,128)(2,1)} fusion(bf16[128,448]{0,1:T(8,128)(2,1)S(1)} %get-tuple-element.5, bf16[128,448]{0,1:T(8,128)(2,1)S(1)} %fusion.4, bf16[16,8,2048]{2,1,0:T(8,128)(2,1)S(1)} %all_to_all.15, f32[2048]{0:T(1024)S(1)} %copy-done.4, f32[128]{0:T(128)S(1)} %rsqrt.20), kind=kOutput, calls=%fused_computation | convolution fusion | flops 474939392 | bytes 4432384 | tf_op jit(solution)/shard_map/dot_general | solution.py:25
  30.5 0.0 reduce-scatter.2.cloned.1.call-update
  30.5 0.0 copy-start.2
  30.5 0.5 fusion.27
  31.0 1.0 copy-done.2
  32.0 0.0 copy-start.3
  32.0 1.3 fusion.1
  33.3 6.0 %all-to-all-start.1 = ((bf16[16,8,2048]{2,1,0:T(8,128)(2,1)}), bf16[16,8,2048]{2,1,0:T(8,128)(2,1)S(1)}, u32[]{:S(2)}, u32[]{:S(2)}) async-start(bf16[16,8,2048]{2,1,0:T(8,128)(2,1)} %fusion.1), calls=%async_computation.1 | async-start | bytes 1048576 | tf_op jit(solution)/shard_map/all_to_all | solution.py:39
  39.3 0.0 copy-done.3
  39.3 0.1 fusion.20
  39.5 8.2 %all-to-all-done.1 = bf16[16,8,2048]{2,1,0:T(8,128)(2,1)S(1)} async-done(((bf16[16,8,2048]{2,1,0:T(8,128)(2,1)}), bf16[16,8,2048]{2,1,0:T(8,128)(2,1)S(1)}, u32[]{:S(2)}, u32[]{:S(2)}) %all-to-all-start.1) | async-done | bytes 524320 | tf_op jit(solution)/shard_map/all_to_all | solution.py:39
  47.7 0.1 convert_reduce_fusion
  47.8 0.2 fusion.16
  48.0 62.5 %reduce-scatter.2.cloned.1.call-done = bf16[128,896]{1,0:T(8,128)(2,1)} async-done(((bf16[2048,896]{1,0:T(8,128)(2,1)}), bf16[128,896]{1,0:T(8,128)(2,1)}) %reduce-scatter.2.cloned.1.call-update) | async-done | bytes 229392 | tf_op jit(solution)/shard_map/reduce_scatter | solution.py:59
  110.6 4.3 %all-to-all-start.2 = ((bf16[2,64,896]{2,1,0:T(8,128)(2,1)}), bf16[2,64,896]{2,1,0:T(8,128)(2,1)S(1)}, u32[]{:S(2)}, u32[]{:S(2)}) async-start(bf16[2,64,896]{2,1,0:T(8,128)(2,1)} %bitcast.22), calls=%async_computation.3 | async-start | bytes 458752 | tf_op jit(solution)/shard_map/all_to_all | solution.py:39
  114.9 0.7 fusion.19
  115.6 5.8 %all-to-all-done.2 = bf16[2,64,896]{2,1,0:T(8,128)(2,1)S(1)} async-done(((bf16[2,64,896]{2,1,0:T(8,128)(2,1)}), bf16[2,64,896]{2,1,0:T(8,128)(2,1)S(1)}, u32[]{:S(2)}, u32[]{:S(2)}) %all-to-all-start.2) | async-done | bytes 229408 | tf_op jit(solution)/shard_map/all_to_all | solution.py:39
  121.4 0.7 fusion.26
  (4 shorter events, 0.1 us)
Async XLA Ops:
  7.2 18.1 %copy-start = (bf16[2048,448]{0,1:T(8,128)(2,1)S(1)}, bf16[2048,448]{0,1:T(8,128)(2,1)}, u32[]{:S(2)}) copy-start(bf16[2048,448]{0,1:T(8,128)(2,1)} %param.7) | copy-start | bytes 5505028
  7.2 18.1 %copy-start.4 = (f32[2048]{0:T(1024)S(1)}, f32[2048]{0:T(1024)}, u32[]{:S(2)}) copy-start(f32[2048]{0:T(1024)} %param.6) | copy-start | bytes 24580
  7.2 18.1 %copy-start.5 = (bf16[128,448]{0,1:T(8,128)(2,1)S(1)}, bf16[128,448]{0,1:T(8,128)(2,1)}, u32[]{:S(2)}) copy-start(bf16[128,448]{0,1:T(8,128)(2,1)} %param.9) | copy-start | bytes 344068
  7.2 103.4 %reduce-scatter.2.cloned.1.call-start = ((), (), s32[]{:S(2)}) async-start(), calls=%async_computation.4 | async-start | bytes 3899392 | tf_op jit(solution)/shard_map/reduce_scatter | solution.py:59
  25.3 1.5 %copy-start.1 = (bf16[2048,448]{0,1:T(8,128)(2,1)S(1)}, bf16[2048,448]{0,1:T(8,128)(2,1)}, u32[]{:S(2)}) copy-start(bf16[2048,448]{0,1:T(8,128)(2,1)} %param.8) | copy-start | bytes 5505028
  30.5 1.5 %copy-start.2 = (bf16[2048,448]{0,1:T(8,128)(2,1)S(1)}, bf16[2048,448]{0,1:T(8,128)(2,1)}, u32[]{:S(2)}) copy-start(bf16[2048,448]{0,1:T(8,128)(2,1)} %param.8) | copy-start | bytes 5505028
  32.0 7.3 %copy-start.3 = (bf16[8,2048]{1,0:T(8,128)(2,1)S(1)}, bf16[8,2048]{1,0:T(8,128)(2,1)}, u32[]{:S(2)}) copy-start(bf16[8,2048]{1,0:T(8,128)(2,1)} %param.5) | copy-start | bytes 98308
  33.3 14.4 %all-to-all-start.1 = ((bf16[16,8,2048]{2,1,0:T(8,128)(2,1)}), bf16[16,8,2048]{2,1,0:T(8,128)(2,1)S(1)}, u32[]{:S(2)}, u32[]{:S(2)}) async-start(bf16[16,8,2048]{2,1,0:T(8,128)(2,1)} %fusion.1), calls=%async_computation.1 | async-start | bytes 1048576 | tf_op jit(solution)/shard_map/all_to_all | solution.py:39
  110.6 10.8 %all-to-all-start.2 = ((bf16[2,64,896]{2,1,0:T(8,128)(2,1)}), bf16[2,64,896]{2,1,0:T(8,128)(2,1)S(1)}, u32[]{:S(2)}, u32[]{:S(2)}) async-start(bf16[2,64,896]{2,1,0:T(8,128)(2,1)} %bitcast.22), calls=%async_computation.3 | async-start | bytes 458752 | tf_op jit(solution)/shard_map/all_to_all | solution.py:39
Sparse Core Ops, SparseCore 0:
  30.6 79.8 reduce-scatter.1

commit v2 on v1

v2 whole, which is shorter than its diff:
```python
import functools

import jax
import jax.numpy as jnp
from jax import lax
from jax.experimental import pallas as pl
from jax.experimental.pallas import tpu as pltpu
from jax.sharding import Mesh
from jax.sharding import PartitionSpec as P

EPSILON = 1e-05
DP = ("z", "yh")
TENSOR = ("x", "yl", "core")
HUBS = (-6, -3, 0, 3, 6)


def normalize(residual):
    values = residual.astype(jnp.float32)
    inverse = lax.rsqrt(jnp.mean(values * values, axis=-1, keepdims=True) + EPSILON)
    return (values * inverse, inverse)


def contract_last(left, right):
    return lax.dot_general(
        left, right, (((1,), (1,)), ((), ())), preferred_element_type=jnp.float32
    )


def contract_first(left, right):
    return lax.dot_general(
        left, right, (((0,), (0,)), ((), ())), preferred_element_type=jnp.float32
    )


def local_kernel(
    factor,
    nz,
    rows_ref,
    gain_ref,
    gate_ref,
    up_ref,
    own_ref,
    other_ref,
    ahead_ref,
    behind_ref,
    far_ref,
    hub_ref,
    gate_own_ref,
    up_own_ref,
    normed_ref,
    grads_ref,
):
    z = lax.axis_index("z")
    half = lax.axis_index("yh")
    rows = own_ref.shape[1]
    width = own_ref.shape[0]
    scaled = normalize(rows_ref[...])[0]
    normed_ref[...] = (scaled * gain_ref[...]).astype(jnp.bfloat16)
    normed = normed_ref[...]
    gate_value = contract_last(normed, gate_ref[...])
    up_value = contract_last(normed, up_ref[...])
    own = own_ref[...].astype(jnp.float32).T
    other = other_ref[...].astype(jnp.float32).T
    first = half == 0
    upstream = jnp.concatenate(
        [jnp.where(first, own, other), jnp.where(first, other, own)], axis=0
    )
    sigmoid_gate = jax.nn.sigmoid(gate_value)
    weighted = upstream * sigmoid_gate
    grads_ref[:, width:] = (weighted * gate_value).astype(jnp.bfloat16)
    grads_ref[:, :width] = (
        weighted * up_value * (1.0 + gate_value * (1.0 - sigmoid_gate))
    ).astype(jnp.bfloat16)
    start = pl.multiple_of(half * rows, rows)
    gate_own_ref[...] = grads_ref[pl.ds(start, rows), :width]
    up_own_ref[...] = grads_ref[pl.ds(start, rows), width:]
    grads = grads_ref[...]
    depth = far_ref.shape[0]

    def block(relative):
        chunk = lax.rem(z - relative + 2 * nz, nz)
        lanes = pl.ds(pl.multiple_of(chunk * 2 * depth, 2 * depth), 2 * depth)
        both = contract_first(normed_ref[:, lanes], grads) * factor
        return jnp.where(first, both[:depth], both[depth:]).astype(jnp.bfloat16)

    for at, hub in enumerate(HUBS):
        ahead_ref[at] = block(hub - 1)
        behind_ref[at] = block(hub + 1)
    far_ref[...] = block(nz // 2)
    for at, hub in enumerate(HUBS):
        hub_ref[at] = block(hub)


def shift(value, hops, nz):
    return lax.ppermute(value, "z", [(i, (i + hops) % nz) for i in range(nz)])


def shards(residual, norm_gain, gate_weight, up_weight, hidden_grad):
    nz, nh, nt = lax.axis_size("z"), lax.axis_size("yh"), lax.axis_size(TENSOR)
    rows, width = hidden_grad.shape
    features = residual.shape[1]
    depth = features // (nz * nh)
    f32, bf16 = jnp.float32, jnp.bfloat16
    own = hidden_grad.T
    other = lax.ppermute(own, "yh", [(0, 1), (1, 0)])
    copies = jnp.broadcast_to(residual[None], (nh * nt,) + residual.shape)
    gathered = lax.all_to_all(copies, ("yh",) + TENSOR, 0, 0, tiled=True)
    gathered = gathered.reshape(nh * rows, features)
    factor = float(rows * nz * nh) ** (-0.5)
    shape = jax.ShapeDtypeStruct
    hubs = len(HUBS)
    ahead, behind, far, hub, gate_own, up_own = pl.pallas_call(
        functools.partial(local_kernel, factor, nz),
        out_shape=(
            shape((hubs, depth, 2 * width), bf16),
            shape((hubs, depth, 2 * width), bf16),
            shape((depth, 2 * width), bf16),
            shape((hubs, depth, 2 * width), bf16),
            shape((rows, width), bf16),
            shape((rows, width), bf16),
        ),
        scratch_shapes=[
            pltpu.VMEM((nh * rows, features), bf16),
            pltpu.VMEM((nh * rows, 2 * width), bf16),
        ],
        compiler_params=pltpu.CompilerParams(vmem_limit_bytes=40 * 1024 * 1024),
        cost_estimate=pl.CostEstimate(
            flops=8 * nh * rows * features * width,
            bytes_accessed=8 * features * width,
            transcendentals=nh * rows * width,
        ),
        name="local",
    )(gathered, norm_gain.reshape(1, features), gate_weight.T, up_weight.T, own, other)

    from_behind = shift(ahead, 1, nz)
    from_ahead = shift(behind, -1, nz)
    from_far = shift(far, -2, nz)

    part = (contract_last(gate_own, gate_weight) + contract_last(up_own, up_weight)).astype(bf16)
    blocks = part.reshape(nt, rows // nt, features)
    moved = lax.all_to_all(blocks, TENSOR, 0, 0, tiled=True)

    sums = hub.astype(f32) + from_behind.astype(f32) + from_ahead.astype(f32)
    last = (sums[hubs - 1] + from_far.astype(f32)).astype(bf16)
    total = sums[2]
    total = total + shift(sums[0].astype(bf16), 6, nz).astype(f32)
    total = total + shift(sums[1].astype(bf16), 3, nz).astype(f32)
    total = total + shift(sums[3].astype(bf16), -3, nz).astype(f32)
    total = total + shift(last, -6, nz).astype(f32)
    total = total.astype(bf16)

    scaled, inverse = normalize(residual)
    normed_grad = jnp.sum(moved.astype(f32), axis=0)
    weighted = normed_grad * norm_gain
    residual_grad = (
        (weighted - scaled * jnp.mean(weighted * scaled, axis=-1, keepdims=True)) * inverse
    ).astype(bf16)
    return (residual_grad, total[:, :width], total[:, width:])


def solution(mesh):
    fine = Mesh(mesh.devices.reshape(16, 2, 4, 2, 2), DP + TENSOR)
    return jax.shard_map(
        shards,
        mesh=fine,
        in_specs=(
            P(DP + TENSOR, None),
            P(),
            P(None, TENSOR),
            P(None, TENSOR),
            P(DP, TENSOR),
        ),
        out_specs=(P(DP + TENSOR, None), P(DP, TENSOR), P(DP, TENSOR)),
        check_vma=False,
    )
```

time: 129 us -> 114 us (0.88)
  the two profiles are of different devices: /device:TPU:4 before, /device:TPU:2 now
where the time goes in v2:
time: 114 us
  starting transfers between devices  55.2 us (48%)
  waiting for transfers between devices  43.7 us (38%)
  local copies, waits for them, and re-layouts  7.31 us (6%)
  Pallas kernels  3.3 us (3%)
  matrix products  1.7 us (1%)
  other arithmetic  1.44 us (1%)
    ppermute x7, starting transfers between devices, shift(): return lax.ppermute(value, 'z', [(i, (i + hops) % nz) for i in range(nz)])  36.1 us
    ppermute x7, waiting for transfers between devices, shift(): return lax.ppermute(value, 'z', [(i, (i + hops) % nz) for i in range(nz)])  30.1 us
    ppermute x1, waiting for transfers between devices, shards(): other = lax.ppermute(own, 'yh', [(0, 1), (1, 0)])  13.6 us
    all_to_all x1, starting transfers between devices, shards(): gathered = lax.all_to_all(copies, ('yh',) + TENSOR, 0, 0, tiled=True)  9.51 us
    ppermute x1, starting transfers between devices, shards(): other = lax.ppermute(own, 'yh', [(0, 1), (1, 0)])  4.98 us
    all_to_all x1, starting transfers between devices, shards(): moved = lax.all_to_all(blocks, TENSOR, 0, 0, tiled=True)  4.64 us
    unnamed x24, local copies, waits for them, and re-layouts  4.56 us
    pallas_call x1, Pallas kernels, shards(): pl.pallas_call(functools.partial(local_kernel, factor, nz), out_shape=(sh...  3.3 us
  transfers between devices with their start and end apart: 10, of which 6 were waited for; matrix products, arithmetic and copies ran while one was open for 1% of the time, Pallas kernels for 0%

profile of v2, /device:TPU:2, one launch (start us, length us, event | category | flops | bytes accessed | tf_op | source)
XLA Modules:
  0.0 113.6 jit_solution(820501008360886056)
XLA Ops:
  0.6 0.0 copy-start.6
  0.6 0.0 copy-start.2
  0.7 0.0 copy-start
  0.7 2.0 %broadcast_in_dim.2 = bf16[32,8,2048]{2,1,0:T(8,128)(2,1)} broadcast(bf16[8,2048]{1,0:T(8,128)(2,1)} %param.5), dimensions={1,2} | broadcast | bytes 1081344 | tf_op jit(solution)/shard_map/broadcast_in_dim | solution.py:106
  2.7 9.5 %all-to-all-start = ((bf16[32,8,2048]{2,1,0:T(8,128)(2,1)}), bf16[32,8,2048]{2,1,0:T(8,128)(2,1)S(1)}, u32[]{:S(2)}, u32[]{:S(2)}) async-start(bf16[32,8,2048]{2,1,0:T(8,128)(2,1)} %broadcast_in_dim.2), calls=%async_computation | async-start | bytes 2097152 | tf_op jit(solution)/shard_map/all_to_all | solution.py:107
  12.2 0.0 copy-done.6
  12.2 5.0 %collective-permute-start = (bf16[448,128]{1,0:T(8,128)(2,1)S(1)}, bf16[448,128]{1,0:T(8,128)(2,1)S(1)}, u32[]{:S(2)}, u32[]{:S(2)}) collective-permute-start(bf16[448,128]{1,0:T(8,128)(2,1)S(1)} %bitcast.39), channel_id=1, source_target_pairs={{0,16},{16,0},{1,17},{17,1},{2,18},{18,2},{3,19},{19,3},{4,20},{20... | collective-permute-start | bytes 344072 | tf_op jit(solution)/shard_map/ppermute | solution.py:105
  17.2 13.6 %collective-permute-done.other_ref = bf16[448,128]{1,0:T(8,128)(2,1)S(1)} collective-permute-done((bf16[448,128]{1,0:T(8,128)(2,1)S(1)}, bf16[448,128]{1,0:T(8,128)(2,1)S(1)}, u32[]{:S(2)}, u32[]{:S(2)}) %collective-permute-start) | collective-permute-done | bytes 114720 | tf_op jit(solution)/shard_map/ppermute | solution.py:105
  30.8 0.0 copy-start.9
  30.8 0.6 copy-done.9
  31.4 0.0 all-to-all-done
  31.4 0.0 copy-done.2
  31.4 0.0 copy-done
  31.4 0.0 copy-start.1
  31.5 1.5 %copy-done.1 = bf16[2048,448]{0,1:T(8,128)(2,1)S(1)} copy-done((bf16[2048,448]{0,1:T(8,128)(2,1)S(1)}, bf16[2048,448]{0,1:T(8,128)(2,1)}, u32[]{:S(2)}) %copy-start.1) | copy-done | bytes 1835032
  33.0 0.0 copy-start.7
  33.0 0.9 copy-done.7
  33.9 0.0 copy-start.10
  33.9 0.9 copy-done.10
  34.8 3.3 %local.1 = (bf16[5,64,896]{2,1,0:T(8,128)(2,1)S(1)}, bf16[5,64,896]{2,1,0:T(8,128)(2,1)S(1)}, bf16[64,896]{1,0:T(8,128)(2,1)S(1)}, bf16[5,64,896]{2,1,0:T(8,128)...) custom-call(bf16[256,2048]{1,0:T(8,128)(2,1)S(1)} %bitcast.37, f32[1,2048]{1,0:T(1,128)S(1)} %bitcast.38, ...), custom_call_target="tpu_custom_call" | custom-call | flops 1879048192 | bytes 7340032 | tf_op jit(solution)/shard_map/local/pallas_call | solution.py:112
  38.1 0.0 copy-start.3
  38.1 0.0 copy-start.5
  38.1 0.0 copy-start.8
  38.1 0.4 fusion.18
  38.5 0.3 copy-done.3
  38.9 0.2 copy-done.5
  39.1 0.0 copy-done.8
  39.1 0.0 copy-start.11
  39.1 0.0 copy-start.4
  39.1 1.3 %fusion.1 = bf16[16,8,2048]{2,1,0:T(8,128)(2,1)} fusion(f32[128,2048]{1,0:T(8,128)S(1)} %fusion.18, bf16[128,448]{1,0:T(8,128)(2,1)S(1)} %get-tuple-element.9, bf16[2048,448]{0,1:T(8,128)(2,1)S(1)} %copy-done), kind=kOutput, calls=%fused_computation.2 | convolution fusion | flops 235405312 | bytes 3522560 | tf_op jit(solution)/shard_map/dot_general | solution.py:24
  40.4 4.6 %all-to-all-start.1 = ((bf16[16,8,2048]{2,1,0:T(8,128)(2,1)}), bf16[16,8,2048]{2,1,0:T(8,128)(2,1)S(1)}, u32[]{:S(2)}, u32[]{:S(2)}) async-start(bf16[16,8,2048]{2,1,0:T(8,128)(2,1)} %fusion.1), calls=%async_computation.1 | async-start | bytes 1048576 | tf_op jit(solution)/shard_map/all_to_all | solution.py:141
  45.0 0.0 copy-done.11
  45.0 0.1 fusion.15
  45.2 9.4 %collective-permute-start.2 = (bf16[5,64,896]{2,1,0:T(8,128)(2,1)}, bf16[5,64,896]{2,1,0:T(8,128)(2,1)S(1)}, u32[]{:S(2)}, u32[]{:S(2)}) collective-permute-start(bf16[5,64,896]{2,1,0:T(8,128)(2,1)} %copy-done.5), channel_id=1, source_target_pairs={{0,480},{32,0},{64,32},{96,64},{128,96},{160,128},{192,160},{224,1... | collective-permute-start | bytes 1720328 | tf_op jit(solution)/shard_map/ppermute | solution.py:95
  54.6 0.0 copy-done.4
  54.6 1.9 %collective-permute-start.1 = (bf16[5,64,896]{2,1,0:T(8,128)(2,1)S(1)}, bf16[5,64,896]{2,1,0:T(8,128)(2,1)S(1)}, u32[]{:S(2)}, u32[]{:S(2)}) collective-permute-start(bf16[5,64,896]{2,1,0:T(8,128)(2,1)S(1)} %copy-done.4), channel_id=1, source_target_pairs={{0,32},{32,64},{64,96},{96,128},{128,160},{160,192},{192,224},{224... | collective-permute-start | bytes 1720328 | tf_op jit(solution)/shard_map/ppermute | solution.py:95
  56.5 4.4 %collective-permute-start.6 = (bf16[64,896]{1,0:T(8,128)(2,1)}, bf16[64,896]{1,0:T(8,128)(2,1)S(1)}, u32[]{:S(2)}, u32[]{:S(2)}) collective-permute-start(bf16[64,896]{1,0:T(8,128)(2,1)} %copy-done.8), channel_id=1, source_target_pairs={{0,448},{32,480},{64,0},{96,32},{128,64},{160,96},{192,128},{224,1... | collective-permute-start | bytes 344072 | tf_op jit(solution)/shard_map/ppermute | solution.py:95
  60.9 0.0 all-to-all-done.1
  60.9 0.1 convert_reduce_fusion
  61.0 0.2 fusion.11
  61.2 9.5 %collective-permute-done.2 = bf16[5,64,896]{2,1,0:T(8,128)(2,1)S(1)} collective-permute-done((bf16[5,64,896]{2,1,0:T(8,128)(2,1)}, bf16[5,64,896]{2,1,0:T(8,128)(2,1)S(1)}, u32[]{:S(2)}, u32[]{:S(2)}) %collective-permute-start.2) | collective-permute-done | bytes 573472 | tf_op jit(solution)/shard_map/ppermute | solution.py:95
  70.7 1.8 %collective-permute-done.1 = bf16[5,64,896]{2,1,0:T(8,128)(2,1)S(1)} collective-permute-done((bf16[5,64,896]{2,1,0:T(8,128)(2,1)S(1)}, bf16[5,64,896]{2,1,0:T(8,128)(2,1)S(1)}, u32[]{:S(2)}, u32[]{:S(2)}) %collective-permute-start.1) | collective-permute-done | bytes 573472 | tf_op jit(solution)/shard_map/ppermute | solution.py:95
  72.5 0.2 fusion.16
  72.7 0.0 collective-permute-done.6
  72.7 9.0 %collective-permute-start.7 = (bf16[64,896]{1,0:T(8,128)(2,1)S(1)}, bf16[64,896]{1,0:T(8,128)(2,1)S(1)}, u32[]{:S(2)}, u32[]{:S(2)}) collective-permute-start(bf16[64,896]{1,0:T(8,128)(2,1)S(1)} %fusion.3), channel_id=1, source_target_pairs={{0,320},{32,352},{64,384},{96,416},{128,448},{160,480},{192,0},{22... | collective-permute-start | bytes 344072 | tf_op jit(solution)/shard_map/ppermute | solution.py:95
  81.8 2.1 %collective-permute-start.5 = (bf16[64,896]{1,0:T(8,128)(2,1)S(1)}, bf16[64,896]{1,0:T(8,128)(2,1)S(1)}, u32[]{:S(2)}, u32[]{:S(2)}) collective-permute-start(bf16[64,896]{1,0:T(8,128)(2,1)S(1)} %get-tuple-element.18), channel_id=1, source_target_pairs={{0,416},{32,448},{64,480},{96,0},{128,32},{160,64},{192,96},{224,1... | collective-permute-start | bytes 344072 | tf_op jit(solution)/shard_map/ppermute | solution.py:95
  84.0 5.5 %collective-permute-start.4 = (bf16[64,896]{1,0:T(8,128)(2,1)S(1)}, bf16[64,896]{1,0:T(8,128)(2,1)S(1)}, u32[]{:S(2)}, u32[]{:S(2)}) collective-permute-start(bf16[64,896]{1,0:T(8,128)(2,1)S(1)} %get-tuple-element.19), channel_id=1, source_target_pairs={{0,96},{32,128},{64,160},{96,192},{128,224},{160,256},{192,288},{2... | collective-permute-start | bytes 344072 | tf_op jit(solution)/shard_map/ppermute | solution.py:95
  89.5 3.7 %collective-permute-start.3 = (bf16[64,896]{1,0:T(8,128)(2,1)S(1)}, bf16[64,896]{1,0:T(8,128)(2,1)S(1)}, u32[]{:S(2)}, u32[]{:S(2)}) collective-permute-start(bf16[64,896]{1,0:T(8,128)(2,1)S(1)} %get-tuple-element.17), channel_id=1, source_target_pairs={{0,192},{32,224},{64,256},{96,288},{128,320},{160,352},{192,384},{... | collective-permute-start | bytes 344072 | tf_op jit(solution)/shard_map/ppermute | solution.py:95
  93.2 0.7 fusion.14
  93.9 1.4 %collective-permute-done.7 = bf16[64,896]{1,0:T(8,128)(2,1)S(1)} collective-permute-done((bf16[64,896]{1,0:T(8,128)(2,1)S(1)}, bf16[64,896]{1,0:T(8,128)(2,1)S(1)}, u32[]{:S(2)}, u32[]{:S(2)}) %collective-permute-start.7) | collective-permute-done | bytes 114720 | tf_op jit(solution)/shard_map/ppermute | solution.py:95
  95.3 5.6 %collective-permute-done.5 = bf16[64,896]{1,0:T(8,128)(2,1)S(1)} collective-permute-done((bf16[64,896]{1,0:T(8,128)(2,1)S(1)}, bf16[64,896]{1,0:T(8,128)(2,1)S(1)}, u32[]{:S(2)}, u32[]{:S(2)}) %collective-permute-start.5) | collective-permute-done | bytes 114720 | tf_op jit(solution)/shard_map/ppermute | solution.py:95
  101.0 0.0 collective-permute-done.4
  101.0 11.8 %collective-permute-done.3 = bf16[64,896]{1,0:T(8,128)(2,1)S(1)} collective-permute-done((bf16[64,896]{1,0:T(8,128)(2,1)S(1)}, bf16[64,896]{1,0:T(8,128)(2,1)S(1)}, u32[]{:S(2)}, u32[]{:S(2)}) %collective-permute-start.3) | collective-permute-done | bytes 114720 | tf_op jit(solution)/shard_map/ppermute | solution.py:95
  112.8 0.1 fusion.8
  112.9 0.7 fusion.17
  (4 shorter events, 0.1 us)
Async XLA Ops:
  0.6 11.5 %copy-start.6 = (bf16[128,448]{0,1:T(8,128)(2,1)S(1)}, bf16[128,448]{0,1:T(8,128)(2,1)}, u32[]{:S(2)}) copy-start(bf16[128,448]{0,1:T(8,128)(2,1)} %param.9) | copy-start | bytes 344068
  0.6 30.8 %copy-start.2 = (f32[2048]{0:T(1024)S(1)}, f32[2048]{0:T(1024)}, u32[]{:S(2)}) copy-start(f32[2048]{0:T(1024)} %param.6) | copy-start | bytes 24580
  0.7 30.8 %copy-start = (bf16[2048,448]{0,1:T(8,128)(2,1)S(1)}, bf16[2048,448]{0,1:T(8,128)(2,1)}, u32[]{:S(2)}) copy-start(bf16[2048,448]{0,1:T(8,128)(2,1)} %param.7) | copy-start | bytes 5505028
  2.7 28.8 %all-to-all-start = ((bf16[32,8,2048]{2,1,0:T(8,128)(2,1)}), bf16[32,8,2048]{2,1,0:T(8,128)(2,1)S(1)}, u32[]{:S(2)}, u32[]{:S(2)}) async-start(bf16[32,8,2048]{2,1,0:T(8,128)(2,1)} %broadcast_in_dim.2), calls=%async_computation | async-start | bytes 2097152 | tf_op jit(solution)/shard_map/all_to_all | solution.py:107
  12.2 18.6 %collective-permute-start = (bf16[448,128]{1,0:T(8,128)(2,1)S(1)}, bf16[448,128]{1,0:T(8,128)(2,1)S(1)}, u32[]{:S(2)}, u32[]{:S(2)}) collective-permute-start(bf16[448,128]{1,0:T(8,128)(2,1)S(1)} %bitcast.39), channel_id=1, source_target_pairs={{0,16},{16,0},{1,17},{17,1},{2,18},{18,2},{3,19},{19,3},{4,20},{20... | collective-permute-start | bytes 344072 | tf_op jit(solution)/shard_map/ppermute | solution.py:105
  30.8 0.7 copy-start.9
  31.4 1.5 %copy-start.1 = (bf16[2048,448]{0,1:T(8,128)(2,1)S(1)}, bf16[2048,448]{0,1:T(8,128)(2,1)}, u32[]{:S(2)}) copy-start(bf16[2048,448]{0,1:T(8,128)(2,1)} %param.8) | copy-start | bytes 5505028
  33.0 0.9 copy-start.7
  33.9 0.9 copy-start.10
  38.1 0.8 copy-start.3
  38.1 1.0 copy-start.5
  38.1 1.0 copy-start.8
  39.1 5.9 %copy-start.11 = (bf16[8,2048]{1,0:T(8,128)(2,1)S(1)}, bf16[8,2048]{1,0:T(8,128)(2,1)}, u32[]{:S(2)}) copy-start(bf16[8,2048]{1,0:T(8,128)(2,1)} %param.5) | copy-start | bytes 98308
  39.1 15.5 %copy-start.4 = (bf16[5,64,896]{2,1,0:T(8,128)(2,1)S(1)}, bf16[5,64,896]{2,1,0:T(8,128)(2,1)}, u32[]{:S(2)}) copy-start(bf16[5,64,896]{2,1,0:T(8,128)(2,1)} %copy-done.3) | copy-start | bytes 1720324
  40.4 20.5 %all-to-all-start.1 = ((bf16[16,8,2048]{2,1,0:T(8,128)(2,1)}), bf16[16,8,2048]{2,1,0:T(8,128)(2,1)S(1)}, u32[]{:S(2)}, u32[]{:S(2)}) async-start(bf16[16,8,2048]{2,1,0:T(8,128)(2,1)} %fusion.1), calls=%async_computation.1 | async-start | bytes 1048576 | tf_op jit(solution)/shard_map/all_to_all | solution.py:141
  45.2 25.5 %collective-permute-start.2 = (bf16[5,64,896]{2,1,0:T(8,128)(2,1)}, bf16[5,64,896]{2,1,0:T(8,128)(2,1)S(1)}, u32[]{:S(2)}, u32[]{:S(2)}) collective-permute-start(bf16[5,64,896]{2,1,0:T(8,128)(2,1)} %copy-done.5), channel_id=1, source_target_pairs={{0,480},{32,0},{64,32},{96,64},{128,96},{160,128},{192,160},{224,1... | collective-permute-start | bytes 1720328 | tf_op jit(solution)/shard_map/ppermute | solution.py:95
  54.6 17.9 %collective-permute-start.1 = (bf16[5,64,896]{2,1,0:T(8,128)(2,1)S(1)}, bf16[5,64,896]{2,1,0:T(8,128)(2,1)S(1)}, u32[]{:S(2)}, u32[]{:S(2)}) collective-permute-start(bf16[5,64,896]{2,1,0:T(8,128)(2,1)S(1)} %copy-done.4), channel_id=1, source_target_pairs={{0,32},{32,64},{64,96},{96,128},{128,160},{160,192},{192,224},{224... | collective-permute-start | bytes 1720328 | tf_op jit(solution)/shard_map/ppermute | solution.py:95
  56.5 16.1 %collective-permute-start.6 = (bf16[64,896]{1,0:T(8,128)(2,1)}, bf16[64,896]{1,0:T(8,128)(2,1)S(1)}, u32[]{:S(2)}, u32[]{:S(2)}) collective-permute-start(bf16[64,896]{1,0:T(8,128)(2,1)} %copy-done.8), channel_id=1, source_target_pairs={{0,448},{32,480},{64,0},{96,32},{128,64},{160,96},{192,128},{224,1... | collective-permute-start | bytes 344072 | tf_op jit(solution)/shard_map/ppermute | solution.py:95
  72.7 22.6 %collective-permute-start.7 = (bf16[64,896]{1,0:T(8,128)(2,1)S(1)}, bf16[64,896]{1,0:T(8,128)(2,1)S(1)}, u32[]{:S(2)}, u32[]{:S(2)}) collective-permute-start(bf16[64,896]{1,0:T(8,128)(2,1)S(1)} %fusion.3), channel_id=1, source_target_pairs={{0,320},{32,352},{64,384},{96,416},{128,448},{160,480},{192,0},{22... | collective-permute-start | bytes 344072 | tf_op jit(solution)/shard_map/ppermute | solution.py:95
  81.8 19.1 %collective-permute-start.5 = (bf16[64,896]{1,0:T(8,128)(2,1)S(1)}, bf16[64,896]{1,0:T(8,128)(2,1)S(1)}, u32[]{:S(2)}, u32[]{:S(2)}) collective-permute-start(bf16[64,896]{1,0:T(8,128)(2,1)S(1)} %get-tuple-element.18), channel_id=1, source_target_pairs={{0,416},{32,448},{64,480},{96,0},{128,32},{160,64},{192,96},{224,1... | collective-permute-start | bytes 344072 | tf_op jit(solution)/shard_map/ppermute | solution.py:95
  84.0 17.0 %collective-permute-start.4 = (bf16[64,896]{1,0:T(8,128)(2,1)S(1)}, bf16[64,896]{1,0:T(8,128)(2,1)S(1)}, u32[]{:S(2)}, u32[]{:S(2)}) collective-permute-start(bf16[64,896]{1,0:T(8,128)(2,1)S(1)} %get-tuple-element.19), channel_id=1, source_target_pairs={{0,96},{32,128},{64,160},{96,192},{128,224},{160,256},{192,288},{2... | collective-permute-start | bytes 344072 | tf_op jit(solution)/shard_map/ppermute | solution.py:95
  89.5 23.3 %collective-permute-start.3 = (bf16[64,896]{1,0:T(8,128)(2,1)S(1)}, bf16[64,896]{1,0:T(8,128)(2,1)S(1)}, u32[]{:S(2)}, u32[]{:S(2)}) collective-permute-start(bf16[64,896]{1,0:T(8,128)(2,1)S(1)} %get-tuple-element.17), channel_id=1, source_target_pairs={{0,192},{32,224},{64,256},{96,288},{128,320},{160,352},{192,384},{... | collective-permute-start | bytes 344072 | tf_op jit(solution)/shard_map/ppermute | solution.py:95

commit v3 on v2

--- a/solution.py
+++ b/solution.py
@@ -37,10 +37,10 @@
     nz,
     rows_ref,
     gain_ref,
-    gate_ref,
-    up_ref,
-    own_ref,
-    other_ref,
+    gate_src,
+    up_src,
+    own_src,
+    other_src,
     ahead_ref,
     behind_ref,
     far_ref,
@@ -49,7 +49,25 @@
     up_own_ref,
     normed_ref,
     grads_ref,
+    gate_ref,
+    up_ref,
+    own_ref,
+    other_ref,
+    sems,
 ):
+    copies = [
+        pltpu.make_async_copy(src, dst, sems.at[at])
+        for at, (src, dst) in enumerate(
+            (
+                (gate_src, gate_ref),
+                (up_src, up_ref),
+                (own_src, own_ref),
+                (other_src, other_ref),
+            )
+        )
+    ]
+    for copy in copies:
+        copy.start()
     z = lax.axis_index("z")
     half = lax.axis_index("yh")
     rows = own_ref.shape[1]
@@ -57,8 +75,12 @@
     scaled = normalize(rows_ref[...])[0]
     normed_ref[...] = (scaled * gain_ref[...]).astype(jnp.bfloat16)
     normed = normed_ref[...]
+    copies[0].wait()
     gate_value = contract_last(normed, gate_ref[...])
+    copies[1].wait()
     up_value = contract_last(normed, up_ref[...])
+    copies[2].wait()
+    copies[3].wait()
     own = own_ref[...].astype(jnp.float32).T
     other = other_ref[...].astype(jnp.float32).T
     first = half == 0
@@ -119,11 +141,18 @@
             shape((rows, width), bf16),
             shape((rows, width), bf16),
         ),
+        in_specs=[pl.BlockSpec(memory_space=pltpu.VMEM)] * 2
+        + [pl.BlockSpec(memory_space=pltpu.HBM)] * 4,
         scratch_shapes=[
             pltpu.VMEM((nh * rows, features), bf16),
             pltpu.VMEM((nh * rows, 2 * width), bf16),
+            pltpu.VMEM((width, features), bf16),
+            pltpu.VMEM((width, features), bf16),
+            pltpu.VMEM((width, rows), bf16),
+            pltpu.VMEM((width, rows), bf16),
+            pltpu.SemaphoreType.DMA((4,)),
         ],
-        compiler_params=pltpu.CompilerParams(vmem_limit_bytes=40 * 1024 * 1024),
+        compiler_params=pltpu.CompilerParams(vmem_limit_bytes=20 * 1024 * 1024),
         cost_estimate=pl.CostEstimate(
             flops=8 * nh * rows * features * width,
             bytes_accessed=8 * features * width,
@@ -132,22 +161,32 @@
         name="local",
     )(gathered, norm_gain.reshape(1, features), gate_weight.T, up_weight.T, own, other)
 
+    from_far = shift(far, -2, nz)
     from_behind = shift(ahead, 1, nz)
     from_ahead = shift(behind, -1, nz)
-    from_far = shift(far, -2, nz)
+    gate_own, up_own, from_far = lax.optimization_barrier((gate_own, up_own, from_far))
 
     part = (contract_last(gate_own, gate_weight) + contract_last(up_own, up_weight)).astype(bf16)
     blocks = part.reshape(nt, rows // nt, features)
     moved = lax.all_to_all(blocks, TENSOR, 0, 0, tiled=True)
 
-    sums = hub.astype(f32) + from_behind.astype(f32) + from_ahead.astype(f32)
-    last = (sums[hubs - 1] + from_far.astype(f32)).astype(bf16)
-    total = sums[2]
-    total = total + shift(sums[0].astype(bf16), 6, nz).astype(f32)
-    total = total + shift(sums[1].astype(bf16), 3, nz).astype(f32)
-    total = total + shift(sums[3].astype(bf16), -3, nz).astype(f32)
-    total = total + shift(last, -6, nz).astype(f32)
-    total = total.astype(bf16)
+    def joined(at):
+        return (
+            hub[at].astype(f32) + from_behind[at].astype(f32) + from_ahead[at].astype(f32)
+        )
+
+    plus, minus = lax.optimization_barrier(
+        (joined(0).astype(bf16), (joined(4) + from_far.astype(f32)).astype(bf16))
+    )
+    plus, minus = lax.optimization_barrier((shift(plus, 3, nz), shift(minus, -3, nz)))
+    plus, minus = lax.optimization_barrier(
+        (
+            (joined(1) + plus.astype(f32)).astype(bf16),
+            (joined(3) + minus.astype(f32)).astype(bf16),
+        )
+    )
+    plus, minus = shift(plus, 3, nz), shift(minus, -3, nz)
+    total = (joined(2) + plus.astype(f32) + minus.astype(f32)).astype(bf16)
 
     scaled, inverse = normalize(residual)
     normed_grad = jnp.sum(moved.astype(f32), axis=0)

time: 114 us -> 107 us (0.939)
  the two profiles are of different devices: /device:TPU:2 before, /device:TPU:36 now
where the time goes in v3:
time: 107 us; the launch traced here: 106 us
  starting transfers between devices  51.8 us (48%)
  waiting for transfers between devices  35.2 us (33%)
  local copies, waits for them, and re-layouts  6.66 us (6%)
  other arithmetic  5.13 us (5%)
  Pallas kernels  4.74 us (4%)
  matrix products  1.69 us (2%)
    ppermute x7, starting transfers between devices, shift(): return lax.ppermute(value, 'z', [(i, (i + hops) % nz) for i in range(nz)])  34.5 us
    ppermute x7, waiting for transfers between devices, shift(): return lax.ppermute(value, 'z', [(i, (i + hops) % nz) for i in range(nz)])  21.8 us
    ppermute x1, waiting for transfers between devices, shards(): other = lax.ppermute(own, 'yh', [(0, 1), (1, 0)])  13.4 us
    all_to_all x1, starting transfers between devices, shards(): gathered = lax.all_to_all(copies, ('yh',) + TENSOR, 0, 0, tiled=True)  7.6 us
    ppermute x1, starting transfers between devices, shards(): other = lax.ppermute(own, 'yh', [(0, 1), (1, 0)])  4.92 us
    all_to_all x1, starting transfers between devices, shards(): moved = lax.all_to_all(blocks, TENSOR, 0, 0, tiled=True)  4.82 us
    pallas_call x1, Pallas kernels, shards(): pl.pallas_call(functools.partial(local_kernel, factor, nz), out_shape=(sh...  4.74 us
    unnamed x16, local copies, waits for them, and re-layouts  3.94 us
  transfers between devices with their start and end apart: 10, of which 7 were waited for; matrix products, arithmetic and copies ran while one was open for 4% of the time, Pallas kernels for 0%

profile of v3, /device:TPU:36, one launch (start us, length us, event | category | flops | bytes accessed | tf_op | source)
XLA Modules:
  0.0 106.1 jit_solution(9687369280799055165)
XLA Ops:
  0.6 0.0 copy-start.3
  0.6 0.0 copy-start.2
  0.7 0.0 copy-start
  0.7 2.0 %broadcast_in_dim.2 = bf16[32,8,2048]{2,1,0:T(8,128)(2,1)} broadcast(bf16[8,2048]{1,0:T(8,128)(2,1)} %param.5), dimensions={1,2} | broadcast | bytes 1081344 | tf_op jit(solution)/shard_map/broadcast_in_dim | solution.py:128
  2.7 7.6 %all-to-all-start = ((bf16[32,8,2048]{2,1,0:T(8,128)(2,1)}), bf16[32,8,2048]{2,1,0:T(8,128)(2,1)S(1)}, u32[]{:S(2)}, u32[]{:S(2)}) async-start(bf16[32,8,2048]{2,1,0:T(8,128)(2,1)} %broadcast_in_dim.2), calls=%async_computation | async-start | bytes 2097152 | tf_op jit(solution)/shard_map/all_to_all | solution.py:129
  10.3 0.0 copy-done.3
  10.3 4.9 %collective-permute-start = (bf16[448,128]{1,0:T(8,128)(2,1)S(1)}, bf16[448,128]{1,0:T(8,128)(2,1)S(1)}, u32[]{:S(2)}, u32[]{:S(2)}) collective-permute-start(bf16[448,128]{1,0:T(8,128)(2,1)S(1)} %bitcast.35), channel_id=1, source_target_pairs={{0,16},{16,0},{1,17},{17,1},{2,18},{18,2},{3,19},{19,3},{4,20},{20... | collective-permute-start | bytes 344072 | tf_op jit(solution)/shard_map/ppermute | solution.py:127
  15.2 13.4 %collective-permute-done.other_src = bf16[448,128]{1,0:T(8,128)(2,1)S(1)} collective-permute-done((bf16[448,128]{1,0:T(8,128)(2,1)S(1)}, bf16[448,128]{1,0:T(8,128)(2,1)S(1)}, u32[]{:S(2)}, u32[]{:S(2)}) %collective-permute-start) | collective-permute-done | bytes 114720 | tf_op jit(solution)/shard_map/ppermute | solution.py:127
  28.6 0.0 copy-start.5
  28.6 0.6 copy-done.5
  29.3 0.0 all-to-all-done
  29.3 0.0 copy-done.2
  29.3 0.0 copy-done
  29.3 0.0 copy-start.1
  29.3 1.5 %copy-done.1 = bf16[2048,448]{0,1:T(8,128)(2,1)S(1)} copy-done((bf16[2048,448]{0,1:T(8,128)(2,1)S(1)}, bf16[2048,448]{0,1:T(8,128)(2,1)}, u32[]{:S(2)}) %copy-start.1) | copy-done | bytes 1835032
  30.8 0.0 copy-start.4
  30.8 0.9 copy-done.4
  31.7 0.0 copy-start.6
  31.7 0.9 copy-done.6
  32.6 0.0 copy-start.7
  32.6 4.7 %local.1 = (bf16[5,64,896]{2,1,0:T(8,128)(2,1)}, bf16[5,64,896]{2,1,0:T(8,128)(2,1)}, bf16[64,896]{1,0:T(8,128)(2,1)S(1)}, bf16[5,64,896]{2,1,0:T(8,128)(2,1)S(1...) custom-call(bf16[256,2048]{1,0:T(8,128)(2,1)S(1)} %bitcast.33, f32[1,2048]{1,0:T(1,128)S(1)} %bitcast.34, ...), custom_call_target="tpu_custom_call" | custom-call | flops 1879048192 | bytes 7340032 | tf_op jit(solution)/shard_map/local/pallas_call | solution.py:134
  37.3 10.9 %collective-permute-start.1 = (bf16[64,896]{1,0:T(8,128)(2,1)S(1)}, bf16[64,896]{1,0:T(8,128)(2,1)S(1)}, u32[]{:S(2)}, u32[]{:S(2)}) collective-permute-start(bf16[64,896]{1,0:T(8,128)(2,1)S(1)} %get-tuple-element.20), channel_id=1, source_target_pairs={{0,448},{32,480},{64,0},{96,32},{128,64},{160,96},{192,128},{224,1... | collective-permute-start | bytes 344072 | tf_op jit(solution)/shard_map/ppermute | solution.py:117
  48.3 0.0 copy-done.7
  48.3 0.1 fusion.14
  48.4 1.9 %collective-permute-start.2 = (bf16[5,64,896]{2,1,0:T(8,128)(2,1)}, bf16[5,64,896]{2,1,0:T(8,128)(2,1)S(1)}, u32[]{:S(2)}, u32[]{:S(2)}) collective-permute-start(bf16[5,64,896]{2,1,0:T(8,128)(2,1)} %get-tuple-element.24), channel_id=1, source_target_pairs={{0,32},{32,64},{64,96},{96,128},{128,160},{160,192},{192,224},{224... | collective-permute-start | bytes 1720328 | tf_op jit(solution)/shard_map/ppermute | solution.py:117
  50.3 3.9 %collective-permute-start.3 = (bf16[5,64,896]{2,1,0:T(8,128)(2,1)}, bf16[5,64,896]{2,1,0:T(8,128)(2,1)}, u32[]{:S(2)}, u32[]{:S(2)}) collective-permute-start(bf16[5,64,896]{2,1,0:T(8,128)(2,1)} %get-tuple-element.25), channel_id=1, source_target_pairs={{0,480},{32,0},{64,32},{96,64},{128,96},{160,128},{192,160},{224,1... | collective-permute-start | bytes 1720328 | tf_op jit(solution)/shard_map/ppermute | solution.py:117
  54.3 0.0 collective-permute-done.1
  54.3 0.4 fusion.16
  54.7 1.3 %fusion.1 = bf16[16,8,2048]{2,1,0:T(8,128)(2,1)} fusion(f32[128,2048]{1,0:T(8,128)S(1)} %fusion.16, bf16[128,448]{1,0:T(8,128)(2,1)S(1)} %get-tuple-element.21, bf16[2048,448]{0,1:T(8,128)(2,1)S(1)} %copy-done), kind=kOutput, calls=%fused_computation.2 | convolution fusion | flops 235405312 | bytes 3522560 | tf_op jit(solution)/shard_map/dot_general | solution.py:24
  56.0 4.8 %all-to-all-start.1 = ((bf16[16,8,2048]{2,1,0:T(8,128)(2,1)}), bf16[16,8,2048]{2,1,0:T(8,128)(2,1)S(1)}, u32[]{:S(2)}, u32[]{:S(2)}) async-start(bf16[16,8,2048]{2,1,0:T(8,128)(2,1)} %fusion.1), calls=%async_computation.1 | async-start | bytes 1048576 | tf_op jit(solution)/shard_map/all_to_all | solution.py:171
  60.8 4.3 %collective-permute-done.2 = bf16[5,64,896]{2,1,0:T(8,128)(2,1)S(1)} collective-permute-done((bf16[5,64,896]{2,1,0:T(8,128)(2,1)}, bf16[5,64,896]{2,1,0:T(8,128)(2,1)S(1)}, u32[]{:S(2)}, u32[]{:S(2)}) %collective-permute-start.2) | collective-permute-done | bytes 573472 | tf_op jit(solution)/shard_map/ppermute | solution.py:117
  65.1 2.0 %collective-permute-done.3 = bf16[5,64,896]{2,1,0:T(8,128)(2,1)} collective-permute-done((bf16[5,64,896]{2,1,0:T(8,128)(2,1)}, bf16[5,64,896]{2,1,0:T(8,128)(2,1)}, u32[]{:S(2)}, u32[]{:S(2)}) %collective-permute-start.3) | collective-permute-done | bytes 573472 | tf_op jit(solution)/shard_map/ppermute | solution.py:117
  67.1 1.0 fusion.7
  68.1 1.0 fusion.3
  69.1 1.9 %collective-permute-start.4 = (bf16[64,896]{1,0:T(8,128)(2,1)S(1)}, bf16[64,896]{1,0:T(8,128)(2,1)S(1)}, u32[]{:S(2)}, u32[]{:S(2)}) collective-permute-start(bf16[64,896]{1,0:T(8,128)(2,1)S(1)} %fusion.7), channel_id=1, source_target_pairs={{0,96},{32,128},{64,160},{96,192},{128,224},{160,256},{192,288},{2... | collective-permute-start | bytes 344072 | tf_op jit(solution)/shard_map/ppermute | solution.py:117
  71.0 6.9 %collective-permute-start.5 = (bf16[64,896]{1,0:T(8,128)(2,1)S(1)}, bf16[64,896]{1,0:T(8,128)(2,1)S(1)}, u32[]{:S(2)}, u32[]{:S(2)}) collective-permute-start(bf16[64,896]{1,0:T(8,128)(2,1)S(1)} %fusion.3), channel_id=1, source_target_pairs={{0,416},{32,448},{64,480},{96,0},{128,32},{160,64},{192,96},{224,1... | collective-permute-start | bytes 344072 | tf_op jit(solution)/shard_map/ppermute | solution.py:117
  77.9 0.0 all-to-all-done.1
  78.0 0.1 convert_reduce_fusion
  78.0 0.2 fusion.10
  78.2 3.8 %collective-permute-done.4 = bf16[64,896]{1,0:T(8,128)(2,1)S(1)} collective-permute-done((bf16[64,896]{1,0:T(8,128)(2,1)S(1)}, bf16[64,896]{1,0:T(8,128)(2,1)S(1)}, u32[]{:S(2)}, u32[]{:S(2)}) %collective-permute-start.4) | collective-permute-done | bytes 114720 | tf_op jit(solution)/shard_map/ppermute | solution.py:117
  82.0 2.8 %collective-permute-done.5 = bf16[64,896]{1,0:T(8,128)(2,1)S(1)} collective-permute-done((bf16[64,896]{1,0:T(8,128)(2,1)S(1)}, bf16[64,896]{1,0:T(8,128)(2,1)S(1)}, u32[]{:S(2)}, u32[]{:S(2)}) %collective-permute-start.5) | collective-permute-done | bytes 114720 | tf_op jit(solution)/shard_map/ppermute | solution.py:117
  84.8 1.1 %fusion.2 = (bf16[64,896]{1,0:T(8,128)(2,1)S(1)}, bf16[64,896]{1,0:T(8,128)(2,1)S(1)}) fusion(bf16[64,896]{1,0:T(8,128)(2,1)S(1)} %collective-permute-done.5, bf16[5,64,896]{2,1,0:T(8,128)(2,1)} %collective-permute-done.3, bf16[5,64,896]{2,1,0:T(8,128)(2,1)S(1)} %collective-permute-done.2, bf16[5,64,896]{2,1,0:T(8,128)(2,1)S(1)} %get-tuple-element.23, ...), kind=kLoop, calls=%fused_computation.5 | loop fusion | flops 917504 | bytes 1146880 | tf_op jit(solution)/shard_map/convert_element_type | solution.py:185
  85.9 4.3 %collective-permute-start.6 = (bf16[64,896]{1,0:T(8,128)(2,1)S(1)}, bf16[64,896]{1,0:T(8,128)(2,1)S(1)}, u32[]{:S(2)}, u32[]{:S(2)}) collective-permute-start(bf16[64,896]{1,0:T(8,128)(2,1)S(1)} %get-tuple-element.31), channel_id=1, source_target_pairs={{0,96},{32,128},{64,160},{96,192},{128,224},{160,256},{192,288},{2... | collective-permute-start | bytes 344072 | tf_op jit(solution)/shard_map/ppermute | solution.py:117
  90.2 4.5 %collective-permute-start.7 = (bf16[64,896]{1,0:T(8,128)(2,1)S(1)}, bf16[64,896]{1,0:T(8,128)(2,1)S(1)}, u32[]{:S(2)}, u32[]{:S(2)}) collective-permute-start(bf16[64,896]{1,0:T(8,128)(2,1)S(1)} %get-tuple-element.32), channel_id=1, source_target_pairs={{0,416},{32,448},{64,480},{96,0},{128,32},{160,64},{192,96},{224,1... | collective-permute-start | bytes 344072 | tf_op jit(solution)/shard_map/ppermute | solution.py:117
  94.7 0.7 fusion.13
  95.4 0.3 collective-permute-done.6
  95.7 8.6 %collective-permute-done.7 = bf16[64,896]{1,0:T(8,128)(2,1)S(1)} collective-permute-done((bf16[64,896]{1,0:T(8,128)(2,1)S(1)}, bf16[64,896]{1,0:T(8,128)(2,1)S(1)}, u32[]{:S(2)}, u32[]{:S(2)}) %collective-permute-start.7) | collective-permute-done | bytes 114720 | tf_op jit(solution)/shard_map/ppermute | solution.py:117
  104.4 1.0 fusion.6
  105.3 0.7 fusion.15
  (2 shorter events, 0.0 us)
Async XLA Ops:
  0.6 9.6 %copy-start.3 = (bf16[128,448]{0,1:T(8,128)(2,1)S(1)}, bf16[128,448]{0,1:T(8,128)(2,1)}, u32[]{:S(2)}) copy-start(bf16[128,448]{0,1:T(8,128)(2,1)} %param.9) | copy-start | bytes 344068
  0.6 28.6 %copy-start.2 = (f32[2048]{0:T(1024)S(1)}, f32[2048]{0:T(1024)}, u32[]{:S(2)}) copy-start(f32[2048]{0:T(1024)} %param.6) | copy-start | bytes 24580
  0.7 28.6 %copy-start = (bf16[2048,448]{0,1:T(8,128)(2,1)S(1)}, bf16[2048,448]{0,1:T(8,128)(2,1)}, u32[]{:S(2)}) copy-start(bf16[2048,448]{0,1:T(8,128)(2,1)} %param.7) | copy-start | bytes 5505028
  2.7 26.6 %all-to-all-start = ((bf16[32,8,2048]{2,1,0:T(8,128)(2,1)}), bf16[32,8,2048]{2,1,0:T(8,128)(2,1)S(1)}, u32[]{:S(2)}, u32[]{:S(2)}) async-start(bf16[32,8,2048]{2,1,0:T(8,128)(2,1)} %broadcast_in_dim.2), calls=%async_computation | async-start | bytes 2097152 | tf_op jit(solution)/shard_map/all_to_all | solution.py:129
  10.3 18.3 %collective-permute-start = (bf16[448,128]{1,0:T(8,128)(2,1)S(1)}, bf16[448,128]{1,0:T(8,128)(2,1)S(1)}, u32[]{:S(2)}, u32[]{:S(2)}) collective-permute-start(bf16[448,128]{1,0:T(8,128)(2,1)S(1)} %bitcast.35), channel_id=1, source_target_pairs={{0,16},{16,0},{1,17},{17,1},{2,18},{18,2},{3,19},{19,3},{4,20},{20... | collective-permute-start | bytes 344072 | tf_op jit(solution)/shard_map/ppermute | solution.py:127
  28.6 0.6 copy-start.5
  29.3 1.5 %copy-start.1 = (bf16[2048,448]{0,1:T(8,128)(2,1)S(1)}, bf16[2048,448]{0,1:T(8,128)(2,1)}, u32[]{:S(2)}) copy-start(bf16[2048,448]{0,1:T(8,128)(2,1)} %param.8) | copy-start | bytes 5505028
  30.8 0.9 copy-start.4
  31.7 0.9 copy-start.6
  32.6 15.7 %copy-start.7 = (bf16[8,2048]{1,0:T(8,128)(2,1)S(1)}, bf16[8,2048]{1,0:T(8,128)(2,1)}, u32[]{:S(2)}) copy-start(bf16[8,2048]{1,0:T(8,128)(2,1)} %param.5) | copy-start | bytes 98308
  37.3 16.9 %collective-permute-start.1 = (bf16[64,896]{1,0:T(8,128)(2,1)S(1)}, bf16[64,896]{1,0:T(8,128)(2,1)S(1)}, u32[]{:S(2)}, u32[]{:S(2)}) collective-permute-start(bf16[64,896]{1,0:T(8,128)(2,1)S(1)} %get-tuple-element.20), channel_id=1, source_target_pairs={{0,448},{32,480},{64,0},{96,32},{128,64},{160,96},{192,128},{224,1... | collective-permute-start | bytes 344072 | tf_op jit(solution)/shard_map/ppermute | solution.py:117
  48.4 16.7 %collective-permute-start.2 = (bf16[5,64,896]{2,1,0:T(8,128)(2,1)}, bf16[5,64,896]{2,1,0:T(8,128)(2,1)S(1)}, u32[]{:S(2)}, u32[]{:S(2)}) collective-permute-start(bf16[5,64,896]{2,1,0:T(8,128)(2,1)} %get-tuple-element.24), channel_id=1, source_target_pairs={{0,32},{32,64},{64,96},{96,128},{128,160},{160,192},{192,224},{224... | collective-permute-start | bytes 1720328 | tf_op jit(solution)/shard_map/ppermute | solution.py:117
  50.3 16.8 %collective-permute-start.3 = (bf16[5,64,896]{2,1,0:T(8,128)(2,1)}, bf16[5,64,896]{2,1,0:T(8,128)(2,1)}, u32[]{:S(2)}, u32[]{:S(2)}) collective-permute-start(bf16[5,64,896]{2,1,0:T(8,128)(2,1)} %get-tuple-element.25), channel_id=1, source_target_pairs={{0,480},{32,0},{64,32},{96,64},{128,96},{160,128},{192,160},{224,1... | collective-permute-start | bytes 1720328 | tf_op jit(solution)/shard_map/ppermute | solution.py:117
  56.0 22.0 %all-to-all-start.1 = ((bf16[16,8,2048]{2,1,0:T(8,128)(2,1)}), bf16[16,8,2048]{2,1,0:T(8,128)(2,1)S(1)}, u32[]{:S(2)}, u32[]{:S(2)}) async-start(bf16[16,8,2048]{2,1,0:T(8,128)(2,1)} %fusion.1), calls=%async_computation.1 | async-start | bytes 1048576 | tf_op jit(solution)/shard_map/all_to_all | solution.py:171
  69.1 12.9 %collective-permute-start.4 = (bf16[64,896]{1,0:T(8,128)(2,1)S(1)}, bf16[64,896]{1,0:T(8,128)(2,1)S(1)}, u32[]{:S(2)}, u32[]{:S(2)}) collective-permute-start(bf16[64,896]{1,0:T(8,128)(2,1)S(1)} %fusion.7), channel_id=1, source_target_pairs={{0,96},{32,128},{64,160},{96,192},{128,224},{160,256},{192,288},{2... | collective-permute-start | bytes 344072 | tf_op jit(solution)/shard_map/ppermute | solution.py:117
  71.0 13.8 %collective-permute-start.5 = (bf16[64,896]{1,0:T(8,128)(2,1)S(1)}, bf16[64,896]{1,0:T(8,128)(2,1)S(1)}, u32[]{:S(2)}, u32[]{:S(2)}) collective-permute-start(bf16[64,896]{1,0:T(8,128)(2,1)S(1)} %fusion.3), channel_id=1, source_target_pairs={{0,416},{32,448},{64,480},{96,0},{128,32},{160,64},{192,96},{224,1... | collective-permute-start | bytes 344072 | tf_op jit(solution)/shard_map/ppermute | solution.py:117
  85.9 9.9 %collective-permute-start.6 = (bf16[64,896]{1,0:T(8,128)(2,1)S(1)}, bf16[64,896]{1,0:T(8,128)(2,1)S(1)}, u32[]{:S(2)}, u32[]{:S(2)}) collective-permute-start(bf16[64,896]{1,0:T(8,128)(2,1)S(1)} %get-tuple-element.31), channel_id=1, source_target_pairs={{0,96},{32,128},{64,160},{96,192},{128,224},{160,256},{192,288},{2... | collective-permute-start | bytes 344072 | tf_op jit(solution)/shard_map/ppermute | solution.py:117
  90.2 14.1 %collective-permute-start.7 = (bf16[64,896]{1,0:T(8,128)(2,1)S(1)}, bf16[64,896]{1,0:T(8,128)(2,1)S(1)}, u32[]{:S(2)}, u32[]{:S(2)}) collective-permute-start(bf16[64,896]{1,0:T(8,128)(2,1)S(1)} %get-tuple-element.32), channel_id=1, source_target_pairs={{0,416},{32,448},{64,480},{96,0},{128,32},{160,64},{192,96},{224,1... | collective-permute-start | bytes 344072 | tf_op jit(solution)/shard_map/ppermute | solution.py:117

commit v4 on v2

v4 whole, which is shorter than its diff:
```python
import functools

import jax
import jax.numpy as jnp
from jax import lax
from jax.experimental import pallas as pl
from jax.experimental.pallas import tpu as pltpu
from jax.sharding import Mesh
from jax.sharding import PartitionSpec as P

EPSILON = 1e-05
DP = ("z", "yh")
TENSOR = ("x", "yl", "core")
OUTER = (-6, 6)
INNER = (-3, 0, 3)


def normalize(residual):
    values = residual.astype(jnp.float32)
    inverse = lax.rsqrt(jnp.mean(values * values, axis=-1, keepdims=True) + EPSILON)
    return (values * inverse, inverse)


def contract_last(left, right):
    return lax.dot_general(
        left, right, (((1,), (1,)), ((), ())), preferred_element_type=jnp.float32
    )


def contract_first(left, right):
    return lax.dot_general(
        left, right, (((0,), (0,)), ((), ())), preferred_element_type=jnp.float32
    )


def local_kernel(
    factor,
    nz,
    rows_ref,
    gain_ref,
    weight_ref,
    own_ref,
    other_ref,
    far_ref,
    outer_ahead_ref,
    outer_behind_ref,
    inner_ahead_ref,
    inner_behind_ref,
    hub_ref,
    grads_own_ref,
    normed_ref,
    grads_ref,
):
    z = lax.axis_index("z")
    half = lax.axis_index("yh")
    rows, width = own_ref.shape
    scaled = normalize(rows_ref[...])[0]
    normed_ref[...] = (scaled * gain_ref[...]).astype(jnp.bfloat16)
    normed = normed_ref[...]
    gate_value = contract_last(normed, weight_ref[:width])
    up_value = contract_last(normed, weight_ref[width:])
    own = own_ref[...].astype(jnp.float32)
    other = other_ref[...].astype(jnp.float32)
    first = half == 0
    upstream = jnp.concatenate(
        [jnp.where(first, own, other), jnp.where(first, other, own)], axis=0
    )
    sigmoid_gate = jax.nn.sigmoid(gate_value)
    weighted = upstream * sigmoid_gate
    grads_ref[:, width:] = (weighted * gate_value).astype(jnp.bfloat16)
    grads_ref[:, :width] = (
        weighted * up_value * (1.0 + gate_value * (1.0 - sigmoid_gate))
    ).astype(jnp.bfloat16)
    start = pl.multiple_of(half * rows, rows)
    grads_own_ref[...] = grads_ref[pl.ds(start, rows), :]
    grads = grads_ref[...]
    depth = far_ref.shape[0]

    def block(relative):
        chunk = lax.rem(z - relative + 2 * nz, nz)
        lanes = pl.ds(pl.multiple_of(chunk * 2 * depth, 2 * depth), 2 * depth)
        both = contract_first(normed_ref[:, lanes], grads) * factor
        return jnp.where(first, both[:depth], both[depth:]).astype(jnp.bfloat16)

    far_ref[...] = block(nz // 2)
    for at, hub in enumerate(OUTER):
        outer_ahead_ref[at] = block(hub - 1)
        outer_behind_ref[at] = block(hub + 1)
    for at, hub in enumerate(INNER):
        inner_ahead_ref[at] = block(hub - 1)
        inner_behind_ref[at] = block(hub + 1)
    for at, hub in enumerate(OUTER + INNER):
        hub_ref[at] = block(hub)


def shift(value, hops, nz):
    return lax.ppermute(value, "z", [(i, (i + hops) % nz) for i in range(nz)])


def shards(residual, norm_gain, gate_weight, up_weight, hidden_grad):
    nz, nh, nt = lax.axis_size("z"), lax.axis_size("yh"), lax.axis_size(TENSOR)
    rows, width = hidden_grad.shape
    features = residual.shape[1]
    depth = features // (nz * nh)
    f32, bf16 = jnp.float32, jnp.bfloat16
    weight = jnp.concatenate([gate_weight.T, up_weight.T], axis=0)
    own = hidden_grad
    other = lax.ppermute(own, "yh", [(0, 1), (1, 0)])
    copies = jnp.broadcast_to(residual[None], (nh * nt,) + residual.shape)
    gathered = lax.all_to_all(copies, ("yh",) + TENSOR, 0, 0, tiled=True)
    gathered = gathered.reshape(nh * rows, features)
    factor = float(rows * nz * nh) ** (-0.5)
    shape = jax.ShapeDtypeStruct
    far, outer_ahead, outer_behind, inner_ahead, inner_behind, hub, grads_own = pl.pallas_call(
        functools.partial(local_kernel, factor, nz),
        out_shape=(
            shape((depth, 2 * width), bf16),
            shape((len(OUTER), depth, 2 * width), bf16),
            shape((len(OUTER), depth, 2 * width), bf16),
            shape((len(INNER), depth, 2 * width), bf16),
            shape((len(INNER), depth, 2 * width), bf16),
            shape((len(OUTER + INNER), depth, 2 * width), bf16),
            shape((rows, 2 * width), bf16),
        ),
        scratch_shapes=[
            pltpu.VMEM((nh * rows, features), bf16),
            pltpu.VMEM((nh * rows, 2 * width), bf16),
        ],
        compiler_params=pltpu.CompilerParams(vmem_limit_bytes=20 * 1024 * 1024),
        cost_estimate=pl.CostEstimate(
            flops=8 * nh * rows * features * width,
            bytes_accessed=8 * features * width,
            transcendentals=nh * rows * width,
        ),
        name="local",
    )(gathered, norm_gain.reshape(1, features), weight, own, other)

    from_far = shift(far, -2, nz).astype(f32)
    outer_ahead, outer_behind = shift(outer_ahead, 1, nz), shift(outer_behind, -1, nz)
    inner_ahead, inner_behind = shift(inner_ahead, 1, nz), shift(inner_behind, -1, nz)
    hub = hub.astype(f32)
    outer = hub[:2] + outer_ahead.astype(f32) + outer_behind.astype(f32)
    plus, minus = lax.optimization_barrier(
        (outer[0].astype(bf16), (outer[1] + from_far).astype(bf16))
    )
    grads_own, first_sum = lax.optimization_barrier((grads_own, plus))
    plus, minus = shift(first_sum, 3, nz), shift(minus, -3, nz)

    part = jnp.dot(grads_own, weight, preferred_element_type=f32).astype(bf16)
    blocks = part.reshape(nt, rows // nt, features)
    moved = lax.all_to_all(blocks, TENSOR, 0, 0, tiled=True)

    inner = hub[2:] + inner_ahead.astype(f32) + inner_behind.astype(f32)
    plus, minus = lax.optimization_barrier((plus, minus))
    plus, minus = lax.optimization_barrier(
        (
            (inner[0] + plus.astype(f32)).astype(bf16),
            (inner[2] + minus.astype(f32)).astype(bf16),
        )
    )
    plus, minus = shift(plus, 3, nz), shift(minus, -3, nz)
    total = (inner[1] + plus.astype(f32) + minus.astype(f32)).astype(bf16)

    scaled, inverse = normalize(residual)
    normed_grad = jnp.sum(moved.astype(f32), axis=0)
    weighted = normed_grad * norm_gain
    residual_grad = (
        (weighted - scaled * jnp.mean(weighted * scaled, axis=-1, keepdims=True)) * inverse
    ).astype(bf16)
    return (residual_grad, total[:, :width], total[:, width:])


def solution(mesh):
    fine = Mesh(mesh.devices.reshape(16, 2, 4, 2, 2), DP + TENSOR)
    return jax.shard_map(
        shards,
        mesh=fine,
        in_specs=(
            P(DP + TENSOR, None),
            P(),
            P(None, TENSOR),
            P(None, TENSOR),
            P(DP, TENSOR),
        ),
        out_specs=(P(DP + TENSOR, None), P(DP, TENSOR), P(DP, TENSOR)),
        check_vma=False,
    )
```

time: 114 us -> 95.9 us (0.84)
  the two profiles are of different devices: /device:TPU:2 before, /device:TPU:4 now
where the time goes in v4:
time: 95.9 us; the launch traced here: 95.2 us
  starting transfers between devices  59.8 us (62%)
  waiting for transfers between devices  18.2 us (19%)
  other arithmetic  5.84 us (6%)
  local copies, waits for them, and re-layouts  5.65 us (6%)
  Pallas kernels  3.32 us (3%)
  matrix products  1.52 us (2%)
    ppermute x9, starting transfers between devices, shift(): return lax.ppermute(value, 'z', [(i, (i + hops) % nz) for i in range(nz)])  40.5 us
    ppermute x9, waiting for transfers between devices, shift(): return lax.ppermute(value, 'z', [(i, (i + hops) % nz) for i in range(nz)])  9.84 us
    all_to_all x1, starting transfers between devices, shards(): gathered = lax.all_to_all(copies, ('yh',) + TENSOR, 0, 0, tiled=True)  9.51 us
    ppermute x1, waiting for transfers between devices, shards(): other = lax.ppermute(own, 'yh', [(0, 1), (1, 0)])  8.38 us
    ppermute x1, starting transfers between devices, shards(): other = lax.ppermute(own, 'yh', [(0, 1), (1, 0)])  4.98 us
    all_to_all x1, starting transfers between devices, shards(): moved = lax.all_to_all(blocks, TENSOR, 0, 0, tiled=True)  4.82 us
    concatenate x1, other arithmetic, shards(): weight = jnp.concatenate([gate_weight.T, up_weight.T], axis=0)  4.37 us
    pallas_call x1, Pallas kernels, shards(): pl.pallas_call(functools.partial(local_kernel, factor, nz), out_shape=(sh...  3.32 us
  transfers between devices with their start and end apart: 12, of which 4 were waited for; matrix products, arithmetic and copies ran while one was open for 9% of the time, Pallas kernels for 0%

profile of v4, /device:TPU:4, one launch (start us, length us, event | category | flops | bytes accessed | tf_op | source)
XLA Modules:
  0.0 95.2 jit_solution(14307650951780751191)
XLA Ops:
  0.6 1.9 %broadcast_in_dim.2 = bf16[32,8,2048]{2,1,0:T(8,128)(2,1)} broadcast(bf16[8,2048]{1,0:T(8,128)(2,1)} %param.5), dimensions={1,2} | broadcast | bytes 1081344 | tf_op jit(solution)/shard_map/broadcast_in_dim | solution.py:109
  2.5 9.5 %all-to-all-start = ((bf16[32,8,2048]{2,1,0:T(8,128)(2,1)}), bf16[32,8,2048]{2,1,0:T(8,128)(2,1)S(1)}, u32[]{:S(2)}, u32[]{:S(2)}) async-start(bf16[32,8,2048]{2,1,0:T(8,128)(2,1)} %broadcast_in_dim.2), calls=%async_computation | async-start | bytes 2097152 | tf_op jit(solution)/shard_map/all_to_all | solution.py:110
  12.0 1.0 %copy.9.own_ref = bf16[128,448]{1,0:T(8,128)(2,1)S(1)} copy(bf16[128,448]{0,1:T(8,128)(2,1)} %param.9) | data formatting | bytes 229376 | tf_op args[4]
  13.0 5.0 %collective-permute-start = (bf16[128,448]{1,0:T(8,128)(2,1)S(1)}, bf16[128,448]{1,0:T(8,128)(2,1)S(1)}, u32[]{:S(2)}, u32[]{:S(2)}) collective-permute-start(bf16[128,448]{1,0:T(8,128)(2,1)S(1)} %copy.9.own_ref), channel_id=1, source_target_pairs={{0,16},{16,0},{1,17},{17,1},{2,18},{18,2},{3,19},{19,3},{4,20},{20... | collective-permute-start | bytes 344072 | tf_op jit(solution)/shard_map/ppermute | solution.py:108
  18.0 0.0 copy-start.1
  18.0 0.0 copy-start.4
  18.0 4.4 %pad_maximum_fusion.weight_ref = bf16[896,2048]{1,0:T(8,128)(2,1)} fusion(bf16[448,2048]{1,0:T(8,128)(2,1)} %bitcast.37, bf16[448,2048]{1,0:T(8,128)(2,1)} %bitcast.39), kind=kLoop, calls=%fused_computation | loop fusion | flops 7340032 | bytes 7340032 | tf_op jit(solution)/shard_map/concatenate | solution.py:106
  22.4 8.4 %collective-permute-done.other_ref = bf16[128,448]{1,0:T(8,128)(2,1)S(1)} collective-permute-done((bf16[128,448]{1,0:T(8,128)(2,1)S(1)}, bf16[128,448]{1,0:T(8,128)(2,1)S(1)}, u32[]{:S(2)}, u32[]{:S(2)}) %collective-permute-start) | collective-permute-done | bytes 114720 | tf_op jit(solution)/shard_map/ppermute | solution.py:108
  30.8 0.0 all-to-all-done
  30.8 0.0 copy-done.1
  30.8 0.0 copy-start
  30.8 2.0 %copy-done = bf16[896,2048]{1,0:T(8,128)(2,1)S(1)} copy-done((bf16[896,2048]{1,0:T(8,128)(2,1)S(1)}, bf16[896,2048]{1,0:T(8,128)(2,1)}, u32[]{:S(2)}) %copy-start) | copy-done | bytes 3670040
  32.8 0.0 copy-start.2
  32.8 0.0 copy-start.3
  32.8 3.3 %local.1 = (bf16[64,896]{1,0:T(8,128)(2,1)S(1)}, bf16[2,64,896]{2,1,0:T(8,128)(2,1)S(1)}, bf16[2,64,896]{2,1,0:T(8,128)(2,1)S(1)}, bf16[3,64,896]{2,1,0:T(8,128)...) custom-call(bf16[256,2048]{1,0:T(8,128)(2,1)S(1)} %bitcast.35, ...), custom_call_target="tpu_custom_call" | custom-call | flops 1879048192 | bytes 7340032 | tf_op jit(solution)/shard_map/local/pallas_call | solution.py:114
  36.2 1.9 %collective-permute-start.1 = (bf16[2,64,896]{2,1,0:T(8,128)(2,1)S(1)}, bf16[2,64,896]{2,1,0:T(8,128)(2,1)S(1)}, u32[]{:S(2)}, u32[]{:S(2)}) collective-permute-start(bf16[2,64,896]{2,1,0:T(8,128)(2,1)S(1)} %get-tuple-element.20), channel_id=1, source_target_pairs={{0,32},{32,64},{64,96},{96,128},{128,160},{160,192},{192,224},{224... | collective-permute-start | bytes 688136 | tf_op jit(solution)/shard_map/ppermute | solution.py:97
  38.1 9.4 %collective-permute-start.2 = (bf16[2,64,896]{2,1,0:T(8,128)(2,1)S(1)}, bf16[2,64,896]{2,1,0:T(8,128)(2,1)S(1)}, u32[]{:S(2)}, u32[]{:S(2)}) collective-permute-start(bf16[2,64,896]{2,1,0:T(8,128)(2,1)S(1)} %get-tuple-element.21), channel_id=1, source_target_pairs={{0,480},{32,0},{64,32},{96,64},{128,96},{160,128},{192,160},{224,1... | collective-permute-start | bytes 688136 | tf_op jit(solution)/shard_map/ppermute | solution.py:97
  47.5 0.0 copy-done.4
  47.5 0.1 fusion.19
  47.7 0.1 convert_element_type.58
  47.7 4.4 %collective-permute-start.3 = (bf16[64,896]{1,0:T(8,128)(2,1)S(1)}, bf16[64,896]{1,0:T(8,128)(2,1)S(1)}, u32[]{:S(2)}, u32[]{:S(2)}) collective-permute-start(bf16[64,896]{1,0:T(8,128)(2,1)S(1)} %get-tuple-element.22), channel_id=1, source_target_pairs={{0,448},{32,480},{64,0},{96,32},{128,64},{160,96},{192,128},{224,1... | collective-permute-start | bytes 344072 | tf_op jit(solution)/shard_map/ppermute | solution.py:97
  52.1 2.9 %collective-permute-start.4 = (bf16[3,64,896]{2,1,0:T(8,128)(2,1)S(1)}, bf16[3,64,896]{2,1,0:T(8,128)(2,1)S(1)}, u32[]{:S(2)}, u32[]{:S(2)}) collective-permute-start(bf16[3,64,896]{2,1,0:T(8,128)(2,1)S(1)} %get-tuple-element.25), channel_id=1, source_target_pairs={{0,32},{32,64},{64,96},{96,128},{128,160},{160,192},{192,224},{224... | collective-permute-start | bytes 1032200 | tf_op jit(solution)/shard_map/ppermute | solution.py:97
  55.1 4.1 %collective-permute-start.5 = (bf16[3,64,896]{2,1,0:T(8,128)(2,1)S(1)}, bf16[3,64,896]{2,1,0:T(8,128)(2,1)S(1)}, u32[]{:S(2)}, u32[]{:S(2)}) collective-permute-start(bf16[3,64,896]{2,1,0:T(8,128)(2,1)S(1)} %get-tuple-element.26), channel_id=1, source_target_pairs={{0,480},{32,0},{64,32},{96,64},{128,96},{160,128},{192,160},{224,1... | collective-permute-start | bytes 1032200 | tf_op jit(solution)/shard_map/ppermute | solution.py:97
  59.2 0.0 collective-permute-done.1
  59.2 0.0 collective-permute-done.2
  59.2 0.1 fusion.2
  59.3 0.0 collective-permute-done.3
  59.3 3.0 %collective-permute-start.6 = (bf16[64,896]{1,0:T(8,128)(2,1)S(1)}, bf16[64,896]{1,0:T(8,128)(2,1)S(1)}, u32[]{:S(2)}, u32[]{:S(2)}) collective-permute-start(bf16[64,896]{1,0:T(8,128)(2,1)S(1)} %fusion.12), channel_id=1, source_target_pairs={{0,96},{32,128},{64,160},{96,192},{128,224},{160,256},{192,288},{2... | collective-permute-start | bytes 344072 | tf_op jit(solution)/shard_map/ppermute | solution.py:97
  62.3 5.9 %collective-permute-start.7 = (bf16[64,896]{1,0:T(8,128)(2,1)S(1)}, bf16[64,896]{1,0:T(8,128)(2,1)S(1)}, u32[]{:S(2)}, u32[]{:S(2)}) collective-permute-start(bf16[64,896]{1,0:T(8,128)(2,1)S(1)} %fusion.11), channel_id=1, source_target_pairs={{0,416},{32,448},{64,480},{96,0},{128,32},{160,64},{192,96},{224,1... | collective-permute-start | bytes 344072 | tf_op jit(solution)/shard_map/ppermute | solution.py:97
  68.2 0.0 copy-done.2
  68.2 0.0 copy-done.3
  68.2 1.5 %fusion = bf16[16,8,2048]{2,1,0:T(8,128)(2,1)} fusion(bf16[128,896]{1,0:T(8,128)(2,1)S(1)} %get-tuple-element.24, bf16[448,2048]{1,0:T(8,128)(2,1)S(1)} %bitcast.38, bf16[448,2048]{1,0:T(8,128)(2,1)S(1)} %bitcast.40), kind=kOutput, calls=%fused_computation.2 | convolution fusion | flops 477364224 | bytes 4423680 | tf_op jit(solution)/shard_map/dot_general | solution.py:149
  69.7 4.8 %all-to-all-start.1 = ((bf16[16,8,2048]{2,1,0:T(8,128)(2,1)}), bf16[16,8,2048]{2,1,0:T(8,128)(2,1)S(1)}, u32[]{:S(2)}, u32[]{:S(2)}) async-start(bf16[16,8,2048]{2,1,0:T(8,128)(2,1)} %fusion), calls=%async_computation.1 | async-start | bytes 1048576 | tf_op jit(solution)/shard_map/all_to_all | solution.py:151
  74.6 0.0 collective-permute-done.6
  74.6 0.8 collective-permute-done.7
  75.4 0.0 collective-permute-done.4
  75.4 0.0 collective-permute-done.5
  75.4 0.1 fusion.1
  75.6 6.8 %collective-permute-start.8 = (bf16[64,896]{1,0:T(8,128)(2,1)S(1)}, bf16[64,896]{1,0:T(8,128)(2,1)S(1)}, u32[]{:S(2)}, u32[]{:S(2)}) collective-permute-start(bf16[64,896]{1,0:T(8,128)(2,1)S(1)} %get-tuple-element.31), channel_id=1, source_target_pairs={{0,96},{32,128},{64,160},{96,192},{128,224},{160,256},{192,288},{2... | collective-permute-start | bytes 344072 | tf_op jit(solution)/shard_map/ppermute | solution.py:97
  82.4 2.0 %collective-permute-start.9 = (bf16[64,896]{1,0:T(8,128)(2,1)S(1)}, bf16[64,896]{1,0:T(8,128)(2,1)S(1)}, u32[]{:S(2)}, u32[]{:S(2)}) collective-permute-start(bf16[64,896]{1,0:T(8,128)(2,1)S(1)} %get-tuple-element.32), channel_id=1, source_target_pairs={{0,416},{32,448},{64,480},{96,0},{128,32},{160,64},{192,96},{224,1... | collective-permute-start | bytes 344072 | tf_op jit(solution)/shard_map/ppermute | solution.py:97
  84.5 3.8 %collective-permute-done.8 = bf16[64,896]{1,0:T(8,128)(2,1)S(1)} collective-permute-done((bf16[64,896]{1,0:T(8,128)(2,1)S(1)}, bf16[64,896]{1,0:T(8,128)(2,1)S(1)}, u32[]{:S(2)}, u32[]{:S(2)}) %collective-permute-start.8) | collective-permute-done | bytes 114720 | tf_op jit(solution)/shard_map/ppermute | solution.py:97
  88.3 5.2 %collective-permute-done.9 = bf16[64,896]{1,0:T(8,128)(2,1)S(1)} collective-permute-done((bf16[64,896]{1,0:T(8,128)(2,1)S(1)}, bf16[64,896]{1,0:T(8,128)(2,1)S(1)}, u32[]{:S(2)}, u32[]{:S(2)}) %collective-permute-start.9) | collective-permute-done | bytes 114720 | tf_op jit(solution)/shard_map/ppermute | solution.py:97
  93.5 0.7 fusion.20
  94.2 0.0 all-to-all-done.1
  94.2 0.1 convert_reduce_fusion
  94.3 0.2 fusion.15
  94.5 0.7 fusion.18
  (6 shorter events, 0.1 us)
Async XLA Ops:
  2.5 28.3 %all-to-all-start = ((bf16[32,8,2048]{2,1,0:T(8,128)(2,1)}), bf16[32,8,2048]{2,1,0:T(8,128)(2,1)S(1)}, u32[]{:S(2)}, u32[]{:S(2)}) async-start(bf16[32,8,2048]{2,1,0:T(8,128)(2,1)} %broadcast_in_dim.2), calls=%async_computation | async-start | bytes 2097152 | tf_op jit(solution)/shard_map/all_to_all | solution.py:110
  13.0 17.8 %collective-permute-start = (bf16[128,448]{1,0:T(8,128)(2,1)S(1)}, bf16[128,448]{1,0:T(8,128)(2,1)S(1)}, u32[]{:S(2)}, u32[]{:S(2)}) collective-permute-start(bf16[128,448]{1,0:T(8,128)(2,1)S(1)} %copy.9.own_ref), channel_id=1, source_target_pairs={{0,16},{16,0},{1,17},{17,1},{2,18},{18,2},{3,19},{19,3},{4,20},{20... | collective-permute-start | bytes 344072 | tf_op jit(solution)/shard_map/ppermute | solution.py:108
  18.0 12.8 %copy-start.1 = (f32[2048]{0:T(1024)S(1)}, f32[2048]{0:T(1024)}, u32[]{:S(2)}) copy-start(f32[2048]{0:T(1024)} %param.6) | copy-start | bytes 24580
  18.0 29.5 %copy-start.4 = (bf16[8,2048]{1,0:T(8,128)(2,1)S(1)}, bf16[8,2048]{1,0:T(8,128)(2,1)}, u32[]{:S(2)}) copy-start(bf16[8,2048]{1,0:T(8,128)(2,1)} %param.5) | copy-start | bytes 98308
  30.8 2.0 %copy-start = (bf16[896,2048]{1,0:T(8,128)(2,1)S(1)}, bf16[896,2048]{1,0:T(8,128)(2,1)}, u32[]{:S(2)}) copy-start(bf16[896,2048]{1,0:T(8,128)(2,1)} %pad_maximum_fusion.weight_ref) | copy-start | bytes 11010052
  32.8 35.4 %copy-start.2 = (bf16[2048,448]{0,1:T(8,128)(2,1)S(1)}, bf16[2048,448]{0,1:T(8,128)(2,1)}, u32[]{:S(2)}) copy-start(bf16[2048,448]{0,1:T(8,128)(2,1)} %param.8) | copy-start | bytes 5505028
  32.8 35.4 %copy-start.3 = (bf16[2048,448]{0,1:T(8,128)(2,1)S(1)}, bf16[2048,448]{0,1:T(8,128)(2,1)}, u32[]{:S(2)}) copy-start(bf16[2048,448]{0,1:T(8,128)(2,1)} %param.7) | copy-start | bytes 5505028
  36.2 23.0 %collective-permute-start.1 = (bf16[2,64,896]{2,1,0:T(8,128)(2,1)S(1)}, bf16[2,64,896]{2,1,0:T(8,128)(2,1)S(1)}, u32[]{:S(2)}, u32[]{:S(2)}) collective-permute-start(bf16[2,64,896]{2,1,0:T(8,128)(2,1)S(1)} %get-tuple-element.20), channel_id=1, source_target_pairs={{0,32},{32,64},{64,96},{96,128},{128,160},{160,192},{192,224},{224... | collective-permute-start | bytes 688136 | tf_op jit(solution)/shard_map/ppermute | solution.py:97
  38.1 21.1 %collective-permute-start.2 = (bf16[2,64,896]{2,1,0:T(8,128)(2,1)S(1)}, bf16[2,64,896]{2,1,0:T(8,128)(2,1)S(1)}, u32[]{:S(2)}, u32[]{:S(2)}) collective-permute-start(bf16[2,64,896]{2,1,0:T(8,128)(2,1)S(1)} %get-tuple-element.21), channel_id=1, source_target_pairs={{0,480},{32,0},{64,32},{96,64},{128,96},{160,128},{192,160},{224,1... | collective-permute-start | bytes 688136 | tf_op jit(solution)/shard_map/ppermute | solution.py:97
  47.7 11.5 %collective-permute-start.3 = (bf16[64,896]{1,0:T(8,128)(2,1)S(1)}, bf16[64,896]{1,0:T(8,128)(2,1)S(1)}, u32[]{:S(2)}, u32[]{:S(2)}) collective-permute-start(bf16[64,896]{1,0:T(8,128)(2,1)S(1)} %get-tuple-element.22), channel_id=1, source_target_pairs={{0,448},{32,480},{64,0},{96,32},{128,64},{160,96},{192,128},{224,1... | collective-permute-start | bytes 344072 | tf_op jit(solution)/shard_map/ppermute | solution.py:97
  52.1 23.3 %collective-permute-start.4 = (bf16[3,64,896]{2,1,0:T(8,128)(2,1)S(1)}, bf16[3,64,896]{2,1,0:T(8,128)(2,1)S(1)}, u32[]{:S(2)}, u32[]{:S(2)}) collective-permute-start(bf16[3,64,896]{2,1,0:T(8,128)(2,1)S(1)} %get-tuple-element.25), channel_id=1, source_target_pairs={{0,32},{32,64},{64,96},{96,128},{128,160},{160,192},{192,224},{224... | collective-permute-start | bytes 1032200 | tf_op jit(solution)/shard_map/ppermute | solution.py:97
  55.1 20.4 %collective-permute-start.5 = (bf16[3,64,896]{2,1,0:T(8,128)(2,1)S(1)}, bf16[3,64,896]{2,1,0:T(8,128)(2,1)S(1)}, u32[]{:S(2)}, u32[]{:S(2)}) collective-permute-start(bf16[3,64,896]{2,1,0:T(8,128)(2,1)S(1)} %get-tuple-element.26), channel_id=1, source_target_pairs={{0,480},{32,0},{64,32},{96,64},{128,96},{160,128},{192,160},{224,1... | collective-permute-start | bytes 1032200 | tf_op jit(solution)/shard_map/ppermute | solution.py:97
  59.3 15.2 %collective-permute-start.6 = (bf16[64,896]{1,0:T(8,128)(2,1)S(1)}, bf16[64,896]{1,0:T(8,128)(2,1)S(1)}, u32[]{:S(2)}, u32[]{:S(2)}) collective-permute-start(bf16[64,896]{1,0:T(8,128)(2,1)S(1)} %fusion.12), channel_id=1, source_target_pairs={{0,96},{32,128},{64,160},{96,192},{128,224},{160,256},{192,288},{2... | collective-permute-start | bytes 344072 | tf_op jit(solution)/shard_map/ppermute | solution.py:97
  62.3 13.1 %collective-permute-start.7 = (bf16[64,896]{1,0:T(8,128)(2,1)S(1)}, bf16[64,896]{1,0:T(8,128)(2,1)S(1)}, u32[]{:S(2)}, u32[]{:S(2)}) collective-permute-start(bf16[64,896]{1,0:T(8,128)(2,1)S(1)} %fusion.11), channel_id=1, source_target_pairs={{0,416},{32,448},{64,480},{96,0},{128,32},{160,64},{192,96},{224,1... | collective-permute-start | bytes 344072 | tf_op jit(solution)/shard_map/ppermute | solution.py:97
  69.7 24.5 %all-to-all-start.1 = ((bf16[16,8,2048]{2,1,0:T(8,128)(2,1)}), bf16[16,8,2048]{2,1,0:T(8,128)(2,1)S(1)}, u32[]{:S(2)}, u32[]{:S(2)}) async-start(bf16[16,8,2048]{2,1,0:T(8,128)(2,1)} %fusion), calls=%async_computation.1 | async-start | bytes 1048576 | tf_op jit(solution)/shard_map/all_to_all | solution.py:151
  75.6 12.7 %collective-permute-start.8 = (bf16[64,896]{1,0:T(8,128)(2,1)S(1)}, bf16[64,896]{1,0:T(8,128)(2,1)S(1)}, u32[]{:S(2)}, u32[]{:S(2)}) collective-permute-start(bf16[64,896]{1,0:T(8,128)(2,1)S(1)} %get-tuple-element.31), channel_id=1, source_target_pairs={{0,96},{32,128},{64,160},{96,192},{128,224},{160,256},{192,288},{2... | collective-permute-start | bytes 344072 | tf_op jit(solution)/shard_map/ppermute | solution.py:97
  82.4 11.0 %collective-permute-start.9 = (bf16[64,896]{1,0:T(8,128)(2,1)S(1)}, bf16[64,896]{1,0:T(8,128)(2,1)S(1)}, u32[]{:S(2)}, u32[]{:S(2)}) collective-permute-start(bf16[64,896]{1,0:T(8,128)(2,1)S(1)} %get-tuple-element.32), channel_id=1, source_target_pairs={{0,416},{32,448},{64,480},{96,0},{128,32},{160,64},{192,96},{224,1... | collective-permute-start | bytes 344072 | tf_op jit(solution)/shard_map/ppermute | solution.py:97

commit v5 on v4

--- a/solution.py
+++ b/solution.py
@@ -76,25 +76,34 @@
     grads = grads_ref[...]
     depth = far_ref.shape[0]
 
+    sign = 1 - 2 * lax.rem(z, 2)
+
     def block(relative):
-        chunk = lax.rem(z - relative + 2 * nz, nz)
+        chunk = lax.rem(z - sign * relative + 2 * nz, nz)
         lanes = pl.ds(pl.multiple_of(chunk * 2 * depth, 2 * depth), 2 * depth)
         both = contract_first(normed_ref[:, lanes], grads) * factor
         return jnp.where(first, both[:depth], both[depth:]).astype(jnp.bfloat16)
 
     far_ref[...] = block(nz // 2)
     for at, hub in enumerate(OUTER):
-        outer_ahead_ref[at] = block(hub - 1)
-        outer_behind_ref[at] = block(hub + 1)
+        outer_ahead_ref[at] = block(-hub - 1)
+        outer_behind_ref[at] = block(-hub + 1)
     for at, hub in enumerate(INNER):
-        inner_ahead_ref[at] = block(hub - 1)
-        inner_behind_ref[at] = block(hub + 1)
+        inner_ahead_ref[at] = block(-hub - 1)
+        inner_behind_ref[at] = block(-hub + 1)
     for at, hub in enumerate(OUTER + INNER):
         hub_ref[at] = block(hub)
 
 
-def shift(value, hops, nz):
-    return lax.ppermute(value, "z", [(i, (i + hops) % nz) for i in range(nz)])
+def join_kernel(gate_ref, up_ref, both_ref):
+    width = gate_ref.shape[0]
+    both_ref[:width] = gate_ref[...]
+    both_ref[width:] = up_ref[...]
+
+
+def move(value, hops, nz):
+    pairs = [(i, (i + (1 - 2 * (i % 2)) * hops) % nz) for i in range(nz)]
+    return lax.ppermute(value, "z", pairs)
 
 
 def shards(residual, norm_gain, gate_weight, up_weight, hidden_grad):
@@ -103,7 +112,12 @@
     features = residual.shape[1]
     depth = features // (nz * nh)
     f32, bf16 = jnp.float32, jnp.bfloat16
-    weight = jnp.concatenate([gate_weight.T, up_weight.T], axis=0)
+    weight = pl.pallas_call(
+        join_kernel,
+        out_shape=jax.ShapeDtypeStruct((2 * width, features), bf16),
+        compiler_params=pltpu.CompilerParams(vmem_limit_bytes=20 * 1024 * 1024),
+        name="join",
+    )(gate_weight.T, up_weight.T)
     own = hidden_grad
     other = lax.ppermute(own, "yh", [(0, 1), (1, 0)])
     copies = jnp.broadcast_to(residual[None], (nh * nt,) + residual.shape)
@@ -135,16 +149,16 @@
         name="local",
     )(gathered, norm_gain.reshape(1, features), weight, own, other)
 
-    from_far = shift(far, -2, nz).astype(f32)
-    outer_ahead, outer_behind = shift(outer_ahead, 1, nz), shift(outer_behind, -1, nz)
-    inner_ahead, inner_behind = shift(inner_ahead, 1, nz), shift(inner_behind, -1, nz)
+    from_far = move(far, -2, nz).astype(f32)
+    outer_ahead, outer_behind = move(outer_ahead, 1, nz), move(outer_behind, -1, nz)
+    inner_ahead, inner_behind = move(inner_ahead, 1, nz), move(inner_behind, -1, nz)
     hub = hub.astype(f32)
     outer = hub[:2] + outer_ahead.astype(f32) + outer_behind.astype(f32)
     plus, minus = lax.optimization_barrier(
         (outer[0].astype(bf16), (outer[1] + from_far).astype(bf16))
     )
     grads_own, first_sum = lax.optimization_barrier((grads_own, plus))
-    plus, minus = shift(first_sum, 3, nz), shift(minus, -3, nz)
+    plus, minus = move(first_sum, 3, nz), move(minus, -3, nz)
 
     part = jnp.dot(grads_own, weight, preferred_element_type=f32).astype(bf16)
     blocks = part.reshape(nt, rows // nt, features)
@@ -154,12 +168,11 @@
     plus, minus = lax.optimization_barrier((plus, minus))
     plus, minus = lax.optimization_barrier(
         (
-            (inner[0] + plus.astype(f32)).astype(bf16),
-            (inner[2] + minus.astype(f32)).astype(bf16),
+            (inner[0] + minus.astype(f32)).astype(bf16),
+            (inner[2] + plus.astype(f32)).astype(bf16),
         )
     )
-    plus, minus = shift(plus, 3, nz), shift(minus, -3, nz)
-    total = (inner[1] + plus.astype(f32) + minus.astype(f32)).astype(bf16)
+    plus, minus = move(plus, 3, nz), move(minus, -3, nz)
 
     scaled, inverse = normalize(residual)
     normed_grad = jnp.sum(moved.astype(f32), axis=0)
@@ -167,6 +180,7 @@
     residual_grad = (
         (weighted - scaled * jnp.mean(weighted * scaled, axis=-1, keepdims=True)) * inverse
     ).astype(bf16)
+    total = (inner[1] + plus.astype(f32) + minus.astype(f32)).astype(bf16)
     return (residual_grad, total[:, :width], total[:, width:])
 
 

time: 95.9 us -> 93.4 us (0.974)
  the two profiles are of different devices: /device:TPU:4 before, /device:TPU:36 now
where the time goes in v5:
time: 93.4 us; the launch traced here: 92.7 us
  starting transfers between devices  57 us (61%)
  waiting for transfers between devices  19.5 us (21%)
  local copies, waits for them, and re-layouts  8.83 us (9%)
  Pallas kernels  3.57 us (4%)
  matrix products  1.51 us (2%)
  other arithmetic  1.46 us (2%)
    ppermute x9, starting transfers between devices, move(): return lax.ppermute(value, 'z', pairs)  39.6 us
    ppermute x1, waiting for transfers between devices, shards(): other = lax.ppermute(own, 'yh', [(0, 1), (1, 0)])  10.1 us
    ppermute x9, waiting for transfers between devices, move(): return lax.ppermute(value, 'z', pairs)  9.38 us
    all_to_all x1, starting transfers between devices, shards(): gathered = lax.all_to_all(copies, ('yh',) + TENSOR, 0, 0, tiled=True)  7.6 us
    unnamed x15, local copies, waits for them, and re-layouts  5.45 us
    ppermute x1, starting transfers between devices, shards(): other = lax.ppermute(own, 'yh', [(0, 1), (1, 0)])  4.92 us
    all_to_all x1, starting transfers between devices, shards(): moved = lax.all_to_all(blocks, TENSOR, 0, 0, tiled=True)  4.82 us
    pallas_call x1, Pallas kernels, shards(): pl.pallas_call(functools.partial(local_kernel, factor, nz), out_shape=(sh...  3.34 us
  transfers between devices with their start and end apart: 12, of which 4 were waited for; matrix products, arithmetic and copies ran while one was open for 4% of the time, Pallas kernels for 0%

profile of v5, /device:TPU:36, one launch (start us, length us, event | category | flops | bytes accessed | tf_op | source)
XLA Modules:
  0.0 92.7 jit_solution(4841818571439090884)
XLA Ops:
  0.6 0.0 copy-start.6
  0.6 0.0 copy-start.2
  0.7 2.0 %broadcast_in_dim.2 = bf16[32,8,2048]{2,1,0:T(8,128)(2,1)} broadcast(bf16[8,2048]{1,0:T(8,128)(2,1)} %param.5), dimensions={1,2} | broadcast | bytes 1081344 | tf_op jit(solution)/shard_map/broadcast_in_dim | solution.py:123
  2.6 7.6 %all-to-all-start = ((bf16[32,8,2048]{2,1,0:T(8,128)(2,1)}), bf16[32,8,2048]{2,1,0:T(8,128)(2,1)S(1)}, u32[]{:S(2)}, u32[]{:S(2)}) async-start(bf16[32,8,2048]{2,1,0:T(8,128)(2,1)} %broadcast_in_dim.2), calls=%async_computation | async-start | bytes 2097152 | tf_op jit(solution)/shard_map/all_to_all | solution.py:124
  10.3 0.0 copy-done.6
  10.3 0.1 copy.9.own_ref
  10.4 4.9 %collective-permute-start = (bf16[128,448]{1,0:T(8,128)(2,1)S(1)}, bf16[128,448]{1,0:T(8,128)(2,1)S(1)}, u32[]{:S(2)}, u32[]{:S(2)}) collective-permute-start(bf16[128,448]{1,0:T(8,128)(2,1)S(1)} %copy.9.own_ref), channel_id=1, source_target_pairs={{0,16},{16,0},{1,17},{17,1},{2,18},{18,2},{3,19},{19,3},{4,20},{20... | collective-permute-start | bytes 344072 | tf_op jit(solution)/shard_map/ppermute | solution.py:122
  15.3 0.0 copy-done.2
  15.3 0.0 copy-start.3
  15.3 1.5 %copy-done.3 = bf16[2048,448]{0,1:T(8,128)(2,1)S(1)} copy-done((bf16[2048,448]{0,1:T(8,128)(2,1)S(1)}, bf16[2048,448]{0,1:T(8,128)(2,1)}, u32[]{:S(2)}) %copy-start.3) | copy-done | bytes 1835032
  16.8 0.0 copy-start.4
  16.8 0.2 join.1.weight_ref
  17.1 0.0 copy-start
  17.1 1.8 %copy-done = bf16[896,2048]{1,0:T(8,128)(2,1)} copy-done((bf16[896,2048]{1,0:T(8,128)(2,1)}, bf16[896,2048]{1,0:T(8,128)(2,1)S(1)}, u32[]{:S(2)}) %copy-start) | copy-done | bytes 3670040
  18.9 10.1 %collective-permute-done.other_ref = bf16[128,448]{1,0:T(8,128)(2,1)S(1)} collective-permute-done((bf16[128,448]{1,0:T(8,128)(2,1)S(1)}, bf16[128,448]{1,0:T(8,128)(2,1)S(1)}, u32[]{:S(2)}, u32[]{:S(2)}) %collective-permute-start) | collective-permute-done | bytes 114720 | tf_op jit(solution)/shard_map/ppermute | solution.py:122
  29.0 0.0 all-to-all-done
  29.0 0.0 copy-done.4
  29.0 0.0 copy-start.1
  29.0 2.0 %copy-done.1 = bf16[896,2048]{1,0:T(8,128)(2,1)S(1)} copy-done((bf16[896,2048]{1,0:T(8,128)(2,1)S(1)}, bf16[896,2048]{1,0:T(8,128)(2,1)}, u32[]{:S(2)}) %copy-start.1) | copy-done | bytes 3670040
  31.0 0.0 copy-start.5
  31.0 3.3 %local.1 = (bf16[64,896]{1,0:T(8,128)(2,1)S(1)}, bf16[2,64,896]{2,1,0:T(8,128)(2,1)S(1)}, bf16[2,64,896]{2,1,0:T(8,128)(2,1)S(1)}, bf16[3,64,896]{2,1,0:T(8,128)...) custom-call(bf16[256,2048]{1,0:T(8,128)(2,1)S(1)} %bitcast.38, ...), custom_call_target="tpu_custom_call" | custom-call | flops 1879048192 | bytes 7340032 | tf_op jit(solution)/shard_map/local/pallas_call | solution.py:128
  34.3 4.0 %collective-permute-start.1 = (bf16[2,64,896]{2,1,0:T(8,128)(2,1)S(1)}, bf16[2,64,896]{2,1,0:T(8,128)(2,1)S(1)}, u32[]{:S(2)}, u32[]{:S(2)}) collective-permute-start(bf16[2,64,896]{2,1,0:T(8,128)(2,1)S(1)} %get-tuple-element.20), channel_id=1, source_target_pairs={{0,32},{32,0},{64,96},{96,64},{128,160},{160,128},{192,224},{224,1... | collective-permute-start | bytes 688136 | tf_op jit(solution)/shard_map/ppermute | solution.py:106
  38.4 3.7 %collective-permute-start.2 = (bf16[2,64,896]{2,1,0:T(8,128)(2,1)S(1)}, bf16[2,64,896]{2,1,0:T(8,128)(2,1)S(1)}, u32[]{:S(2)}, u32[]{:S(2)}) collective-permute-start(bf16[2,64,896]{2,1,0:T(8,128)(2,1)S(1)} %get-tuple-element.21), channel_id=1, source_target_pairs={{0,480},{32,64},{64,32},{96,128},{128,96},{160,192},{192,160},{224... | collective-permute-start | bytes 688136 | tf_op jit(solution)/shard_map/ppermute | solution.py:106
  42.0 0.0 copy-done.5
  42.0 0.1 fusion.19
  42.2 0.1 convert_element_type.58
  42.2 6.4 %collective-permute-start.3 = (bf16[64,896]{1,0:T(8,128)(2,1)S(1)}, bf16[64,896]{1,0:T(8,128)(2,1)S(1)}, u32[]{:S(2)}, u32[]{:S(2)}) collective-permute-start(bf16[64,896]{1,0:T(8,128)(2,1)S(1)} %get-tuple-element.22), channel_id=1, source_target_pairs={{0,448},{32,96},{64,0},{96,160},{128,64},{160,224},{192,128},{224,... | collective-permute-start | bytes 344072 | tf_op jit(solution)/shard_map/ppermute | solution.py:106
  48.6 5.7 %collective-permute-start.4 = (bf16[3,64,896]{2,1,0:T(8,128)(2,1)S(1)}, bf16[3,64,896]{2,1,0:T(8,128)(2,1)S(1)}, u32[]{:S(2)}, u32[]{:S(2)}) collective-permute-start(bf16[3,64,896]{2,1,0:T(8,128)(2,1)S(1)} %get-tuple-element.25), channel_id=1, source_target_pairs={{0,32},{32,0},{64,96},{96,64},{128,160},{160,128},{192,224},{224,1... | collective-permute-start | bytes 1032200 | tf_op jit(solution)/shard_map/ppermute | solution.py:106
  54.3 2.0 %collective-permute-start.5 = (bf16[3,64,896]{2,1,0:T(8,128)(2,1)S(1)}, bf16[3,64,896]{2,1,0:T(8,128)(2,1)S(1)}, u32[]{:S(2)}, u32[]{:S(2)}) collective-permute-start(bf16[3,64,896]{2,1,0:T(8,128)(2,1)S(1)} %get-tuple-element.26), channel_id=1, source_target_pairs={{0,480},{32,64},{64,32},{96,128},{128,96},{160,192},{192,160},{224... | collective-permute-start | bytes 1032200 | tf_op jit(solution)/shard_map/ppermute | solution.py:106
  56.3 0.0 collective-permute-done.1
  56.3 0.0 collective-permute-done.2
  56.3 0.1 fusion.2
  56.4 0.0 collective-permute-done.3
  56.5 0.7 fusion.12
  57.1 5.9 %collective-permute-start.6 = (bf16[64,896]{1,0:T(8,128)(2,1)}, bf16[64,896]{1,0:T(8,128)(2,1)S(1)}, u32[]{:S(2)}, u32[]{:S(2)}) collective-permute-start(bf16[64,896]{1,0:T(8,128)(2,1)} %fusion.12), channel_id=1, source_target_pairs={{0,96},{32,448},{64,160},{96,0},{128,224},{160,64},{192,288},{224,... | collective-permute-start | bytes 344072 | tf_op jit(solution)/shard_map/ppermute | solution.py:106
  63.0 3.9 %collective-permute-start.7 = (bf16[64,896]{1,0:T(8,128)(2,1)S(1)}, bf16[64,896]{1,0:T(8,128)(2,1)S(1)}, u32[]{:S(2)}, u32[]{:S(2)}) collective-permute-start(bf16[64,896]{1,0:T(8,128)(2,1)S(1)} %fusion.11), channel_id=1, source_target_pairs={{0,416},{32,128},{64,480},{96,192},{128,32},{160,256},{192,96},{22... | collective-permute-start | bytes 344072 | tf_op jit(solution)/shard_map/ppermute | solution.py:106
  66.9 1.5 %fusion = bf16[16,8,2048]{2,1,0:T(8,128)(2,1)} fusion(bf16[128,896]{1,0:T(8,128)(2,1)S(1)} %get-tuple-element.24, bf16[896,2048]{1,0:T(8,128)(2,1)S(1)} %copy-done.1), kind=kOutput, calls=%fused_computation.1 | convolution fusion | flops 470024192 | bytes 4423680 | tf_op jit(solution)/shard_map/dot_general | solution.py:163
  68.4 4.8 %all-to-all-start.1 = ((bf16[16,8,2048]{2,1,0:T(8,128)(2,1)}), bf16[16,8,2048]{2,1,0:T(8,128)(2,1)S(1)}, u32[]{:S(2)}, u32[]{:S(2)}) async-start(bf16[16,8,2048]{2,1,0:T(8,128)(2,1)} %fusion), calls=%async_computation.1 | async-start | bytes 1048576 | tf_op jit(solution)/shard_map/all_to_all | solution.py:165
  73.2 0.0 collective-permute-done.6
  73.2 1.2 %collective-permute-done.7 = bf16[64,896]{1,0:T(8,128)(2,1)S(1)} collective-permute-done((bf16[64,896]{1,0:T(8,128)(2,1)S(1)}, bf16[64,896]{1,0:T(8,128)(2,1)S(1)}, u32[]{:S(2)}, u32[]{:S(2)}) %collective-permute-start.7) | collective-permute-done | bytes 114720 | tf_op jit(solution)/shard_map/ppermute | solution.py:106
  74.4 0.0 collective-permute-done.4
  74.4 0.0 collective-permute-done.5
  74.4 0.1 fusion.1
  74.6 4.4 %collective-permute-start.8 = (bf16[64,896]{1,0:T(8,128)(2,1)S(1)}, bf16[64,896]{1,0:T(8,128)(2,1)S(1)}, u32[]{:S(2)}, u32[]{:S(2)}) collective-permute-start(bf16[64,896]{1,0:T(8,128)(2,1)S(1)} %get-tuple-element.31), channel_id=1, source_target_pairs={{0,96},{32,448},{64,160},{96,0},{128,224},{160,64},{192,288},{224,... | collective-permute-start | bytes 344072 | tf_op jit(solution)/shard_map/ppermute | solution.py:106
  79.0 3.8 %collective-permute-start.9 = (bf16[64,896]{1,0:T(8,128)(2,1)S(1)}, bf16[64,896]{1,0:T(8,128)(2,1)S(1)}, u32[]{:S(2)}, u32[]{:S(2)}) collective-permute-start(bf16[64,896]{1,0:T(8,128)(2,1)S(1)} %get-tuple-element.32), channel_id=1, source_target_pairs={{0,416},{32,128},{64,480},{96,192},{128,32},{160,256},{192,96},{22... | collective-permute-start | bytes 344072 | tf_op jit(solution)/shard_map/ppermute | solution.py:106
  82.8 4.5 %collective-permute-done.8 = bf16[64,896]{1,0:T(8,128)(2,1)S(1)} collective-permute-done((bf16[64,896]{1,0:T(8,128)(2,1)S(1)}, bf16[64,896]{1,0:T(8,128)(2,1)S(1)}, u32[]{:S(2)}, u32[]{:S(2)}) %collective-permute-start.8) | collective-permute-done | bytes 114720 | tf_op jit(solution)/shard_map/ppermute | solution.py:106
  87.3 3.7 %collective-permute-done.9 = bf16[64,896]{1,0:T(8,128)(2,1)S(1)} collective-permute-done((bf16[64,896]{1,0:T(8,128)(2,1)S(1)}, bf16[64,896]{1,0:T(8,128)(2,1)S(1)}, u32[]{:S(2)}, u32[]{:S(2)}) %collective-permute-start.9) | collective-permute-done | bytes 114720 | tf_op jit(solution)/shard_map/ppermute | solution.py:106
  91.0 0.7 fusion.20
  91.7 0.0 all-to-all-done.1
  91.7 0.1 convert_reduce_fusion
  91.8 0.2 fusion.15
  92.0 0.7 fusion.18
  (5 shorter events, 0.1 us)
Async XLA Ops:
  0.6 9.6 %copy-start.6 = (bf16[128,448]{0,1:T(8,128)(2,1)S(1)}, bf16[128,448]{0,1:T(8,128)(2,1)}, u32[]{:S(2)}) copy-start(bf16[128,448]{0,1:T(8,128)(2,1)} %param.9) | copy-start | bytes 344068
  0.6 14.7 %copy-start.2 = (bf16[2048,448]{0,1:T(8,128)(2,1)S(1)}, bf16[2048,448]{0,1:T(8,128)(2,1)}, u32[]{:S(2)}) copy-start(bf16[2048,448]{0,1:T(8,128)(2,1)} %param.7) | copy-start | bytes 5505028
  2.6 26.3 %all-to-all-start = ((bf16[32,8,2048]{2,1,0:T(8,128)(2,1)}), bf16[32,8,2048]{2,1,0:T(8,128)(2,1)S(1)}, u32[]{:S(2)}, u32[]{:S(2)}) async-start(bf16[32,8,2048]{2,1,0:T(8,128)(2,1)} %broadcast_in_dim.2), calls=%async_computation | async-start | bytes 2097152 | tf_op jit(solution)/shard_map/all_to_all | solution.py:124
  10.4 18.6 %collective-permute-start = (bf16[128,448]{1,0:T(8,128)(2,1)S(1)}, bf16[128,448]{1,0:T(8,128)(2,1)S(1)}, u32[]{:S(2)}, u32[]{:S(2)}) collective-permute-start(bf16[128,448]{1,0:T(8,128)(2,1)S(1)} %copy.9.own_ref), channel_id=1, source_target_pairs={{0,16},{16,0},{1,17},{17,1},{2,18},{18,2},{3,19},{19,3},{4,20},{20... | collective-permute-start | bytes 344072 | tf_op jit(solution)/shard_map/ppermute | solution.py:122
  15.3 1.5 %copy-start.3 = (bf16[2048,448]{0,1:T(8,128)(2,1)S(1)}, bf16[2048,448]{0,1:T(8,128)(2,1)}, u32[]{:S(2)}) copy-start(bf16[2048,448]{0,1:T(8,128)(2,1)} %param.8) | copy-start | bytes 5505028
  16.8 12.1 %copy-start.4 = (f32[2048]{0:T(1024)S(1)}, f32[2048]{0:T(1024)}, u32[]{:S(2)}) copy-start(f32[2048]{0:T(1024)} %param.6) | copy-start | bytes 24580
  17.1 1.8 %copy-start = (bf16[896,2048]{1,0:T(8,128)(2,1)}, bf16[896,2048]{1,0:T(8,128)(2,1)S(1)}, u32[]{:S(2)}) copy-start(bf16[896,2048]{1,0:T(8,128)(2,1)S(1)} %join.1.weight_ref) | copy-start | bytes 11010052
  29.0 2.0 %copy-start.1 = (bf16[896,2048]{1,0:T(8,128)(2,1)S(1)}, bf16[896,2048]{1,0:T(8,128)(2,1)}, u32[]{:S(2)}) copy-start(bf16[896,2048]{1,0:T(8,128)(2,1)} %copy-done) | copy-start | bytes 11010052
  31.0 11.0 %copy-start.5 = (bf16[8,2048]{1,0:T(8,128)(2,1)S(1)}, bf16[8,2048]{1,0:T(8,128)(2,1)}, u32[]{:S(2)}) copy-start(bf16[8,2048]{1,0:T(8,128)(2,1)} %param.5) | copy-start | bytes 98308
  34.3 22.0 %collective-permute-start.1 = (bf16[2,64,896]{2,1,0:T(8,128)(2,1)S(1)}, bf16[2,64,896]{2,1,0:T(8,128)(2,1)S(1)}, u32[]{:S(2)}, u32[]{:S(2)}) collective-permute-start(bf16[2,64,896]{2,1,0:T(8,128)(2,1)S(1)} %get-tuple-element.20), channel_id=1, source_target_pairs={{0,32},{32,0},{64,96},{96,64},{128,160},{160,128},{192,224},{224,1... | collective-permute-start | bytes 688136 | tf_op jit(solution)/shard_map/ppermute | solution.py:106
  38.4 18.0 %collective-permute-start.2 = (bf16[2,64,896]{2,1,0:T(8,128)(2,1)S(1)}, bf16[2,64,896]{2,1,0:T(8,128)(2,1)S(1)}, u32[]{:S(2)}, u32[]{:S(2)}) collective-permute-start(bf16[2,64,896]{2,1,0:T(8,128)(2,1)S(1)} %get-tuple-element.21), channel_id=1, source_target_pairs={{0,480},{32,64},{64,32},{96,128},{128,96},{160,192},{192,160},{224... | collective-permute-start | bytes 688136 | tf_op jit(solution)/shard_map/ppermute | solution.py:106
  42.2 14.2 %collective-permute-start.3 = (bf16[64,896]{1,0:T(8,128)(2,1)S(1)}, bf16[64,896]{1,0:T(8,128)(2,1)S(1)}, u32[]{:S(2)}, u32[]{:S(2)}) collective-permute-start(bf16[64,896]{1,0:T(8,128)(2,1)S(1)} %get-tuple-element.22), channel_id=1, source_target_pairs={{0,448},{32,96},{64,0},{96,160},{128,64},{160,224},{192,128},{224,... | collective-permute-start | bytes 344072 | tf_op jit(solution)/shard_map/ppermute | solution.py:106
  48.6 25.8 %collective-permute-start.4 = (bf16[3,64,896]{2,1,0:T(8,128)(2,1)S(1)}, bf16[3,64,896]{2,1,0:T(8,128)(2,1)S(1)}, u32[]{:S(2)}, u32[]{:S(2)}) collective-permute-start(bf16[3,64,896]{2,1,0:T(8,128)(2,1)S(1)} %get-tuple-element.25), channel_id=1, source_target_pairs={{0,32},{32,0},{64,96},{96,64},{128,160},{160,128},{192,224},{224,1... | collective-permute-start | bytes 1032200 | tf_op jit(solution)/shard_map/ppermute | solution.py:106
  54.3 20.2 %collective-permute-start.5 = (bf16[3,64,896]{2,1,0:T(8,128)(2,1)S(1)}, bf16[3,64,896]{2,1,0:T(8,128)(2,1)S(1)}, u32[]{:S(2)}, u32[]{:S(2)}) collective-permute-start(bf16[3,64,896]{2,1,0:T(8,128)(2,1)S(1)} %get-tuple-element.26), channel_id=1, source_target_pairs={{0,480},{32,64},{64,32},{96,128},{128,96},{160,192},{192,160},{224... | collective-permute-start | bytes 1032200 | tf_op jit(solution)/shard_map/ppermute | solution.py:106
  57.1 16.1 %collective-permute-start.6 = (bf16[64,896]{1,0:T(8,128)(2,1)}, bf16[64,896]{1,0:T(8,128)(2,1)S(1)}, u32[]{:S(2)}, u32[]{:S(2)}) collective-permute-start(bf16[64,896]{1,0:T(8,128)(2,1)} %fusion.12), channel_id=1, source_target_pairs={{0,96},{32,448},{64,160},{96,0},{128,224},{160,64},{192,288},{224,... | collective-permute-start | bytes 344072 | tf_op jit(solution)/shard_map/ppermute | solution.py:106
  63.0 11.4 %collective-permute-start.7 = (bf16[64,896]{1,0:T(8,128)(2,1)S(1)}, bf16[64,896]{1,0:T(8,128)(2,1)S(1)}, u32[]{:S(2)}, u32[]{:S(2)}) collective-permute-start(bf16[64,896]{1,0:T(8,128)(2,1)S(1)} %fusion.11), channel_id=1, source_target_pairs={{0,416},{32,128},{64,480},{96,192},{128,32},{160,256},{192,96},{22... | collective-permute-start | bytes 344072 | tf_op jit(solution)/shard_map/ppermute | solution.py:106
  68.4 23.3 %all-to-all-start.1 = ((bf16[16,8,2048]{2,1,0:T(8,128)(2,1)}), bf16[16,8,2048]{2,1,0:T(8,128)(2,1)S(1)}, u32[]{:S(2)}, u32[]{:S(2)}) async-start(bf16[16,8,2048]{2,1,0:T(8,128)(2,1)} %fusion), calls=%async_computation.1 | async-start | bytes 1048576 | tf_op jit(solution)/shard_map/all_to_all | solution.py:165
  74.6 12.7 %collective-permute-start.8 = (bf16[64,896]{1,0:T(8,128)(2,1)S(1)}, bf16[64,896]{1,0:T(8,128)(2,1)S(1)}, u32[]{:S(2)}, u32[]{:S(2)}) collective-permute-start(bf16[64,896]{1,0:T(8,128)(2,1)S(1)} %get-tuple-element.31), channel_id=1, source_target_pairs={{0,96},{32,448},{64,160},{96,0},{128,224},{160,64},{192,288},{224,... | collective-permute-start | bytes 344072 | tf_op jit(solution)/shard_map/ppermute | solution.py:106
  79.0 12.0 %collective-permute-start.9 = (bf16[64,896]{1,0:T(8,128)(2,1)S(1)}, bf16[64,896]{1,0:T(8,128)(2,1)S(1)}, u32[]{:S(2)}, u32[]{:S(2)}) collective-permute-start(bf16[64,896]{1,0:T(8,128)(2,1)S(1)} %get-tuple-element.32), channel_id=1, source_target_pairs={{0,416},{32,128},{64,480},{96,192},{128,32},{160,256},{192,96},{22... | collective-permute-start | bytes 344072 | tf_op jit(solution)/shard_map/ppermute | solution.py:106

commit v6 on v5

v6 whole, which is shorter than its diff:
```python
import functools

import jax
import jax.numpy as jnp
from jax import lax
from jax.experimental import pallas as pl
from jax.experimental.pallas import tpu as pltpu
from jax.sharding import Mesh
from jax.sharding import PartitionSpec as P

EPSILON = 1e-05
DP = ("z", "yh")
TENSOR = ("x", "yl", "core")
OUTER = (-6, 6)
INNER = (-3, 0, 3)


def normalize(residual):
    values = residual.astype(jnp.float32)
    inverse = lax.rsqrt(jnp.mean(values * values, axis=-1, keepdims=True) + EPSILON)
    return (values * inverse, inverse)


def contract_last(left, right):
    return lax.dot_general(
        left, right, (((1,), (1,)), ((), ())), preferred_element_type=jnp.float32
    )


def contract_first(left, right):
    return lax.dot_general(
        left, right, (((0,), (0,)), ((), ())), preferred_element_type=jnp.float32
    )


def local_kernel(
    factor,
    nz,
    block_rows,
    same_ref,
    swapped_ref,
    gain_ref,
    gate_ref,
    up_ref,
    own_ref,
    other_ref,
    far_ref,
    outer_ahead_ref,
    outer_behind_ref,
    inner_ahead_ref,
    inner_behind_ref,
    outer_hub_ref,
    inner_hub_ref,
    grads_own_ref,
    normed_ref,
    grads_ref,
):
    z = lax.axis_index("z")
    half = lax.axis_index("yh")
    rows, width = own_ref.shape
    tokens = same_ref.shape[0]
    gain = gain_ref[...]
    normed_ref[:tokens] = (normalize(same_ref[...])[0] * gain).astype(jnp.bfloat16)
    normed_ref[tokens:] = (normalize(swapped_ref[...])[0] * gain).astype(jnp.bfloat16)
    normed = normed_ref[...]
    gate_value = contract_last(normed, gate_ref[...])
    up_value = contract_last(normed, up_ref[...])
    first = half == 0
    even = lax.axis_index("core") == 0
    count = lax.axis_size("core")
    split = (rows // (count * block_rows), count, block_rows, width)
    own = own_ref[...].astype(jnp.float32).reshape(split)
    other = other_ref[...].astype(jnp.float32).reshape(split)

    def by_core(values, same):
        near, away = (0, 1) if same else (1, 0)
        return jnp.where(even, values[:, near], values[:, away]).reshape(rows // count, width)

    pieces = []
    for same in (True, False):
        mine, theirs = by_core(own, same), by_core(other, same)
        pieces += [jnp.where(first, mine, theirs), jnp.where(first, theirs, mine)]
    upstream = jnp.concatenate(pieces, axis=0)
    sigmoid_gate = jax.nn.sigmoid(gate_value)
    weighted = upstream * sigmoid_gate
    gate_grad = weighted * up_value * (1.0 + gate_value * (1.0 - sigmoid_gate))
    up_grad = weighted * gate_value
    grads_ref[:, :width] = gate_grad.astype(jnp.bfloat16)
    grads_ref[:, width:] = up_grad.astype(jnp.bfloat16)
    piece = rows // count

    def own_rows(values):
        near = jnp.where(first, values[:piece], values[piece : 2 * piece])
        away = jnp.where(first, values[2 * piece : 3 * piece], values[3 * piece :])
        near = near.reshape(piece // block_rows, 1, block_rows, width)
        away = away.reshape(piece // block_rows, 1, block_rows, width)
        both = jnp.concatenate(
            [jnp.where(even, near, away), jnp.where(even, away, near)], axis=1
        )
        return both.reshape(rows, width).astype(jnp.bfloat16)

    grads_own_ref[:, :width] = own_rows(gate_grad)
    grads_own_ref[:, width:] = own_rows(up_grad)
    grads = grads_ref[...]
    depth = far_ref.shape[0]

    sign = 1 - 2 * lax.rem(z, 2)

    def block(relative):
        chunk = lax.rem(z - sign * relative + 2 * nz, nz)
        lanes = pl.ds(pl.multiple_of(chunk * 2 * depth, 2 * depth), 2 * depth)
        both = contract_first(normed_ref[:, lanes], grads) * factor
        return jnp.where(first, both[:depth], both[depth:]).astype(jnp.bfloat16)

    far_ref[...] = block(nz // 2)
    for at, hub in enumerate(OUTER):
        outer_ahead_ref[at] = block(-hub - 1)
        outer_behind_ref[at] = block(-hub + 1)
    for at, hub in enumerate(INNER):
        inner_ahead_ref[at] = block(-hub - 1)
        inner_behind_ref[at] = block(-hub + 1)
    for at, hub in enumerate(OUTER):
        outer_hub_ref[at] = block(hub)
    for at, hub in enumerate(INNER):
        inner_hub_ref[at] = block(hub)


def move(value, hops, nz):
    pairs = [(i, (i + (1 - 2 * (i % 2)) * hops) % nz) for i in range(nz)]
    return lax.ppermute(value, "z", pairs)


def shards(residual, norm_gain, gate_weight, up_weight, hidden_grad):
    nz, nh, nt = lax.axis_size("z"), lax.axis_size("yh"), lax.axis_size(TENSOR)
    rows, width = hidden_grad.shape
    features = residual.shape[1]
    depth = features // (nz * nh)
    f32, bf16 = jnp.float32, jnp.bfloat16
    own = hidden_grad
    other = lax.ppermute(own, "yh", [(0, 1), (1, 0)])
    chips = nh * nt // lax.axis_size("core")
    copies = jnp.broadcast_to(residual[None], (chips,) + residual.shape)
    same = lax.all_to_all(copies, ("yh", "x", "yl"), 0, 0, tiled=True)
    same = same.reshape(chips * residual.shape[0], features)
    same, other = lax.optimization_barrier((same, other))
    swapped = lax.ppermute(same, "core", [(0, 1), (1, 0)])
    factor = float(rows * nz * nh) ** (-0.5)
    shape = jax.ShapeDtypeStruct
    far, outer_ahead, outer_behind, inner_ahead, inner_behind, outer_hub, inner_hub, grads_own = pl.pallas_call(
        functools.partial(local_kernel, factor, nz, residual.shape[0]),
        out_shape=(
            shape((depth, 2 * width), bf16),
            shape((len(OUTER), depth, 2 * width), bf16),
            shape((len(OUTER), depth, 2 * width), bf16),
            shape((len(INNER), depth, 2 * width), bf16),
            shape((len(INNER), depth, 2 * width), bf16),
            shape((len(OUTER), depth, 2 * width), bf16),
            shape((len(INNER), depth, 2 * width), bf16),
            shape((rows, 2 * width), bf16),
        ),
        scratch_shapes=[
            pltpu.VMEM((nh * rows, features), bf16),
            pltpu.VMEM((nh * rows, 2 * width), bf16),
        ],
        compiler_params=pltpu.CompilerParams(vmem_limit_bytes=20 * 1024 * 1024),
        cost_estimate=pl.CostEstimate(
            flops=8 * nh * rows * features * width,
            bytes_accessed=8 * features * width,
            transcendentals=nh * rows * width,
        ),
        name="local",
    )(same, swapped, norm_gain.reshape(1, features), gate_weight.T, up_weight.T, own, other)

    from_far = move(far, -2, nz).astype(f32)
    outer_ahead, outer_behind = move(outer_ahead, 1, nz), move(outer_behind, -1, nz)
    inner_ahead, inner_behind = move(inner_ahead, 1, nz), move(inner_behind, -1, nz)

    def outer(at):
        return (
            outer_hub[at].astype(f32)
            + outer_ahead[at].astype(f32)
            + outer_behind[at].astype(f32)
        )

    def inner(at):
        return (
            inner_hub[at].astype(f32)
            + inner_ahead[at].astype(f32)
            + inner_behind[at].astype(f32)
        )

    plus, minus = lax.optimization_barrier(
        (outer(0).astype(bf16), (outer(1) + from_far).astype(bf16))
    )
    grads_own, first_sum = lax.optimization_barrier((grads_own, plus))
    plus, minus = move(first_sum, 3, nz), move(minus, -3, nz)

    part = contract_last(grads_own[:, :width], gate_weight)
    part = (part + contract_last(grads_own[:, width:], up_weight)).astype(bf16)
    blocks = part.reshape(nt, rows // nt, features)
    moved = lax.all_to_all(blocks, TENSOR, 0, 0, tiled=True)

    plus, minus = lax.optimization_barrier((plus, minus))
    plus, minus = lax.optimization_barrier(
        (
            (inner(0) + minus.astype(f32)).astype(bf16),
            (inner(2) + plus.astype(f32)).astype(bf16),
        )
    )
    plus, minus = move(plus, 3, nz), move(minus, -3, nz)

    scaled, inverse = normalize(residual)
    normed_grad = jnp.sum(moved.astype(f32), axis=0)
    weighted = normed_grad * norm_gain
    residual_grad = (
        (weighted - scaled * jnp.mean(weighted * scaled, axis=-1, keepdims=True)) * inverse
    ).astype(bf16)
    total = (inner(1) + plus.astype(f32) + minus.astype(f32)).astype(bf16)
    return (residual_grad, total[:, :width], total[:, width:])


def solution(mesh):
    fine = Mesh(mesh.devices.reshape(16, 2, 4, 2, 2), DP + TENSOR)
    return jax.shard_map(
        shards,
        mesh=fine,
        in_specs=(
            P(DP + TENSOR, None),
            P(),
            P(None, TENSOR),
            P(None, TENSOR),
            P(DP, TENSOR),
        ),
        out_specs=(P(DP + TENSOR, None), P(DP, TENSOR), P(DP, TENSOR)),
        check_vma=False,
    )
```

time: 93.4 us -> 93.7 us (level)
  the two profiles are of different devices: /device:TPU:36 before, /device:TPU:67 now
where the time goes in v6:
time: 93.7 us; the launch traced here: 92.9 us
  starting transfers between devices  57.9 us (62%)
  waiting for transfers between devices  18.1 us (19%)
  local copies, waits for them, and re-layouts  6.54 us (7%)
  other arithmetic  4.55 us (5%)
  Pallas kernels  3.29 us (4%)
  matrix products  1.73 us (2%)
    ppermute x9, starting transfers between devices, move(): return lax.ppermute(value, 'z', pairs)  37.1 us
    ppermute x9, waiting for transfers between devices, move(): return lax.ppermute(value, 'z', pairs)  9.77 us
    all_to_all x1, starting transfers between devices, shards(): same = lax.all_to_all(copies, ('yh', 'x', 'yl'), 0, 0, tiled=True)  6.92 us
    ppermute x1, waiting for transfers between devices, shards(): other = lax.ppermute(own, 'yh', [(0, 1), (1, 0)])  6.76 us
    all_to_all x1, starting transfers between devices, shards(): moved = lax.all_to_all(blocks, TENSOR, 0, 0, tiled=True)  6.51 us
    ppermute x1, starting transfers between devices, shards(): other = lax.ppermute(own, 'yh', [(0, 1), (1, 0)])  4.6 us
    unnamed x15, local copies, waits for them, and re-layouts  4.08 us
    pallas_call x1, Pallas kernels, shards(): pl.pallas_call(functools.partial(local_kernel, factor, nz, residual.shape...  3.29 us
  transfers between devices with their start and end apart: 13, of which 3 were waited for; matrix products, arithmetic and copies ran while one was open for 8% of the time, Pallas kernels for 0%

profile of v6, /device:TPU:67, one launch (start us, length us, event | category | flops | bytes accessed | tf_op | source)
XLA Modules:
  0.0 92.9 jit_solution(14494910734036208140)
XLA Ops:
  0.6 0.0 copy-start.2
  0.6 0.0 copy-start
  0.7 1.7 %broadcast_in_dim.2 = bf16[16,8,2048]{2,1,0:T(8,128)(2,1)} broadcast(bf16[8,2048]{1,0:T(8,128)(2,1)} %param.5), dimensions={1,2} | broadcast | bytes 557056 | tf_op jit(solution)/shard_map/broadcast_in_dim | solution.py:142
  2.4 6.9 %all-to-all-start = ((bf16[16,8,2048]{2,1,0:T(8,128)(2,1)}), bf16[16,8,2048]{2,1,0:T(8,128)(2,1)S(1)}, u32[]{:S(2)}, u32[]{:S(2)}) async-start(bf16[16,8,2048]{2,1,0:T(8,128)(2,1)} %broadcast_in_dim.2), calls=%async_computation | async-start | bytes 1048576 | tf_op jit(solution)/shard_map/all_to_all | solution.py:143
  9.3 1.0 %copy.8.own_ref = bf16[128,448]{1,0:T(8,128)(2,1)S(1)} copy(bf16[128,448]{0,1:T(8,128)(2,1)} %param.9) | data formatting | bytes 229376 | tf_op args[4]
  10.3 4.6 %collective-permute-start = (bf16[128,448]{1,0:T(8,128)(2,1)S(1)}, bf16[128,448]{1,0:T(8,128)(2,1)S(1)}, u32[]{:S(2)}, u32[]{:S(2)}) collective-permute-start(bf16[128,448]{1,0:T(8,128)(2,1)S(1)} %copy.8.own_ref), channel_id=1, source_target_pairs={{0,16},{16,0},{1,17},{17,1},{2,18},{18,2},{3,19},{19,3},{4,20},{20... | collective-permute-start | bytes 344072 | tf_op jit(solution)/shard_map/ppermute | solution.py:140
  14.9 6.8 %collective-permute-done.other_ref = bf16[128,448]{1,0:T(8,128)(2,1)S(1)} collective-permute-done((bf16[128,448]{1,0:T(8,128)(2,1)S(1)}, bf16[128,448]{1,0:T(8,128)(2,1)S(1)}, u32[]{:S(2)}, u32[]{:S(2)}) %collective-permute-start) | collective-permute-done | bytes 114720 | tf_op jit(solution)/shard_map/ppermute | solution.py:140
  21.7 0.0 copy-start.3
  21.7 0.7 copy-done.3
  22.3 0.0 all-to-all-done
  22.4 2.7 %collective-permute-start.1 = (bf16[128,2048]{1,0:T(8,128)(2,1)S(1)}, bf16[128,2048]{1,0:T(8,128)(2,1)S(1)}, u32[]{:S(2)}, u32[]{:S(2)}) collective-permute-start(bf16[128,2048]{1,0:T(8,128)(2,1)S(1)} %bitcast.30), channel_id=1, source_target_pairs={{0,1},{1,0},{2,3},{3,2},{4,5},{5,4},{6,7},{7,6},{8,9},{9,8},{10,11... | collective-permute-start | bytes 1572872 | tf_op jit(solution)/shard_map/ppermute | solution.py:146
  25.1 1.5 %collective-permute-done.1.swapped_ref = bf16[128,2048]{1,0:T(8,128)(2,1)S(1)} collective-permute-done((bf16[128,2048]{1,0:T(8,128)(2,1)S(1)}, bf16[128,2048]{1,0:T(8,128)(2,1)S(1)}, u32[]{:S(2)}, u32[]{:S(2)}) %collective-permute-start.1) | collective-permute-done | bytes 524320 | tf_op jit(solution)/shard_map/ppermute | solution.py:146
  26.6 0.0 copy-done.2
  26.6 0.0 copy-done
  26.6 0.0 copy-start.1
  26.6 1.5 %copy-done.1 = bf16[2048,448]{0,1:T(8,128)(2,1)S(1)} copy-done((bf16[2048,448]{0,1:T(8,128)(2,1)S(1)}, bf16[2048,448]{0,1:T(8,128)(2,1)}, u32[]{:S(2)}) %copy-start.1) | copy-done | bytes 1835032
  28.1 0.0 copy-start.4
  28.1 0.9 copy-done.4
  29.0 0.0 copy-start.5
  29.0 3.3 %local.1 = (bf16[64,896]{1,0:T(8,128)(2,1)S(1)}, bf16[2,64,896]{2,1,0:T(8,128)(2,1)S(1)}, bf16[2,64,896]{2,1,0:T(8,128)(2,1)S(1)}, bf16[3,64,896]{2,1,0:T(8,128)...) custom-call(bf16[128,2048]{1,0:T(8,128)(2,1)S(1)} %bitcast.31, ...), custom_call_target="tpu_custom_call" | custom-call | flops 1879048192 | bytes 7340032 | tf_op jit(solution)/shard_map/local/pallas_call | solution.py:149
  32.3 3.5 %collective-permute-start.2 = (bf16[2,64,896]{2,1,0:T(8,128)(2,1)S(1)}, bf16[2,64,896]{2,1,0:T(8,128)(2,1)S(1)}, u32[]{:S(2)}, u32[]{:S(2)}) collective-permute-start(bf16[2,64,896]{2,1,0:T(8,128)(2,1)S(1)} %get-tuple-element.25), channel_id=1, source_target_pairs={{0,32},{32,0},{64,96},{96,64},{128,160},{160,128},{192,224},{224,1... | collective-permute-start | bytes 688136 | tf_op jit(solution)/shard_map/ppermute | solution.py:130
  35.8 1.9 %collective-permute-start.3 = (bf16[2,64,896]{2,1,0:T(8,128)(2,1)S(1)}, bf16[2,64,896]{2,1,0:T(8,128)(2,1)S(1)}, u32[]{:S(2)}, u32[]{:S(2)}) collective-permute-start(bf16[2,64,896]{2,1,0:T(8,128)(2,1)S(1)} %get-tuple-element.26), channel_id=1, source_target_pairs={{0,480},{32,64},{64,32},{96,128},{128,96},{160,192},{192,160},{224... | collective-permute-start | bytes 688136 | tf_op jit(solution)/shard_map/ppermute | solution.py:130
  37.8 0.0 copy-done.5
  37.8 0.1 fusion.17
  37.9 9.6 %collective-permute-start.4 = (bf16[64,896]{1,0:T(8,128)(2,1)S(1)}, bf16[64,896]{1,0:T(8,128)(2,1)S(1)}, u32[]{:S(2)}, u32[]{:S(2)}) collective-permute-start(bf16[64,896]{1,0:T(8,128)(2,1)S(1)} %get-tuple-element.27), channel_id=1, source_target_pairs={{0,448},{32,96},{64,0},{96,160},{128,64},{160,224},{192,128},{224,... | collective-permute-start | bytes 344072 | tf_op jit(solution)/shard_map/ppermute | solution.py:130
  47.5 1.9 %collective-permute-start.5 = (bf16[3,64,896]{2,1,0:T(8,128)(2,1)S(1)}, bf16[3,64,896]{2,1,0:T(8,128)(2,1)S(1)}, u32[]{:S(2)}, u32[]{:S(2)}) collective-permute-start(bf16[3,64,896]{2,1,0:T(8,128)(2,1)S(1)} %get-tuple-element.31), channel_id=1, source_target_pairs={{0,32},{32,0},{64,96},{96,64},{128,160},{160,128},{192,224},{224,1... | collective-permute-start | bytes 1032200 | tf_op jit(solution)/shard_map/ppermute | solution.py:130
  49.4 3.3 %collective-permute-start.6 = (bf16[3,64,896]{2,1,0:T(8,128)(2,1)S(1)}, bf16[3,64,896]{2,1,0:T(8,128)(2,1)}, u32[]{:S(2)}, u32[]{:S(2)}) collective-permute-start(bf16[3,64,896]{2,1,0:T(8,128)(2,1)S(1)} %get-tuple-element.32), channel_id=1, source_target_pairs={{0,480},{32,64},{64,32},{96,128},{128,96},{160,192},{192,160},{224... | collective-permute-start | bytes 1032200 | tf_op jit(solution)/shard_map/ppermute | solution.py:130
  52.8 0.0 collective-permute-done.2
  52.8 0.0 collective-permute-done.3
  52.8 0.7 fusion.10
  53.5 0.0 collective-permute-done.4
  53.5 0.7 fusion.6
  54.2 4.7 %collective-permute-start.7 = (bf16[64,896]{1,0:T(8,128)(2,1)}, bf16[64,896]{1,0:T(8,128)(2,1)S(1)}, u32[]{:S(2)}, u32[]{:S(2)}) collective-permute-start(bf16[64,896]{1,0:T(8,128)(2,1)} %fusion.10), channel_id=1, source_target_pairs={{0,96},{32,448},{64,160},{96,0},{128,224},{160,64},{192,288},{224,... | collective-permute-start | bytes 344072 | tf_op jit(solution)/shard_map/ppermute | solution.py:130
  58.9 2.9 %collective-permute-start.8 = (bf16[64,896]{1,0:T(8,128)(2,1)}, bf16[64,896]{1,0:T(8,128)(2,1)S(1)}, u32[]{:S(2)}, u32[]{:S(2)}) collective-permute-start(bf16[64,896]{1,0:T(8,128)(2,1)} %fusion.6), channel_id=1, source_target_pairs={{0,416},{32,128},{64,480},{96,192},{128,32},{160,256},{192,96},{22... | collective-permute-start | bytes 344072 | tf_op jit(solution)/shard_map/ppermute | solution.py:130
  61.8 0.5 fusion.8
  62.3 1.3 %fusion.1 = bf16[16,8,2048]{2,1,0:T(8,128)(2,1)} fusion(f32[128,2048]{1,0:T(8,128)S(1)} %fusion.8, bf16[2048,448]{0,1:T(8,128)(2,1)S(1)} %copy-done, bf16[128,896]{1,0:T(8,128)(2,1)S(1)} %get-tuple-element.29), kind=kOutput, calls=%fused_computation.2 | convolution fusion | flops 235405312 | bytes 3538944 | tf_op jit(solution)/shard_map/dot_general | solution.py:25
  63.5 0.0 copy-start.6
  63.5 6.5 %all-to-all-start.1 = ((bf16[16,8,2048]{2,1,0:T(8,128)(2,1)}), bf16[16,8,2048]{2,1,0:T(8,128)(2,1)S(1)}, u32[]{:S(2)}, u32[]{:S(2)}) async-start(bf16[16,8,2048]{2,1,0:T(8,128)(2,1)} %fusion.1), calls=%async_computation.1 | async-start | bytes 1048576 | tf_op jit(solution)/shard_map/all_to_all | solution.py:201
  70.1 0.0 collective-permute-done.7
  70.1 0.0 collective-permute-done.8
  70.1 0.0 collective-permute-done.5
  70.1 0.0 collective-permute-done.6
  70.1 1.1 %fusion.2 = (bf16[64,896]{1,0:T(8,128)(2,1)S(1)}, bf16[64,896]{1,0:T(8,128)(2,1)S(1)}) fusion(bf16[64,896]{1,0:T(8,128)(2,1)S(1)} %collective-permute-done.7, bf16[3,64,896]{2,1,0:T(8,128)(2,1)} %collective-permute-done.6, bf16[3,64,896]{2,1,0:T(8,128)(2,1)S(1)} %collective-permute-done.5, bf16[3,64,896]{2,1,0:T(8,128)(2,1)S(1)} %get-tuple-element.30, ...), kind=kLoop, calls=%fused_computation.5 | loop fusion | flops 917504 | bytes 1146880 | tf_op jit(solution)/shard_map/convert_element_type | solution.py:207
  71.2 5.7 %collective-permute-start.10 = (bf16[64,896]{1,0:T(8,128)(2,1)S(1)}, bf16[64,896]{1,0:T(8,128)(2,1)S(1)}, u32[]{:S(2)}, u32[]{:S(2)}) collective-permute-start(bf16[64,896]{1,0:T(8,128)(2,1)S(1)} %get-tuple-element.38), channel_id=1, source_target_pairs={{0,416},{32,128},{64,480},{96,192},{128,32},{160,256},{192,96},{22... | collective-permute-start | bytes 344072 | tf_op jit(solution)/shard_map/ppermute | solution.py:130
  76.9 3.6 %collective-permute-start.9 = (bf16[64,896]{1,0:T(8,128)(2,1)S(1)}, bf16[64,896]{1,0:T(8,128)(2,1)S(1)}, u32[]{:S(2)}, u32[]{:S(2)}) collective-permute-start(bf16[64,896]{1,0:T(8,128)(2,1)S(1)} %get-tuple-element.37), channel_id=1, source_target_pairs={{0,96},{32,448},{64,160},{96,0},{128,224},{160,64},{192,288},{224,... | collective-permute-start | bytes 344072 | tf_op jit(solution)/shard_map/ppermute | solution.py:130
  80.4 0.0 collective-permute-done.10
  80.4 9.7 %collective-permute-done.9 = bf16[64,896]{1,0:T(8,128)(2,1)S(1)} collective-permute-done((bf16[64,896]{1,0:T(8,128)(2,1)S(1)}, bf16[64,896]{1,0:T(8,128)(2,1)S(1)}, u32[]{:S(2)}, u32[]{:S(2)}) %collective-permute-start.9) | collective-permute-done | bytes 114720 | tf_op jit(solution)/shard_map/ppermute | solution.py:130
  90.2 1.0 %fusion.5 = bf16[64,896]{1,0:T(8,128)(2,1)S(1)} fusion(bf16[64,896]{1,0:T(8,128)(2,1)S(1)} %collective-permute-done.10, bf16[64,896]{1,0:T(8,128)(2,1)S(1)} %collective-permute-done.9, bf16[3,64,896]{2,1,0:T(8,128)(2,1)} %collective-permute-done.6, bf16[3,64,896]{2,1,0:T(8,128)(2,1)S(1)} %collective-permute-done.5, bf16[3,64,896]{2,1,0:T(8,128)(2,1)S(1)} %get-tuple-element.30), kind=kLoop, calls=%fused_computation.10 | loop fusion | flops 573440 | bytes 688128 | tf_op jit(solution)/shard_map/convert_element_type | solution.py:218
  91.2 0.7 fusion.18
  91.9 0.0 all-to-all-done.1
  91.9 0.1 convert_reduce_fusion
  92.0 0.0 copy-done.6
  92.0 0.2 fusion.13
  92.2 0.7 fusion.16
  (2 shorter events, 0.0 us)
Async XLA Ops:
  0.6 26.0 %copy-start.2 = (f32[2048]{0:T(1024)S(1)}, f32[2048]{0:T(1024)}, u32[]{:S(2)}) copy-start(f32[2048]{0:T(1024)} %param.6) | copy-start | bytes 24580
  0.6 26.0 %copy-start = (bf16[2048,448]{0,1:T(8,128)(2,1)S(1)}, bf16[2048,448]{0,1:T(8,128)(2,1)}, u32[]{:S(2)}) copy-start(bf16[2048,448]{0,1:T(8,128)(2,1)} %param.8) | copy-start | bytes 5505028
  2.4 20.0 %all-to-all-start = ((bf16[16,8,2048]{2,1,0:T(8,128)(2,1)}), bf16[16,8,2048]{2,1,0:T(8,128)(2,1)S(1)}, u32[]{:S(2)}, u32[]{:S(2)}) async-start(bf16[16,8,2048]{2,1,0:T(8,128)(2,1)} %broadcast_in_dim.2), calls=%async_computation | async-start | bytes 1048576 | tf_op jit(solution)/shard_map/all_to_all | solution.py:143
  10.3 11.4 %collective-permute-start = (bf16[128,448]{1,0:T(8,128)(2,1)S(1)}, bf16[128,448]{1,0:T(8,128)(2,1)S(1)}, u32[]{:S(2)}, u32[]{:S(2)}) collective-permute-start(bf16[128,448]{1,0:T(8,128)(2,1)S(1)} %copy.8.own_ref), channel_id=1, source_target_pairs={{0,16},{16,0},{1,17},{17,1},{2,18},{18,2},{3,19},{19,3},{4,20},{20... | collective-permute-start | bytes 344072 | tf_op jit(solution)/shard_map/ppermute | solution.py:140
  21.7 0.7 copy-start.3
  22.4 4.2 %collective-permute-start.1 = (bf16[128,2048]{1,0:T(8,128)(2,1)S(1)}, bf16[128,2048]{1,0:T(8,128)(2,1)S(1)}, u32[]{:S(2)}, u32[]{:S(2)}) collective-permute-start(bf16[128,2048]{1,0:T(8,128)(2,1)S(1)} %bitcast.30), channel_id=1, source_target_pairs={{0,1},{1,0},{2,3},{3,2},{4,5},{5,4},{6,7},{7,6},{8,9},{9,8},{10,11... | collective-permute-start | bytes 1572872 | tf_op jit(solution)/shard_map/ppermute | solution.py:146
  26.6 1.5 %copy-start.1 = (bf16[2048,448]{0,1:T(8,128)(2,1)S(1)}, bf16[2048,448]{0,1:T(8,128)(2,1)}, u32[]{:S(2)}) copy-start(bf16[2048,448]{0,1:T(8,128)(2,1)} %param.7) | copy-start | bytes 5505028
  28.1 0.9 copy-start.4
  29.0 8.8 %copy-start.5 = (bf16[8,2048]{1,0:T(8,128)(2,1)S(1)}, bf16[8,2048]{1,0:T(8,128)(2,1)}, u32[]{:S(2)}) copy-start(bf16[8,2048]{1,0:T(8,128)(2,1)} %param.5) | copy-start | bytes 98308
  32.3 20.5 %collective-permute-start.2 = (bf16[2,64,896]{2,1,0:T(8,128)(2,1)S(1)}, bf16[2,64,896]{2,1,0:T(8,128)(2,1)S(1)}, u32[]{:S(2)}, u32[]{:S(2)}) collective-permute-start(bf16[2,64,896]{2,1,0:T(8,128)(2,1)S(1)} %get-tuple-element.25), channel_id=1, source_target_pairs={{0,32},{32,0},{64,96},{96,64},{128,160},{160,128},{192,224},{224,1... | collective-permute-start | bytes 688136 | tf_op jit(solution)/shard_map/ppermute | solution.py:130
  35.8 17.0 %collective-permute-start.3 = (bf16[2,64,896]{2,1,0:T(8,128)(2,1)S(1)}, bf16[2,64,896]{2,1,0:T(8,128)(2,1)S(1)}, u32[]{:S(2)}, u32[]{:S(2)}) collective-permute-start(bf16[2,64,896]{2,1,0:T(8,128)(2,1)S(1)} %get-tuple-element.26), channel_id=1, source_target_pairs={{0,480},{32,64},{64,32},{96,128},{128,96},{160,192},{192,160},{224... | collective-permute-start | bytes 688136 | tf_op jit(solution)/shard_map/ppermute | solution.py:130
  37.9 15.6 %collective-permute-start.4 = (bf16[64,896]{1,0:T(8,128)(2,1)S(1)}, bf16[64,896]{1,0:T(8,128)(2,1)S(1)}, u32[]{:S(2)}, u32[]{:S(2)}) collective-permute-start(bf16[64,896]{1,0:T(8,128)(2,1)S(1)} %get-tuple-element.27), channel_id=1, source_target_pairs={{0,448},{32,96},{64,0},{96,160},{128,64},{160,224},{192,128},{224,... | collective-permute-start | bytes 344072 | tf_op jit(solution)/shard_map/ppermute | solution.py:130
  47.5 22.6 %collective-permute-start.5 = (bf16[3,64,896]{2,1,0:T(8,128)(2,1)S(1)}, bf16[3,64,896]{2,1,0:T(8,128)(2,1)S(1)}, u32[]{:S(2)}, u32[]{:S(2)}) collective-permute-start(bf16[3,64,896]{2,1,0:T(8,128)(2,1)S(1)} %get-tuple-element.31), channel_id=1, source_target_pairs={{0,32},{32,0},{64,96},{96,64},{128,160},{160,128},{192,224},{224,1... | collective-permute-start | bytes 1032200 | tf_op jit(solution)/shard_map/ppermute | solution.py:130
  49.4 20.6 %collective-permute-start.6 = (bf16[3,64,896]{2,1,0:T(8,128)(2,1)S(1)}, bf16[3,64,896]{2,1,0:T(8,128)(2,1)}, u32[]{:S(2)}, u32[]{:S(2)}) collective-permute-start(bf16[3,64,896]{2,1,0:T(8,128)(2,1)S(1)} %get-tuple-element.32), channel_id=1, source_target_pairs={{0,480},{32,64},{64,32},{96,128},{128,96},{160,192},{192,160},{224... | collective-permute-start | bytes 1032200 | tf_op jit(solution)/shard_map/ppermute | solution.py:130
  54.2 15.9 %collective-permute-start.7 = (bf16[64,896]{1,0:T(8,128)(2,1)}, bf16[64,896]{1,0:T(8,128)(2,1)S(1)}, u32[]{:S(2)}, u32[]{:S(2)}) collective-permute-start(bf16[64,896]{1,0:T(8,128)(2,1)} %fusion.10), channel_id=1, source_target_pairs={{0,96},{32,448},{64,160},{96,0},{128,224},{160,64},{192,288},{224,... | collective-permute-start | bytes 344072 | tf_op jit(solution)/shard_map/ppermute | solution.py:130
  58.9 11.1 %collective-permute-start.8 = (bf16[64,896]{1,0:T(8,128)(2,1)}, bf16[64,896]{1,0:T(8,128)(2,1)S(1)}, u32[]{:S(2)}, u32[]{:S(2)}) collective-permute-start(bf16[64,896]{1,0:T(8,128)(2,1)} %fusion.6), channel_id=1, source_target_pairs={{0,416},{32,128},{64,480},{96,192},{128,32},{160,256},{192,96},{22... | collective-permute-start | bytes 344072 | tf_op jit(solution)/shard_map/ppermute | solution.py:130
  63.5 28.4 %copy-start.6 = (bf16[8,2048]{1,0:T(8,128)(2,1)S(1)}, bf16[8,2048]{1,0:T(8,128)(2,1)}, u32[]{:S(2)}) copy-start(bf16[8,2048]{1,0:T(8,128)(2,1)} %param.5) | copy-start | bytes 98308
  63.5 28.3 %all-to-all-start.1 = ((bf16[16,8,2048]{2,1,0:T(8,128)(2,1)}), bf16[16,8,2048]{2,1,0:T(8,128)(2,1)S(1)}, u32[]{:S(2)}, u32[]{:S(2)}) async-start(bf16[16,8,2048]{2,1,0:T(8,128)(2,1)} %fusion.1), calls=%async_computation.1 | async-start | bytes 1048576 | tf_op jit(solution)/shard_map/all_to_all | solution.py:201
  71.2 9.3 %collective-permute-start.10 = (bf16[64,896]{1,0:T(8,128)(2,1)S(1)}, bf16[64,896]{1,0:T(8,128)(2,1)S(1)}, u32[]{:S(2)}, u32[]{:S(2)}) collective-permute-start(bf16[64,896]{1,0:T(8,128)(2,1)S(1)} %get-tuple-element.38), channel_id=1, source_target_pairs={{0,416},{32,128},{64,480},{96,192},{128,32},{160,256},{192,96},{22... | collective-permute-start | bytes 344072 | tf_op jit(solution)/shard_map/ppermute | solution.py:130
  76.9 13.3 %collective-permute-start.9 = (bf16[64,896]{1,0:T(8,128)(2,1)S(1)}, bf16[64,896]{1,0:T(8,128)(2,1)S(1)}, u32[]{:S(2)}, u32[]{:S(2)}) collective-permute-start(bf16[64,896]{1,0:T(8,128)(2,1)S(1)} %get-tuple-element.37), channel_id=1, source_target_pairs={{0,96},{32,448},{64,160},{96,0},{128,224},{160,64},{192,288},{224,... | collective-permute-start | bytes 344072 | tf_op jit(solution)/shard_map/ppermute | solution.py:130

commit v7 on v6

--- a/solution.py
+++ b/solution.py
@@ -11,8 +11,7 @@
 EPSILON = 1e-05
 DP = ("z", "yh")
 TENSOR = ("x", "yl", "core")
-OUTER = (-6, 6)
-INNER = (-3, 0, 3)
+HUBS = (-6, 6, -3, 0, 3)
 
 
 def normalize(residual):
@@ -45,12 +44,9 @@
     own_ref,
     other_ref,
     far_ref,
-    outer_ahead_ref,
-    outer_behind_ref,
-    inner_ahead_ref,
-    inner_behind_ref,
-    outer_hub_ref,
-    inner_hub_ref,
+    ahead_ref,
+    behind_ref,
+    hub_ref,
     grads_own_ref,
     normed_ref,
     grads_ref,
@@ -113,16 +109,10 @@
         return jnp.where(first, both[:depth], both[depth:]).astype(jnp.bfloat16)
 
     far_ref[...] = block(nz // 2)
-    for at, hub in enumerate(OUTER):
-        outer_ahead_ref[at] = block(-hub - 1)
-        outer_behind_ref[at] = block(-hub + 1)
-    for at, hub in enumerate(INNER):
-        inner_ahead_ref[at] = block(-hub - 1)
-        inner_behind_ref[at] = block(-hub + 1)
-    for at, hub in enumerate(OUTER):
-        outer_hub_ref[at] = block(hub)
-    for at, hub in enumerate(INNER):
-        inner_hub_ref[at] = block(hub)
+    for at, hub in enumerate(HUBS):
+        ahead_ref[at] = block(-hub - 1)
+        behind_ref[at] = block(-hub + 1)
+        hub_ref[at] = block(hub)
 
 
 def move(value, hops, nz):
@@ -146,16 +136,13 @@
     swapped = lax.ppermute(same, "core", [(0, 1), (1, 0)])
     factor = float(rows * nz * nh) ** (-0.5)
     shape = jax.ShapeDtypeStruct
-    far, outer_ahead, outer_behind, inner_ahead, inner_behind, outer_hub, inner_hub, grads_own = pl.pallas_call(
+    far, ahead, behind, hub, grads_own = pl.pallas_call(
         functools.partial(local_kernel, factor, nz, residual.shape[0]),
         out_shape=(
             shape((depth, 2 * width), bf16),
-            shape((len(OUTER), depth, 2 * width), bf16),
-            shape((len(OUTER), depth, 2 * width), bf16),
-            shape((len(INNER), depth, 2 * width), bf16),
-            shape((len(INNER), depth, 2 * width), bf16),
-            shape((len(OUTER), depth, 2 * width), bf16),
-            shape((len(INNER), depth, 2 * width), bf16),
+            shape((len(HUBS), depth, 2 * width), bf16),
+            shape((len(HUBS), depth, 2 * width), bf16),
+            shape((len(HUBS), depth, 2 * width), bf16),
             shape((rows, 2 * width), bf16),
         ),
         scratch_shapes=[
@@ -171,43 +158,31 @@
         name="local",
     )(same, swapped, norm_gain.reshape(1, features), gate_weight.T, up_weight.T, own, other)
 
-    from_far = move(far, -2, nz).astype(f32)
-    outer_ahead, outer_behind = move(outer_ahead, 1, nz), move(outer_behind, -1, nz)
-    inner_ahead, inner_behind = move(inner_ahead, 1, nz), move(inner_behind, -1, nz)
-
-    def outer(at):
-        return (
-            outer_hub[at].astype(f32)
-            + outer_ahead[at].astype(f32)
-            + outer_behind[at].astype(f32)
-        )
-
-    def inner(at):
-        return (
-            inner_hub[at].astype(f32)
-            + inner_ahead[at].astype(f32)
-            + inner_behind[at].astype(f32)
-        )
-
-    plus, minus = lax.optimization_barrier(
-        (outer(0).astype(bf16), (outer(1) + from_far).astype(bf16))
-    )
-    grads_own, first_sum = lax.optimization_barrier((grads_own, plus))
-    plus, minus = move(first_sum, 3, nz), move(minus, -3, nz)
+    from_far = move(far, -2, nz)
+    ahead, behind = move(ahead, 1, nz), move(behind, -1, nz)
+    grads_own, from_far = lax.optimization_barrier((grads_own, from_far))
 
     part = contract_last(grads_own[:, :width], gate_weight)
     part = (part + contract_last(grads_own[:, width:], up_weight)).astype(bf16)
     blocks = part.reshape(nt, rows // nt, features)
     moved = lax.all_to_all(blocks, TENSOR, 0, 0, tiled=True)
 
+    def joined(at):
+        return hub[at].astype(f32) + ahead[at].astype(f32) + behind[at].astype(f32)
+
+    plus, minus = lax.optimization_barrier(
+        (joined(0).astype(bf16), (joined(1) + from_far.astype(f32)).astype(bf16))
+    )
+    plus, minus = move(plus, 3, nz), move(minus, -3, nz)
     plus, minus = lax.optimization_barrier((plus, minus))
     plus, minus = lax.optimization_barrier(
         (
-            (inner(0) + minus.astype(f32)).astype(bf16),
-            (inner(2) + plus.astype(f32)).astype(bf16),
+            (joined(2) + minus.astype(f32)).astype(bf16),
+            (joined(4) + plus.astype(f32)).astype(bf16),
         )
     )
     plus, minus = move(plus, 3, nz), move(minus, -3, nz)
+    total = (joined(3) + plus.astype(f32) + minus.astype(f32)).astype(bf16)
 
     scaled, inverse = normalize(residual)
     normed_grad = jnp.sum(moved.astype(f32), axis=0)
@@ -215,7 +190,6 @@
     residual_grad = (
         (weighted - scaled * jnp.mean(weighted * scaled, axis=-1, keepdims=True)) * inverse
     ).astype(bf16)
-    total = (inner(1) + plus.astype(f32) + minus.astype(f32)).astype(bf16)
     return (residual_grad, total[:, :width], total[:, width:])
 
 

time: 93.7 us -> 99.3 us (1.060)
  the two profiles are of different devices: /device:TPU:67 before, /device:TPU:32 now
where the time goes in v7:
time: 99.3 us; the launch traced here: 98.6 us
  starting transfers between devices  50.2 us (51%)
  waiting for transfers between devices  31.4 us (32%)
  other arithmetic  5.34 us (5%)
  local copies, waits for them, and re-layouts  4.97 us (5%)
  Pallas kernels  4.19 us (4%)
  matrix products  1.73 us (2%)
    ppermute x7, starting transfers between devices, move(): return lax.ppermute(value, 'z', pairs)  32.3 us
    ppermute x7, waiting for transfers between devices, move(): return lax.ppermute(value, 'z', pairs)  22.7 us
    all_to_all x1, starting transfers between devices, shards(): same = lax.all_to_all(copies, ('yh', 'x', 'yl'), 0, 0, tiled=True)  7.03 us
    ppermute x1, waiting for transfers between devices, shards(): other = lax.ppermute(own, 'yh', [(0, 1), (1, 0)])  6.78 us
    ppermute x1, starting transfers between devices, shards(): other = lax.ppermute(own, 'yh', [(0, 1), (1, 0)])  5.34 us
    pallas_call x1, Pallas kernels, shards(): pl.pallas_call(functools.partial(local_kernel, factor, nz, residual.shape...  4.19 us
    all_to_all x1, starting transfers between devices, shards(): moved = lax.all_to_all(blocks, TENSOR, 0, 0, tiled=True)  3.57 us
    unnamed x9, local copies, waits for them, and re-layouts  2.51 us
  transfers between devices with their start and end apart: 11, of which 8 were waited for; matrix products, arithmetic and copies ran while one was open for 6% of the time, Pallas kernels for 0%

profile of v7, /device:TPU:32, one launch (start us, length us, event | category | flops | bytes accessed | tf_op | source)
XLA Modules:
  0.0 98.6 jit_solution(5708544923997913115)
XLA Ops:
  0.6 0.0 copy-start.2
  0.6 0.0 copy-start
  0.7 1.7 %broadcast_in_dim.2 = bf16[16,8,2048]{2,1,0:T(8,128)(2,1)} broadcast(bf16[8,2048]{1,0:T(8,128)(2,1)} %param.5), dimensions={1,2} | broadcast | bytes 557056 | tf_op jit(solution)/shard_map/broadcast_in_dim | solution.py:132
  2.4 7.0 %all-to-all-start = ((bf16[16,8,2048]{2,1,0:T(8,128)(2,1)}), bf16[16,8,2048]{2,1,0:T(8,128)(2,1)S(1)}, u32[]{:S(2)}, u32[]{:S(2)}) async-start(bf16[16,8,2048]{2,1,0:T(8,128)(2,1)} %broadcast_in_dim.2), calls=%async_computation | async-start | bytes 1048576 | tf_op jit(solution)/shard_map/all_to_all | solution.py:133
  9.4 1.0 %copy.8.own_ref = bf16[128,448]{1,0:T(8,128)(2,1)S(1)} copy(bf16[128,448]{0,1:T(8,128)(2,1)} %param.9) | data formatting | bytes 229376 | tf_op args[4]
  10.4 5.3 %collective-permute-start = (bf16[128,448]{1,0:T(8,128)(2,1)S(1)}, bf16[128,448]{1,0:T(8,128)(2,1)S(1)}, u32[]{:S(2)}, u32[]{:S(2)}) collective-permute-start(bf16[128,448]{1,0:T(8,128)(2,1)S(1)} %copy.8.own_ref), channel_id=1, source_target_pairs={{0,16},{16,0},{1,17},{17,1},{2,18},{18,2},{3,19},{19,3},{4,20},{20... | collective-permute-start | bytes 344072 | tf_op jit(solution)/shard_map/ppermute | solution.py:130
  15.8 6.8 %collective-permute-done.other_ref = bf16[128,448]{1,0:T(8,128)(2,1)S(1)} collective-permute-done((bf16[128,448]{1,0:T(8,128)(2,1)S(1)}, bf16[128,448]{1,0:T(8,128)(2,1)S(1)}, u32[]{:S(2)}, u32[]{:S(2)}) %collective-permute-start) | collective-permute-done | bytes 114720 | tf_op jit(solution)/shard_map/ppermute | solution.py:130
  22.6 0.0 all-to-all-done
  22.6 1.9 %collective-permute-start.1 = (bf16[128,2048]{1,0:T(8,128)(2,1)S(1)}, bf16[128,2048]{1,0:T(8,128)(2,1)S(1)}, u32[]{:S(2)}, u32[]{:S(2)}) collective-permute-start(bf16[128,2048]{1,0:T(8,128)(2,1)S(1)} %bitcast.30), channel_id=1, source_target_pairs={{0,1},{1,0},{2,3},{3,2},{4,5},{5,4},{6,7},{7,6},{8,9},{9,8},{10,11... | collective-permute-start | bytes 1572872 | tf_op jit(solution)/shard_map/ppermute | solution.py:136
  24.5 1.9 %collective-permute-done.1.swapped_ref = bf16[128,2048]{1,0:T(8,128)(2,1)S(1)} collective-permute-done((bf16[128,2048]{1,0:T(8,128)(2,1)S(1)}, bf16[128,2048]{1,0:T(8,128)(2,1)S(1)}, u32[]{:S(2)}, u32[]{:S(2)}) %collective-permute-start.1) | collective-permute-done | bytes 524320 | tf_op jit(solution)/shard_map/ppermute | solution.py:136
  26.4 0.0 copy-done.2
  26.4 0.0 copy-done
  26.4 0.0 copy-start.1
  26.4 1.5 %copy-done.1 = bf16[2048,448]{0,1:T(8,128)(2,1)S(1)} copy-done((bf16[2048,448]{0,1:T(8,128)(2,1)S(1)}, bf16[2048,448]{0,1:T(8,128)(2,1)}, u32[]{:S(2)}) %copy-start.1) | copy-done | bytes 1835032
  27.9 0.0 copy-start.3
  27.9 4.2 %local.1 = (bf16[64,896]{1,0:T(8,128)(2,1)S(1)}, bf16[5,64,896]{2,1,0:T(8,128)(2,1)}, bf16[5,64,896]{2,1,0:T(8,128)(2,1)}, bf16[5,64,896]{2,1,0:T(8,128)(2,1)S(1)}, bf16[128,896]{1,0:T(8,128)(2,1)S(1)}) custom-call(bf16[128,2048]{1,0:T(8,128)(2,1)S(1)} %bitcast.31, bf16[128,2048]{1,0:T(8,128)(2,1)S(1)} %collective-permute-done.1.swapped_ref, ...), custom_call_target="tpu_custom_call" | custom-call | flops 1879048192 | bytes 7340032 | tf_op jit(solution)/shard_map/local/pallas_call | solution.py:139
  32.1 5.2 %collective-permute-start.2 = (bf16[64,896]{1,0:T(8,128)(2,1)S(1)}, bf16[64,896]{1,0:T(8,128)(2,1)S(1)}, u32[]{:S(2)}, u32[]{:S(2)}) collective-permute-start(bf16[64,896]{1,0:T(8,128)(2,1)S(1)} %get-tuple-element.21), channel_id=1, source_target_pairs={{0,448},{32,96},{64,0},{96,160},{128,64},{160,224},{192,128},{224,... | collective-permute-start | bytes 344072 | tf_op jit(solution)/shard_map/ppermute | solution.py:120
  37.2 0.0 copy-done.3
  37.3 0.1 fusion.17
  37.4 8.7 %collective-permute-start.3 = (bf16[5,64,896]{2,1,0:T(8,128)(2,1)}, bf16[5,64,896]{2,1,0:T(8,128)(2,1)}, u32[]{:S(2)}, u32[]{:S(2)}) collective-permute-start(bf16[5,64,896]{2,1,0:T(8,128)(2,1)} %get-tuple-element.24), channel_id=1, source_target_pairs={{0,32},{32,0},{64,96},{96,64},{128,160},{160,128},{192,224},{224,1... | collective-permute-start | bytes 1720328 | tf_op jit(solution)/shard_map/ppermute | solution.py:120
  46.1 1.9 %collective-permute-start.4 = (bf16[5,64,896]{2,1,0:T(8,128)(2,1)}, bf16[5,64,896]{2,1,0:T(8,128)(2,1)}, u32[]{:S(2)}, u32[]{:S(2)}) collective-permute-start(bf16[5,64,896]{2,1,0:T(8,128)(2,1)} %get-tuple-element.25), channel_id=1, source_target_pairs={{0,480},{32,64},{64,32},{96,128},{128,96},{160,192},{192,160},{224... | collective-permute-start | bytes 1720328 | tf_op jit(solution)/shard_map/ppermute | solution.py:120
  48.0 0.0 collective-permute-done.2
  48.0 0.5 fusion.7
  48.5 1.2 %fusion.1 = bf16[16,8,2048]{2,1,0:T(8,128)(2,1)} fusion(f32[128,2048]{1,0:T(8,128)S(1)} %fusion.7, bf16[2048,448]{0,1:T(8,128)(2,1)S(1)} %copy-done, bf16[128,896]{1,0:T(8,128)(2,1)S(1)} %get-tuple-element.22), kind=kOutput, calls=%fused_computation.2 | convolution fusion | flops 235405312 | bytes 3538944 | tf_op jit(solution)/shard_map/dot_general | solution.py:24
  49.8 3.6 %all-to-all-start.1 = ((bf16[16,8,2048]{2,1,0:T(8,128)(2,1)}), bf16[16,8,2048]{2,1,0:T(8,128)(2,1)S(1)}, u32[]{:S(2)}, u32[]{:S(2)}) async-start(bf16[16,8,2048]{2,1,0:T(8,128)(2,1)} %fusion.1), calls=%async_computation.1 | async-start | bytes 1048576 | tf_op jit(solution)/shard_map/all_to_all | solution.py:168
  53.3 6.0 %collective-permute-done.3 = bf16[5,64,896]{2,1,0:T(8,128)(2,1)} collective-permute-done((bf16[5,64,896]{2,1,0:T(8,128)(2,1)}, bf16[5,64,896]{2,1,0:T(8,128)(2,1)}, u32[]{:S(2)}, u32[]{:S(2)}) %collective-permute-start.3) | collective-permute-done | bytes 573472 | tf_op jit(solution)/shard_map/ppermute | solution.py:120
  59.4 3.4 %collective-permute-done.4 = bf16[5,64,896]{2,1,0:T(8,128)(2,1)} collective-permute-done((bf16[5,64,896]{2,1,0:T(8,128)(2,1)}, bf16[5,64,896]{2,1,0:T(8,128)(2,1)}, u32[]{:S(2)}, u32[]{:S(2)}) %collective-permute-start.4) | collective-permute-done | bytes 573472 | tf_op jit(solution)/shard_map/ppermute | solution.py:120
  62.7 1.0 %fusion.10 = bf16[64,896]{1,0:T(8,128)(2,1)S(1)} fusion(bf16[5,64,896]{2,1,0:T(8,128)(2,1)} %collective-permute-done.4, bf16[5,64,896]{2,1,0:T(8,128)(2,1)} %collective-permute-done.3, bf16[5,64,896]{2,1,0:T(8,128)(2,1)S(1)} %get-tuple-element.23), kind=kLoop, calls=%fused_computation.17 | loop fusion | flops 344064 | bytes 458752 | tf_op jit(solution)/shard_map/convert_element_type | solution.py:174
  63.7 1.0 %fusion.3 = bf16[64,896]{1,0:T(8,128)(2,1)S(1)} fusion(bf16[64,896]{1,0:T(8,128)(2,1)S(1)} %collective-permute-done.2, bf16[5,64,896]{2,1,0:T(8,128)(2,1)} %collective-permute-done.4, bf16[5,64,896]{2,1,0:T(8,128)(2,1)} %collective-permute-done.3, bf16[5,64,896]{2,1,0:T(8,128)(2,1)S(1)} %get-tuple-element.23), kind=kLoop, calls=%fused_computation.7 | loop fusion | flops 458752 | bytes 573440 | tf_op jit(solution)/shard_map/convert_element_type | solution.py:174
  64.8 4.3 %collective-permute-start.5 = (bf16[64,896]{1,0:T(8,128)(2,1)S(1)}, bf16[64,896]{1,0:T(8,128)(2,1)S(1)}, u32[]{:S(2)}, u32[]{:S(2)}) collective-permute-start(bf16[64,896]{1,0:T(8,128)(2,1)S(1)} %fusion.10), channel_id=1, source_target_pairs={{0,96},{32,448},{64,160},{96,0},{128,224},{160,64},{192,288},{224,... | collective-permute-start | bytes 344072 | tf_op jit(solution)/shard_map/ppermute | solution.py:120
  69.1 5.0 %collective-permute-start.6 = (bf16[64,896]{1,0:T(8,128)(2,1)S(1)}, bf16[64,896]{1,0:T(8,128)(2,1)S(1)}, u32[]{:S(2)}, u32[]{:S(2)}) collective-permute-start(bf16[64,896]{1,0:T(8,128)(2,1)S(1)} %fusion.3), channel_id=1, source_target_pairs={{0,416},{32,128},{64,480},{96,192},{128,32},{160,256},{192,96},{22... | collective-permute-start | bytes 344072 | tf_op jit(solution)/shard_map/ppermute | solution.py:120
  74.1 0.0 all-to-all-done.1
  74.1 0.1 convert_reduce_fusion
  74.2 0.2 fusion.13
  74.4 3.1 %collective-permute-done.5 = bf16[64,896]{1,0:T(8,128)(2,1)S(1)} collective-permute-done((bf16[64,896]{1,0:T(8,128)(2,1)S(1)}, bf16[64,896]{1,0:T(8,128)(2,1)S(1)}, u32[]{:S(2)}, u32[]{:S(2)}) %collective-permute-start.5) | collective-permute-done | bytes 114720 | tf_op jit(solution)/shard_map/ppermute | solution.py:120
  77.5 2.9 %collective-permute-done.6 = bf16[64,896]{1,0:T(8,128)(2,1)S(1)} collective-permute-done((bf16[64,896]{1,0:T(8,128)(2,1)S(1)}, bf16[64,896]{1,0:T(8,128)(2,1)S(1)}, u32[]{:S(2)}, u32[]{:S(2)}) %collective-permute-start.6) | collective-permute-done | bytes 114720 | tf_op jit(solution)/shard_map/ppermute | solution.py:120
  80.4 1.2 %fusion.2 = (bf16[64,896]{1,0:T(8,128)(2,1)S(1)}, bf16[64,896]{1,0:T(8,128)(2,1)S(1)}) fusion(bf16[64,896]{1,0:T(8,128)(2,1)S(1)} %collective-permute-done.5, bf16[5,64,896]{2,1,0:T(8,128)(2,1)} %collective-permute-done.4, bf16[5,64,896]{2,1,0:T(8,128)(2,1)} %collective-permute-done.3, bf16[5,64,896]{2,1,0:T(8,128)(2,1)S(1)} %get-tuple-element.23, ...), kind=kLoop, calls=%fused_computation.5 | loop fusion | flops 917504 | bytes 1146880 | tf_op jit(solution)/shard_map/convert_element_type | solution.py:181
  81.6 4.8 %collective-permute-start.7 = (bf16[64,896]{1,0:T(8,128)(2,1)S(1)}, bf16[64,896]{1,0:T(8,128)(2,1)S(1)}, u32[]{:S(2)}, u32[]{:S(2)}) collective-permute-start(bf16[64,896]{1,0:T(8,128)(2,1)S(1)} %get-tuple-element.31), channel_id=1, source_target_pairs={{0,96},{32,448},{64,160},{96,0},{128,224},{160,64},{192,288},{224,... | collective-permute-start | bytes 344072 | tf_op jit(solution)/shard_map/ppermute | solution.py:120
  86.4 2.4 %collective-permute-start.8 = (bf16[64,896]{1,0:T(8,128)(2,1)S(1)}, bf16[64,896]{1,0:T(8,128)(2,1)S(1)}, u32[]{:S(2)}, u32[]{:S(2)}) collective-permute-start(bf16[64,896]{1,0:T(8,128)(2,1)S(1)} %get-tuple-element.32), channel_id=1, source_target_pairs={{0,416},{32,128},{64,480},{96,192},{128,32},{160,256},{192,96},{22... | collective-permute-start | bytes 344072 | tf_op jit(solution)/shard_map/ppermute | solution.py:120
  88.8 0.7 fusion.16
  89.5 4.0 %collective-permute-done.7 = bf16[64,896]{1,0:T(8,128)(2,1)S(1)} collective-permute-done((bf16[64,896]{1,0:T(8,128)(2,1)S(1)}, bf16[64,896]{1,0:T(8,128)(2,1)S(1)}, u32[]{:S(2)}, u32[]{:S(2)}) %collective-permute-start.7) | collective-permute-done | bytes 114720 | tf_op jit(solution)/shard_map/ppermute | solution.py:120
  93.5 3.3 %collective-permute-done.8 = bf16[64,896]{1,0:T(8,128)(2,1)S(1)} collective-permute-done((bf16[64,896]{1,0:T(8,128)(2,1)S(1)}, bf16[64,896]{1,0:T(8,128)(2,1)S(1)}, u32[]{:S(2)}, u32[]{:S(2)}) %collective-permute-start.8) | collective-permute-done | bytes 114720 | tf_op jit(solution)/shard_map/ppermute | solution.py:120
  96.8 1.0 %fusion.6 = bf16[64,896]{1,0:T(8,128)(2,1)S(1)} fusion(bf16[64,896]{1,0:T(8,128)(2,1)S(1)} %collective-permute-done.8, bf16[64,896]{1,0:T(8,128)(2,1)S(1)} %collective-permute-done.7, bf16[5,64,896]{2,1,0:T(8,128)(2,1)} %collective-permute-done.4, bf16[5,64,896]{2,1,0:T(8,128)(2,1)} %collective-permute-done.3, bf16[5,64,896]{2,1,0:T(8,128)(2,1)S(1)} %get-tuple-element.23), kind=kLoop, calls=%fused_computation.12 | loop fusion | flops 573440 | bytes 688128 | tf_op jit(solution)/shard_map/convert_element_type | solution.py:185
  97.9 0.7 fusion.18
  (2 shorter events, 0.0 us)
Async XLA Ops:
  0.6 25.7 %copy-start.2 = (f32[2048]{0:T(1024)S(1)}, f32[2048]{0:T(1024)}, u32[]{:S(2)}) copy-start(f32[2048]{0:T(1024)} %param.6) | copy-start | bytes 24580
  0.6 25.7 %copy-start = (bf16[2048,448]{0,1:T(8,128)(2,1)S(1)}, bf16[2048,448]{0,1:T(8,128)(2,1)}, u32[]{:S(2)}) copy-start(bf16[2048,448]{0,1:T(8,128)(2,1)} %param.7) | copy-start | bytes 5505028
  2.4 20.2 %all-to-all-start = ((bf16[16,8,2048]{2,1,0:T(8,128)(2,1)}), bf16[16,8,2048]{2,1,0:T(8,128)(2,1)S(1)}, u32[]{:S(2)}, u32[]{:S(2)}) async-start(bf16[16,8,2048]{2,1,0:T(8,128)(2,1)} %broadcast_in_dim.2), calls=%async_computation | async-start | bytes 1048576 | tf_op jit(solution)/shard_map/all_to_all | solution.py:133
  10.4 12.1 %collective-permute-start = (bf16[128,448]{1,0:T(8,128)(2,1)S(1)}, bf16[128,448]{1,0:T(8,128)(2,1)S(1)}, u32[]{:S(2)}, u32[]{:S(2)}) collective-permute-start(bf16[128,448]{1,0:T(8,128)(2,1)S(1)} %copy.8.own_ref), channel_id=1, source_target_pairs={{0,16},{16,0},{1,17},{17,1},{2,18},{18,2},{3,19},{19,3},{4,20},{20... | collective-permute-start | bytes 344072 | tf_op jit(solution)/shard_map/ppermute | solution.py:130
  22.6 3.8 %collective-permute-start.1 = (bf16[128,2048]{1,0:T(8,128)(2,1)S(1)}, bf16[128,2048]{1,0:T(8,128)(2,1)S(1)}, u32[]{:S(2)}, u32[]{:S(2)}) collective-permute-start(bf16[128,2048]{1,0:T(8,128)(2,1)S(1)} %bitcast.30), channel_id=1, source_target_pairs={{0,1},{1,0},{2,3},{3,2},{4,5},{5,4},{6,7},{7,6},{8,9},{9,8},{10,11... | collective-permute-start | bytes 1572872 | tf_op jit(solution)/shard_map/ppermute | solution.py:136
  26.4 1.5 %copy-start.1 = (bf16[2048,448]{0,1:T(8,128)(2,1)S(1)}, bf16[2048,448]{0,1:T(8,128)(2,1)}, u32[]{:S(2)}) copy-start(bf16[2048,448]{0,1:T(8,128)(2,1)} %param.8) | copy-start | bytes 5505028
  27.9 9.4 %copy-start.3 = (bf16[8,2048]{1,0:T(8,128)(2,1)S(1)}, bf16[8,2048]{1,0:T(8,128)(2,1)}, u32[]{:S(2)}) copy-start(bf16[8,2048]{1,0:T(8,128)(2,1)} %param.5) | copy-start | bytes 98308
  32.1 15.9 %collective-permute-start.2 = (bf16[64,896]{1,0:T(8,128)(2,1)S(1)}, bf16[64,896]{1,0:T(8,128)(2,1)S(1)}, u32[]{:S(2)}, u32[]{:S(2)}) collective-permute-start(bf16[64,896]{1,0:T(8,128)(2,1)S(1)} %get-tuple-element.21), channel_id=1, source_target_pairs={{0,448},{32,96},{64,0},{96,160},{128,64},{160,224},{192,128},{224,... | collective-permute-start | bytes 344072 | tf_op jit(solution)/shard_map/ppermute | solution.py:120
  37.4 22.0 %collective-permute-start.3 = (bf16[5,64,896]{2,1,0:T(8,128)(2,1)}, bf16[5,64,896]{2,1,0:T(8,128)(2,1)}, u32[]{:S(2)}, u32[]{:S(2)}) collective-permute-start(bf16[5,64,896]{2,1,0:T(8,128)(2,1)} %get-tuple-element.24), channel_id=1, source_target_pairs={{0,32},{32,0},{64,96},{96,64},{128,160},{160,128},{192,224},{224,1... | collective-permute-start | bytes 1720328 | tf_op jit(solution)/shard_map/ppermute | solution.py:120
  46.1 16.7 %collective-permute-start.4 = (bf16[5,64,896]{2,1,0:T(8,128)(2,1)}, bf16[5,64,896]{2,1,0:T(8,128)(2,1)}, u32[]{:S(2)}, u32[]{:S(2)}) collective-permute-start(bf16[5,64,896]{2,1,0:T(8,128)(2,1)} %get-tuple-element.25), channel_id=1, source_target_pairs={{0,480},{32,64},{64,32},{96,128},{128,96},{160,192},{192,160},{224... | collective-permute-start | bytes 1720328 | tf_op jit(solution)/shard_map/ppermute | solution.py:120
  49.8 24.3 %all-to-all-start.1 = ((bf16[16,8,2048]{2,1,0:T(8,128)(2,1)}), bf16[16,8,2048]{2,1,0:T(8,128)(2,1)S(1)}, u32[]{:S(2)}, u32[]{:S(2)}) async-start(bf16[16,8,2048]{2,1,0:T(8,128)(2,1)} %fusion.1), calls=%async_computation.1 | async-start | bytes 1048576 | tf_op jit(solution)/shard_map/all_to_all | solution.py:168
  64.8 12.7 %collective-permute-start.5 = (bf16[64,896]{1,0:T(8,128)(2,1)S(1)}, bf16[64,896]{1,0:T(8,128)(2,1)S(1)}, u32[]{:S(2)}, u32[]{:S(2)}) collective-permute-start(bf16[64,896]{1,0:T(8,128)(2,1)S(1)} %fusion.10), channel_id=1, source_target_pairs={{0,96},{32,448},{64,160},{96,0},{128,224},{160,64},{192,288},{224,... | collective-permute-start | bytes 344072 | tf_op jit(solution)/shard_map/ppermute | solution.py:120
  69.1 11.3 %collective-permute-start.6 = (bf16[64,896]{1,0:T(8,128)(2,1)S(1)}, bf16[64,896]{1,0:T(8,128)(2,1)S(1)}, u32[]{:S(2)}, u32[]{:S(2)}) collective-permute-start(bf16[64,896]{1,0:T(8,128)(2,1)S(1)} %fusion.3), channel_id=1, source_target_pairs={{0,416},{32,128},{64,480},{96,192},{128,32},{160,256},{192,96},{22... | collective-permute-start | bytes 344072 | tf_op jit(solution)/shard_map/ppermute | solution.py:120
  81.6 12.0 %collective-permute-start.7 = (bf16[64,896]{1,0:T(8,128)(2,1)S(1)}, bf16[64,896]{1,0:T(8,128)(2,1)S(1)}, u32[]{:S(2)}, u32[]{:S(2)}) collective-permute-start(bf16[64,896]{1,0:T(8,128)(2,1)S(1)} %get-tuple-element.31), channel_id=1, source_target_pairs={{0,96},{32,448},{64,160},{96,0},{128,224},{160,64},{192,288},{224,... | collective-permute-start | bytes 344072 | tf_op jit(solution)/shard_map/ppermute | solution.py:120
  86.4 10.4 %collective-permute-start.8 = (bf16[64,896]{1,0:T(8,128)(2,1)S(1)}, bf16[64,896]{1,0:T(8,128)(2,1)S(1)}, u32[]{:S(2)}, u32[]{:S(2)}) collective-permute-start(bf16[64,896]{1,0:T(8,128)(2,1)S(1)} %get-tuple-element.32), channel_id=1, source_target_pairs={{0,416},{32,128},{64,480},{96,192},{128,32},{160,256},{192,96},{22... | collective-permute-start | bytes 344072 | tf_op jit(solution)/shard_map/ppermute | solution.py:120

commit v8 on v7

--- a/solution.py
+++ b/solution.py
@@ -11,7 +11,8 @@
 EPSILON = 1e-05
 DP = ("z", "yh")
 TENSOR = ("x", "yl", "core")
-HUBS = (-6, 6, -3, 0, 3)
+HUBS = (3, -3, 0)
+LOWER = (0, 2)
 
 
 def normalize(residual):
@@ -43,7 +44,6 @@
     up_ref,
     own_ref,
     other_ref,
-    far_ref,
     ahead_ref,
     behind_ref,
     hub_ref,
@@ -53,7 +53,7 @@
 ):
     z = lax.axis_index("z")
     half = lax.axis_index("yh")
-    rows, width = own_ref.shape
+    planes, rows, width = own_ref.shape
     tokens = same_ref.shape[0]
     gain = gain_ref[...]
     normed_ref[:tokens] = (normalize(same_ref[...])[0] * gain).astype(jnp.bfloat16)
@@ -64,13 +64,15 @@
     first = half == 0
     even = lax.axis_index("core") == 0
     count = lax.axis_size("core")
-    split = (rows // (count * block_rows), count, block_rows, width)
+    split = (planes, rows // (count * block_rows), count, block_rows, width)
     own = own_ref[...].astype(jnp.float32).reshape(split)
     other = other_ref[...].astype(jnp.float32).reshape(split)
+    piece = planes * rows // count
 
     def by_core(values, same):
         near, away = (0, 1) if same else (1, 0)
-        return jnp.where(even, values[:, near], values[:, away]).reshape(rows // count, width)
+        chosen = jnp.where(even, values[:, :, near], values[:, :, away])
+        return jnp.stack([chosen[at] for at in range(planes)], axis=1).reshape(piece, width)
 
     pieces = []
     for same in (True, False):
@@ -83,13 +85,12 @@
     up_grad = weighted * gate_value
     grads_ref[:, :width] = gate_grad.astype(jnp.bfloat16)
     grads_ref[:, width:] = up_grad.astype(jnp.bfloat16)
-    piece = rows // count
 
     def own_rows(values):
         near = jnp.where(first, values[:piece], values[piece : 2 * piece])
         away = jnp.where(first, values[2 * piece : 3 * piece], values[3 * piece :])
-        near = near.reshape(piece // block_rows, 1, block_rows, width)
-        away = away.reshape(piece // block_rows, 1, block_rows, width)
+        shape = (piece // (planes * block_rows), planes, block_rows, width)
+        near, away = near.reshape(shape)[:, :1], away.reshape(shape)[:, :1]
         both = jnp.concatenate(
             [jnp.where(even, near, away), jnp.where(even, away, near)], axis=1
         )
@@ -98,25 +99,28 @@
     grads_own_ref[:, :width] = own_rows(gate_grad)
     grads_own_ref[:, width:] = own_rows(up_grad)
     grads = grads_ref[...]
-    depth = far_ref.shape[0]
-
-    sign = 1 - 2 * lax.rem(z, 2)
+    depth = hub_ref.shape[1]
+    pair, parity = z // planes, lax.rem(z, planes)
+    pairs = nz // planes
+
+    sign = 1 - 2 * lax.rem(pair, 2)
 
     def block(relative):
-        chunk = lax.rem(z - sign * relative + 2 * nz, nz)
+        chunk = lax.rem(pair - sign * relative + 2 * pairs, pairs) * planes + parity
         lanes = pl.ds(pl.multiple_of(chunk * 2 * depth, 2 * depth), 2 * depth)
         both = contract_first(normed_ref[:, lanes], grads) * factor
         return jnp.where(first, both[:depth], both[depth:]).astype(jnp.bfloat16)
 
-    far_ref[...] = block(nz // 2)
     for at, hub in enumerate(HUBS):
         ahead_ref[at] = block(-hub - 1)
-        behind_ref[at] = block(-hub + 1)
+    for at, source in enumerate(LOWER):
+        behind_ref[at] = block(-HUBS[source] + 1)
+    for at, hub in enumerate(HUBS):
         hub_ref[at] = block(hub)
 
 
 def move(value, hops, nz):
-    pairs = [(i, (i + (1 - 2 * (i % 2)) * hops) % nz) for i in range(nz)]
+    pairs = [(i, (i + (1 - 2 * (i // 2 % 2)) * 2 * hops) % nz) for i in range(nz)]
     return lax.ppermute(value, "z", pairs)
 
 
@@ -126,30 +130,32 @@
     features = residual.shape[1]
     depth = features // (nz * nh)
     f32, bf16 = jnp.float32, jnp.bfloat16
-    own = hidden_grad
-    other = lax.ppermute(own, "yh", [(0, 1), (1, 0)])
+    flip = [(i, i ^ 1) for i in range(nz)]
+    swap = [(0, 1), (1, 0)]
+    near = jnp.concatenate([residual, lax.ppermute(residual, "z", flip)], axis=0)
+    own = jnp.stack([hidden_grad, lax.ppermute(hidden_grad, "z", flip)])
+    other = lax.ppermute(own, "yh", swap)
     chips = nh * nt // lax.axis_size("core")
-    copies = jnp.broadcast_to(residual[None], (chips,) + residual.shape)
+    copies = jnp.broadcast_to(near[None], (chips,) + near.shape)
     same = lax.all_to_all(copies, ("yh", "x", "yl"), 0, 0, tiled=True)
-    same = same.reshape(chips * residual.shape[0], features)
+    same = same.reshape(chips * near.shape[0], features)
     same, other = lax.optimization_barrier((same, other))
-    swapped = lax.ppermute(same, "core", [(0, 1), (1, 0)])
+    swapped = lax.ppermute(same, "core", swap)
     factor = float(rows * nz * nh) ** (-0.5)
     shape = jax.ShapeDtypeStruct
-    far, ahead, behind, hub, grads_own = pl.pallas_call(
+    ahead, behind, hub, grads_own = pl.pallas_call(
         functools.partial(local_kernel, factor, nz, residual.shape[0]),
         out_shape=(
-            shape((depth, 2 * width), bf16),
             shape((len(HUBS), depth, 2 * width), bf16),
-            shape((len(HUBS), depth, 2 * width), bf16),
+            shape((len(LOWER), depth, 2 * width), bf16),
             shape((len(HUBS), depth, 2 * width), bf16),
             shape((rows, 2 * width), bf16),
         ),
         scratch_shapes=[
-            pltpu.VMEM((nh * rows, features), bf16),
-            pltpu.VMEM((nh * rows, 2 * width), bf16),
+            pltpu.VMEM((2 * nh * rows, features), bf16),
+            pltpu.VMEM((2 * nh * rows, 2 * width), bf16),
         ],
-        compiler_params=pltpu.CompilerParams(vmem_limit_bytes=20 * 1024 * 1024),
+        compiler_params=pltpu.CompilerParams(vmem_limit_bytes=36 * 1024 * 1024),
         cost_estimate=pl.CostEstimate(
             flops=8 * nh * rows * features * width,
             bytes_accessed=8 * features * width,
@@ -158,31 +164,23 @@
         name="local",
     )(same, swapped, norm_gain.reshape(1, features), gate_weight.T, up_weight.T, own, other)
 
-    from_far = move(far, -2, nz)
     ahead, behind = move(ahead, 1, nz), move(behind, -1, nz)
-    grads_own, from_far = lax.optimization_barrier((grads_own, from_far))
+    grads_own, kept = lax.optimization_barrier((grads_own, hub))
 
     part = contract_last(grads_own[:, :width], gate_weight)
     part = (part + contract_last(grads_own[:, width:], up_weight)).astype(bf16)
     blocks = part.reshape(nt, rows // nt, features)
     moved = lax.all_to_all(blocks, TENSOR, 0, 0, tiled=True)
 
-    def joined(at):
-        return hub[at].astype(f32) + ahead[at].astype(f32) + behind[at].astype(f32)
-
-    plus, minus = lax.optimization_barrier(
-        (joined(0).astype(bf16), (joined(1) + from_far.astype(f32)).astype(bf16))
-    )
-    plus, minus = move(plus, 3, nz), move(minus, -3, nz)
-    plus, minus = lax.optimization_barrier((plus, minus))
     plus, minus = lax.optimization_barrier(
         (
-            (joined(2) + minus.astype(f32)).astype(bf16),
-            (joined(4) + plus.astype(f32)).astype(bf16),
+            (kept[1].astype(f32) + ahead[1].astype(f32)).astype(bf16),
+            (kept[0].astype(f32) + ahead[0].astype(f32) + behind[0].astype(f32)).astype(bf16),
         )
     )
     plus, minus = move(plus, 3, nz), move(minus, -3, nz)
-    total = (joined(3) + plus.astype(f32) + minus.astype(f32)).astype(bf16)
+    total = kept[2].astype(f32) + ahead[2].astype(f32) + behind[1].astype(f32)
+    total = (total + plus.astype(f32) + minus.astype(f32)).astype(bf16)
 
     scaled, inverse = normalize(residual)
     normed_grad = jnp.sum(moved.astype(f32), axis=0)

time: 99.3 us -> 111 us (1.12)
  the two profiles are of different devices: /device:TPU:32 before, /device:TPU:1 now
where the time goes in v8:
time: 111 us; the launch traced here: 110 us
  starting transfers between devices  60.7 us (55%)
  waiting for transfers between devices  32.4 us (29%)
  Pallas kernels  5.32 us (5%)
  local copies, waits for them, and re-layouts  5.11 us (5%)
  other arithmetic  3.95 us (4%)
  matrix products  1.74 us (2%)
    ppermute x4, starting transfers between devices, move(): return lax.ppermute(value, 'z', pairs)  33 us
    ppermute x4, waiting for transfers between devices, move(): return lax.ppermute(value, 'z', pairs)  15.9 us
    ppermute x1, waiting for transfers between devices, shards(): other = lax.ppermute(own, 'yh', swap)  10.5 us
    all_to_all x1, starting transfers between devices, shards(): same = lax.all_to_all(copies, ('yh', 'x', 'yl'), 0, 0, tiled=True)  6.75 us
    pallas_call x1, Pallas kernels, shards(): pl.pallas_call(functools.partial(local_kernel, factor, nz, residual.shape...  5.32 us
    ppermute x1, starting transfers between devices, shards(): other = lax.ppermute(own, 'yh', swap)  5.07 us
    ppermute x1, starting transfers between devices, shards(): lax.ppermute(residual, 'z', flip)  4.51 us
    all_to_all x1, starting transfers between devices, shards(): moved = lax.all_to_all(blocks, TENSOR, 0, 0, tiled=True)  4.26 us
  transfers between devices with their start and end apart: 10, of which 7 were waited for; matrix products, arithmetic and copies ran while one was open for 4% of the time, Pallas kernels for 0%

profile of v8, /device:TPU:1, one launch (start us, length us, event | category | flops | bytes accessed | tf_op | source)
XLA Modules:
  0.0 109.9 jit_solution(9980328397766593980)
XLA Ops:
  0.6 0.0 copy-start.6
  0.6 4.5 %collective-permute-start = (bf16[8,2048]{1,0:T(8,128)(2,1)}, bf16[8,2048]{1,0:T(8,128)(2,1)S(1)}, u32[]{:S(2)}, u32[]{:S(2)}) collective-permute-start(bf16[8,2048]{1,0:T(8,128)(2,1)} %param.5), channel_id=1, source_target_pairs={{0,32},{32,0},{64,96},{96,64},{128,160},{160,128},{192,224},{224,1... | collective-permute-start | bytes 98312 | tf_op jit(solution)/shard_map/ppermute | solution.py:135
  5.2 1.5 %collective-permute-done = bf16[8,2048]{1,0:T(8,128)(2,1)S(1)} collective-permute-done((bf16[8,2048]{1,0:T(8,128)(2,1)}, bf16[8,2048]{1,0:T(8,128)(2,1)S(1)}, u32[]{:S(2)}, u32[]{:S(2)}) %collective-permute-start) | collective-permute-done | bytes 32800 | tf_op jit(solution)/shard_map/ppermute | solution.py:135
  6.7 0.8 pad_maximum_fusion.1
  7.4 0.0 copy-start.5
  7.4 0.0 copy-start
  7.4 0.0 copy-start.2
  7.4 1.1 broadcast_in_dim.2
  8.5 6.8 %all-to-all-start = ((bf16[16,16,2048]{2,1,0:T(8,128)(2,1)}), bf16[16,16,2048]{2,1,0:T(8,128)(2,1)S(1)}, u32[]{:S(2)}, u32[]{:S(2)}) async-start(bf16[16,16,2048]{2,1,0:T(8,128)(2,1)} %broadcast_in_dim.2), calls=%async_computation | async-start | bytes 2097152 | tf_op jit(solution)/shard_map/all_to_all | solution.py:140
  15.3 0.0 copy-done.6
  15.3 0.1 copy.8
  15.4 3.4 %collective-permute-start.1 = (bf16[128,448]{1,0:T(8,128)(2,1)S(1)}, bf16[128,448]{1,0:T(8,128)(2,1)S(1)}, u32[]{:S(2)}, u32[]{:S(2)}) collective-permute-start(bf16[128,448]{1,0:T(8,128)(2,1)S(1)} %copy.8), channel_id=1, source_target_pairs={{0,32},{32,0},{64,96},{96,64},{128,160},{160,128},{192,224},{224,1... | collective-permute-start | bytes 344072 | tf_op jit(solution)/shard_map/ppermute | solution.py:136
  18.8 2.3 %collective-permute-done.1 = bf16[128,448]{1,0:T(8,128)(2,1)S(1)} collective-permute-done((bf16[128,448]{1,0:T(8,128)(2,1)S(1)}, bf16[128,448]{1,0:T(8,128)(2,1)S(1)}, u32[]{:S(2)}, u32[]{:S(2)}) %collective-permute-start.1) | collective-permute-done | bytes 114720 | tf_op jit(solution)/shard_map/ppermute | solution.py:136
  21.2 5.1 %collective-permute-start.2 = (bf16[2,128,448]{2,1,0:T(8,128)(2,1)S(1)}, bf16[2,128,448]{2,1,0:T(8,128)(2,1)S(1)}, u32[]{:S(2)}, u32[]{:S(2)}) collective-permute-start(bf16[2,128,448]{2,1,0:T(8,128)(2,1)S(1)} %pad_maximum_fusion.own_ref), channel_id=1, source_target_pairs={{0,16},{16,0},{1,17},{17,1},{2,18},{18,2},{3,19},{19,3},{4,20},{20... | collective-permute-start | bytes 688136 | tf_op jit(solution)/shard_map/ppermute | solution.py:137
  26.3 10.5 %collective-permute-done.2.other_ref = bf16[2,128,448]{2,1,0:T(8,128)(2,1)S(1)} collective-permute-done((bf16[2,128,448]{2,1,0:T(8,128)(2,1)S(1)}, bf16[2,128,448]{2,1,0:T(8,128)(2,1)S(1)}, u32[]{:S(2)}, u32[]{:S(2)}) %collective-permute-start.2) | collective-permute-done | bytes 229408 | tf_op jit(solution)/shard_map/ppermute | solution.py:137
  36.7 0.0 copy-start.3
  36.7 0.7 copy-done.3
  37.4 0.0 all-to-all-done
  37.4 3.7 %collective-permute-start.3 = (bf16[256,2048]{1,0:T(8,128)(2,1)S(1)}, bf16[256,2048]{1,0:T(8,128)(2,1)S(1)}, u32[]{:S(2)}, u32[]{:S(2)}) collective-permute-start(bf16[256,2048]{1,0:T(8,128)(2,1)S(1)} %bitcast.22), channel_id=1, source_target_pairs={{0,1},{1,0},{2,3},{3,2},{4,5},{5,4},{6,7},{7,6},{8,9},{9,8},{10,11... | collective-permute-start | bytes 3145736 | tf_op jit(solution)/shard_map/ppermute | solution.py:143
  41.1 0.0 copy-done.5
  41.1 0.1 fusion.15
  41.2 2.1 %collective-permute-done.3.swapped_ref = bf16[256,2048]{1,0:T(8,128)(2,1)S(1)} collective-permute-done((bf16[256,2048]{1,0:T(8,128)(2,1)S(1)}, bf16[256,2048]{1,0:T(8,128)(2,1)S(1)}, u32[]{:S(2)}, u32[]{:S(2)}) %collective-permute-start.3) | collective-permute-done | bytes 1048608 | tf_op jit(solution)/shard_map/ppermute | solution.py:143
  43.4 0.0 copy-done
  43.4 0.0 copy-done.2
  43.4 0.0 copy-start.1
  43.4 1.5 %copy-done.1 = bf16[2048,448]{0,1:T(8,128)(2,1)S(1)} copy-done((bf16[2048,448]{0,1:T(8,128)(2,1)S(1)}, bf16[2048,448]{0,1:T(8,128)(2,1)}, u32[]{:S(2)}) %copy-start.1) | copy-done | bytes 1835032
  44.9 0.0 copy-start.4
  44.9 0.9 copy-done.4
  45.8 5.3 %local.1 = (bf16[3,64,896]{2,1,0:T(8,128)(2,1)}, bf16[2,64,896]{2,1,0:T(8,128)(2,1)}, bf16[3,64,896]{2,1,0:T(8,128)(2,1)S(1)}, bf16[128,896]{1,0:T(8,128)(2,1)S(1)}) custom-call(bf16[256,2048]{1,0:T(8,128)(2,1)S(1)} %bitcast.23, bf16[256,2048]{1,0:T(8,128)(2,1)S(1)} %collective-permute-done.3.swapped_ref, f32[1,2048]{1,0:T(1,128)S(1)} %bitcast.24, ...), custom_call_target="tpu_custom_call" | custom-call | flops 1879048192 | bytes 7340032 | tf_op jit(solution)/shard_map/local/pallas_call | solution.py:146
  51.1 5.0 %collective-permute-start.4 = (bf16[3,64,896]{2,1,0:T(8,128)(2,1)}, bf16[3,64,896]{2,1,0:T(8,128)(2,1)}, u32[]{:S(2)}, u32[]{:S(2)}) collective-permute-start(bf16[3,64,896]{2,1,0:T(8,128)(2,1)} %get-tuple-element.19), channel_id=1, source_target_pairs={{0,64},{32,96},{64,0},{96,32},{128,192},{160,224},{192,128},{224,1... | collective-permute-start | bytes 1032200 | tf_op jit(solution)/shard_map/ppermute | solution.py:124
  56.1 9.5 %collective-permute-start.5 = (bf16[2,64,896]{2,1,0:T(8,128)(2,1)}, bf16[2,64,896]{2,1,0:T(8,128)(2,1)S(1)}, u32[]{:S(2)}, u32[]{:S(2)}) collective-permute-start(bf16[2,64,896]{2,1,0:T(8,128)(2,1)} %get-tuple-element.20), channel_id=1, source_target_pairs={{0,448},{32,480},{64,128},{96,160},{128,64},{160,96},{192,256},{22... | collective-permute-start | bytes 688136 | tf_op jit(solution)/shard_map/ppermute | solution.py:124
  65.7 0.4 fusion.5
  66.1 1.3 %fusion.1 = bf16[16,8,2048]{2,1,0:T(8,128)(2,1)} fusion(f32[128,2048]{1,0:T(8,128)S(1)} %fusion.5, bf16[2048,448]{0,1:T(8,128)(2,1)S(1)} %copy-done, bf16[128,896]{1,0:T(8,128)(2,1)S(1)} %get-tuple-element.17), kind=kOutput, calls=%fused_computation.2 | convolution fusion | flops 235405312 | bytes 3538944 | tf_op jit(solution)/shard_map/dot_general | solution.py:25
  67.4 4.3 %all-to-all-start.1 = ((bf16[16,8,2048]{2,1,0:T(8,128)(2,1)}), bf16[16,8,2048]{2,1,0:T(8,128)(2,1)S(1)}, u32[]{:S(2)}, u32[]{:S(2)}) async-start(bf16[16,8,2048]{2,1,0:T(8,128)(2,1)} %fusion.1), calls=%async_computation.1 | async-start | bytes 1048576 | tf_op jit(solution)/shard_map/all_to_all | solution.py:173
  71.7 0.2 collective-permute-done.5
  71.9 0.1 collective-permute-done.4
  72.0 1.1 fusion.8
  73.0 11.8 %collective-permute-start.6 = (bf16[64,896]{1,0:T(8,128)(2,1)S(1)}, bf16[64,896]{1,0:T(8,128)(2,1)S(1)}, u32[]{:S(2)}, u32[]{:S(2)}) collective-permute-start(bf16[64,896]{1,0:T(8,128)(2,1)S(1)} %get-tuple-element.21), channel_id=1, source_target_pairs={{0,192},{32,224},{64,384},{96,416},{128,320},{160,352},{192,0},{22... | collective-permute-start | bytes 344072 | tf_op jit(solution)/shard_map/ppermute | solution.py:124
  84.9 6.7 %collective-permute-start.7 = (bf16[64,896]{1,0:T(8,128)(2,1)S(1)}, bf16[64,896]{1,0:T(8,128)(2,1)S(1)}, u32[]{:S(2)}, u32[]{:S(2)}) collective-permute-start(bf16[64,896]{1,0:T(8,128)(2,1)S(1)} %get-tuple-element.22), channel_id=1, source_target_pairs={{0,320},{32,352},{64,256},{96,288},{128,448},{160,480},{192,384},{... | collective-permute-start | bytes 344072 | tf_op jit(solution)/shard_map/ppermute | solution.py:124
  91.6 0.0 collective-permute-done.6
  91.6 15.7 %collective-permute-done.7 = bf16[64,896]{1,0:T(8,128)(2,1)S(1)} collective-permute-done((bf16[64,896]{1,0:T(8,128)(2,1)S(1)}, bf16[64,896]{1,0:T(8,128)(2,1)S(1)}, u32[]{:S(2)}, u32[]{:S(2)}) %collective-permute-start.7) | collective-permute-done | bytes 114720 | tf_op jit(solution)/shard_map/ppermute | solution.py:124
  107.2 1.0 fusion.3
  108.2 0.7 fusion.16
  108.9 0.0 all-to-all-done.1
  108.9 0.1 convert_reduce_fusion
  109.0 0.2 fusion.11
  109.2 0.7 fusion.14
  (3 shorter events, 0.0 us)
Async XLA Ops:
  0.6 14.7 %copy-start.6 = (bf16[128,448]{0,1:T(8,128)(2,1)S(1)}, bf16[128,448]{0,1:T(8,128)(2,1)}, u32[]{:S(2)}) copy-start(bf16[128,448]{0,1:T(8,128)(2,1)} %param.9) | copy-start | bytes 344068
  0.6 6.0 %collective-permute-start = (bf16[8,2048]{1,0:T(8,128)(2,1)}, bf16[8,2048]{1,0:T(8,128)(2,1)S(1)}, u32[]{:S(2)}, u32[]{:S(2)}) collective-permute-start(bf16[8,2048]{1,0:T(8,128)(2,1)} %param.5), channel_id=1, source_target_pairs={{0,32},{32,0},{64,96},{96,64},{128,160},{160,128},{192,224},{224,1... | collective-permute-start | bytes 98312 | tf_op jit(solution)/shard_map/ppermute | solution.py:135
  7.4 33.7 %copy-start.5 = (bf16[8,2048]{1,0:T(8,128)(2,1)S(1)}, bf16[8,2048]{1,0:T(8,128)(2,1)}, u32[]{:S(2)}) copy-start(bf16[8,2048]{1,0:T(8,128)(2,1)} %param.5) | copy-start | bytes 98308
  7.4 35.9 %copy-start = (bf16[2048,448]{0,1:T(8,128)(2,1)S(1)}, bf16[2048,448]{0,1:T(8,128)(2,1)}, u32[]{:S(2)}) copy-start(bf16[2048,448]{0,1:T(8,128)(2,1)} %param.8) | copy-start | bytes 5505028
  7.4 35.9 %copy-start.2 = (f32[2048]{0:T(1024)S(1)}, f32[2048]{0:T(1024)}, u32[]{:S(2)}) copy-start(f32[2048]{0:T(1024)} %param.6) | copy-start | bytes 24580
  8.5 28.9 %all-to-all-start = ((bf16[16,16,2048]{2,1,0:T(8,128)(2,1)}), bf16[16,16,2048]{2,1,0:T(8,128)(2,1)S(1)}, u32[]{:S(2)}, u32[]{:S(2)}) async-start(bf16[16,16,2048]{2,1,0:T(8,128)(2,1)} %broadcast_in_dim.2), calls=%async_computation | async-start | bytes 2097152 | tf_op jit(solution)/shard_map/all_to_all | solution.py:140
  15.4 5.7 %collective-permute-start.1 = (bf16[128,448]{1,0:T(8,128)(2,1)S(1)}, bf16[128,448]{1,0:T(8,128)(2,1)S(1)}, u32[]{:S(2)}, u32[]{:S(2)}) collective-permute-start(bf16[128,448]{1,0:T(8,128)(2,1)S(1)} %copy.8), channel_id=1, source_target_pairs={{0,32},{32,0},{64,96},{96,64},{128,160},{160,128},{192,224},{224,1... | collective-permute-start | bytes 344072 | tf_op jit(solution)/shard_map/ppermute | solution.py:136
  21.2 15.5 %collective-permute-start.2 = (bf16[2,128,448]{2,1,0:T(8,128)(2,1)S(1)}, bf16[2,128,448]{2,1,0:T(8,128)(2,1)S(1)}, u32[]{:S(2)}, u32[]{:S(2)}) collective-permute-start(bf16[2,128,448]{2,1,0:T(8,128)(2,1)S(1)} %pad_maximum_fusion.own_ref), channel_id=1, source_target_pairs={{0,16},{16,0},{1,17},{17,1},{2,18},{18,2},{3,19},{19,3},{4,20},{20... | collective-permute-start | bytes 688136 | tf_op jit(solution)/shard_map/ppermute | solution.py:137
  36.7 0.7 copy-start.3
  37.4 5.9 %collective-permute-start.3 = (bf16[256,2048]{1,0:T(8,128)(2,1)S(1)}, bf16[256,2048]{1,0:T(8,128)(2,1)S(1)}, u32[]{:S(2)}, u32[]{:S(2)}) collective-permute-start(bf16[256,2048]{1,0:T(8,128)(2,1)S(1)} %bitcast.22), channel_id=1, source_target_pairs={{0,1},{1,0},{2,3},{3,2},{4,5},{5,4},{6,7},{7,6},{8,9},{9,8},{10,11... | collective-permute-start | bytes 3145736 | tf_op jit(solution)/shard_map/ppermute | solution.py:143
  43.4 1.5 %copy-start.1 = (bf16[2048,448]{0,1:T(8,128)(2,1)S(1)}, bf16[2048,448]{0,1:T(8,128)(2,1)}, u32[]{:S(2)}) copy-start(bf16[2048,448]{0,1:T(8,128)(2,1)} %param.7) | copy-start | bytes 5505028
  44.9 0.9 copy-start.4
  51.1 20.8 %collective-permute-start.4 = (bf16[3,64,896]{2,1,0:T(8,128)(2,1)}, bf16[3,64,896]{2,1,0:T(8,128)(2,1)}, u32[]{:S(2)}, u32[]{:S(2)}) collective-permute-start(bf16[3,64,896]{2,1,0:T(8,128)(2,1)} %get-tuple-element.19), channel_id=1, source_target_pairs={{0,64},{32,96},{64,0},{96,32},{128,192},{160,224},{192,128},{224,1... | collective-permute-start | bytes 1032200 | tf_op jit(solution)/shard_map/ppermute | solution.py:124
  56.1 15.7 %collective-permute-start.5 = (bf16[2,64,896]{2,1,0:T(8,128)(2,1)}, bf16[2,64,896]{2,1,0:T(8,128)(2,1)S(1)}, u32[]{:S(2)}, u32[]{:S(2)}) collective-permute-start(bf16[2,64,896]{2,1,0:T(8,128)(2,1)} %get-tuple-element.20), channel_id=1, source_target_pairs={{0,448},{32,480},{64,128},{96,160},{128,64},{160,96},{192,256},{22... | collective-permute-start | bytes 688136 | tf_op jit(solution)/shard_map/ppermute | solution.py:124
  67.4 41.5 %all-to-all-start.1 = ((bf16[16,8,2048]{2,1,0:T(8,128)(2,1)}), bf16[16,8,2048]{2,1,0:T(8,128)(2,1)S(1)}, u32[]{:S(2)}, u32[]{:S(2)}) async-start(bf16[16,8,2048]{2,1,0:T(8,128)(2,1)} %fusion.1), calls=%async_computation.1 | async-start | bytes 1048576 | tf_op jit(solution)/shard_map/all_to_all | solution.py:173
  73.0 18.5 %collective-permute-start.6 = (bf16[64,896]{1,0:T(8,128)(2,1)S(1)}, bf16[64,896]{1,0:T(8,128)(2,1)S(1)}, u32[]{:S(2)}, u32[]{:S(2)}) collective-permute-start(bf16[64,896]{1,0:T(8,128)(2,1)S(1)} %get-tuple-element.21), channel_id=1, source_target_pairs={{0,192},{32,224},{64,384},{96,416},{128,320},{160,352},{192,0},{22... | collective-permute-start | bytes 344072 | tf_op jit(solution)/shard_map/ppermute | solution.py:124
  84.9 22.4 %collective-permute-start.7 = (bf16[64,896]{1,0:T(8,128)(2,1)S(1)}, bf16[64,896]{1,0:T(8,128)(2,1)S(1)}, u32[]{:S(2)}, u32[]{:S(2)}) collective-permute-start(bf16[64,896]{1,0:T(8,128)(2,1)S(1)} %get-tuple-element.22), channel_id=1, source_target_pairs={{0,320},{32,352},{64,256},{96,288},{128,448},{160,480},{192,384},{... | collective-permute-start | bytes 344072 | tf_op jit(solution)/shard_map/ppermute | solution.py:124

commit v9 on v6

--- a/solution.py
+++ b/solution.py
@@ -59,9 +59,8 @@
     half = lax.axis_index("yh")
     rows, width = own_ref.shape
     tokens = same_ref.shape[0]
-    gain = gain_ref[...]
-    normed_ref[:tokens] = (normalize(same_ref[...])[0] * gain).astype(jnp.bfloat16)
-    normed_ref[tokens:] = (normalize(swapped_ref[...])[0] * gain).astype(jnp.bfloat16)
+    normed_ref[:tokens] = same_ref[...]
+    normed_ref[tokens:] = (normalize(swapped_ref[...])[0] * gain_ref[...]).astype(jnp.bfloat16)
     normed = normed_ref[...]
     gate_value = contract_last(normed, gate_ref[...])
     up_value = contract_last(normed, up_ref[...])
@@ -123,6 +122,10 @@
         outer_hub_ref[at] = block(hub)
     for at, hub in enumerate(INNER):
         inner_hub_ref[at] = block(hub)
+
+
+def norm_kernel(rows_ref, gain_ref, normed_ref):
+    normed_ref[...] = (normalize(rows_ref[...])[0] * gain_ref[...]).astype(jnp.bfloat16)
 
 
 def move(value, hops, nz):
@@ -144,6 +147,16 @@
     same = same.reshape(chips * residual.shape[0], features)
     same, other = lax.optimization_barrier((same, other))
     swapped = lax.ppermute(same, "core", [(0, 1), (1, 0)])
+    gain = norm_gain.reshape(1, features)
+    normed_same = pl.pallas_call(
+        norm_kernel,
+        out_shape=jax.ShapeDtypeStruct(same.shape, bf16),
+        cost_estimate=pl.CostEstimate(
+            flops=8 * rows * features, bytes_accessed=4 * rows * features, transcendentals=rows
+        ),
+        compiler_params=pltpu.CompilerParams(vmem_limit_bytes=8 * 1024 * 1024),
+        name="norm",
+    )(same, gain)
     factor = float(rows * nz * nh) ** (-0.5)
     shape = jax.ShapeDtypeStruct
     far, outer_ahead, outer_behind, inner_ahead, inner_behind, outer_hub, inner_hub, grads_own = pl.pallas_call(
@@ -169,7 +182,7 @@
             transcendentals=nh * rows * width,
         ),
         name="local",
-    )(same, swapped, norm_gain.reshape(1, features), gate_weight.T, up_weight.T, own, other)
+    )(normed_same, swapped, gain, gate_weight.T, up_weight.T, own, other)
 
     from_far = move(far, -2, nz).astype(f32)
     outer_ahead, outer_behind = move(outer_ahead, 1, nz), move(outer_behind, -1, nz)
@@ -182,11 +195,11 @@
             + outer_behind[at].astype(f32)
         )
 
-    def inner(at):
+    def inner(at, columns=slice(None)):
         return (
-            inner_hub[at].astype(f32)
-            + inner_ahead[at].astype(f32)
-            + inner_behind[at].astype(f32)
+            inner_hub[at, :, columns].astype(f32)
+            + inner_ahead[at, :, columns].astype(f32)
+            + inner_behind[at, :, columns].astype(f32)
         )
 
     plus, minus = lax.optimization_barrier(
@@ -215,8 +228,15 @@
     residual_grad = (
         (weighted - scaled * jnp.mean(weighted * scaled, axis=-1, keepdims=True)) * inverse
     ).astype(bf16)
-    total = (inner(1) + plus.astype(f32) + minus.astype(f32)).astype(bf16)
-    return (residual_grad, total[:, :width], total[:, width:])
+    totals = [
+        (
+            inner(1, columns)
+            + plus[:, columns].astype(f32)
+            + minus[:, columns].astype(f32)
+        ).astype(bf16)
+        for columns in (slice(0, width), slice(width, None))
+    ]
+    return (residual_grad, totals[0], totals[1])
 
 
 def solution(mesh):

time: 93.7 us -> 91.7 us (0.979)
  local copies, waits for them, and re-layouts: 6.54 us -> 4.25 us
    unnamed x15 -> x9, local copies, waits for them, and re-layouts: 4.08 us -> 2.51 us
where the time goes in v9:
time: 91.7 us; the launch traced here: 90.9 us
  starting transfers between devices  57.7 us (63%)
  waiting for transfers between devices  17.8 us (19%)
  other arithmetic  5.35 us (6%)
  local copies, waits for them, and re-layouts  4.25 us (5%)
  Pallas kernels  3.25 us (4%)
  matrix products  1.75 us (2%)
    ppermute x9, starting transfers between devices, move(): return lax.ppermute(value, 'z', pairs)  37.1 us
    ppermute x9, waiting for transfers between devices, move(): return lax.ppermute(value, 'z', pairs)  9.75 us
    all_to_all x1, starting transfers between devices, shards(): same = lax.all_to_all(copies, ('yh', 'x', 'yl'), 0, 0, tiled=True)  6.92 us
    ppermute x1, waiting for transfers between devices, shards(): other = lax.ppermute(own, 'yh', [(0, 1), (1, 0)])  6.76 us
    all_to_all x1, starting transfers between devices, shards(): moved = lax.all_to_all(blocks, TENSOR, 0, 0, tiled=True)  6.35 us
    ppermute x1, starting transfers between devices, shards(): other = lax.ppermute(own, 'yh', [(0, 1), (1, 0)])  4.6 us
    pallas_call x1, Pallas kernels, shards(): pl.pallas_call(functools.partial(local_kernel, factor, nz, residual.shape...  3.03 us
    ppermute x1, starting transfers between devices, shards(): swapped = lax.ppermute(same, 'core', [(0, 1), (1, 0)])  2.71 us
  transfers between devices with their start and end apart: 13, of which 3 were waited for; matrix products, arithmetic and copies ran while one was open for 8% of the time, Pallas kernels for 0%

profile of v9, /device:TPU:67, one launch (start us, length us, event | category | flops | bytes accessed | tf_op | source)
XLA Modules:
  0.0 90.9 jit_solution(15693449272351443974)
XLA Ops:
  0.6 0.0 copy-start.2
  0.6 0.0 copy-start
  0.7 1.7 %broadcast_in_dim.2 = bf16[16,8,2048]{2,1,0:T(8,128)(2,1)} broadcast(bf16[8,2048]{1,0:T(8,128)(2,1)} %param.5), dimensions={1,2} | broadcast | bytes 557056 | tf_op jit(solution)/shard_map/broadcast_in_dim | solution.py:145
  2.4 6.9 %all-to-all-start = ((bf16[16,8,2048]{2,1,0:T(8,128)(2,1)}), bf16[16,8,2048]{2,1,0:T(8,128)(2,1)S(1)}, u32[]{:S(2)}, u32[]{:S(2)}) async-start(bf16[16,8,2048]{2,1,0:T(8,128)(2,1)} %broadcast_in_dim.2), calls=%async_computation | async-start | bytes 1048576 | tf_op jit(solution)/shard_map/all_to_all | solution.py:146
  9.3 1.0 %copy.8.own_ref = bf16[128,448]{1,0:T(8,128)(2,1)S(1)} copy(bf16[128,448]{0,1:T(8,128)(2,1)} %param.9) | data formatting | bytes 229376 | tf_op args[4]
  10.3 4.6 %collective-permute-start = (bf16[128,448]{1,0:T(8,128)(2,1)S(1)}, bf16[128,448]{1,0:T(8,128)(2,1)S(1)}, u32[]{:S(2)}, u32[]{:S(2)}) collective-permute-start(bf16[128,448]{1,0:T(8,128)(2,1)S(1)} %copy.8.own_ref), channel_id=1, source_target_pairs={{0,16},{16,0},{1,17},{17,1},{2,18},{18,2},{3,19},{19,3},{4,20},{20... | collective-permute-start | bytes 344072 | tf_op jit(solution)/shard_map/ppermute | solution.py:143
  14.9 6.8 %collective-permute-done.other_ref = bf16[128,448]{1,0:T(8,128)(2,1)S(1)} collective-permute-done((bf16[128,448]{1,0:T(8,128)(2,1)S(1)}, bf16[128,448]{1,0:T(8,128)(2,1)S(1)}, u32[]{:S(2)}, u32[]{:S(2)}) %collective-permute-start) | collective-permute-done | bytes 114720 | tf_op jit(solution)/shard_map/ppermute | solution.py:143
  21.7 0.0 all-to-all-done
  21.7 2.7 %collective-permute-start.1 = (bf16[128,2048]{1,0:T(8,128)(2,1)S(1)}, bf16[128,2048]{1,0:T(8,128)(2,1)S(1)}, u32[]{:S(2)}, u32[]{:S(2)}) collective-permute-start(bf16[128,2048]{1,0:T(8,128)(2,1)S(1)} %bitcast.34), channel_id=1, source_target_pairs={{0,1},{1,0},{2,3},{3,2},{4,5},{5,4},{6,7},{7,6},{8,9},{9,8},{10,11... | collective-permute-start | bytes 1572872 | tf_op jit(solution)/shard_map/ppermute | solution.py:149
  24.4 0.0 copy-done.2
  24.4 0.2 norm.1.same_ref
  24.6 1.3 %collective-permute-done.1.swapped_ref = bf16[128,2048]{1,0:T(8,128)(2,1)S(1)} collective-permute-done((bf16[128,2048]{1,0:T(8,128)(2,1)S(1)}, bf16[128,2048]{1,0:T(8,128)(2,1)S(1)}, u32[]{:S(2)}, u32[]{:S(2)}) %collective-permute-start.1) | collective-permute-done | bytes 524320 | tf_op jit(solution)/shard_map/ppermute | solution.py:149
  25.9 0.0 copy-done
  25.9 0.0 copy-start.1
  25.9 1.5 %copy-done.1 = bf16[2048,448]{0,1:T(8,128)(2,1)S(1)} copy-done((bf16[2048,448]{0,1:T(8,128)(2,1)S(1)}, bf16[2048,448]{0,1:T(8,128)(2,1)}, u32[]{:S(2)}) %copy-start.1) | copy-done | bytes 1835032
  27.4 0.0 copy-start.3
  27.4 3.0 %local.1 = (bf16[64,896]{1,0:T(8,128)(2,1)S(1)}, bf16[2,64,896]{2,1,0:T(8,128)(2,1)S(1)}, bf16[2,64,896]{2,1,0:T(8,128)(2,1)S(1)}, bf16[3,64,896]{2,1,0:T(8,128)...) custom-call(bf16[128,2048]{1,0:T(8,128)(2,1)S(1)} %norm.1.same_ref, ...), custom_call_target="tpu_custom_call" | custom-call | flops 1879048192 | bytes 7340032 | tf_op jit(solution)/shard_map/local/pallas_call | solution.py:162
  30.5 3.5 %collective-permute-start.2 = (bf16[2,64,896]{2,1,0:T(8,128)(2,1)S(1)}, bf16[2,64,896]{2,1,0:T(8,128)(2,1)S(1)}, u32[]{:S(2)}, u32[]{:S(2)}) collective-permute-start(bf16[2,64,896]{2,1,0:T(8,128)(2,1)S(1)} %get-tuple-element.25), channel_id=1, source_target_pairs={{0,32},{32,0},{64,96},{96,64},{128,160},{160,128},{192,224},{224,1... | collective-permute-start | bytes 688136 | tf_op jit(solution)/shard_map/ppermute | solution.py:133
  34.0 1.9 %collective-permute-start.3 = (bf16[2,64,896]{2,1,0:T(8,128)(2,1)S(1)}, bf16[2,64,896]{2,1,0:T(8,128)(2,1)S(1)}, u32[]{:S(2)}, u32[]{:S(2)}) collective-permute-start(bf16[2,64,896]{2,1,0:T(8,128)(2,1)S(1)} %get-tuple-element.26), channel_id=1, source_target_pairs={{0,480},{32,64},{64,32},{96,128},{128,96},{160,192},{192,160},{224... | collective-permute-start | bytes 688136 | tf_op jit(solution)/shard_map/ppermute | solution.py:133
  35.9 0.0 copy-done.3
  35.9 0.1 fusion.19
  36.1 9.6 %collective-permute-start.4 = (bf16[64,896]{1,0:T(8,128)(2,1)S(1)}, bf16[64,896]{1,0:T(8,128)(2,1)S(1)}, u32[]{:S(2)}, u32[]{:S(2)}) collective-permute-start(bf16[64,896]{1,0:T(8,128)(2,1)S(1)} %get-tuple-element.27), channel_id=1, source_target_pairs={{0,448},{32,96},{64,0},{96,160},{128,64},{160,224},{192,128},{224,... | collective-permute-start | bytes 344072 | tf_op jit(solution)/shard_map/ppermute | solution.py:133
  45.6 1.9 %collective-permute-start.5 = (bf16[3,64,896]{2,1,0:T(8,128)(2,1)S(1)}, bf16[3,64,896]{2,1,0:T(8,128)(2,1)S(1)}, u32[]{:S(2)}, u32[]{:S(2)}) collective-permute-start(bf16[3,64,896]{2,1,0:T(8,128)(2,1)S(1)} %get-tuple-element.31), channel_id=1, source_target_pairs={{0,32},{32,0},{64,96},{96,64},{128,160},{160,128},{192,224},{224,1... | collective-permute-start | bytes 1032200 | tf_op jit(solution)/shard_map/ppermute | solution.py:133
  47.6 3.3 %collective-permute-start.6 = (bf16[3,64,896]{2,1,0:T(8,128)(2,1)S(1)}, bf16[3,64,896]{2,1,0:T(8,128)(2,1)}, u32[]{:S(2)}, u32[]{:S(2)}) collective-permute-start(bf16[3,64,896]{2,1,0:T(8,128)(2,1)S(1)} %get-tuple-element.32), channel_id=1, source_target_pairs={{0,480},{32,64},{64,32},{96,128},{128,96},{160,192},{192,160},{224... | collective-permute-start | bytes 1032200 | tf_op jit(solution)/shard_map/ppermute | solution.py:133
  50.9 0.0 collective-permute-done.2
  50.9 0.0 collective-permute-done.3
  50.9 0.7 fusion.12
  51.6 0.0 collective-permute-done.4
  51.6 0.7 fusion.4
  52.3 4.8 %collective-permute-start.7 = (bf16[64,896]{1,0:T(8,128)(2,1)}, bf16[64,896]{1,0:T(8,128)(2,1)S(1)}, u32[]{:S(2)}, u32[]{:S(2)}) collective-permute-start(bf16[64,896]{1,0:T(8,128)(2,1)} %fusion.12), channel_id=1, source_target_pairs={{0,96},{32,448},{64,160},{96,0},{128,224},{160,64},{192,288},{224,... | collective-permute-start | bytes 344072 | tf_op jit(solution)/shard_map/ppermute | solution.py:133
  57.1 2.8 %collective-permute-start.8 = (bf16[64,896]{1,0:T(8,128)(2,1)}, bf16[64,896]{1,0:T(8,128)(2,1)S(1)}, u32[]{:S(2)}, u32[]{:S(2)}) collective-permute-start(bf16[64,896]{1,0:T(8,128)(2,1)} %fusion.4), channel_id=1, source_target_pairs={{0,416},{32,128},{64,480},{96,192},{128,32},{160,256},{192,96},{22... | collective-permute-start | bytes 344072 | tf_op jit(solution)/shard_map/ppermute | solution.py:133
  60.0 0.4 fusion.10
  60.4 1.3 %fusion.1 = bf16[16,8,2048]{2,1,0:T(8,128)(2,1)} fusion(f32[128,2048]{1,0:T(8,128)S(1)} %fusion.10, bf16[2048,448]{0,1:T(8,128)(2,1)S(1)} %copy-done, bf16[128,896]{1,0:T(8,128)(2,1)S(1)} %get-tuple-element.29), kind=kOutput, calls=%fused_computation.2 | convolution fusion | flops 235405312 | bytes 3538944 | tf_op jit(solution)/shard_map/dot_general | solution.py:25
  61.7 6.3 %all-to-all-start.1 = ((bf16[16,8,2048]{2,1,0:T(8,128)(2,1)}), bf16[16,8,2048]{2,1,0:T(8,128)(2,1)S(1)}, u32[]{:S(2)}, u32[]{:S(2)}) async-start(bf16[16,8,2048]{2,1,0:T(8,128)(2,1)} %fusion.1), calls=%async_computation.1 | async-start | bytes 1048576 | tf_op jit(solution)/shard_map/all_to_all | solution.py:214
  68.1 0.0 collective-permute-done.7
  68.1 0.0 collective-permute-done.8
  68.1 0.0 collective-permute-done.5
  68.1 0.0 collective-permute-done.6
  68.1 1.1 %fusion.2 = (bf16[64,896]{1,0:T(8,128)(2,1)S(1)}, bf16[64,896]{1,0:T(8,128)(2,1)S(1)}) fusion(bf16[64,896]{1,0:T(8,128)(2,1)S(1)} %collective-permute-done.7, bf16[3,64,896]{2,1,0:T(8,128)(2,1)} %collective-permute-done.6, bf16[3,64,896]{2,1,0:T(8,128)(2,1)S(1)} %collective-permute-done.5, bf16[3,64,896]{2,1,0:T(8,128)(2,1)S(1)} %get-tuple-element.30, ...), kind=kLoop, calls=%fused_computation.5 | loop fusion | flops 917504 | bytes 1146880 | tf_op jit(solution)/shard_map/convert_element_type | solution.py:220
  69.2 5.7 %collective-permute-start.10 = (bf16[64,896]{1,0:T(8,128)(2,1)S(1)}, bf16[64,896]{1,0:T(8,128)(2,1)S(1)}, u32[]{:S(2)}, u32[]{:S(2)}) collective-permute-start(bf16[64,896]{1,0:T(8,128)(2,1)S(1)} %get-tuple-element.38), channel_id=1, source_target_pairs={{0,416},{32,128},{64,480},{96,192},{128,32},{160,256},{192,96},{22... | collective-permute-start | bytes 344072 | tf_op jit(solution)/shard_map/ppermute | solution.py:133
  74.9 3.5 %collective-permute-start.9 = (bf16[64,896]{1,0:T(8,128)(2,1)S(1)}, bf16[64,896]{1,0:T(8,128)(2,1)S(1)}, u32[]{:S(2)}, u32[]{:S(2)}) collective-permute-start(bf16[64,896]{1,0:T(8,128)(2,1)S(1)} %get-tuple-element.37), channel_id=1, source_target_pairs={{0,96},{32,448},{64,160},{96,0},{128,224},{160,64},{192,288},{224,... | collective-permute-start | bytes 344072 | tf_op jit(solution)/shard_map/ppermute | solution.py:133
  78.5 0.0 collective-permute-done.10
  78.5 9.7 %collective-permute-done.9 = bf16[64,896]{1,0:T(8,128)(2,1)S(1)} collective-permute-done((bf16[64,896]{1,0:T(8,128)(2,1)S(1)}, bf16[64,896]{1,0:T(8,128)(2,1)S(1)}, u32[]{:S(2)}, u32[]{:S(2)}) %collective-permute-start.9) | collective-permute-done | bytes 114720 | tf_op jit(solution)/shard_map/ppermute | solution.py:133
  88.2 1.7 %fusion.6 = (bf16[64,448]{1,0:T(8,128)(2,1)}, bf16[64,448]{1,0:T(8,128)(2,1)}) fusion(bf16[64,896]{1,0:T(8,128)(2,1)S(1)} %collective-permute-done.10, bf16[64,896]{1,0:T(8,128)(2,1)S(1)} %collective-permute-done.9, bf16[3,64,896]{2,1,0:T(8,128)(2,1)} %collective-permute-done.6, bf16[3,64,896]{2,1,0:T(8,128)(2,1)S(1)} %collective-permute-done.5, ...), kind=kLoop, calls=%fused_computation.13 | loop fusion | flops 573440 | bytes 688128 | tf_op jit(solution)/shard_map/convert_element_type | solution.py:236
  89.9 0.0 all-to-all-done.1
  89.9 0.1 convert_reduce_fusion
  90.0 0.2 fusion.15
  90.2 0.7 fusion.18
  (2 shorter events, 0.0 us)
Async XLA Ops:
  0.6 23.8 %copy-start.2 = (f32[2048]{0:T(1024)S(1)}, f32[2048]{0:T(1024)}, u32[]{:S(2)}) copy-start(f32[2048]{0:T(1024)} %param.6) | copy-start | bytes 24580
  0.6 25.3 %copy-start = (bf16[2048,448]{0,1:T(8,128)(2,1)S(1)}, bf16[2048,448]{0,1:T(8,128)(2,1)}, u32[]{:S(2)}) copy-start(bf16[2048,448]{0,1:T(8,128)(2,1)} %param.8) | copy-start | bytes 5505028
  2.4 19.3 %all-to-all-start = ((bf16[16,8,2048]{2,1,0:T(8,128)(2,1)}), bf16[16,8,2048]{2,1,0:T(8,128)(2,1)S(1)}, u32[]{:S(2)}, u32[]{:S(2)}) async-start(bf16[16,8,2048]{2,1,0:T(8,128)(2,1)} %broadcast_in_dim.2), calls=%async_computation | async-start | bytes 1048576 | tf_op jit(solution)/shard_map/all_to_all | solution.py:146
  10.3 11.4 %collective-permute-start = (bf16[128,448]{1,0:T(8,128)(2,1)S(1)}, bf16[128,448]{1,0:T(8,128)(2,1)S(1)}, u32[]{:S(2)}, u32[]{:S(2)}) collective-permute-start(bf16[128,448]{1,0:T(8,128)(2,1)S(1)} %copy.8.own_ref), channel_id=1, source_target_pairs={{0,16},{16,0},{1,17},{17,1},{2,18},{18,2},{3,19},{19,3},{4,20},{20... | collective-permute-start | bytes 344072 | tf_op jit(solution)/shard_map/ppermute | solution.py:143
  21.7 4.2 %collective-permute-start.1 = (bf16[128,2048]{1,0:T(8,128)(2,1)S(1)}, bf16[128,2048]{1,0:T(8,128)(2,1)S(1)}, u32[]{:S(2)}, u32[]{:S(2)}) collective-permute-start(bf16[128,2048]{1,0:T(8,128)(2,1)S(1)} %bitcast.34), channel_id=1, source_target_pairs={{0,1},{1,0},{2,3},{3,2},{4,5},{5,4},{6,7},{7,6},{8,9},{9,8},{10,11... | collective-permute-start | bytes 1572872 | tf_op jit(solution)/shard_map/ppermute | solution.py:149
  25.9 1.5 %copy-start.1 = (bf16[2048,448]{0,1:T(8,128)(2,1)S(1)}, bf16[2048,448]{0,1:T(8,128)(2,1)}, u32[]{:S(2)}) copy-start(bf16[2048,448]{0,1:T(8,128)(2,1)} %param.7) | copy-start | bytes 5505028
  27.4 8.5 %copy-start.3 = (bf16[8,2048]{1,0:T(8,128)(2,1)S(1)}, bf16[8,2048]{1,0:T(8,128)(2,1)}, u32[]{:S(2)}) copy-start(bf16[8,2048]{1,0:T(8,128)(2,1)} %param.5) | copy-start | bytes 98308
  30.5 20.5 %collective-permute-start.2 = (bf16[2,64,896]{2,1,0:T(8,128)(2,1)S(1)}, bf16[2,64,896]{2,1,0:T(8,128)(2,1)S(1)}, u32[]{:S(2)}, u32[]{:S(2)}) collective-permute-start(bf16[2,64,896]{2,1,0:T(8,128)(2,1)S(1)} %get-tuple-element.25), channel_id=1, source_target_pairs={{0,32},{32,0},{64,96},{96,64},{128,160},{160,128},{192,224},{224,1... | collective-permute-start | bytes 688136 | tf_op jit(solution)/shard_map/ppermute | solution.py:133
  34.0 16.9 %collective-permute-start.3 = (bf16[2,64,896]{2,1,0:T(8,128)(2,1)S(1)}, bf16[2,64,896]{2,1,0:T(8,128)(2,1)S(1)}, u32[]{:S(2)}, u32[]{:S(2)}) collective-permute-start(bf16[2,64,896]{2,1,0:T(8,128)(2,1)S(1)} %get-tuple-element.26), channel_id=1, source_target_pairs={{0,480},{32,64},{64,32},{96,128},{128,96},{160,192},{192,160},{224... | collective-permute-start | bytes 688136 | tf_op jit(solution)/shard_map/ppermute | solution.py:133
  36.1 15.6 %collective-permute-start.4 = (bf16[64,896]{1,0:T(8,128)(2,1)S(1)}, bf16[64,896]{1,0:T(8,128)(2,1)S(1)}, u32[]{:S(2)}, u32[]{:S(2)}) collective-permute-start(bf16[64,896]{1,0:T(8,128)(2,1)S(1)} %get-tuple-element.27), channel_id=1, source_target_pairs={{0,448},{32,96},{64,0},{96,160},{128,64},{160,224},{192,128},{224,... | collective-permute-start | bytes 344072 | tf_op jit(solution)/shard_map/ppermute | solution.py:133
  45.6 22.4 %collective-permute-start.5 = (bf16[3,64,896]{2,1,0:T(8,128)(2,1)S(1)}, bf16[3,64,896]{2,1,0:T(8,128)(2,1)S(1)}, u32[]{:S(2)}, u32[]{:S(2)}) collective-permute-start(bf16[3,64,896]{2,1,0:T(8,128)(2,1)S(1)} %get-tuple-element.31), channel_id=1, source_target_pairs={{0,32},{32,0},{64,96},{96,64},{128,160},{160,128},{192,224},{224,1... | collective-permute-start | bytes 1032200 | tf_op jit(solution)/shard_map/ppermute | solution.py:133
  47.6 20.5 %collective-permute-start.6 = (bf16[3,64,896]{2,1,0:T(8,128)(2,1)S(1)}, bf16[3,64,896]{2,1,0:T(8,128)(2,1)}, u32[]{:S(2)}, u32[]{:S(2)}) collective-permute-start(bf16[3,64,896]{2,1,0:T(8,128)(2,1)S(1)} %get-tuple-element.32), channel_id=1, source_target_pairs={{0,480},{32,64},{64,32},{96,128},{128,96},{160,192},{192,160},{224... | collective-permute-start | bytes 1032200 | tf_op jit(solution)/shard_map/ppermute | solution.py:133
  52.3 15.7 %collective-permute-start.7 = (bf16[64,896]{1,0:T(8,128)(2,1)}, bf16[64,896]{1,0:T(8,128)(2,1)S(1)}, u32[]{:S(2)}, u32[]{:S(2)}) collective-permute-start(bf16[64,896]{1,0:T(8,128)(2,1)} %fusion.12), channel_id=1, source_target_pairs={{0,96},{32,448},{64,160},{96,0},{128,224},{160,64},{192,288},{224,... | collective-permute-start | bytes 344072 | tf_op jit(solution)/shard_map/ppermute | solution.py:133
  57.1 11.0 %collective-permute-start.8 = (bf16[64,896]{1,0:T(8,128)(2,1)}, bf16[64,896]{1,0:T(8,128)(2,1)S(1)}, u32[]{:S(2)}, u32[]{:S(2)}) collective-permute-start(bf16[64,896]{1,0:T(8,128)(2,1)} %fusion.4), channel_id=1, source_target_pairs={{0,416},{32,128},{64,480},{96,192},{128,32},{160,256},{192,96},{22... | collective-permute-start | bytes 344072 | tf_op jit(solution)/shard_map/ppermute | solution.py:133
  61.7 28.2 %all-to-all-start.1 = ((bf16[16,8,2048]{2,1,0:T(8,128)(2,1)}), bf16[16,8,2048]{2,1,0:T(8,128)(2,1)S(1)}, u32[]{:S(2)}, u32[]{:S(2)}) async-start(bf16[16,8,2048]{2,1,0:T(8,128)(2,1)} %fusion.1), calls=%async_computation.1 | async-start | bytes 1048576 | tf_op jit(solution)/shard_map/all_to_all | solution.py:214
  69.2 9.3 %collective-permute-start.10 = (bf16[64,896]{1,0:T(8,128)(2,1)S(1)}, bf16[64,896]{1,0:T(8,128)(2,1)S(1)}, u32[]{:S(2)}, u32[]{:S(2)}) collective-permute-start(bf16[64,896]{1,0:T(8,128)(2,1)S(1)} %get-tuple-element.38), channel_id=1, source_target_pairs={{0,416},{32,128},{64,480},{96,192},{128,32},{160,256},{192,96},{22... | collective-permute-start | bytes 344072 | tf_op jit(solution)/shard_map/ppermute | solution.py:133
  74.9 13.3 %collective-permute-start.9 = (bf16[64,896]{1,0:T(8,128)(2,1)S(1)}, bf16[64,896]{1,0:T(8,128)(2,1)S(1)}, u32[]{:S(2)}, u32[]{:S(2)}) collective-permute-start(bf16[64,896]{1,0:T(8,128)(2,1)S(1)} %get-tuple-element.37), channel_id=1, source_target_pairs={{0,96},{32,448},{64,160},{96,0},{128,224},{160,64},{192,288},{224,... | collective-permute-start | bytes 344072 | tf_op jit(solution)/shard_map/ppermute | solution.py:133

commit v10 on v9

--- a/solution.py
+++ b/solution.py
@@ -31,6 +31,21 @@
     return lax.dot_general(
         left, right, (((0,), (0,)), ((), ())), preferred_element_type=jnp.float32
     )
+
+
+def blocks_of(factor, nz, depth, normed_ref, grads_ref):
+    z = lax.axis_index("z")
+    first = lax.axis_index("yh") == 0
+    sign = 1 - 2 * lax.rem(z, 2)
+    grads = grads_ref[...]
+
+    def block(relative):
+        chunk = lax.rem(z - sign * relative + 2 * nz, nz)
+        lanes = pl.ds(pl.multiple_of(chunk * 2 * depth, 2 * depth), 2 * depth)
+        both = contract_first(normed_ref[:, lanes], grads) * factor
+        return jnp.where(first, both[:depth], both[depth:]).astype(jnp.bfloat16)
+
+    return block
 
 
 def local_kernel(
@@ -47,15 +62,10 @@
     far_ref,
     outer_ahead_ref,
     outer_behind_ref,
-    inner_ahead_ref,
-    inner_behind_ref,
-    outer_hub_ref,
-    inner_hub_ref,
     grads_own_ref,
     normed_ref,
     grads_ref,
 ):
-    z = lax.axis_index("z")
     half = lax.axis_index("yh")
     rows, width = own_ref.shape
     tokens = same_ref.shape[0]
@@ -100,21 +110,24 @@
 
     grads_own_ref[:, :width] = own_rows(gate_grad)
     grads_own_ref[:, width:] = own_rows(up_grad)
-    grads = grads_ref[...]
-    depth = far_ref.shape[0]
-
-    sign = 1 - 2 * lax.rem(z, 2)
-
-    def block(relative):
-        chunk = lax.rem(z - sign * relative + 2 * nz, nz)
-        lanes = pl.ds(pl.multiple_of(chunk * 2 * depth, 2 * depth), 2 * depth)
-        both = contract_first(normed_ref[:, lanes], grads) * factor
-        return jnp.where(first, both[:depth], both[depth:]).astype(jnp.bfloat16)
-
+    block = blocks_of(factor, nz, far_ref.shape[0], normed_ref, grads_ref)
     far_ref[...] = block(nz // 2)
     for at, hub in enumerate(OUTER):
         outer_ahead_ref[at] = block(-hub - 1)
         outer_behind_ref[at] = block(-hub + 1)
+
+
+def rest_kernel(
+    factor,
+    nz,
+    normed_ref,
+    grads_ref,
+    inner_ahead_ref,
+    inner_behind_ref,
+    outer_hub_ref,
+    inner_hub_ref,
+):
+    block = blocks_of(factor, nz, outer_hub_ref.shape[1], normed_ref, grads_ref)
     for at, hub in enumerate(INNER):
         inner_ahead_ref[at] = block(-hub - 1)
         inner_behind_ref[at] = block(-hub + 1)
@@ -122,6 +135,54 @@
         outer_hub_ref[at] = block(hub)
     for at, hub in enumerate(INNER):
         inner_hub_ref[at] = block(hub)
+
+
+def f32_sum(*values):
+    total = values[0].astype(jnp.float32)
+    for value in values[1:]:
+        total = total + value.astype(jnp.float32)
+    return total
+
+
+def outer_kernel(hub_ref, ahead_ref, behind_ref, far_ref, plus_ref, minus_ref):
+    plus_ref[...] = f32_sum(hub_ref[0], ahead_ref[0], behind_ref[0]).astype(jnp.bfloat16)
+    minus_ref[...] = f32_sum(hub_ref[1], ahead_ref[1], behind_ref[1], far_ref[...]).astype(
+        jnp.bfloat16
+    )
+
+
+def inner_kernel(hub_ref, ahead_ref, behind_ref, upper_ref, lower_ref, plus_ref, minus_ref):
+    plus_ref[...] = f32_sum(hub_ref[0], ahead_ref[0], behind_ref[0], lower_ref[...]).astype(
+        jnp.bfloat16
+    )
+    minus_ref[...] = f32_sum(hub_ref[2], ahead_ref[2], behind_ref[2], upper_ref[...]).astype(
+        jnp.bfloat16
+    )
+
+
+def total_kernel(hub_ref, ahead_ref, behind_ref, plus_ref, minus_ref, gate_ref, up_ref):
+    width = gate_ref.shape[1]
+    total = f32_sum(hub_ref[1], ahead_ref[1], behind_ref[1], plus_ref[...], minus_ref[...])
+    gate_ref[...] = total[:, :width].astype(jnp.bfloat16)
+    up_ref[...] = total[:, width:].astype(jnp.bfloat16)
+
+
+def tail_kernel(rows_ref, gain_ref, moved_ref, out_ref):
+    scaled, inverse = normalize(rows_ref[...])
+    weighted = jnp.sum(moved_ref[...].astype(jnp.float32), axis=0) * gain_ref[...]
+    mean = jnp.mean(weighted * scaled, axis=-1, keepdims=True)
+    out_ref[...] = ((weighted - scaled * mean) * inverse).astype(jnp.bfloat16)
+
+
+def call(kernel, name, shapes, *values):
+    size = sum(value.size * 2 for value in values)
+    return pl.pallas_call(
+        kernel,
+        out_shape=[jax.ShapeDtypeStruct(shape, jnp.bfloat16) for shape in shapes],
+        compiler_params=pltpu.CompilerParams(vmem_limit_bytes=8 * 1024 * 1024),
+        cost_estimate=pl.CostEstimate(flops=size, bytes_accessed=size, transcendentals=0),
+        name=name,
+    )(*values)
 
 
 def norm_kernel(rows_ref, gain_ref, normed_ref):
@@ -159,30 +220,42 @@
     )(same, gain)
     factor = float(rows * nz * nh) ** (-0.5)
     shape = jax.ShapeDtypeStruct
-    far, outer_ahead, outer_behind, inner_ahead, inner_behind, outer_hub, inner_hub, grads_own = pl.pallas_call(
+    wide = 2 * width
+    far, outer_ahead, outer_behind, grads_own, normed, grads = pl.pallas_call(
         functools.partial(local_kernel, factor, nz, residual.shape[0]),
-        out_shape=(
-            shape((depth, 2 * width), bf16),
-            shape((len(OUTER), depth, 2 * width), bf16),
-            shape((len(OUTER), depth, 2 * width), bf16),
-            shape((len(INNER), depth, 2 * width), bf16),
-            shape((len(INNER), depth, 2 * width), bf16),
-            shape((len(OUTER), depth, 2 * width), bf16),
-            shape((len(INNER), depth, 2 * width), bf16),
-            shape((rows, 2 * width), bf16),
-        ),
-        scratch_shapes=[
-            pltpu.VMEM((nh * rows, features), bf16),
-            pltpu.VMEM((nh * rows, 2 * width), bf16),
+        out_shape=[
+            jax.ShapeDtypeStruct(shape, bf16)
+            for shape in (
+                (depth, wide),
+                (len(OUTER), depth, wide),
+                (len(OUTER), depth, wide),
+                (rows, wide),
+                (nh * rows, features),
+                (nh * rows, wide),
+            )
         ],
         compiler_params=pltpu.CompilerParams(vmem_limit_bytes=20 * 1024 * 1024),
         cost_estimate=pl.CostEstimate(
-            flops=8 * nh * rows * features * width,
+            flops=6 * nh * rows * features * width,
             bytes_accessed=8 * features * width,
             transcendentals=nh * rows * width,
         ),
         name="local",
     )(normed_same, swapped, gain, gate_weight.T, up_weight.T, own, other)
+    inner_ahead, inner_behind, outer_hub, inner_hub = pl.pallas_call(
+        functools.partial(rest_kernel, factor, nz),
+        out_shape=[
+            jax.ShapeDtypeStruct((count, depth, wide), bf16)
+            for count in (len(INNER), len(INNER), len(OUTER), len(INNER))
+        ],
+        compiler_params=pltpu.CompilerParams(vmem_limit_bytes=12 * 1024 * 1024),
+        cost_estimate=pl.CostEstimate(
+            flops=4 * nh * rows * features * width,
+            bytes_accessed=4 * nh * rows * features,
+            transcendentals=0,
+        ),
+        name="rest",
+    )(normed, grads)
 
     from_far = move(far, -2, nz).astype(f32)
     outer_ahead, outer_behind = move(outer_ahead, 1, nz), move(outer_behind, -1, nz)
@@ -228,14 +301,16 @@
     residual_grad = (
         (weighted - scaled * jnp.mean(weighted * scaled, axis=-1, keepdims=True)) * inverse
     ).astype(bf16)
-    totals = [
-        (
-            inner(1, columns)
-            + plus[:, columns].astype(f32)
-            + minus[:, columns].astype(f32)
-        ).astype(bf16)
-        for columns in (slice(0, width), slice(width, None))
-    ]
+    totals = call(
+        total_kernel,
+        "total",
+        [(depth, width)] * 2,
+        inner_hub,
+        inner_ahead,
+        inner_behind,
+        plus,
+        minus,
+    )
     return (residual_grad, totals[0], totals[1])
 
 

time: 91.7 us -> 89.5 us (0.976)
  the two profiles are of different devices: /device:TPU:67 before, /device:TPU:1 now
where the time goes in v10:
time: 89.5 us; the launch traced here: 88.1 us
  starting transfers between devices  59.6 us (67%)
  waiting for transfers between devices  14.5 us (16%)
  Pallas kernels  4.51 us (5%)
  local copies, waits for them, and re-layouts  4.25 us (5%)
  other arithmetic  2.64 us (3%)
  matrix products  1.72 us (2%)
    ppermute x9, starting transfers between devices, move(): return lax.ppermute(value, 'z', pairs)  38.3 us
    all_to_all x1, starting transfers between devices, shards(): same = lax.all_to_all(copies, ('yh', 'x', 'yl'), 0, 0, tiled=True)  7.58 us
    ppermute x1, waiting for transfers between devices, shards(): other = lax.ppermute(own, 'yh', [(0, 1), (1, 0)])  7.39 us
    ppermute x9, waiting for transfers between devices, move(): return lax.ppermute(value, 'z', pairs)  5.86 us
    all_to_all x1, starting transfers between devices, shards(): moved = lax.all_to_all(blocks, TENSOR, 0, 0, tiled=True)  5.56 us
    ppermute x1, starting transfers between devices, shards(): other = lax.ppermute(own, 'yh', [(0, 1), (1, 0)])  4.78 us
    ppermute x1, starting transfers between devices, shards(): swapped = lax.ppermute(same, 'core', [(0, 1), (1, 0)])  3.31 us
    unnamed x9, local copies, waits for them, and re-layouts  2.52 us
  transfers between devices with their start and end apart: 13, of which 4 were waited for; matrix products, arithmetic and copies ran while one was open for 5% of the time, Pallas kernels for 3%

profile of v10, /device:TPU:1, one launch (start us, length us, event | category | flops | bytes accessed | tf_op | source)
XLA Modules:
  0.0 88.1 jit_solution(7829660406213690797)
XLA Ops:
  0.6 0.0 copy-start.2
  0.6 0.0 copy-start
  0.7 1.7 %broadcast_in_dim.2 = bf16[16,8,2048]{2,1,0:T(8,128)(2,1)} broadcast(bf16[8,2048]{1,0:T(8,128)(2,1)} %param.5), dimensions={1,2} | broadcast | bytes 557056 | tf_op jit(solution)/shard_map/broadcast_in_dim | solution.py:206
  2.4 7.6 %all-to-all-start = ((bf16[16,8,2048]{2,1,0:T(8,128)(2,1)}), bf16[16,8,2048]{2,1,0:T(8,128)(2,1)S(1)}, u32[]{:S(2)}, u32[]{:S(2)}) async-start(bf16[16,8,2048]{2,1,0:T(8,128)(2,1)} %broadcast_in_dim.2), calls=%async_computation | async-start | bytes 1048576 | tf_op jit(solution)/shard_map/all_to_all | solution.py:207
  10.0 1.0 %copy.8.own_ref = bf16[128,448]{1,0:T(8,128)(2,1)S(1)} copy(bf16[128,448]{0,1:T(8,128)(2,1)} %param.9) | data formatting | bytes 229376 | tf_op args[4]
  11.0 4.8 %collective-permute-start = (bf16[128,448]{1,0:T(8,128)(2,1)S(1)}, bf16[128,448]{1,0:T(8,128)(2,1)S(1)}, u32[]{:S(2)}, u32[]{:S(2)}) collective-permute-start(bf16[128,448]{1,0:T(8,128)(2,1)S(1)} %copy.8.own_ref), channel_id=1, source_target_pairs={{0,16},{16,0},{1,17},{17,1},{2,18},{18,2},{3,19},{19,3},{4,20},{20... | collective-permute-start | bytes 344072 | tf_op jit(solution)/shard_map/ppermute | solution.py:204
  15.8 7.4 %collective-permute-done.other_ref = bf16[128,448]{1,0:T(8,128)(2,1)S(1)} collective-permute-done((bf16[128,448]{1,0:T(8,128)(2,1)S(1)}, bf16[128,448]{1,0:T(8,128)(2,1)S(1)}, u32[]{:S(2)}, u32[]{:S(2)}) %collective-permute-start) | collective-permute-done | bytes 114720 | tf_op jit(solution)/shard_map/ppermute | solution.py:204
  23.2 0.0 all-to-all-done
  23.2 3.3 %collective-permute-start.1 = (bf16[128,2048]{1,0:T(8,128)(2,1)S(1)}, bf16[128,2048]{1,0:T(8,128)(2,1)S(1)}, u32[]{:S(2)}, u32[]{:S(2)}) collective-permute-start(bf16[128,2048]{1,0:T(8,128)(2,1)S(1)} %bitcast.22), channel_id=1, source_target_pairs={{0,1},{1,0},{2,3},{3,2},{4,5},{5,4},{6,7},{7,6},{8,9},{9,8},{10,11... | collective-permute-start | bytes 1572872 | tf_op jit(solution)/shard_map/ppermute | solution.py:210
  26.5 0.0 copy-done.2
  26.5 0.2 norm.1.same_ref
  26.7 1.3 %collective-permute-done.1.swapped_ref = bf16[128,2048]{1,0:T(8,128)(2,1)S(1)} collective-permute-done((bf16[128,2048]{1,0:T(8,128)(2,1)S(1)}, bf16[128,2048]{1,0:T(8,128)(2,1)S(1)}, u32[]{:S(2)}, u32[]{:S(2)}) %collective-permute-start.1) | collective-permute-done | bytes 524320 | tf_op jit(solution)/shard_map/ppermute | solution.py:210
  28.0 0.0 copy-done
  28.0 0.0 copy-start.1
  28.0 1.5 %copy-done.1 = bf16[2048,448]{0,1:T(8,128)(2,1)S(1)} copy-done((bf16[2048,448]{0,1:T(8,128)(2,1)S(1)}, bf16[2048,448]{0,1:T(8,128)(2,1)}, u32[]{:S(2)}) %copy-start.1) | copy-done | bytes 1835032
  29.5 2.2 %local.1 = (bf16[64,896]{1,0:T(8,128)(2,1)S(1)}, bf16[2,64,896]{2,1,0:T(8,128)(2,1)S(1)}, bf16[2,64,896]{2,1,0:T(8,128)(2,1)S(1)}, bf16[128,896]{1,0:T(8,128)(2,...) custom-call(bf16[128,2048]{1,0:T(8,128)(2,1)S(1)} %norm.1.same_ref, ...), custom_call_target="tpu_custom_call" | custom-call | flops 1409286144 | bytes 7340032 | tf_op jit(solution)/shard_map/local/pallas_call | solution.py:224
  31.7 3.1 %collective-permute-start.2 = (bf16[2,64,896]{2,1,0:T(8,128)(2,1)S(1)}, bf16[2,64,896]{2,1,0:T(8,128)(2,1)S(1)}, u32[]{:S(2)}, u32[]{:S(2)}) collective-permute-start(bf16[2,64,896]{2,1,0:T(8,128)(2,1)S(1)} %get-tuple-element.31), channel_id=1, source_target_pairs={{0,32},{32,0},{64,96},{96,64},{128,160},{160,128},{192,224},{224,1... | collective-permute-start | bytes 688136 | tf_op jit(solution)/shard_map/ppermute | solution.py:194
  34.8 10.2 %collective-permute-start.3 = (bf16[2,64,896]{2,1,0:T(8,128)(2,1)S(1)}, bf16[2,64,896]{2,1,0:T(8,128)(2,1)S(1)}, u32[]{:S(2)}, u32[]{:S(2)}) collective-permute-start(bf16[2,64,896]{2,1,0:T(8,128)(2,1)S(1)} %get-tuple-element.32), channel_id=1, source_target_pairs={{0,480},{32,64},{64,32},{96,128},{128,96},{160,192},{192,160},{224... | collective-permute-start | bytes 688136 | tf_op jit(solution)/shard_map/ppermute | solution.py:194
  45.0 3.1 %collective-permute-start.4 = (bf16[64,896]{1,0:T(8,128)(2,1)S(1)}, bf16[64,896]{1,0:T(8,128)(2,1)S(1)}, u32[]{:S(2)}, u32[]{:S(2)}) collective-permute-start(bf16[64,896]{1,0:T(8,128)(2,1)S(1)} %get-tuple-element.33), channel_id=1, source_target_pairs={{0,448},{32,96},{64,0},{96,160},{128,64},{160,224},{192,128},{224,... | collective-permute-start | bytes 344072 | tf_op jit(solution)/shard_map/ppermute | solution.py:194
  48.1 1.3 %rest.1 = (bf16[3,64,896]{2,1,0:T(8,128)(2,1)}, bf16[3,64,896]{2,1,0:T(8,128)(2,1)S(1)}, bf16[2,64,896]{2,1,0:T(8,128)(2,1)S(1)}, bf16[3,64,896]{2,1,0:T(8,128)(2,1)S(1)}) custom-call(bf16[256,2048]{1,0:T(8,128)(2,1)S(1)} %get-tuple-element.28.normed_ref, bf16[256,896]{1,0:T(8,128)(2,1)S(1)} %get-tuple-element.29.grads_ref), custom_call_target="tpu_custom_call" | custom-call | flops 939524096 | bytes 2097152 | tf_op jit(solution)/shard_map/rest/pallas_call | solution.py:245
  49.4 1.9 %collective-permute-start.5 = (bf16[3,64,896]{2,1,0:T(8,128)(2,1)}, bf16[3,64,896]{2,1,0:T(8,128)(2,1)S(1)}, u32[]{:S(2)}, u32[]{:S(2)}) collective-permute-start(bf16[3,64,896]{2,1,0:T(8,128)(2,1)} %get-tuple-element.37), channel_id=1, source_target_pairs={{0,32},{32,0},{64,96},{96,64},{128,160},{160,128},{192,224},{224,1... | collective-permute-start | bytes 1032200 | tf_op jit(solution)/shard_map/ppermute | solution.py:194
  51.3 4.6 %collective-permute-start.6 = (bf16[3,64,896]{2,1,0:T(8,128)(2,1)S(1)}, bf16[3,64,896]{2,1,0:T(8,128)(2,1)S(1)}, u32[]{:S(2)}, u32[]{:S(2)}) collective-permute-start(bf16[3,64,896]{2,1,0:T(8,128)(2,1)S(1)} %get-tuple-element.38), channel_id=1, source_target_pairs={{0,480},{32,64},{64,32},{96,128},{128,96},{160,192},{192,160},{224... | collective-permute-start | bytes 1032200 | tf_op jit(solution)/shard_map/ppermute | solution.py:194
  55.9 0.0 collective-permute-done.2
  55.9 0.0 collective-permute-done.3
  55.9 0.7 fusion.8
  56.6 0.0 collective-permute-done.4
  56.6 0.7 fusion.4
  57.3 3.5 %collective-permute-start.7 = (bf16[64,896]{1,0:T(8,128)(2,1)}, bf16[64,896]{1,0:T(8,128)(2,1)S(1)}, u32[]{:S(2)}, u32[]{:S(2)}) collective-permute-start(bf16[64,896]{1,0:T(8,128)(2,1)} %fusion.8), channel_id=1, source_target_pairs={{0,96},{32,448},{64,160},{96,0},{128,224},{160,64},{192,288},{224,... | collective-permute-start | bytes 344072 | tf_op jit(solution)/shard_map/ppermute | solution.py:194
  60.9 3.0 %collective-permute-start.8 = (bf16[64,896]{1,0:T(8,128)(2,1)}, bf16[64,896]{1,0:T(8,128)(2,1)S(1)}, u32[]{:S(2)}, u32[]{:S(2)}) collective-permute-start(bf16[64,896]{1,0:T(8,128)(2,1)} %fusion.4), channel_id=1, source_target_pairs={{0,416},{32,128},{64,480},{96,192},{128,32},{160,256},{192,96},{22... | collective-permute-start | bytes 344072 | tf_op jit(solution)/shard_map/ppermute | solution.py:194
  63.8 0.4 fusion.6
  64.3 0.0 copy-start.3
  64.3 1.3 %fusion.1 = bf16[16,8,2048]{2,1,0:T(8,128)(2,1)} fusion(f32[128,2048]{1,0:T(8,128)S(1)} %fusion.6, bf16[2048,448]{0,1:T(8,128)(2,1)S(1)} %copy-done, bf16[128,896]{1,0:T(8,128)(2,1)S(1)} %get-tuple-element.35), kind=kOutput, calls=%fused_computation.2 | convolution fusion | flops 235405312 | bytes 3538944 | tf_op jit(solution)/shard_map/dot_general | solution.py:25
  65.6 5.6 %all-to-all-start.1 = ((bf16[16,8,2048]{2,1,0:T(8,128)(2,1)}), bf16[16,8,2048]{2,1,0:T(8,128)(2,1)S(1)}, u32[]{:S(2)}, u32[]{:S(2)}) async-start(bf16[16,8,2048]{2,1,0:T(8,128)(2,1)} %fusion.1), calls=%async_computation.1 | async-start | bytes 1048576 | tf_op jit(solution)/shard_map/all_to_all | solution.py:287
  71.1 0.0 copy-done.3
  71.1 0.1 fusion.15
  71.3 0.0 collective-permute-done.7
  71.3 0.0 collective-permute-done.8
  71.3 0.0 collective-permute-done.5.ahead_ref
  71.3 0.0 collective-permute-done.6.behind_ref
  71.3 0.1 fusion.2
  71.4 6.4 %collective-permute-start.10 = (bf16[64,896]{1,0:T(8,128)(2,1)S(1)}, bf16[64,896]{1,0:T(8,128)(2,1)S(1)}, u32[]{:S(2)}, u32[]{:S(2)}) collective-permute-start(bf16[64,896]{1,0:T(8,128)(2,1)S(1)} %get-tuple-element.44), channel_id=1, source_target_pairs={{0,416},{32,128},{64,480},{96,192},{128,32},{160,256},{192,96},{22... | collective-permute-start | bytes 344072 | tf_op jit(solution)/shard_map/ppermute | solution.py:194
  77.8 2.7 %collective-permute-start.9 = (bf16[64,896]{1,0:T(8,128)(2,1)S(1)}, bf16[64,896]{1,0:T(8,128)(2,1)S(1)}, u32[]{:S(2)}, u32[]{:S(2)}) collective-permute-start(bf16[64,896]{1,0:T(8,128)(2,1)S(1)} %get-tuple-element.43), channel_id=1, source_target_pairs={{0,96},{32,448},{64,160},{96,0},{128,224},{160,64},{192,288},{224,... | collective-permute-start | bytes 344072 | tf_op jit(solution)/shard_map/ppermute | solution.py:194
  80.5 4.2 %collective-permute-done.10.minus_ref = bf16[64,896]{1,0:T(8,128)(2,1)S(1)} collective-permute-done((bf16[64,896]{1,0:T(8,128)(2,1)S(1)}, bf16[64,896]{1,0:T(8,128)(2,1)S(1)}, u32[]{:S(2)}, u32[]{:S(2)}) %collective-permute-start.10) | collective-permute-done | bytes 114720 | tf_op jit(solution)/shard_map/ppermute | solution.py:194
  84.6 1.7 %collective-permute-done.9.plus_ref = bf16[64,896]{1,0:T(8,128)(2,1)S(1)} collective-permute-done((bf16[64,896]{1,0:T(8,128)(2,1)S(1)}, bf16[64,896]{1,0:T(8,128)(2,1)S(1)}, u32[]{:S(2)}, u32[]{:S(2)}) %collective-permute-start.9) | collective-permute-done | bytes 114720 | tf_op jit(solution)/shard_map/ppermute | solution.py:194
  86.3 0.8 total.1
  87.1 0.0 all-to-all-done.1
  87.1 0.1 convert_reduce_fusion
  87.1 0.2 fusion.11
  87.4 0.7 fusion.14
  (2 shorter events, 0.0 us)
Async XLA Ops:
  0.6 25.9 %copy-start.2 = (f32[2048]{0:T(1024)S(1)}, f32[2048]{0:T(1024)}, u32[]{:S(2)}) copy-start(f32[2048]{0:T(1024)} %param.6) | copy-start | bytes 24580
  0.6 27.4 %copy-start = (bf16[2048,448]{0,1:T(8,128)(2,1)S(1)}, bf16[2048,448]{0,1:T(8,128)(2,1)}, u32[]{:S(2)}) copy-start(bf16[2048,448]{0,1:T(8,128)(2,1)} %param.8) | copy-start | bytes 5505028
  2.4 20.8 %all-to-all-start = ((bf16[16,8,2048]{2,1,0:T(8,128)(2,1)}), bf16[16,8,2048]{2,1,0:T(8,128)(2,1)S(1)}, u32[]{:S(2)}, u32[]{:S(2)}) async-start(bf16[16,8,2048]{2,1,0:T(8,128)(2,1)} %broadcast_in_dim.2), calls=%async_computation | async-start | bytes 1048576 | tf_op jit(solution)/shard_map/all_to_all | solution.py:207
  11.0 12.2 %collective-permute-start = (bf16[128,448]{1,0:T(8,128)(2,1)S(1)}, bf16[128,448]{1,0:T(8,128)(2,1)S(1)}, u32[]{:S(2)}, u32[]{:S(2)}) collective-permute-start(bf16[128,448]{1,0:T(8,128)(2,1)S(1)} %copy.8.own_ref), channel_id=1, source_target_pairs={{0,16},{16,0},{1,17},{17,1},{2,18},{18,2},{3,19},{19,3},{4,20},{20... | collective-permute-start | bytes 344072 | tf_op jit(solution)/shard_map/ppermute | solution.py:204
  23.2 4.8 %collective-permute-start.1 = (bf16[128,2048]{1,0:T(8,128)(2,1)S(1)}, bf16[128,2048]{1,0:T(8,128)(2,1)S(1)}, u32[]{:S(2)}, u32[]{:S(2)}) collective-permute-start(bf16[128,2048]{1,0:T(8,128)(2,1)S(1)} %bitcast.22), channel_id=1, source_target_pairs={{0,1},{1,0},{2,3},{3,2},{4,5},{5,4},{6,7},{7,6},{8,9},{9,8},{10,11... | collective-permute-start | bytes 1572872 | tf_op jit(solution)/shard_map/ppermute | solution.py:210
  28.0 1.5 %copy-start.1 = (bf16[2048,448]{0,1:T(8,128)(2,1)S(1)}, bf16[2048,448]{0,1:T(8,128)(2,1)}, u32[]{:S(2)}) copy-start(bf16[2048,448]{0,1:T(8,128)(2,1)} %param.7) | copy-start | bytes 5505028
  31.7 24.2 %collective-permute-start.2 = (bf16[2,64,896]{2,1,0:T(8,128)(2,1)S(1)}, bf16[2,64,896]{2,1,0:T(8,128)(2,1)S(1)}, u32[]{:S(2)}, u32[]{:S(2)}) collective-permute-start(bf16[2,64,896]{2,1,0:T(8,128)(2,1)S(1)} %get-tuple-element.31), channel_id=1, source_target_pairs={{0,32},{32,0},{64,96},{96,64},{128,160},{160,128},{192,224},{224,1... | collective-permute-start | bytes 688136 | tf_op jit(solution)/shard_map/ppermute | solution.py:194
  34.8 21.1 %collective-permute-start.3 = (bf16[2,64,896]{2,1,0:T(8,128)(2,1)S(1)}, bf16[2,64,896]{2,1,0:T(8,128)(2,1)S(1)}, u32[]{:S(2)}, u32[]{:S(2)}) collective-permute-start(bf16[2,64,896]{2,1,0:T(8,128)(2,1)S(1)} %get-tuple-element.32), channel_id=1, source_target_pairs={{0,480},{32,64},{64,32},{96,128},{128,96},{160,192},{192,160},{224... | collective-permute-start | bytes 688136 | tf_op jit(solution)/shard_map/ppermute | solution.py:194
  45.0 11.6 %collective-permute-start.4 = (bf16[64,896]{1,0:T(8,128)(2,1)S(1)}, bf16[64,896]{1,0:T(8,128)(2,1)S(1)}, u32[]{:S(2)}, u32[]{:S(2)}) collective-permute-start(bf16[64,896]{1,0:T(8,128)(2,1)S(1)} %get-tuple-element.33), channel_id=1, source_target_pairs={{0,448},{32,96},{64,0},{96,160},{128,64},{160,224},{192,128},{224,... | collective-permute-start | bytes 344072 | tf_op jit(solution)/shard_map/ppermute | solution.py:194
  49.4 21.9 %collective-permute-start.5 = (bf16[3,64,896]{2,1,0:T(8,128)(2,1)}, bf16[3,64,896]{2,1,0:T(8,128)(2,1)S(1)}, u32[]{:S(2)}, u32[]{:S(2)}) collective-permute-start(bf16[3,64,896]{2,1,0:T(8,128)(2,1)} %get-tuple-element.37), channel_id=1, source_target_pairs={{0,32},{32,0},{64,96},{96,64},{128,160},{160,128},{192,224},{224,1... | collective-permute-start | bytes 1032200 | tf_op jit(solution)/shard_map/ppermute | solution.py:194
  51.3 20.0 %collective-permute-start.6 = (bf16[3,64,896]{2,1,0:T(8,128)(2,1)S(1)}, bf16[3,64,896]{2,1,0:T(8,128)(2,1)S(1)}, u32[]{:S(2)}, u32[]{:S(2)}) collective-permute-start(bf16[3,64,896]{2,1,0:T(8,128)(2,1)S(1)} %get-tuple-element.38), channel_id=1, source_target_pairs={{0,480},{32,64},{64,32},{96,128},{128,96},{160,192},{192,160},{224... | collective-permute-start | bytes 1032200 | tf_op jit(solution)/shard_map/ppermute | solution.py:194
  57.3 13.9 %collective-permute-start.7 = (bf16[64,896]{1,0:T(8,128)(2,1)}, bf16[64,896]{1,0:T(8,128)(2,1)S(1)}, u32[]{:S(2)}, u32[]{:S(2)}) collective-permute-start(bf16[64,896]{1,0:T(8,128)(2,1)} %fusion.8), channel_id=1, source_target_pairs={{0,96},{32,448},{64,160},{96,0},{128,224},{160,64},{192,288},{224,... | collective-permute-start | bytes 344072 | tf_op jit(solution)/shard_map/ppermute | solution.py:194
  60.9 10.4 %collective-permute-start.8 = (bf16[64,896]{1,0:T(8,128)(2,1)}, bf16[64,896]{1,0:T(8,128)(2,1)S(1)}, u32[]{:S(2)}, u32[]{:S(2)}) collective-permute-start(bf16[64,896]{1,0:T(8,128)(2,1)} %fusion.4), channel_id=1, source_target_pairs={{0,416},{32,128},{64,480},{96,192},{128,32},{160,256},{192,96},{22... | collective-permute-start | bytes 344072 | tf_op jit(solution)/shard_map/ppermute | solution.py:194
  64.3 6.9 %copy-start.3 = (bf16[8,2048]{1,0:T(8,128)(2,1)S(1)}, bf16[8,2048]{1,0:T(8,128)(2,1)}, u32[]{:S(2)}) copy-start(bf16[8,2048]{1,0:T(8,128)(2,1)} %param.5) | copy-start | bytes 98308
  65.6 21.5 %all-to-all-start.1 = ((bf16[16,8,2048]{2,1,0:T(8,128)(2,1)}), bf16[16,8,2048]{2,1,0:T(8,128)(2,1)S(1)}, u32[]{:S(2)}, u32[]{:S(2)}) async-start(bf16[16,8,2048]{2,1,0:T(8,128)(2,1)} %fusion.1), calls=%async_computation.1 | async-start | bytes 1048576 | tf_op jit(solution)/shard_map/all_to_all | solution.py:287
  71.4 13.2 %collective-permute-start.10 = (bf16[64,896]{1,0:T(8,128)(2,1)S(1)}, bf16[64,896]{1,0:T(8,128)(2,1)S(1)}, u32[]{:S(2)}, u32[]{:S(2)}) collective-permute-start(bf16[64,896]{1,0:T(8,128)(2,1)S(1)} %get-tuple-element.44), channel_id=1, source_target_pairs={{0,416},{32,128},{64,480},{96,192},{128,32},{160,256},{192,96},{22... | collective-permute-start | bytes 344072 | tf_op jit(solution)/shard_map/ppermute | solution.py:194
  77.8 8.5 %collective-permute-start.9 = (bf16[64,896]{1,0:T(8,128)(2,1)S(1)}, bf16[64,896]{1,0:T(8,128)(2,1)S(1)}, u32[]{:S(2)}, u32[]{:S(2)}) collective-permute-start(bf16[64,896]{1,0:T(8,128)(2,1)S(1)} %get-tuple-element.43), channel_id=1, source_target_pairs={{0,96},{32,448},{64,160},{96,0},{128,224},{160,64},{192,288},{224,... | collective-permute-start | bytes 344072 | tf_op jit(solution)/shard_map/ppermute | solution.py:194

commit v11 on v10

--- a/solution.py
+++ b/solution.py
@@ -122,11 +122,16 @@
     nz,
     normed_ref,
     grads_ref,
+    grads_own_ref,
+    gate_ref,
+    up_ref,
     inner_ahead_ref,
     inner_behind_ref,
     outer_hub_ref,
     inner_hub_ref,
+    part_ref,
 ):
+    width = gate_ref.shape[0]
     block = blocks_of(factor, nz, outer_hub_ref.shape[1], normed_ref, grads_ref)
     for at, hub in enumerate(INNER):
         inner_ahead_ref[at] = block(-hub - 1)
@@ -135,6 +140,10 @@
         outer_hub_ref[at] = block(hub)
     for at, hub in enumerate(INNER):
         inner_hub_ref[at] = block(hub)
+    f32 = jnp.float32
+    gate_part = jnp.dot(grads_own_ref[:, :width], gate_ref[...], preferred_element_type=f32)
+    up_part = jnp.dot(grads_own_ref[:, width:], up_ref[...], preferred_element_type=f32)
+    part_ref[...] = (gate_part + up_part).astype(jnp.bfloat16)
 
 
 def f32_sum(*values):
@@ -242,22 +251,23 @@
         ),
         name="local",
     )(normed_same, swapped, gain, gate_weight.T, up_weight.T, own, other)
-    inner_ahead, inner_behind, outer_hub, inner_hub = pl.pallas_call(
+    inner_ahead, inner_behind, outer_hub, inner_hub, part = pl.pallas_call(
         functools.partial(rest_kernel, factor, nz),
         out_shape=[
             jax.ShapeDtypeStruct((count, depth, wide), bf16)
             for count in (len(INNER), len(INNER), len(OUTER), len(INNER))
-        ],
-        compiler_params=pltpu.CompilerParams(vmem_limit_bytes=12 * 1024 * 1024),
+        ]
+        + [jax.ShapeDtypeStruct((rows, features), bf16)],
+        compiler_params=pltpu.CompilerParams(vmem_limit_bytes=16 * 1024 * 1024),
         cost_estimate=pl.CostEstimate(
-            flops=4 * nh * rows * features * width,
-            bytes_accessed=4 * nh * rows * features,
+            flops=6 * nh * rows * features * width,
+            bytes_accessed=8 * nh * rows * features,
             transcendentals=0,
         ),
         name="rest",
-    )(normed, grads)
-
-    from_far = move(far, -2, nz).astype(f32)
+    )(normed, grads, grads_own, gate_weight.T, up_weight.T)
+
+    far_in = move(far, -2, nz)
     outer_ahead, outer_behind = move(outer_ahead, 1, nz), move(outer_behind, -1, nz)
     inner_ahead, inner_behind = move(inner_ahead, 1, nz), move(inner_behind, -1, nz)
 
@@ -275,14 +285,12 @@
             + inner_behind[at, :, columns].astype(f32)
         )
 
-    plus, minus = lax.optimization_barrier(
-        (outer(0).astype(bf16), (outer(1) + from_far).astype(bf16))
-    )
-    grads_own, first_sum = lax.optimization_barrier((grads_own, plus))
+    plus, minus = call(
+        outer_kernel, "outer", [(depth, wide)] * 2, outer_hub, outer_ahead, outer_behind, far_in
+    )
+    part, first_sum = lax.optimization_barrier((part, plus))
     plus, minus = move(first_sum, 3, nz), move(minus, -3, nz)
 
-    part = contract_last(grads_own[:, :width], gate_weight)
-    part = (part + contract_last(grads_own[:, width:], up_weight)).astype(bf16)
     blocks = part.reshape(nt, rows // nt, features)
     moved = lax.all_to_all(blocks, TENSOR, 0, 0, tiled=True)
 

time: 89.5 us -> 96.7 us (1.080)
  the two profiles are of different devices: /device:TPU:1 before, /device:TPU:24 now
where the time goes in v11:
time: 96.7 us; the launch traced here: 96 us
  starting transfers between devices  63 us (65%)
  waiting for transfers between devices  21 us (22%)
  Pallas kernels  5.63 us (6%)
  local copies, waits for them, and re-layouts  4.25 us (4%)
  other arithmetic  1.24 us (1%)
    ppermute x9, starting transfers between devices, move(): return lax.ppermute(value, 'z', pairs)  44.4 us
    ppermute x9, waiting for transfers between devices, move(): return lax.ppermute(value, 'z', pairs)  13.5 us
    all_to_all x1, starting transfers between devices, shards(): same = lax.all_to_all(copies, ('yh', 'x', 'yl'), 0, 0, tiled=True)  9.01 us
    ppermute x1, waiting for transfers between devices, shards(): other = lax.ppermute(own, 'yh', [(0, 1), (1, 0)])  5.84 us
    all_to_all x1, starting transfers between devices, shards(): moved = lax.all_to_all(blocks, TENSOR, 0, 0, tiled=True)  4.37 us
    ppermute x1, starting transfers between devices, shards(): other = lax.ppermute(own, 'yh', [(0, 1), (1, 0)])  3.32 us
    unnamed x11, local copies, waits for them, and re-layouts  2.51 us
    pallas_call x1, Pallas kernels, shards(): pl.pallas_call(functools.partial(rest_kernel, factor, nz), out_shape=[jax...  2.34 us
  transfers between devices with their start and end apart: 13, of which 5 were waited for; matrix products, arithmetic and copies ran while one was open for 1% of the time, Pallas kernels for 4%

profile of v11, /device:TPU:24, one launch (start us, length us, event | category | flops | bytes accessed | tf_op | source)
XLA Modules:
  0.0 96.0 jit_solution(2223167890447546051)
XLA Ops:
  0.6 0.0 copy-start.3
  0.6 0.0 copy-start
  0.7 1.7 %broadcast_in_dim.2 = bf16[16,8,2048]{2,1,0:T(8,128)(2,1)} broadcast(bf16[8,2048]{1,0:T(8,128)(2,1)} %param.5), dimensions={1,2} | broadcast | bytes 557056 | tf_op jit(solution)/shard_map/broadcast_in_dim | solution.py:215
  2.4 9.0 %all-to-all-start = ((bf16[16,8,2048]{2,1,0:T(8,128)(2,1)}), bf16[16,8,2048]{2,1,0:T(8,128)(2,1)S(1)}, u32[]{:S(2)}, u32[]{:S(2)}) async-start(bf16[16,8,2048]{2,1,0:T(8,128)(2,1)} %broadcast_in_dim.2), calls=%async_computation | async-start | bytes 1048576 | tf_op jit(solution)/shard_map/all_to_all | solution.py:216
  11.4 1.0 %copy.8.own_ref = bf16[128,448]{1,0:T(8,128)(2,1)S(1)} copy(bf16[128,448]{0,1:T(8,128)(2,1)} %param.9) | data formatting | bytes 229376 | tf_op args[4]
  12.4 3.3 %collective-permute-start = (bf16[128,448]{1,0:T(8,128)(2,1)S(1)}, bf16[128,448]{1,0:T(8,128)(2,1)S(1)}, u32[]{:S(2)}, u32[]{:S(2)}) collective-permute-start(bf16[128,448]{1,0:T(8,128)(2,1)S(1)} %copy.8.own_ref), channel_id=1, source_target_pairs={{0,16},{16,0},{1,17},{17,1},{2,18},{18,2},{3,19},{19,3},{4,20},{20... | collective-permute-start | bytes 344072 | tf_op jit(solution)/shard_map/ppermute | solution.py:213
  15.7 5.8 %collective-permute-done.other_ref = bf16[128,448]{1,0:T(8,128)(2,1)S(1)} collective-permute-done((bf16[128,448]{1,0:T(8,128)(2,1)S(1)}, bf16[128,448]{1,0:T(8,128)(2,1)S(1)}, u32[]{:S(2)}, u32[]{:S(2)}) %collective-permute-start) | collective-permute-done | bytes 114720 | tf_op jit(solution)/shard_map/ppermute | solution.py:213
  21.6 0.0 all-to-all-done
  21.6 1.9 %collective-permute-start.1 = (bf16[128,2048]{1,0:T(8,128)(2,1)S(1)}, bf16[128,2048]{1,0:T(8,128)(2,1)S(1)}, u32[]{:S(2)}, u32[]{:S(2)}) collective-permute-start(bf16[128,2048]{1,0:T(8,128)(2,1)S(1)} %bitcast.13), channel_id=1, source_target_pairs={{0,1},{1,0},{2,3},{3,2},{4,5},{5,4},{6,7},{7,6},{8,9},{9,8},{10,11... | collective-permute-start | bytes 1572872 | tf_op jit(solution)/shard_map/ppermute | solution.py:219
  23.5 0.0 copy-done.3
  23.5 0.2 norm.1.same_ref
  23.7 1.6 %collective-permute-done.1.swapped_ref = bf16[128,2048]{1,0:T(8,128)(2,1)S(1)} collective-permute-done((bf16[128,2048]{1,0:T(8,128)(2,1)S(1)}, bf16[128,2048]{1,0:T(8,128)(2,1)S(1)}, u32[]{:S(2)}, u32[]{:S(2)}) %collective-permute-start.1) | collective-permute-done | bytes 524320 | tf_op jit(solution)/shard_map/ppermute | solution.py:219
  25.4 0.0 copy-done
  25.4 0.0 copy-start.1
  25.4 1.5 %copy-done.1 = bf16[2048,448]{0,1:T(8,128)(2,1)S(1)} copy-done((bf16[2048,448]{0,1:T(8,128)(2,1)S(1)}, bf16[2048,448]{0,1:T(8,128)(2,1)}, u32[]{:S(2)}) %copy-start.1) | copy-done | bytes 1835032
  26.9 0.0 copy-start.2
  26.9 2.2 %local.1 = (bf16[64,896]{1,0:T(8,128)(2,1)S(1)}, bf16[2,64,896]{2,1,0:T(8,128)(2,1)S(1)}, bf16[2,64,896]{2,1,0:T(8,128)(2,1)S(1)}, bf16[128,896]{1,0:T(8,128)(2,...) custom-call(bf16[128,2048]{1,0:T(8,128)(2,1)S(1)} %norm.1.same_ref, ...), custom_call_target="tpu_custom_call" | custom-call | flops 1409286144 | bytes 7340032 | tf_op jit(solution)/shard_map/local/pallas_call | solution.py:233
  29.1 3.5 %collective-permute-start.2 = (bf16[2,64,896]{2,1,0:T(8,128)(2,1)S(1)}, bf16[2,64,896]{2,1,0:T(8,128)(2,1)S(1)}, u32[]{:S(2)}, u32[]{:S(2)}) collective-permute-start(bf16[2,64,896]{2,1,0:T(8,128)(2,1)S(1)} %get-tuple-element.33), channel_id=1, source_target_pairs={{0,32},{32,0},{64,96},{96,64},{128,160},{160,128},{192,224},{224,1... | collective-permute-start | bytes 688136 | tf_op jit(solution)/shard_map/ppermute | solution.py:203
  32.6 10.5 %collective-permute-start.3 = (bf16[2,64,896]{2,1,0:T(8,128)(2,1)S(1)}, bf16[2,64,896]{2,1,0:T(8,128)(2,1)S(1)}, u32[]{:S(2)}, u32[]{:S(2)}) collective-permute-start(bf16[2,64,896]{2,1,0:T(8,128)(2,1)S(1)} %get-tuple-element.34), channel_id=1, source_target_pairs={{0,480},{32,64},{64,32},{96,128},{128,96},{160,192},{192,160},{224... | collective-permute-start | bytes 688136 | tf_op jit(solution)/shard_map/ppermute | solution.py:203
  43.1 0.0 copy-done.2
  43.1 2.3 %rest.1 = (bf16[3,64,896]{2,1,0:T(8,128)(2,1)S(1)}, bf16[3,64,896]{2,1,0:T(8,128)(2,1)S(1)}, bf16[2,64,896]{2,1,0:T(8,128)(2,1)S(1)}, bf16[3,64,896]{2,1,0:T(8,128)(2,1)S(1)}, bf16[128,2048]{1,0:T(8,128)(2,1)}) custom-call(bf16[256,2048]{1,0:T(8,128)(2,1)S(1)} %get-tuple-element.28.normed_ref, bf16[256,896]{1,0:T(8,128)(2,1)S(1)} %get-tuple-element.29.grads_ref, ...), custom_call_target="tpu_custom_call" | custom-call | flops 1409286144 | bytes 4194304 | tf_op jit(solution)/shard_map/rest/pallas_call | solution.py:254
  45.5 0.0 copy-start.4
  45.5 2.0 %collective-permute-start.5 = (bf16[3,64,896]{2,1,0:T(8,128)(2,1)S(1)}, bf16[3,64,896]{2,1,0:T(8,128)(2,1)S(1)}, u32[]{:S(2)}, u32[]{:S(2)}) collective-permute-start(bf16[3,64,896]{2,1,0:T(8,128)(2,1)S(1)} %get-tuple-element.39), channel_id=1, source_target_pairs={{0,32},{32,0},{64,96},{96,64},{128,160},{160,128},{192,224},{224,1... | collective-permute-start | bytes 1032200 | tf_op jit(solution)/shard_map/ppermute | solution.py:203
  47.5 3.9 %collective-permute-start.6 = (bf16[3,64,896]{2,1,0:T(8,128)(2,1)S(1)}, bf16[3,64,896]{2,1,0:T(8,128)(2,1)S(1)}, u32[]{:S(2)}, u32[]{:S(2)}) collective-permute-start(bf16[3,64,896]{2,1,0:T(8,128)(2,1)S(1)} %get-tuple-element.40), channel_id=1, source_target_pairs={{0,480},{32,64},{64,32},{96,128},{128,96},{160,192},{192,160},{224... | collective-permute-start | bytes 1032200 | tf_op jit(solution)/shard_map/ppermute | solution.py:203
  51.4 4.6 %collective-permute-start.4 = (bf16[64,896]{1,0:T(8,128)(2,1)S(1)}, bf16[64,896]{1,0:T(8,128)(2,1)S(1)}, u32[]{:S(2)}, u32[]{:S(2)}) collective-permute-start(bf16[64,896]{1,0:T(8,128)(2,1)S(1)} %get-tuple-element.35), channel_id=1, source_target_pairs={{0,448},{32,96},{64,0},{96,160},{128,64},{160,224},{192,128},{224,... | collective-permute-start | bytes 344072 | tf_op jit(solution)/shard_map/ppermute | solution.py:203
  56.0 6.6 %collective-permute-done.4.far_ref = bf16[64,896]{1,0:T(8,128)(2,1)S(1)} collective-permute-done((bf16[64,896]{1,0:T(8,128)(2,1)S(1)}, bf16[64,896]{1,0:T(8,128)(2,1)S(1)}, u32[]{:S(2)}, u32[]{:S(2)}) %collective-permute-start.4) | collective-permute-done | bytes 114720 | tf_op jit(solution)/shard_map/ppermute | solution.py:203
  62.6 0.0 collective-permute-done.2.ahead_ref
  62.6 0.0 collective-permute-done.3.behind_ref
  62.6 0.1 outer.1
  62.7 3.1 %collective-permute-start.7 = (bf16[64,896]{1,0:T(8,128)(2,1)S(1)}, bf16[64,896]{1,0:T(8,128)(2,1)S(1)}, u32[]{:S(2)}, u32[]{:S(2)}) collective-permute-start(bf16[64,896]{1,0:T(8,128)(2,1)S(1)} %get-tuple-element.41), channel_id=1, source_target_pairs={{0,96},{32,448},{64,160},{96,0},{128,224},{160,64},{192,288},{224,... | collective-permute-start | bytes 344072 | tf_op jit(solution)/shard_map/ppermute | solution.py:203
  65.8 6.9 %collective-permute-start.8 = (bf16[64,896]{1,0:T(8,128)(2,1)S(1)}, bf16[64,896]{1,0:T(8,128)(2,1)S(1)}, u32[]{:S(2)}, u32[]{:S(2)}) collective-permute-start(bf16[64,896]{1,0:T(8,128)(2,1)S(1)} %get-tuple-element.42), channel_id=1, source_target_pairs={{0,416},{32,128},{64,480},{96,192},{128,32},{160,256},{192,96},{22... | collective-permute-start | bytes 344072 | tf_op jit(solution)/shard_map/ppermute | solution.py:203
  72.7 4.4 %all-to-all-start.1 = ((bf16[16,8,2048]{2,1,0:T(8,128)(2,1)}), bf16[16,8,2048]{2,1,0:T(8,128)(2,1)S(1)}, u32[]{:S(2)}, u32[]{:S(2)}) async-start(bf16[16,8,2048]{2,1,0:T(8,128)(2,1)} %bitcast.4), calls=%async_computation.1 | async-start | bytes 1048576 | tf_op jit(solution)/shard_map/all_to_all | solution.py:295
  77.1 0.0 copy-done.4
  77.1 0.1 fusion.8
  77.2 0.0 collective-permute-done.7
  77.2 0.0 collective-permute-done.8
  77.2 0.0 collective-permute-done.5.ahead_ref
  77.2 0.0 collective-permute-done.6.behind_ref
  77.2 0.1 fusion
  77.4 6.4 %collective-permute-start.10 = (bf16[64,896]{1,0:T(8,128)(2,1)S(1)}, bf16[64,896]{1,0:T(8,128)(2,1)S(1)}, u32[]{:S(2)}, u32[]{:S(2)}) collective-permute-start(bf16[64,896]{1,0:T(8,128)(2,1)S(1)} %get-tuple-element.46), channel_id=1, source_target_pairs={{0,416},{32,128},{64,480},{96,192},{128,32},{160,256},{192,96},{22... | collective-permute-start | bytes 344072 | tf_op jit(solution)/shard_map/ppermute | solution.py:203
  83.7 3.6 %collective-permute-start.9 = (bf16[64,896]{1,0:T(8,128)(2,1)S(1)}, bf16[64,896]{1,0:T(8,128)(2,1)S(1)}, u32[]{:S(2)}, u32[]{:S(2)}) collective-permute-start(bf16[64,896]{1,0:T(8,128)(2,1)S(1)} %get-tuple-element.45), channel_id=1, source_target_pairs={{0,96},{32,448},{64,160},{96,0},{128,224},{160,64},{192,288},{224,... | collective-permute-start | bytes 344072 | tf_op jit(solution)/shard_map/ppermute | solution.py:203
  87.3 0.3 collective-permute-done.10.minus_ref
  87.6 6.7 %collective-permute-done.9.plus_ref = bf16[64,896]{1,0:T(8,128)(2,1)S(1)} collective-permute-done((bf16[64,896]{1,0:T(8,128)(2,1)S(1)}, bf16[64,896]{1,0:T(8,128)(2,1)S(1)}, u32[]{:S(2)}, u32[]{:S(2)}) %collective-permute-start.9) | collective-permute-done | bytes 114720 | tf_op jit(solution)/shard_map/ppermute | solution.py:203
  94.2 0.8 total.1
  95.0 0.0 all-to-all-done.1
  95.0 0.1 convert_reduce_fusion
  95.1 0.2 fusion.4
  95.3 0.7 fusion.7
  (2 shorter events, 0.0 us)
Async XLA Ops:
  0.6 22.9 %copy-start.3 = (f32[2048]{0:T(1024)S(1)}, f32[2048]{0:T(1024)}, u32[]{:S(2)}) copy-start(f32[2048]{0:T(1024)} %param.6) | copy-start | bytes 24580
  0.6 24.7 %copy-start = (bf16[2048,448]{0,1:T(8,128)(2,1)S(1)}, bf16[2048,448]{0,1:T(8,128)(2,1)}, u32[]{:S(2)}) copy-start(bf16[2048,448]{0,1:T(8,128)(2,1)} %param.7) | copy-start | bytes 5505028
  2.4 19.2 %all-to-all-start = ((bf16[16,8,2048]{2,1,0:T(8,128)(2,1)}), bf16[16,8,2048]{2,1,0:T(8,128)(2,1)S(1)}, u32[]{:S(2)}, u32[]{:S(2)}) async-start(bf16[16,8,2048]{2,1,0:T(8,128)(2,1)} %broadcast_in_dim.2), calls=%async_computation | async-start | bytes 1048576 | tf_op jit(solution)/shard_map/all_to_all | solution.py:216
  12.4 9.2 %collective-permute-start = (bf16[128,448]{1,0:T(8,128)(2,1)S(1)}, bf16[128,448]{1,0:T(8,128)(2,1)S(1)}, u32[]{:S(2)}, u32[]{:S(2)}) collective-permute-start(bf16[128,448]{1,0:T(8,128)(2,1)S(1)} %copy.8.own_ref), channel_id=1, source_target_pairs={{0,16},{16,0},{1,17},{17,1},{2,18},{18,2},{3,19},{19,3},{4,20},{20... | collective-permute-start | bytes 344072 | tf_op jit(solution)/shard_map/ppermute | solution.py:213
  21.6 3.8 %collective-permute-start.1 = (bf16[128,2048]{1,0:T(8,128)(2,1)S(1)}, bf16[128,2048]{1,0:T(8,128)(2,1)S(1)}, u32[]{:S(2)}, u32[]{:S(2)}) collective-permute-start(bf16[128,2048]{1,0:T(8,128)(2,1)S(1)} %bitcast.13), channel_id=1, source_target_pairs={{0,1},{1,0},{2,3},{3,2},{4,5},{5,4},{6,7},{7,6},{8,9},{9,8},{10,11... | collective-permute-start | bytes 1572872 | tf_op jit(solution)/shard_map/ppermute | solution.py:219
  25.4 1.5 %copy-start.1 = (bf16[2048,448]{0,1:T(8,128)(2,1)S(1)}, bf16[2048,448]{0,1:T(8,128)(2,1)}, u32[]{:S(2)}) copy-start(bf16[2048,448]{0,1:T(8,128)(2,1)} %param.8) | copy-start | bytes 5505028
  26.9 16.2 %copy-start.2 = (bf16[2048,448]{0,1:T(8,128)(2,1)S(1)}, bf16[2048,448]{0,1:T(8,128)(2,1)}, u32[]{:S(2)}) copy-start(bf16[2048,448]{0,1:T(8,128)(2,1)} %param.8) | copy-start | bytes 5505028
  29.1 33.5 %collective-permute-start.2 = (bf16[2,64,896]{2,1,0:T(8,128)(2,1)S(1)}, bf16[2,64,896]{2,1,0:T(8,128)(2,1)S(1)}, u32[]{:S(2)}, u32[]{:S(2)}) collective-permute-start(bf16[2,64,896]{2,1,0:T(8,128)(2,1)S(1)} %get-tuple-element.33), channel_id=1, source_target_pairs={{0,32},{32,0},{64,96},{96,64},{128,160},{160,128},{192,224},{224,1... | collective-permute-start | bytes 688136 | tf_op jit(solution)/shard_map/ppermute | solution.py:203
  32.6 30.0 %collective-permute-start.3 = (bf16[2,64,896]{2,1,0:T(8,128)(2,1)S(1)}, bf16[2,64,896]{2,1,0:T(8,128)(2,1)S(1)}, u32[]{:S(2)}, u32[]{:S(2)}) collective-permute-start(bf16[2,64,896]{2,1,0:T(8,128)(2,1)S(1)} %get-tuple-element.34), channel_id=1, source_target_pairs={{0,480},{32,64},{64,32},{96,128},{128,96},{160,192},{192,160},{224... | collective-permute-start | bytes 688136 | tf_op jit(solution)/shard_map/ppermute | solution.py:203
  45.5 31.6 %copy-start.4 = (bf16[8,2048]{1,0:T(8,128)(2,1)S(1)}, bf16[8,2048]{1,0:T(8,128)(2,1)}, u32[]{:S(2)}) copy-start(bf16[8,2048]{1,0:T(8,128)(2,1)} %param.5) | copy-start | bytes 98308
  45.5 31.8 %collective-permute-start.5 = (bf16[3,64,896]{2,1,0:T(8,128)(2,1)S(1)}, bf16[3,64,896]{2,1,0:T(8,128)(2,1)S(1)}, u32[]{:S(2)}, u32[]{:S(2)}) collective-permute-start(bf16[3,64,896]{2,1,0:T(8,128)(2,1)S(1)} %get-tuple-element.39), channel_id=1, source_target_pairs={{0,32},{32,0},{64,96},{96,64},{128,160},{160,128},{192,224},{224,1... | collective-permute-start | bytes 1032200 | tf_op jit(solution)/shard_map/ppermute | solution.py:203
  47.5 29.7 %collective-permute-start.6 = (bf16[3,64,896]{2,1,0:T(8,128)(2,1)S(1)}, bf16[3,64,896]{2,1,0:T(8,128)(2,1)S(1)}, u32[]{:S(2)}, u32[]{:S(2)}) collective-permute-start(bf16[3,64,896]{2,1,0:T(8,128)(2,1)S(1)} %get-tuple-element.40), channel_id=1, source_target_pairs={{0,480},{32,64},{64,32},{96,128},{128,96},{160,192},{192,160},{224... | collective-permute-start | bytes 1032200 | tf_op jit(solution)/shard_map/ppermute | solution.py:203
  51.4 11.2 %collective-permute-start.4 = (bf16[64,896]{1,0:T(8,128)(2,1)S(1)}, bf16[64,896]{1,0:T(8,128)(2,1)S(1)}, u32[]{:S(2)}, u32[]{:S(2)}) collective-permute-start(bf16[64,896]{1,0:T(8,128)(2,1)S(1)} %get-tuple-element.35), channel_id=1, source_target_pairs={{0,448},{32,96},{64,0},{96,160},{128,64},{160,224},{192,128},{224,... | collective-permute-start | bytes 344072 | tf_op jit(solution)/shard_map/ppermute | solution.py:203
  62.7 14.5 %collective-permute-start.7 = (bf16[64,896]{1,0:T(8,128)(2,1)S(1)}, bf16[64,896]{1,0:T(8,128)(2,1)S(1)}, u32[]{:S(2)}, u32[]{:S(2)}) collective-permute-start(bf16[64,896]{1,0:T(8,128)(2,1)S(1)} %get-tuple-element.41), channel_id=1, source_target_pairs={{0,96},{32,448},{64,160},{96,0},{128,224},{160,64},{192,288},{224,... | collective-permute-start | bytes 344072 | tf_op jit(solution)/shard_map/ppermute | solution.py:203
  65.8 11.4 %collective-permute-start.8 = (bf16[64,896]{1,0:T(8,128)(2,1)S(1)}, bf16[64,896]{1,0:T(8,128)(2,1)S(1)}, u32[]{:S(2)}, u32[]{:S(2)}) collective-permute-start(bf16[64,896]{1,0:T(8,128)(2,1)S(1)} %get-tuple-element.42), channel_id=1, source_target_pairs={{0,416},{32,128},{64,480},{96,192},{128,32},{160,256},{192,96},{22... | collective-permute-start | bytes 344072 | tf_op jit(solution)/shard_map/ppermute | solution.py:203
  72.7 22.3 %all-to-all-start.1 = ((bf16[16,8,2048]{2,1,0:T(8,128)(2,1)}), bf16[16,8,2048]{2,1,0:T(8,128)(2,1)S(1)}, u32[]{:S(2)}, u32[]{:S(2)}) async-start(bf16[16,8,2048]{2,1,0:T(8,128)(2,1)} %bitcast.4), calls=%async_computation.1 | async-start | bytes 1048576 | tf_op jit(solution)/shard_map/all_to_all | solution.py:295
  77.4 10.2 %collective-permute-start.10 = (bf16[64,896]{1,0:T(8,128)(2,1)S(1)}, bf16[64,896]{1,0:T(8,128)(2,1)S(1)}, u32[]{:S(2)}, u32[]{:S(2)}) collective-permute-start(bf16[64,896]{1,0:T(8,128)(2,1)S(1)} %get-tuple-element.46), channel_id=1, source_target_pairs={{0,416},{32,128},{64,480},{96,192},{128,32},{160,256},{192,96},{22... | collective-permute-start | bytes 344072 | tf_op jit(solution)/shard_map/ppermute | solution.py:203
  83.7 10.5 %collective-permute-start.9 = (bf16[64,896]{1,0:T(8,128)(2,1)S(1)}, bf16[64,896]{1,0:T(8,128)(2,1)S(1)}, u32[]{:S(2)}, u32[]{:S(2)}) collective-permute-start(bf16[64,896]{1,0:T(8,128)(2,1)S(1)} %get-tuple-element.45), channel_id=1, source_target_pairs={{0,96},{32,448},{64,160},{96,0},{128,224},{160,64},{192,288},{224,... | collective-permute-start | bytes 344072 | tf_op jit(solution)/shard_map/ppermute | solution.py:203

commit v12 on v10

--- a/solution.py
+++ b/solution.py
@@ -53,6 +53,7 @@
     nz,
     block_rows,
     same_ref,
+    up_same_ref,
     swapped_ref,
     gain_ref,
     gate_ref,
@@ -73,7 +74,8 @@
     normed_ref[tokens:] = (normalize(swapped_ref[...])[0] * gain_ref[...]).astype(jnp.bfloat16)
     normed = normed_ref[...]
     gate_value = contract_last(normed, gate_ref[...])
-    up_value = contract_last(normed, up_ref[...])
+    up_swapped = contract_last(normed_ref[tokens:], up_ref[...])
+    up_value = jnp.concatenate([up_same_ref[...], up_swapped], axis=0)
     first = half == 0
     even = lax.axis_index("core") == 0
     count = lax.axis_size("core")
@@ -185,8 +187,9 @@
     )(*values)
 
 
-def norm_kernel(rows_ref, gain_ref, normed_ref):
+def norm_kernel(rows_ref, gain_ref, up_ref, normed_ref, value_ref):
     normed_ref[...] = (normalize(rows_ref[...])[0] * gain_ref[...]).astype(jnp.bfloat16)
+    value_ref[...] = contract_last(normed_ref[...], up_ref[...])
 
 
 def move(value, hops, nz):
@@ -209,15 +212,18 @@
     same, other = lax.optimization_barrier((same, other))
     swapped = lax.ppermute(same, "core", [(0, 1), (1, 0)])
     gain = norm_gain.reshape(1, features)
-    normed_same = pl.pallas_call(
+    normed_same, up_same = pl.pallas_call(
         norm_kernel,
-        out_shape=jax.ShapeDtypeStruct(same.shape, bf16),
+        out_shape=[
+            jax.ShapeDtypeStruct(same.shape, bf16),
+            jax.ShapeDtypeStruct((same.shape[0], width), f32),
+        ],
         cost_estimate=pl.CostEstimate(
             flops=8 * rows * features, bytes_accessed=4 * rows * features, transcendentals=rows
         ),
         compiler_params=pltpu.CompilerParams(vmem_limit_bytes=8 * 1024 * 1024),
         name="norm",
-    )(same, gain)
+    )(same, gain, up_weight.T)
     factor = float(rows * nz * nh) ** (-0.5)
     shape = jax.ShapeDtypeStruct
     wide = 2 * width
@@ -241,7 +247,7 @@
             transcendentals=nh * rows * width,
         ),
         name="local",
-    )(normed_same, swapped, gain, gate_weight.T, up_weight.T, own, other)
+    )(normed_same, up_same, swapped, gain, gate_weight.T, up_weight.T, own, other)
     inner_ahead, inner_behind, outer_hub, inner_hub = pl.pallas_call(
         functools.partial(rest_kernel, factor, nz),
         out_shape=[

time: 89.5 us -> 88.1 us (0.984)
  local copies, waits for them, and re-layouts: 4.25 us -> 2.75 us
    unnamed x9, local copies, waits for them, and re-layouts: 2.52 us -> 1.02 us
where the time goes in v12:
time: 88.1 us; the launch traced here: 86.6 us
  starting transfers between devices  59.7 us (68%)
  waiting for transfers between devices  13.9 us (16%)
  Pallas kernels  5.08 us (6%)
  local copies, waits for them, and re-layouts  2.75 us (3%)
  other arithmetic  2.62 us (3%)
  matrix products  1.71 us (2%)
    ppermute x9, starting transfers between devices, move(): return lax.ppermute(value, 'z', pairs)  38.3 us
    all_to_all x1, starting transfers between devices, shards(): same = lax.all_to_all(copies, ('yh', 'x', 'yl'), 0, 0, tiled=True)  7.58 us
    ppermute x1, waiting for transfers between devices, shards(): other = lax.ppermute(own, 'yh', [(0, 1), (1, 0)])  7.39 us
    ppermute x9, waiting for transfers between devices, move(): return lax.ppermute(value, 'z', pairs)  5.81 us
    all_to_all x1, starting transfers between devices, shards(): moved = lax.all_to_all(blocks, TENSOR, 0, 0, tiled=True)  5.57 us
    ppermute x1, starting transfers between devices, shards(): other = lax.ppermute(own, 'yh', [(0, 1), (1, 0)])  4.78 us
    ppermute x1, starting transfers between devices, shards(): swapped = lax.ppermute(same, 'core', [(0, 1), (1, 0)])  3.44 us
    pallas_call x1, Pallas kernels, shards(): pl.pallas_call(functools.partial(local_kernel, factor, nz, residual.shape...  2.19 us
  transfers between devices with their start and end apart: 13, of which 4 were waited for; matrix products, arithmetic and copies ran while one was open for 5% of the time, Pallas kernels for 3%

profile of v12, /device:TPU:1, one launch (start us, length us, event | category | flops | bytes accessed | tf_op | source)
XLA Modules:
  0.0 86.6 jit_solution(5520340856778809923)
XLA Ops:
  0.6 0.0 copy-start.2
  0.6 0.0 copy-start
  0.7 1.7 %broadcast_in_dim.2 = bf16[16,8,2048]{2,1,0:T(8,128)(2,1)} broadcast(bf16[8,2048]{1,0:T(8,128)(2,1)} %param.5), dimensions={1,2} | broadcast | bytes 557056 | tf_op jit(solution)/shard_map/broadcast_in_dim | solution.py:209
  2.4 7.6 %all-to-all-start = ((bf16[16,8,2048]{2,1,0:T(8,128)(2,1)}), bf16[16,8,2048]{2,1,0:T(8,128)(2,1)S(1)}, u32[]{:S(2)}, u32[]{:S(2)}) async-start(bf16[16,8,2048]{2,1,0:T(8,128)(2,1)} %broadcast_in_dim.2), calls=%async_computation | async-start | bytes 1048576 | tf_op jit(solution)/shard_map/all_to_all | solution.py:210
  10.0 1.0 %copy.8.own_ref = bf16[128,448]{1,0:T(8,128)(2,1)S(1)} copy(bf16[128,448]{0,1:T(8,128)(2,1)} %param.9) | data formatting | bytes 229376 | tf_op args[4]
  11.0 4.8 %collective-permute-start = (bf16[128,448]{1,0:T(8,128)(2,1)S(1)}, bf16[128,448]{1,0:T(8,128)(2,1)S(1)}, u32[]{:S(2)}, u32[]{:S(2)}) collective-permute-start(bf16[128,448]{1,0:T(8,128)(2,1)S(1)} %copy.8.own_ref), channel_id=1, source_target_pairs={{0,16},{16,0},{1,17},{17,1},{2,18},{18,2},{3,19},{19,3},{4,20},{20... | collective-permute-start | bytes 344072 | tf_op jit(solution)/shard_map/ppermute | solution.py:207
  15.8 7.4 %collective-permute-done.other_ref = bf16[128,448]{1,0:T(8,128)(2,1)S(1)} collective-permute-done((bf16[128,448]{1,0:T(8,128)(2,1)S(1)}, bf16[128,448]{1,0:T(8,128)(2,1)S(1)}, u32[]{:S(2)}, u32[]{:S(2)}) %collective-permute-start) | collective-permute-done | bytes 114720 | tf_op jit(solution)/shard_map/ppermute | solution.py:207
  23.2 0.0 all-to-all-done
  23.2 0.0 copy-start.1
  23.2 3.4 %collective-permute-start.1 = (bf16[128,2048]{1,0:T(8,128)(2,1)S(1)}, bf16[128,2048]{1,0:T(8,128)(2,1)S(1)}, u32[]{:S(2)}, u32[]{:S(2)}) collective-permute-start(bf16[128,2048]{1,0:T(8,128)(2,1)S(1)} %bitcast.25), channel_id=1, source_target_pairs={{0,1},{1,0},{2,3},{3,2},{4,5},{5,4},{6,7},{7,6},{8,9},{9,8},{10,11... | collective-permute-start | bytes 1572872 | tf_op jit(solution)/shard_map/ppermute | solution.py:213
  26.6 0.0 copy-done.2
  26.6 0.0 copy-done
  26.6 0.8 norm.1
  27.4 0.7 collective-permute-done.1.swapped_ref
  28.1 0.0 copy-done.1
  28.1 2.2 %local.1 = (bf16[64,896]{1,0:T(8,128)(2,1)S(1)}, bf16[2,64,896]{2,1,0:T(8,128)(2,1)S(1)}, bf16[2,64,896]{2,1,0:T(8,128)(2,1)S(1)}, bf16[128,896]{1,0:T(8,128)(2,...) custom-call(bf16[128,2048]{1,0:T(8,128)(2,1)S(1)} %get-tuple-element.28.same_ref, ...), custom_call_target="tpu_custom_call" | custom-call | flops 1409286144 | bytes 7340032 | tf_op jit(solution)/shard_map/local/pallas_call | solution.py:230
  30.3 3.0 %collective-permute-start.2 = (bf16[2,64,896]{2,1,0:T(8,128)(2,1)S(1)}, bf16[2,64,896]{2,1,0:T(8,128)(2,1)S(1)}, u32[]{:S(2)}, u32[]{:S(2)}) collective-permute-start(bf16[2,64,896]{2,1,0:T(8,128)(2,1)S(1)} %get-tuple-element.35), channel_id=1, source_target_pairs={{0,32},{32,0},{64,96},{96,64},{128,160},{160,128},{192,224},{224,1... | collective-permute-start | bytes 688136 | tf_op jit(solution)/shard_map/ppermute | solution.py:197
  33.4 10.2 %collective-permute-start.3 = (bf16[2,64,896]{2,1,0:T(8,128)(2,1)S(1)}, bf16[2,64,896]{2,1,0:T(8,128)(2,1)S(1)}, u32[]{:S(2)}, u32[]{:S(2)}) collective-permute-start(bf16[2,64,896]{2,1,0:T(8,128)(2,1)S(1)} %get-tuple-element.36), channel_id=1, source_target_pairs={{0,480},{32,64},{64,32},{96,128},{128,96},{160,192},{192,160},{224... | collective-permute-start | bytes 688136 | tf_op jit(solution)/shard_map/ppermute | solution.py:197
  43.6 3.1 %collective-permute-start.4 = (bf16[64,896]{1,0:T(8,128)(2,1)S(1)}, bf16[64,896]{1,0:T(8,128)(2,1)S(1)}, u32[]{:S(2)}, u32[]{:S(2)}) collective-permute-start(bf16[64,896]{1,0:T(8,128)(2,1)S(1)} %get-tuple-element.37), channel_id=1, source_target_pairs={{0,448},{32,96},{64,0},{96,160},{128,64},{160,224},{192,128},{224,... | collective-permute-start | bytes 344072 | tf_op jit(solution)/shard_map/ppermute | solution.py:197
  46.7 1.3 %rest.1 = (bf16[3,64,896]{2,1,0:T(8,128)(2,1)}, bf16[3,64,896]{2,1,0:T(8,128)(2,1)S(1)}, bf16[2,64,896]{2,1,0:T(8,128)(2,1)S(1)}, bf16[3,64,896]{2,1,0:T(8,128)(2,1)S(1)}) custom-call(bf16[256,2048]{1,0:T(8,128)(2,1)S(1)} %get-tuple-element.32.normed_ref, bf16[256,896]{1,0:T(8,128)(2,1)S(1)} %get-tuple-element.33.grads_ref), custom_call_target="tpu_custom_call" | custom-call | flops 939524096 | bytes 2097152 | tf_op jit(solution)/shard_map/rest/pallas_call | solution.py:251
  48.0 1.9 %collective-permute-start.5 = (bf16[3,64,896]{2,1,0:T(8,128)(2,1)}, bf16[3,64,896]{2,1,0:T(8,128)(2,1)S(1)}, u32[]{:S(2)}, u32[]{:S(2)}) collective-permute-start(bf16[3,64,896]{2,1,0:T(8,128)(2,1)} %get-tuple-element.41), channel_id=1, source_target_pairs={{0,32},{32,0},{64,96},{96,64},{128,160},{160,128},{192,224},{224,1... | collective-permute-start | bytes 1032200 | tf_op jit(solution)/shard_map/ppermute | solution.py:197
  50.0 4.5 %collective-permute-start.6 = (bf16[3,64,896]{2,1,0:T(8,128)(2,1)S(1)}, bf16[3,64,896]{2,1,0:T(8,128)(2,1)S(1)}, u32[]{:S(2)}, u32[]{:S(2)}) collective-permute-start(bf16[3,64,896]{2,1,0:T(8,128)(2,1)S(1)} %get-tuple-element.42), channel_id=1, source_target_pairs={{0,480},{32,64},{64,32},{96,128},{128,96},{160,192},{192,160},{224... | collective-permute-start | bytes 1032200 | tf_op jit(solution)/shard_map/ppermute | solution.py:197
  54.5 0.0 collective-permute-done.2
  54.5 0.0 collective-permute-done.3
  54.5 0.7 fusion.8
  55.2 0.0 collective-permute-done.4
  55.2 0.7 fusion.4
  55.9 3.5 %collective-permute-start.7 = (bf16[64,896]{1,0:T(8,128)(2,1)}, bf16[64,896]{1,0:T(8,128)(2,1)S(1)}, u32[]{:S(2)}, u32[]{:S(2)}) collective-permute-start(bf16[64,896]{1,0:T(8,128)(2,1)} %fusion.8), channel_id=1, source_target_pairs={{0,96},{32,448},{64,160},{96,0},{128,224},{160,64},{192,288},{224,... | collective-permute-start | bytes 344072 | tf_op jit(solution)/shard_map/ppermute | solution.py:197
  59.5 3.0 %collective-permute-start.8 = (bf16[64,896]{1,0:T(8,128)(2,1)}, bf16[64,896]{1,0:T(8,128)(2,1)S(1)}, u32[]{:S(2)}, u32[]{:S(2)}) collective-permute-start(bf16[64,896]{1,0:T(8,128)(2,1)} %fusion.4), channel_id=1, source_target_pairs={{0,416},{32,128},{64,480},{96,192},{128,32},{160,256},{192,96},{22... | collective-permute-start | bytes 344072 | tf_op jit(solution)/shard_map/ppermute | solution.py:197
  62.4 0.4 fusion.6
  62.9 0.0 copy-start.3
  62.9 1.3 %fusion.1 = bf16[16,8,2048]{2,1,0:T(8,128)(2,1)} fusion(f32[128,2048]{1,0:T(8,128)S(1)} %fusion.6, bf16[2048,448]{0,1:T(8,128)(2,1)S(1)} %copy-done, bf16[128,896]{1,0:T(8,128)(2,1)S(1)} %get-tuple-element.39), kind=kOutput, calls=%fused_computation.2 | convolution fusion | flops 235405312 | bytes 3538944 | tf_op jit(solution)/shard_map/dot_general | solution.py:25
  64.2 5.6 %all-to-all-start.1 = ((bf16[16,8,2048]{2,1,0:T(8,128)(2,1)}), bf16[16,8,2048]{2,1,0:T(8,128)(2,1)S(1)}, u32[]{:S(2)}, u32[]{:S(2)}) async-start(bf16[16,8,2048]{2,1,0:T(8,128)(2,1)} %fusion.1), calls=%async_computation.1 | async-start | bytes 1048576 | tf_op jit(solution)/shard_map/all_to_all | solution.py:293
  69.7 0.0 copy-done.3
  69.7 0.1 fusion.15
  69.9 0.0 collective-permute-done.7
  69.9 0.0 collective-permute-done.8
  69.9 0.0 collective-permute-done.5.ahead_ref
  69.9 0.0 collective-permute-done.6.behind_ref
  69.9 0.1 fusion.2
  70.0 6.4 %collective-permute-start.10 = (bf16[64,896]{1,0:T(8,128)(2,1)S(1)}, bf16[64,896]{1,0:T(8,128)(2,1)S(1)}, u32[]{:S(2)}, u32[]{:S(2)}) collective-permute-start(bf16[64,896]{1,0:T(8,128)(2,1)S(1)} %get-tuple-element.48), channel_id=1, source_target_pairs={{0,416},{32,128},{64,480},{96,192},{128,32},{160,256},{192,96},{22... | collective-permute-start | bytes 344072 | tf_op jit(solution)/shard_map/ppermute | solution.py:197
  76.4 2.7 %collective-permute-start.9 = (bf16[64,896]{1,0:T(8,128)(2,1)S(1)}, bf16[64,896]{1,0:T(8,128)(2,1)S(1)}, u32[]{:S(2)}, u32[]{:S(2)}) collective-permute-start(bf16[64,896]{1,0:T(8,128)(2,1)S(1)} %get-tuple-element.47), channel_id=1, source_target_pairs={{0,96},{32,448},{64,160},{96,0},{128,224},{160,64},{192,288},{224,... | collective-permute-start | bytes 344072 | tf_op jit(solution)/shard_map/ppermute | solution.py:197
  79.1 4.1 %collective-permute-done.10.minus_ref = bf16[64,896]{1,0:T(8,128)(2,1)S(1)} collective-permute-done((bf16[64,896]{1,0:T(8,128)(2,1)S(1)}, bf16[64,896]{1,0:T(8,128)(2,1)S(1)}, u32[]{:S(2)}, u32[]{:S(2)}) %collective-permute-start.10) | collective-permute-done | bytes 114720 | tf_op jit(solution)/shard_map/ppermute | solution.py:197
  83.2 1.7 %collective-permute-done.9.plus_ref = bf16[64,896]{1,0:T(8,128)(2,1)S(1)} collective-permute-done((bf16[64,896]{1,0:T(8,128)(2,1)S(1)}, bf16[64,896]{1,0:T(8,128)(2,1)S(1)}, u32[]{:S(2)}, u32[]{:S(2)}) %collective-permute-start.9) | collective-permute-done | bytes 114720 | tf_op jit(solution)/shard_map/ppermute | solution.py:197
  84.9 0.8 total.1
  85.6 0.0 all-to-all-done.1
  85.6 0.1 convert_reduce_fusion
  85.7 0.2 fusion.11
  85.9 0.7 fusion.14
  (2 shorter events, 0.0 us)
Async XLA Ops:
  0.6 26.0 %copy-start.2 = (f32[2048]{0:T(1024)S(1)}, f32[2048]{0:T(1024)}, u32[]{:S(2)}) copy-start(f32[2048]{0:T(1024)} %param.6) | copy-start | bytes 24580
  0.6 26.0 %copy-start = (bf16[2048,448]{0,1:T(8,128)(2,1)S(1)}, bf16[2048,448]{0,1:T(8,128)(2,1)}, u32[]{:S(2)}) copy-start(bf16[2048,448]{0,1:T(8,128)(2,1)} %param.8) | copy-start | bytes 5505028
  2.4 20.8 %all-to-all-start = ((bf16[16,8,2048]{2,1,0:T(8,128)(2,1)}), bf16[16,8,2048]{2,1,0:T(8,128)(2,1)S(1)}, u32[]{:S(2)}, u32[]{:S(2)}) async-start(bf16[16,8,2048]{2,1,0:T(8,128)(2,1)} %broadcast_in_dim.2), calls=%async_computation | async-start | bytes 1048576 | tf_op jit(solution)/shard_map/all_to_all | solution.py:210
  11.0 12.2 %collective-permute-start = (bf16[128,448]{1,0:T(8,128)(2,1)S(1)}, bf16[128,448]{1,0:T(8,128)(2,1)S(1)}, u32[]{:S(2)}, u32[]{:S(2)}) collective-permute-start(bf16[128,448]{1,0:T(8,128)(2,1)S(1)} %copy.8.own_ref), channel_id=1, source_target_pairs={{0,16},{16,0},{1,17},{17,1},{2,18},{18,2},{3,19},{19,3},{4,20},{20... | collective-permute-start | bytes 344072 | tf_op jit(solution)/shard_map/ppermute | solution.py:207
  23.2 5.0 %copy-start.1 = (bf16[2048,448]{0,1:T(8,128)(2,1)S(1)}, bf16[2048,448]{0,1:T(8,128)(2,1)}, u32[]{:S(2)}) copy-start(bf16[2048,448]{0,1:T(8,128)(2,1)} %param.7) | copy-start | bytes 5505028
  23.2 5.0 %collective-permute-start.1 = (bf16[128,2048]{1,0:T(8,128)(2,1)S(1)}, bf16[128,2048]{1,0:T(8,128)(2,1)S(1)}, u32[]{:S(2)}, u32[]{:S(2)}) collective-permute-start(bf16[128,2048]{1,0:T(8,128)(2,1)S(1)} %bitcast.25), channel_id=1, source_target_pairs={{0,1},{1,0},{2,3},{3,2},{4,5},{5,4},{6,7},{7,6},{8,9},{9,8},{10,11... | collective-permute-start | bytes 1572872 | tf_op jit(solution)/shard_map/ppermute | solution.py:213
  30.3 24.2 %collective-permute-start.2 = (bf16[2,64,896]{2,1,0:T(8,128)(2,1)S(1)}, bf16[2,64,896]{2,1,0:T(8,128)(2,1)S(1)}, u32[]{:S(2)}, u32[]{:S(2)}) collective-permute-start(bf16[2,64,896]{2,1,0:T(8,128)(2,1)S(1)} %get-tuple-element.35), channel_id=1, source_target_pairs={{0,32},{32,0},{64,96},{96,64},{128,160},{160,128},{192,224},{224,1... | collective-permute-start | bytes 688136 | tf_op jit(solution)/shard_map/ppermute | solution.py:197
  33.4 21.1 %collective-permute-start.3 = (bf16[2,64,896]{2,1,0:T(8,128)(2,1)S(1)}, bf16[2,64,896]{2,1,0:T(8,128)(2,1)S(1)}, u32[]{:S(2)}, u32[]{:S(2)}) collective-permute-start(bf16[2,64,896]{2,1,0:T(8,128)(2,1)S(1)} %get-tuple-element.36), channel_id=1, source_target_pairs={{0,480},{32,64},{64,32},{96,128},{128,96},{160,192},{192,160},{224... | collective-permute-start | bytes 688136 | tf_op jit(solution)/shard_map/ppermute | solution.py:197
  43.6 11.6 %collective-permute-start.4 = (bf16[64,896]{1,0:T(8,128)(2,1)S(1)}, bf16[64,896]{1,0:T(8,128)(2,1)S(1)}, u32[]{:S(2)}, u32[]{:S(2)}) collective-permute-start(bf16[64,896]{1,0:T(8,128)(2,1)S(1)} %get-tuple-element.37), channel_id=1, source_target_pairs={{0,448},{32,96},{64,0},{96,160},{128,64},{160,224},{192,128},{224,... | collective-permute-start | bytes 344072 | tf_op jit(solution)/shard_map/ppermute | solution.py:197
  48.0 21.8 %collective-permute-start.5 = (bf16[3,64,896]{2,1,0:T(8,128)(2,1)}, bf16[3,64,896]{2,1,0:T(8,128)(2,1)S(1)}, u32[]{:S(2)}, u32[]{:S(2)}) collective-permute-start(bf16[3,64,896]{2,1,0:T(8,128)(2,1)} %get-tuple-element.41), channel_id=1, source_target_pairs={{0,32},{32,0},{64,96},{96,64},{128,160},{160,128},{192,224},{224,1... | collective-permute-start | bytes 1032200 | tf_op jit(solution)/shard_map/ppermute | solution.py:197
  50.0 19.9 %collective-permute-start.6 = (bf16[3,64,896]{2,1,0:T(8,128)(2,1)S(1)}, bf16[3,64,896]{2,1,0:T(8,128)(2,1)S(1)}, u32[]{:S(2)}, u32[]{:S(2)}) collective-permute-start(bf16[3,64,896]{2,1,0:T(8,128)(2,1)S(1)} %get-tuple-element.42), channel_id=1, source_target_pairs={{0,480},{32,64},{64,32},{96,128},{128,96},{160,192},{192,160},{224... | collective-permute-start | bytes 1032200 | tf_op jit(solution)/shard_map/ppermute | solution.py:197
  55.9 13.9 %collective-permute-start.7 = (bf16[64,896]{1,0:T(8,128)(2,1)}, bf16[64,896]{1,0:T(8,128)(2,1)S(1)}, u32[]{:S(2)}, u32[]{:S(2)}) collective-permute-start(bf16[64,896]{1,0:T(8,128)(2,1)} %fusion.8), channel_id=1, source_target_pairs={{0,96},{32,448},{64,160},{96,0},{128,224},{160,64},{192,288},{224,... | collective-permute-start | bytes 344072 | tf_op jit(solution)/shard_map/ppermute | solution.py:197
  59.5 10.4 %collective-permute-start.8 = (bf16[64,896]{1,0:T(8,128)(2,1)}, bf16[64,896]{1,0:T(8,128)(2,1)S(1)}, u32[]{:S(2)}, u32[]{:S(2)}) collective-permute-start(bf16[64,896]{1,0:T(8,128)(2,1)} %fusion.4), channel_id=1, source_target_pairs={{0,416},{32,128},{64,480},{96,192},{128,32},{160,256},{192,96},{22... | collective-permute-start | bytes 344072 | tf_op jit(solution)/shard_map/ppermute | solution.py:197
  62.9 6.9 %copy-start.3 = (bf16[8,2048]{1,0:T(8,128)(2,1)S(1)}, bf16[8,2048]{1,0:T(8,128)(2,1)}, u32[]{:S(2)}) copy-start(bf16[8,2048]{1,0:T(8,128)(2,1)} %param.5) | copy-start | bytes 98308
  64.2 21.5 %all-to-all-start.1 = ((bf16[16,8,2048]{2,1,0:T(8,128)(2,1)}), bf16[16,8,2048]{2,1,0:T(8,128)(2,1)S(1)}, u32[]{:S(2)}, u32[]{:S(2)}) async-start(bf16[16,8,2048]{2,1,0:T(8,128)(2,1)} %fusion.1), calls=%async_computation.1 | async-start | bytes 1048576 | tf_op jit(solution)/shard_map/all_to_all | solution.py:293
  70.0 13.2 %collective-permute-start.10 = (bf16[64,896]{1,0:T(8,128)(2,1)S(1)}, bf16[64,896]{1,0:T(8,128)(2,1)S(1)}, u32[]{:S(2)}, u32[]{:S(2)}) collective-permute-start(bf16[64,896]{1,0:T(8,128)(2,1)S(1)} %get-tuple-element.48), channel_id=1, source_target_pairs={{0,416},{32,128},{64,480},{96,192},{128,32},{160,256},{192,96},{22... | collective-permute-start | bytes 344072 | tf_op jit(solution)/shard_map/ppermute | solution.py:197
  76.4 8.5 %collective-permute-start.9 = (bf16[64,896]{1,0:T(8,128)(2,1)S(1)}, bf16[64,896]{1,0:T(8,128)(2,1)S(1)}, u32[]{:S(2)}, u32[]{:S(2)}) collective-permute-start(bf16[64,896]{1,0:T(8,128)(2,1)S(1)} %get-tuple-element.47), channel_id=1, source_target_pairs={{0,96},{32,448},{64,160},{96,0},{128,224},{160,64},{192,288},{224,... | collective-permute-start | bytes 344072 | tf_op jit(solution)/shard_map/ppermute | solution.py:197

commit v13 on v11

--- a/solution.py
+++ b/solution.py
@@ -53,6 +53,7 @@
     nz,
     block_rows,
     same_ref,
+    up_same_ref,
     swapped_ref,
     gain_ref,
     gate_ref,
@@ -73,7 +74,8 @@
     normed_ref[tokens:] = (normalize(swapped_ref[...])[0] * gain_ref[...]).astype(jnp.bfloat16)
     normed = normed_ref[...]
     gate_value = contract_last(normed, gate_ref[...])
-    up_value = contract_last(normed, up_ref[...])
+    up_swapped = contract_last(normed_ref[tokens:], up_ref[...])
+    up_value = jnp.concatenate([up_same_ref[...], up_swapped], axis=0)
     first = half == 0
     even = lax.axis_index("core") == 0
     count = lax.axis_size("core")
@@ -194,8 +196,9 @@
     )(*values)
 
 
-def norm_kernel(rows_ref, gain_ref, normed_ref):
+def norm_kernel(rows_ref, gain_ref, up_ref, normed_ref, value_ref):
     normed_ref[...] = (normalize(rows_ref[...])[0] * gain_ref[...]).astype(jnp.bfloat16)
+    value_ref[...] = contract_last(normed_ref[...], up_ref[...])
 
 
 def move(value, hops, nz):
@@ -218,15 +221,18 @@
     same, other = lax.optimization_barrier((same, other))
     swapped = lax.ppermute(same, "core", [(0, 1), (1, 0)])
     gain = norm_gain.reshape(1, features)
-    normed_same = pl.pallas_call(
+    normed_same, up_same = pl.pallas_call(
         norm_kernel,
-        out_shape=jax.ShapeDtypeStruct(same.shape, bf16),
+        out_shape=[
+            jax.ShapeDtypeStruct(same.shape, bf16),
+            jax.ShapeDtypeStruct((same.shape[0], width), f32),
+        ],
         cost_estimate=pl.CostEstimate(
             flops=8 * rows * features, bytes_accessed=4 * rows * features, transcendentals=rows
         ),
         compiler_params=pltpu.CompilerParams(vmem_limit_bytes=8 * 1024 * 1024),
         name="norm",
-    )(same, gain)
+    )(same, gain, up_weight.T)
     factor = float(rows * nz * nh) ** (-0.5)
     shape = jax.ShapeDtypeStruct
     wide = 2 * width
@@ -250,7 +256,7 @@
             transcendentals=nh * rows * width,
         ),
         name="local",
-    )(normed_same, swapped, gain, gate_weight.T, up_weight.T, own, other)
+    )(normed_same, up_same, swapped, gain, gate_weight.T, up_weight.T, own, other)
     inner_ahead, inner_behind, outer_hub, inner_hub, part = pl.pallas_call(
         functools.partial(rest_kernel, factor, nz),
         out_shape=[
@@ -267,7 +273,7 @@
         name="rest",
     )(normed, grads, grads_own, gate_weight.T, up_weight.T)
 
-    far_in = move(far, -2, nz)
+    from_far = move(far, -2, nz).astype(f32)
     outer_ahead, outer_behind = move(outer_ahead, 1, nz), move(outer_behind, -1, nz)
     inner_ahead, inner_behind = move(inner_ahead, 1, nz), move(inner_behind, -1, nz)
 
@@ -285,8 +291,8 @@
             + inner_behind[at, :, columns].astype(f32)
         )
 
-    plus, minus = call(
-        outer_kernel, "outer", [(depth, wide)] * 2, outer_hub, outer_ahead, outer_behind, far_in
+    plus, minus = lax.optimization_barrier(
+        (outer(0).astype(bf16), (outer(1) + from_far).astype(bf16))
     )
     part, first_sum = lax.optimization_barrier((part, plus))
     plus, minus = move(first_sum, 3, nz), move(minus, -3, nz)

time: 96.7 us -> 89.9 us (0.930)
  the two profiles are of different devices: /device:TPU:24 before, /device:TPU:1 now
where the time goes in v13:
time: 89.9 us; the launch traced here: 89.2 us
  starting transfers between devices  60.7 us (68%)
  waiting for transfers between devices  17.6 us (20%)
  Pallas kernels  5.98 us (7%)
  local copies, waits for them, and re-layouts  2.75 us (3%)
  other arithmetic  1.35 us (2%)
    ppermute x9, starting transfers between devices, move(): return lax.ppermute(value, 'z', pairs)  39.4 us
    ppermute x9, waiting for transfers between devices, move(): return lax.ppermute(value, 'z', pairs)  9.52 us
    all_to_all x1, starting transfers between devices, shards(): same = lax.all_to_all(copies, ('yh', 'x', 'yl'), 0, 0, tiled=True)  7.58 us
    ppermute x1, waiting for transfers between devices, shards(): other = lax.ppermute(own, 'yh', [(0, 1), (1, 0)])  7.39 us
    all_to_all x1, starting transfers between devices, shards(): moved = lax.all_to_all(blocks, TENSOR, 0, 0, tiled=True)  5.42 us
    ppermute x1, starting transfers between devices, shards(): other = lax.ppermute(own, 'yh', [(0, 1), (1, 0)])  4.78 us
    ppermute x1, starting transfers between devices, shards(): swapped = lax.ppermute(same, 'core', [(0, 1), (1, 0)])  3.44 us
    pallas_call x1, Pallas kernels, shards(): pl.pallas_call(functools.partial(rest_kernel, factor, nz), out_shape=[jax...  2.31 us
  transfers between devices with their start and end apart: 13, of which 4 were waited for; matrix products, arithmetic and copies ran while one was open for 2% of the time, Pallas kernels for 4%

profile of v13, /device:TPU:1, one launch (start us, length us, event | category | flops | bytes accessed | tf_op | source)
XLA Modules:
  0.0 89.2 jit_solution(9050736378224085613)
XLA Ops:
  0.6 0.0 copy-start
  0.6 0.0 copy-start.2
  0.7 1.7 %broadcast_in_dim.2 = bf16[16,8,2048]{2,1,0:T(8,128)(2,1)} broadcast(bf16[8,2048]{1,0:T(8,128)(2,1)} %param.5), dimensions={1,2} | broadcast | bytes 557056 | tf_op jit(solution)/shard_map/broadcast_in_dim | solution.py:218
  2.4 7.6 %all-to-all-start = ((bf16[16,8,2048]{2,1,0:T(8,128)(2,1)}), bf16[16,8,2048]{2,1,0:T(8,128)(2,1)S(1)}, u32[]{:S(2)}, u32[]{:S(2)}) async-start(bf16[16,8,2048]{2,1,0:T(8,128)(2,1)} %broadcast_in_dim.2), calls=%async_computation | async-start | bytes 1048576 | tf_op jit(solution)/shard_map/all_to_all | solution.py:219
  10.0 1.0 %copy.8.own_ref = bf16[128,448]{1,0:T(8,128)(2,1)S(1)} copy(bf16[128,448]{0,1:T(8,128)(2,1)} %param.9) | data formatting | bytes 229376 | tf_op args[4]
  11.0 4.8 %collective-permute-start = (bf16[128,448]{1,0:T(8,128)(2,1)S(1)}, bf16[128,448]{1,0:T(8,128)(2,1)S(1)}, u32[]{:S(2)}, u32[]{:S(2)}) collective-permute-start(bf16[128,448]{1,0:T(8,128)(2,1)S(1)} %copy.8.own_ref), channel_id=1, source_target_pairs={{0,16},{16,0},{1,17},{17,1},{2,18},{18,2},{3,19},{19,3},{4,20},{20... | collective-permute-start | bytes 344072 | tf_op jit(solution)/shard_map/ppermute | solution.py:216
  15.8 7.4 %collective-permute-done.other_ref = bf16[128,448]{1,0:T(8,128)(2,1)S(1)} collective-permute-done((bf16[128,448]{1,0:T(8,128)(2,1)S(1)}, bf16[128,448]{1,0:T(8,128)(2,1)S(1)}, u32[]{:S(2)}, u32[]{:S(2)}) %collective-permute-start) | collective-permute-done | bytes 114720 | tf_op jit(solution)/shard_map/ppermute | solution.py:216
  23.2 0.0 all-to-all-done
  23.2 0.0 copy-start.1
  23.2 3.4 %collective-permute-start.1 = (bf16[128,2048]{1,0:T(8,128)(2,1)S(1)}, bf16[128,2048]{1,0:T(8,128)(2,1)S(1)}, u32[]{:S(2)}, u32[]{:S(2)}) collective-permute-start(bf16[128,2048]{1,0:T(8,128)(2,1)S(1)} %bitcast.24), channel_id=1, source_target_pairs={{0,1},{1,0},{2,3},{3,2},{4,5},{5,4},{6,7},{7,6},{8,9},{9,8},{10,11... | collective-permute-start | bytes 1572872 | tf_op jit(solution)/shard_map/ppermute | solution.py:222
  26.6 0.0 copy-done
  26.6 0.0 copy-done.2
  26.6 0.8 norm.1
  27.4 0.7 collective-permute-done.1.swapped_ref
  28.1 0.0 copy-done.1
  28.1 2.1 %local.1 = (bf16[64,896]{1,0:T(8,128)(2,1)S(1)}, bf16[2,64,896]{2,1,0:T(8,128)(2,1)S(1)}, bf16[2,64,896]{2,1,0:T(8,128)(2,1)S(1)}, bf16[128,896]{1,0:T(8,128)(2,...) custom-call(bf16[128,2048]{1,0:T(8,128)(2,1)S(1)} %get-tuple-element.29.same_ref, ...), custom_call_target="tpu_custom_call" | custom-call | flops 1409286144 | bytes 7340032 | tf_op jit(solution)/shard_map/local/pallas_call | solution.py:239
  30.3 3.0 %collective-permute-start.2 = (bf16[2,64,896]{2,1,0:T(8,128)(2,1)S(1)}, bf16[2,64,896]{2,1,0:T(8,128)(2,1)S(1)}, u32[]{:S(2)}, u32[]{:S(2)}) collective-permute-start(bf16[2,64,896]{2,1,0:T(8,128)(2,1)S(1)} %get-tuple-element.37), channel_id=1, source_target_pairs={{0,32},{32,0},{64,96},{96,64},{128,160},{160,128},{192,224},{224,1... | collective-permute-start | bytes 688136 | tf_op jit(solution)/shard_map/ppermute | solution.py:206
  33.3 10.2 %collective-permute-start.3 = (bf16[2,64,896]{2,1,0:T(8,128)(2,1)S(1)}, bf16[2,64,896]{2,1,0:T(8,128)(2,1)S(1)}, u32[]{:S(2)}, u32[]{:S(2)}) collective-permute-start(bf16[2,64,896]{2,1,0:T(8,128)(2,1)S(1)} %get-tuple-element.38), channel_id=1, source_target_pairs={{0,480},{32,64},{64,32},{96,128},{128,96},{160,192},{192,160},{224... | collective-permute-start | bytes 688136 | tf_op jit(solution)/shard_map/ppermute | solution.py:206
  43.5 3.1 %collective-permute-start.4 = (bf16[64,896]{1,0:T(8,128)(2,1)S(1)}, bf16[64,896]{1,0:T(8,128)(2,1)S(1)}, u32[]{:S(2)}, u32[]{:S(2)}) collective-permute-start(bf16[64,896]{1,0:T(8,128)(2,1)S(1)} %get-tuple-element.39), channel_id=1, source_target_pairs={{0,448},{32,96},{64,0},{96,160},{128,64},{160,224},{192,128},{224,... | collective-permute-start | bytes 344072 | tf_op jit(solution)/shard_map/ppermute | solution.py:206
  46.6 2.3 %rest.1 = (bf16[3,64,896]{2,1,0:T(8,128)(2,1)S(1)}, bf16[3,64,896]{2,1,0:T(8,128)(2,1)S(1)}, bf16[2,64,896]{2,1,0:T(8,128)(2,1)S(1)}, bf16[3,64,896]{2,1,0:T(8,128)(2,1)S(1)}, bf16[128,2048]{1,0:T(8,128)(2,1)}) custom-call(bf16[256,2048]{1,0:T(8,128)(2,1)S(1)} %get-tuple-element.32.normed_ref, bf16[256,896]{1,0:T(8,128)(2,1)S(1)} %get-tuple-element.33.grads_ref, ...), custom_call_target="tpu_custom_call" | custom-call | flops 1409286144 | bytes 4194304 | tf_op jit(solution)/shard_map/rest/pallas_call | solution.py:260
  48.9 0.0 copy-start.3
  48.9 2.0 %collective-permute-start.5 = (bf16[3,64,896]{2,1,0:T(8,128)(2,1)S(1)}, bf16[3,64,896]{2,1,0:T(8,128)(2,1)S(1)}, u32[]{:S(2)}, u32[]{:S(2)}) collective-permute-start(bf16[3,64,896]{2,1,0:T(8,128)(2,1)S(1)} %get-tuple-element.43), channel_id=1, source_target_pairs={{0,32},{32,0},{64,96},{96,64},{128,160},{160,128},{192,224},{224,1... | collective-permute-start | bytes 1032200 | tf_op jit(solution)/shard_map/ppermute | solution.py:206
  51.0 4.6 %collective-permute-start.6 = (bf16[3,64,896]{2,1,0:T(8,128)(2,1)S(1)}, bf16[3,64,896]{2,1,0:T(8,128)(2,1)S(1)}, u32[]{:S(2)}, u32[]{:S(2)}) collective-permute-start(bf16[3,64,896]{2,1,0:T(8,128)(2,1)S(1)} %get-tuple-element.44), channel_id=1, source_target_pairs={{0,480},{32,64},{64,32},{96,128},{128,96},{160,192},{192,160},{224... | collective-permute-start | bytes 1032200 | tf_op jit(solution)/shard_map/ppermute | solution.py:206
  55.6 0.0 collective-permute-done.4
  55.6 0.0 collective-permute-done.2
  55.6 0.0 collective-permute-done.3
  55.6 0.1 fusion.2
  55.7 0.1 fusion.3
  55.7 3.5 %collective-permute-start.7 = (bf16[64,896]{1,0:T(8,128)(2,1)S(1)}, bf16[64,896]{1,0:T(8,128)(2,1)S(1)}, u32[]{:S(2)}, u32[]{:S(2)}) collective-permute-start(bf16[64,896]{1,0:T(8,128)(2,1)S(1)} %fusion.3), channel_id=1, source_target_pairs={{0,96},{32,448},{64,160},{96,0},{128,224},{160,64},{192,288},{224,... | collective-permute-start | bytes 344072 | tf_op jit(solution)/shard_map/ppermute | solution.py:206
  59.3 2.9 %collective-permute-start.8 = (bf16[64,896]{1,0:T(8,128)(2,1)S(1)}, bf16[64,896]{1,0:T(8,128)(2,1)S(1)}, u32[]{:S(2)}, u32[]{:S(2)}) collective-permute-start(bf16[64,896]{1,0:T(8,128)(2,1)S(1)} %fusion.2), channel_id=1, source_target_pairs={{0,416},{32,128},{64,480},{96,192},{128,32},{160,256},{192,96},{22... | collective-permute-start | bytes 344072 | tf_op jit(solution)/shard_map/ppermute | solution.py:206
  62.1 5.4 %all-to-all-start.1 = ((bf16[16,8,2048]{2,1,0:T(8,128)(2,1)}), bf16[16,8,2048]{2,1,0:T(8,128)(2,1)S(1)}, u32[]{:S(2)}, u32[]{:S(2)}) async-start(bf16[16,8,2048]{2,1,0:T(8,128)(2,1)} %bitcast.6), calls=%async_computation.1 | async-start | bytes 1048576 | tf_op jit(solution)/shard_map/all_to_all | solution.py:301
  67.6 0.0 copy-done.3
  67.6 0.1 fusion.10
  67.7 0.0 collective-permute-done.7
  67.7 1.5 %collective-permute-done.8 = bf16[64,896]{1,0:T(8,128)(2,1)S(1)} collective-permute-done((bf16[64,896]{1,0:T(8,128)(2,1)S(1)}, bf16[64,896]{1,0:T(8,128)(2,1)S(1)}, u32[]{:S(2)}, u32[]{:S(2)}) %collective-permute-start.8) | collective-permute-done | bytes 114720 | tf_op jit(solution)/shard_map/ppermute | solution.py:206
  69.2 0.0 collective-permute-done.5.ahead_ref
  69.2 0.0 collective-permute-done.6.behind_ref
  69.2 0.1 fusion
  69.3 6.5 %collective-permute-start.10 = (bf16[64,896]{1,0:T(8,128)(2,1)S(1)}, bf16[64,896]{1,0:T(8,128)(2,1)S(1)}, u32[]{:S(2)}, u32[]{:S(2)}) collective-permute-start(bf16[64,896]{1,0:T(8,128)(2,1)S(1)} %get-tuple-element.50), channel_id=1, source_target_pairs={{0,416},{32,128},{64,480},{96,192},{128,32},{160,256},{192,96},{22... | collective-permute-start | bytes 344072 | tf_op jit(solution)/shard_map/ppermute | solution.py:206
  75.9 3.6 %collective-permute-start.9 = (bf16[64,896]{1,0:T(8,128)(2,1)S(1)}, bf16[64,896]{1,0:T(8,128)(2,1)S(1)}, u32[]{:S(2)}, u32[]{:S(2)}) collective-permute-start(bf16[64,896]{1,0:T(8,128)(2,1)S(1)} %get-tuple-element.49), channel_id=1, source_target_pairs={{0,96},{32,448},{64,160},{96,0},{128,224},{160,64},{192,288},{224,... | collective-permute-start | bytes 344072 | tf_op jit(solution)/shard_map/ppermute | solution.py:206
  79.5 0.0 collective-permute-done.10.minus_ref
  79.5 8.0 %collective-permute-done.9.plus_ref = bf16[64,896]{1,0:T(8,128)(2,1)S(1)} collective-permute-done((bf16[64,896]{1,0:T(8,128)(2,1)S(1)}, bf16[64,896]{1,0:T(8,128)(2,1)S(1)}, u32[]{:S(2)}, u32[]{:S(2)}) %collective-permute-start.9) | collective-permute-done | bytes 114720 | tf_op jit(solution)/shard_map/ppermute | solution.py:206
  87.5 0.8 total.1
  88.2 0.0 all-to-all-done.1
  88.2 0.1 convert_reduce_fusion
  88.3 0.2 fusion.6
  88.5 0.7 fusion.9
  (2 shorter events, 0.0 us)
Async XLA Ops:
  0.6 26.0 %copy-start = (bf16[2048,448]{0,1:T(8,128)(2,1)S(1)}, bf16[2048,448]{0,1:T(8,128)(2,1)}, u32[]{:S(2)}) copy-start(bf16[2048,448]{0,1:T(8,128)(2,1)} %param.8) | copy-start | bytes 5505028
  0.6 26.0 %copy-start.2 = (f32[2048]{0:T(1024)S(1)}, f32[2048]{0:T(1024)}, u32[]{:S(2)}) copy-start(f32[2048]{0:T(1024)} %param.6) | copy-start | bytes 24580
  2.4 20.8 %all-to-all-start = ((bf16[16,8,2048]{2,1,0:T(8,128)(2,1)}), bf16[16,8,2048]{2,1,0:T(8,128)(2,1)S(1)}, u32[]{:S(2)}, u32[]{:S(2)}) async-start(bf16[16,8,2048]{2,1,0:T(8,128)(2,1)} %broadcast_in_dim.2), calls=%async_computation | async-start | bytes 1048576 | tf_op jit(solution)/shard_map/all_to_all | solution.py:219
  11.0 12.2 %collective-permute-start = (bf16[128,448]{1,0:T(8,128)(2,1)S(1)}, bf16[128,448]{1,0:T(8,128)(2,1)S(1)}, u32[]{:S(2)}, u32[]{:S(2)}) collective-permute-start(bf16[128,448]{1,0:T(8,128)(2,1)S(1)} %copy.8.own_ref), channel_id=1, source_target_pairs={{0,16},{16,0},{1,17},{17,1},{2,18},{18,2},{3,19},{19,3},{4,20},{20... | collective-permute-start | bytes 344072 | tf_op jit(solution)/shard_map/ppermute | solution.py:216
  23.2 5.0 %copy-start.1 = (bf16[2048,448]{0,1:T(8,128)(2,1)S(1)}, bf16[2048,448]{0,1:T(8,128)(2,1)}, u32[]{:S(2)}) copy-start(bf16[2048,448]{0,1:T(8,128)(2,1)} %param.7) | copy-start | bytes 5505028
  23.2 5.0 %collective-permute-start.1 = (bf16[128,2048]{1,0:T(8,128)(2,1)S(1)}, bf16[128,2048]{1,0:T(8,128)(2,1)S(1)}, u32[]{:S(2)}, u32[]{:S(2)}) collective-permute-start(bf16[128,2048]{1,0:T(8,128)(2,1)S(1)} %bitcast.24), channel_id=1, source_target_pairs={{0,1},{1,0},{2,3},{3,2},{4,5},{5,4},{6,7},{7,6},{8,9},{9,8},{10,11... | collective-permute-start | bytes 1572872 | tf_op jit(solution)/shard_map/ppermute | solution.py:222
  30.3 25.3 %collective-permute-start.2 = (bf16[2,64,896]{2,1,0:T(8,128)(2,1)S(1)}, bf16[2,64,896]{2,1,0:T(8,128)(2,1)S(1)}, u32[]{:S(2)}, u32[]{:S(2)}) collective-permute-start(bf16[2,64,896]{2,1,0:T(8,128)(2,1)S(1)} %get-tuple-element.37), channel_id=1, source_target_pairs={{0,32},{32,0},{64,96},{96,64},{128,160},{160,128},{192,224},{224,1... | collective-permute-start | bytes 688136 | tf_op jit(solution)/shard_map/ppermute | solution.py:206
  33.3 22.3 %collective-permute-start.3 = (bf16[2,64,896]{2,1,0:T(8,128)(2,1)S(1)}, bf16[2,64,896]{2,1,0:T(8,128)(2,1)S(1)}, u32[]{:S(2)}, u32[]{:S(2)}) collective-permute-start(bf16[2,64,896]{2,1,0:T(8,128)(2,1)S(1)} %get-tuple-element.38), channel_id=1, source_target_pairs={{0,480},{32,64},{64,32},{96,128},{128,96},{160,192},{192,160},{224... | collective-permute-start | bytes 688136 | tf_op jit(solution)/shard_map/ppermute | solution.py:206
  43.5 12.0 %collective-permute-start.4 = (bf16[64,896]{1,0:T(8,128)(2,1)S(1)}, bf16[64,896]{1,0:T(8,128)(2,1)S(1)}, u32[]{:S(2)}, u32[]{:S(2)}) collective-permute-start(bf16[64,896]{1,0:T(8,128)(2,1)S(1)} %get-tuple-element.39), channel_id=1, source_target_pairs={{0,448},{32,96},{64,0},{96,160},{128,64},{160,224},{192,128},{224,... | collective-permute-start | bytes 344072 | tf_op jit(solution)/shard_map/ppermute | solution.py:206
  48.9 18.6 %copy-start.3 = (bf16[8,2048]{1,0:T(8,128)(2,1)S(1)}, bf16[8,2048]{1,0:T(8,128)(2,1)}, u32[]{:S(2)}) copy-start(bf16[8,2048]{1,0:T(8,128)(2,1)} %param.5) | copy-start | bytes 98308
  48.9 20.3 %collective-permute-start.5 = (bf16[3,64,896]{2,1,0:T(8,128)(2,1)S(1)}, bf16[3,64,896]{2,1,0:T(8,128)(2,1)S(1)}, u32[]{:S(2)}, u32[]{:S(2)}) collective-permute-start(bf16[3,64,896]{2,1,0:T(8,128)(2,1)S(1)} %get-tuple-element.43), channel_id=1, source_target_pairs={{0,32},{32,0},{64,96},{96,64},{128,160},{160,128},{192,224},{224,1... | collective-permute-start | bytes 1032200 | tf_op jit(solution)/shard_map/ppermute | solution.py:206
  51.0 18.2 %collective-permute-start.6 = (bf16[3,64,896]{2,1,0:T(8,128)(2,1)S(1)}, bf16[3,64,896]{2,1,0:T(8,128)(2,1)S(1)}, u32[]{:S(2)}, u32[]{:S(2)}) collective-permute-start(bf16[3,64,896]{2,1,0:T(8,128)(2,1)S(1)} %get-tuple-element.44), channel_id=1, source_target_pairs={{0,480},{32,64},{64,32},{96,128},{128,96},{160,192},{192,160},{224... | collective-permute-start | bytes 1032200 | tf_op jit(solution)/shard_map/ppermute | solution.py:206
  55.7 12.0 %collective-permute-start.7 = (bf16[64,896]{1,0:T(8,128)(2,1)S(1)}, bf16[64,896]{1,0:T(8,128)(2,1)S(1)}, u32[]{:S(2)}, u32[]{:S(2)}) collective-permute-start(bf16[64,896]{1,0:T(8,128)(2,1)S(1)} %fusion.3), channel_id=1, source_target_pairs={{0,96},{32,448},{64,160},{96,0},{128,224},{160,64},{192,288},{224,... | collective-permute-start | bytes 344072 | tf_op jit(solution)/shard_map/ppermute | solution.py:206
  59.3 9.9 %collective-permute-start.8 = (bf16[64,896]{1,0:T(8,128)(2,1)S(1)}, bf16[64,896]{1,0:T(8,128)(2,1)S(1)}, u32[]{:S(2)}, u32[]{:S(2)}) collective-permute-start(bf16[64,896]{1,0:T(8,128)(2,1)S(1)} %fusion.2), channel_id=1, source_target_pairs={{0,416},{32,128},{64,480},{96,192},{128,32},{160,256},{192,96},{22... | collective-permute-start | bytes 344072 | tf_op jit(solution)/shard_map/ppermute | solution.py:206
  62.1 26.1 %all-to-all-start.1 = ((bf16[16,8,2048]{2,1,0:T(8,128)(2,1)}), bf16[16,8,2048]{2,1,0:T(8,128)(2,1)S(1)}, u32[]{:S(2)}, u32[]{:S(2)}) async-start(bf16[16,8,2048]{2,1,0:T(8,128)(2,1)} %bitcast.6), calls=%async_computation.1 | async-start | bytes 1048576 | tf_op jit(solution)/shard_map/all_to_all | solution.py:301
  69.3 10.1 %collective-permute-start.10 = (bf16[64,896]{1,0:T(8,128)(2,1)S(1)}, bf16[64,896]{1,0:T(8,128)(2,1)S(1)}, u32[]{:S(2)}, u32[]{:S(2)}) collective-permute-start(bf16[64,896]{1,0:T(8,128)(2,1)S(1)} %get-tuple-element.50), channel_id=1, source_target_pairs={{0,416},{32,128},{64,480},{96,192},{128,32},{160,256},{192,96},{22... | collective-permute-start | bytes 344072 | tf_op jit(solution)/shard_map/ppermute | solution.py:206
  75.9 11.6 %collective-permute-start.9 = (bf16[64,896]{1,0:T(8,128)(2,1)S(1)}, bf16[64,896]{1,0:T(8,128)(2,1)S(1)}, u32[]{:S(2)}, u32[]{:S(2)}) collective-permute-start(bf16[64,896]{1,0:T(8,128)(2,1)S(1)} %get-tuple-element.49), channel_id=1, source_target_pairs={{0,96},{32,448},{64,160},{96,0},{128,224},{160,64},{192,288},{224,... | collective-permute-start | bytes 344072 | tf_op jit(solution)/shard_map/ppermute | solution.py:206

commit v14 on v12

--- a/solution.py
+++ b/solution.py
@@ -264,6 +264,7 @@
     )(normed, grads)
 
     from_far = move(far, -2, nz).astype(f32)
+    base = lax.optimization_barrier(outer_hub[1].astype(f32) + from_far)
     outer_ahead, outer_behind = move(outer_ahead, 1, nz), move(outer_behind, -1, nz)
     inner_ahead, inner_behind = move(inner_ahead, 1, nz), move(inner_behind, -1, nz)
 
@@ -282,7 +283,10 @@
         )
 
     plus, minus = lax.optimization_barrier(
-        (outer(0).astype(bf16), (outer(1) + from_far).astype(bf16))
+        (
+            outer(0).astype(bf16),
+            (base + outer_ahead[1].astype(f32) + outer_behind[1].astype(f32)).astype(bf16),
+        )
     )
     grads_own, first_sum = lax.optimization_barrier((grads_own, plus))
     plus, minus = move(first_sum, 3, nz), move(minus, -3, nz)

time: 88.1 us -> 88.9 us (level)
  starting transfers between devices: 59.7 us -> 60.7 us
    ppermute x9, starting transfers between devices: 38.3 us -> 39.5 us  [move(): return lax.ppermute(value, 'z', pairs)]
where the time goes in v14:
time: 88.9 us; the launch traced here: 87.8 us
  starting transfers between devices  60.7 us (68%)
  waiting for transfers between devices  14 us (16%)
  Pallas kernels  5.07 us (6%)
  local copies, waits for them, and re-layouts  2.75 us (3%)
  other arithmetic  2.63 us (3%)
  matrix products  1.71 us (2%)
    ppermute x9, starting transfers between devices, move(): return lax.ppermute(value, 'z', pairs)  39.5 us
    all_to_all x1, starting transfers between devices, shards(): same = lax.all_to_all(copies, ('yh', 'x', 'yl'), 0, 0, tiled=True)  7.58 us
    ppermute x1, waiting for transfers between devices, shards(): other = lax.ppermute(own, 'yh', [(0, 1), (1, 0)])  7.39 us
    ppermute x9, waiting for transfers between devices, move(): return lax.ppermute(value, 'z', pairs)  5.93 us
    all_to_all x1, starting transfers between devices, shards(): moved = lax.all_to_all(blocks, TENSOR, 0, 0, tiled=True)  5.4 us
    ppermute x1, starting transfers between devices, shards(): other = lax.ppermute(own, 'yh', [(0, 1), (1, 0)])  4.78 us
    ppermute x1, starting transfers between devices, shards(): swapped = lax.ppermute(same, 'core', [(0, 1), (1, 0)])  3.44 us
    pallas_call x1, Pallas kernels, shards(): pl.pallas_call(functools.partial(local_kernel, factor, nz, residual.shape...  2.19 us
  transfers between devices with their start and end apart: 13, of which 4 were waited for; matrix products, arithmetic and copies ran while one was open for 5% of the time, Pallas kernels for 3%

profile of v14, /device:TPU:1, one launch (start us, length us, event | category | flops | bytes accessed | tf_op | source)
XLA Modules:
  0.0 87.8 jit_solution(12833616041550816626)
XLA Ops:
  0.6 0.0 copy-start.2
  0.6 0.0 copy-start
  0.7 1.7 %broadcast_in_dim.2 = bf16[16,8,2048]{2,1,0:T(8,128)(2,1)} broadcast(bf16[8,2048]{1,0:T(8,128)(2,1)} %param.5), dimensions={1,2} | broadcast | bytes 557056 | tf_op jit(solution)/shard_map/broadcast_in_dim | solution.py:209
  2.4 7.6 %all-to-all-start = ((bf16[16,8,2048]{2,1,0:T(8,128)(2,1)}), bf16[16,8,2048]{2,1,0:T(8,128)(2,1)S(1)}, u32[]{:S(2)}, u32[]{:S(2)}) async-start(bf16[16,8,2048]{2,1,0:T(8,128)(2,1)} %broadcast_in_dim.2), calls=%async_computation | async-start | bytes 1048576 | tf_op jit(solution)/shard_map/all_to_all | solution.py:210
  10.0 1.0 %copy.8.own_ref = bf16[128,448]{1,0:T(8,128)(2,1)S(1)} copy(bf16[128,448]{0,1:T(8,128)(2,1)} %param.9) | data formatting | bytes 229376 | tf_op args[4]
  11.0 4.8 %collective-permute-start = (bf16[128,448]{1,0:T(8,128)(2,1)S(1)}, bf16[128,448]{1,0:T(8,128)(2,1)S(1)}, u32[]{:S(2)}, u32[]{:S(2)}) collective-permute-start(bf16[128,448]{1,0:T(8,128)(2,1)S(1)} %copy.8.own_ref), channel_id=1, source_target_pairs={{0,16},{16,0},{1,17},{17,1},{2,18},{18,2},{3,19},{19,3},{4,20},{20... | collective-permute-start | bytes 344072 | tf_op jit(solution)/shard_map/ppermute | solution.py:207
  15.8 7.4 %collective-permute-done.other_ref = bf16[128,448]{1,0:T(8,128)(2,1)S(1)} collective-permute-done((bf16[128,448]{1,0:T(8,128)(2,1)S(1)}, bf16[128,448]{1,0:T(8,128)(2,1)S(1)}, u32[]{:S(2)}, u32[]{:S(2)}) %collective-permute-start) | collective-permute-done | bytes 114720 | tf_op jit(solution)/shard_map/ppermute | solution.py:207
  23.2 0.0 all-to-all-done
  23.2 0.0 copy-start.1
  23.2 3.4 %collective-permute-start.1 = (bf16[128,2048]{1,0:T(8,128)(2,1)S(1)}, bf16[128,2048]{1,0:T(8,128)(2,1)S(1)}, u32[]{:S(2)}, u32[]{:S(2)}) collective-permute-start(bf16[128,2048]{1,0:T(8,128)(2,1)S(1)} %bitcast.34), channel_id=1, source_target_pairs={{0,1},{1,0},{2,3},{3,2},{4,5},{5,4},{6,7},{7,6},{8,9},{9,8},{10,11... | collective-permute-start | bytes 1572872 | tf_op jit(solution)/shard_map/ppermute | solution.py:213
  26.6 0.0 copy-done.2
  26.6 0.0 copy-done
  26.6 0.8 norm.1
  27.4 0.7 collective-permute-done.1.swapped_ref
  28.1 0.0 copy-done.1
  28.1 2.2 %local.1 = (bf16[64,896]{1,0:T(8,128)(2,1)S(1)}, bf16[2,64,896]{2,1,0:T(8,128)(2,1)S(1)}, bf16[2,64,896]{2,1,0:T(8,128)(2,1)S(1)}, bf16[128,896]{1,0:T(8,128)(2,...) custom-call(bf16[128,2048]{1,0:T(8,128)(2,1)S(1)} %get-tuple-element.28.same_ref, ...), custom_call_target="tpu_custom_call" | custom-call | flops 1409286144 | bytes 7340032 | tf_op jit(solution)/shard_map/local/pallas_call | solution.py:230
  30.3 11.1 %collective-permute-start.4 = (bf16[64,896]{1,0:T(8,128)(2,1)S(1)}, bf16[64,896]{1,0:T(8,128)(2,1)S(1)}, u32[]{:S(2)}, u32[]{:S(2)}) collective-permute-start(bf16[64,896]{1,0:T(8,128)(2,1)S(1)} %get-tuple-element.37), channel_id=1, source_target_pairs={{0,448},{32,96},{64,0},{96,160},{128,64},{160,224},{192,128},{224,... | collective-permute-start | bytes 344072 | tf_op jit(solution)/shard_map/ppermute | solution.py:197
  41.4 1.9 %collective-permute-start.2 = (bf16[2,64,896]{2,1,0:T(8,128)(2,1)S(1)}, bf16[2,64,896]{2,1,0:T(8,128)(2,1)S(1)}, u32[]{:S(2)}, u32[]{:S(2)}) collective-permute-start(bf16[2,64,896]{2,1,0:T(8,128)(2,1)S(1)} %get-tuple-element.35), channel_id=1, source_target_pairs={{0,32},{32,0},{64,96},{96,64},{128,160},{160,128},{192,224},{224,1... | collective-permute-start | bytes 688136 | tf_op jit(solution)/shard_map/ppermute | solution.py:197
  43.3 3.4 %collective-permute-start.3 = (bf16[2,64,896]{2,1,0:T(8,128)(2,1)S(1)}, bf16[2,64,896]{2,1,0:T(8,128)(2,1)S(1)}, u32[]{:S(2)}, u32[]{:S(2)}) collective-permute-start(bf16[2,64,896]{2,1,0:T(8,128)(2,1)S(1)} %get-tuple-element.36), channel_id=1, source_target_pairs={{0,480},{32,64},{64,32},{96,128},{128,96},{160,192},{192,160},{224... | collective-permute-start | bytes 688136 | tf_op jit(solution)/shard_map/ppermute | solution.py:197
  46.7 1.3 %rest.1 = (bf16[3,64,896]{2,1,0:T(8,128)(2,1)}, bf16[3,64,896]{2,1,0:T(8,128)(2,1)S(1)}, bf16[2,64,896]{2,1,0:T(8,128)(2,1)S(1)}, bf16[3,64,896]{2,1,0:T(8,128)(2,1)S(1)}) custom-call(bf16[256,2048]{1,0:T(8,128)(2,1)S(1)} %get-tuple-element.32.normed_ref, bf16[256,896]{1,0:T(8,128)(2,1)S(1)} %get-tuple-element.33.grads_ref), custom_call_target="tpu_custom_call" | custom-call | flops 939524096 | bytes 2097152 | tf_op jit(solution)/shard_map/rest/pallas_call | solution.py:251
  48.0 1.9 %collective-permute-start.5 = (bf16[3,64,896]{2,1,0:T(8,128)(2,1)}, bf16[3,64,896]{2,1,0:T(8,128)(2,1)S(1)}, u32[]{:S(2)}, u32[]{:S(2)}) collective-permute-start(bf16[3,64,896]{2,1,0:T(8,128)(2,1)} %get-tuple-element.41), channel_id=1, source_target_pairs={{0,32},{32,0},{64,96},{96,64},{128,160},{160,128},{192,224},{224,1... | collective-permute-start | bytes 1032200 | tf_op jit(solution)/shard_map/ppermute | solution.py:197
  50.0 4.5 %collective-permute-start.6 = (bf16[3,64,896]{2,1,0:T(8,128)(2,1)S(1)}, bf16[3,64,896]{2,1,0:T(8,128)(2,1)S(1)}, u32[]{:S(2)}, u32[]{:S(2)}) collective-permute-start(bf16[3,64,896]{2,1,0:T(8,128)(2,1)S(1)} %get-tuple-element.42), channel_id=1, source_target_pairs={{0,480},{32,64},{64,32},{96,128},{128,96},{160,192},{192,160},{224... | collective-permute-start | bytes 1032200 | tf_op jit(solution)/shard_map/ppermute | solution.py:197
  54.5 0.0 collective-permute-done.4
  54.6 0.0 collective-permute-done.2
  54.6 0.0 collective-permute-done.3
  54.6 0.7 fusion.8
  55.3 0.7 fusion.2
  55.9 3.5 %collective-permute-start.7 = (bf16[64,896]{1,0:T(8,128)(2,1)}, bf16[64,896]{1,0:T(8,128)(2,1)S(1)}, u32[]{:S(2)}, u32[]{:S(2)}) collective-permute-start(bf16[64,896]{1,0:T(8,128)(2,1)} %fusion.8), channel_id=1, source_target_pairs={{0,96},{32,448},{64,160},{96,0},{128,224},{160,64},{192,288},{224,... | collective-permute-start | bytes 344072 | tf_op jit(solution)/shard_map/ppermute | solution.py:197
  59.5 4.0 %collective-permute-start.8 = (bf16[64,896]{1,0:T(8,128)(2,1)}, bf16[64,896]{1,0:T(8,128)(2,1)S(1)}, u32[]{:S(2)}, u32[]{:S(2)}) collective-permute-start(bf16[64,896]{1,0:T(8,128)(2,1)} %fusion.2), channel_id=1, source_target_pairs={{0,416},{32,128},{64,480},{96,192},{128,32},{160,256},{192,96},{22... | collective-permute-start | bytes 344072 | tf_op jit(solution)/shard_map/ppermute | solution.py:197
  63.5 0.4 fusion.6
  64.0 0.0 copy-start.3
  64.0 1.3 %fusion.1 = bf16[16,8,2048]{2,1,0:T(8,128)(2,1)} fusion(f32[128,2048]{1,0:T(8,128)S(1)} %fusion.6, bf16[2048,448]{0,1:T(8,128)(2,1)S(1)} %copy-done, bf16[128,896]{1,0:T(8,128)(2,1)S(1)} %get-tuple-element.39), kind=kOutput, calls=%fused_computation.2 | convolution fusion | flops 235405312 | bytes 3538944 | tf_op jit(solution)/shard_map/dot_general | solution.py:25
  65.3 5.4 %all-to-all-start.1 = ((bf16[16,8,2048]{2,1,0:T(8,128)(2,1)}), bf16[16,8,2048]{2,1,0:T(8,128)(2,1)S(1)}, u32[]{:S(2)}, u32[]{:S(2)}) async-start(bf16[16,8,2048]{2,1,0:T(8,128)(2,1)} %fusion.1), calls=%async_computation.1 | async-start | bytes 1048576 | tf_op jit(solution)/shard_map/all_to_all | solution.py:297
  70.7 0.0 copy-done.3
  70.7 0.1 fusion.15
  70.8 0.0 collective-permute-done.7
  70.8 0.0 collective-permute-done.8
  70.8 0.0 collective-permute-done.5.ahead_ref
  70.8 0.0 collective-permute-done.6.behind_ref
  70.8 0.1 fusion.3
  71.0 5.2 %collective-permute-start.10 = (bf16[64,896]{1,0:T(8,128)(2,1)S(1)}, bf16[64,896]{1,0:T(8,128)(2,1)S(1)}, u32[]{:S(2)}, u32[]{:S(2)}) collective-permute-start(bf16[64,896]{1,0:T(8,128)(2,1)S(1)} %get-tuple-element.48), channel_id=1, source_target_pairs={{0,416},{32,128},{64,480},{96,192},{128,32},{160,256},{192,96},{22... | collective-permute-start | bytes 344072 | tf_op jit(solution)/shard_map/ppermute | solution.py:197
  76.2 3.9 %collective-permute-start.9 = (bf16[64,896]{1,0:T(8,128)(2,1)S(1)}, bf16[64,896]{1,0:T(8,128)(2,1)S(1)}, u32[]{:S(2)}, u32[]{:S(2)}) collective-permute-start(bf16[64,896]{1,0:T(8,128)(2,1)S(1)} %get-tuple-element.47), channel_id=1, source_target_pairs={{0,96},{32,448},{64,160},{96,0},{128,224},{160,64},{192,288},{224,... | collective-permute-start | bytes 344072 | tf_op jit(solution)/shard_map/ppermute | solution.py:197
  80.1 0.5 collective-permute-done.10.minus_ref
  80.7 5.4 %collective-permute-done.9.plus_ref = bf16[64,896]{1,0:T(8,128)(2,1)S(1)} collective-permute-done((bf16[64,896]{1,0:T(8,128)(2,1)S(1)}, bf16[64,896]{1,0:T(8,128)(2,1)S(1)}, u32[]{:S(2)}, u32[]{:S(2)}) %collective-permute-start.9) | collective-permute-done | bytes 114720 | tf_op jit(solution)/shard_map/ppermute | solution.py:197
  86.1 0.8 total.1
  86.8 0.0 all-to-all-done.1
  86.8 0.1 convert_reduce_fusion
  86.9 0.2 fusion.11
  87.1 0.7 fusion.14
  (3 shorter events, 0.0 us)
Async XLA Ops:
  0.6 26.0 %copy-start.2 = (f32[2048]{0:T(1024)S(1)}, f32[2048]{0:T(1024)}, u32[]{:S(2)}) copy-start(f32[2048]{0:T(1024)} %param.6) | copy-start | bytes 24580
  0.6 26.0 %copy-start = (bf16[2048,448]{0,1:T(8,128)(2,1)S(1)}, bf16[2048,448]{0,1:T(8,128)(2,1)}, u32[]{:S(2)}) copy-start(bf16[2048,448]{0,1:T(8,128)(2,1)} %param.8) | copy-start | bytes 5505028
  2.4 20.8 %all-to-all-start = ((bf16[16,8,2048]{2,1,0:T(8,128)(2,1)}), bf16[16,8,2048]{2,1,0:T(8,128)(2,1)S(1)}, u32[]{:S(2)}, u32[]{:S(2)}) async-start(bf16[16,8,2048]{2,1,0:T(8,128)(2,1)} %broadcast_in_dim.2), calls=%async_computation | async-start | bytes 1048576 | tf_op jit(solution)/shard_map/all_to_all | solution.py:210
  11.0 12.2 %collective-permute-start = (bf16[128,448]{1,0:T(8,128)(2,1)S(1)}, bf16[128,448]{1,0:T(8,128)(2,1)S(1)}, u32[]{:S(2)}, u32[]{:S(2)}) collective-permute-start(bf16[128,448]{1,0:T(8,128)(2,1)S(1)} %copy.8.own_ref), channel_id=1, source_target_pairs={{0,16},{16,0},{1,17},{17,1},{2,18},{18,2},{3,19},{19,3},{4,20},{20... | collective-permute-start | bytes 344072 | tf_op jit(solution)/shard_map/ppermute | solution.py:207
  23.2 5.0 %copy-start.1 = (bf16[2048,448]{0,1:T(8,128)(2,1)S(1)}, bf16[2048,448]{0,1:T(8,128)(2,1)}, u32[]{:S(2)}) copy-start(bf16[2048,448]{0,1:T(8,128)(2,1)} %param.7) | copy-start | bytes 5505028
  23.2 5.0 %collective-permute-start.1 = (bf16[128,2048]{1,0:T(8,128)(2,1)S(1)}, bf16[128,2048]{1,0:T(8,128)(2,1)S(1)}, u32[]{:S(2)}, u32[]{:S(2)}) collective-permute-start(bf16[128,2048]{1,0:T(8,128)(2,1)S(1)} %bitcast.34), channel_id=1, source_target_pairs={{0,1},{1,0},{2,3},{3,2},{4,5},{5,4},{6,7},{7,6},{8,9},{9,8},{10,11... | collective-permute-start | bytes 1572872 | tf_op jit(solution)/shard_map/ppermute | solution.py:213
  30.3 24.2 %collective-permute-start.4 = (bf16[64,896]{1,0:T(8,128)(2,1)S(1)}, bf16[64,896]{1,0:T(8,128)(2,1)S(1)}, u32[]{:S(2)}, u32[]{:S(2)}) collective-permute-start(bf16[64,896]{1,0:T(8,128)(2,1)S(1)} %get-tuple-element.37), channel_id=1, source_target_pairs={{0,448},{32,96},{64,0},{96,160},{128,64},{160,224},{192,128},{224,... | collective-permute-start | bytes 344072 | tf_op jit(solution)/shard_map/ppermute | solution.py:197
  41.4 13.2 %collective-permute-start.2 = (bf16[2,64,896]{2,1,0:T(8,128)(2,1)S(1)}, bf16[2,64,896]{2,1,0:T(8,128)(2,1)S(1)}, u32[]{:S(2)}, u32[]{:S(2)}) collective-permute-start(bf16[2,64,896]{2,1,0:T(8,128)(2,1)S(1)} %get-tuple-element.35), channel_id=1, source_target_pairs={{0,32},{32,0},{64,96},{96,64},{128,160},{160,128},{192,224},{224,1... | collective-permute-start | bytes 688136 | tf_op jit(solution)/shard_map/ppermute | solution.py:197
  43.3 11.2 %collective-permute-start.3 = (bf16[2,64,896]{2,1,0:T(8,128)(2,1)S(1)}, bf16[2,64,896]{2,1,0:T(8,128)(2,1)S(1)}, u32[]{:S(2)}, u32[]{:S(2)}) collective-permute-start(bf16[2,64,896]{2,1,0:T(8,128)(2,1)S(1)} %get-tuple-element.36), channel_id=1, source_target_pairs={{0,480},{32,64},{64,32},{96,128},{128,96},{160,192},{192,160},{224... | collective-permute-start | bytes 688136 | tf_op jit(solution)/shard_map/ppermute | solution.py:197
  48.0 22.8 %collective-permute-start.5 = (bf16[3,64,896]{2,1,0:T(8,128)(2,1)}, bf16[3,64,896]{2,1,0:T(8,128)(2,1)S(1)}, u32[]{:S(2)}, u32[]{:S(2)}) collective-permute-start(bf16[3,64,896]{2,1,0:T(8,128)(2,1)} %get-tuple-element.41), channel_id=1, source_target_pairs={{0,32},{32,0},{64,96},{96,64},{128,160},{160,128},{192,224},{224,1... | collective-permute-start | bytes 1032200 | tf_op jit(solution)/shard_map/ppermute | solution.py:197
  50.0 20.9 %collective-permute-start.6 = (bf16[3,64,896]{2,1,0:T(8,128)(2,1)S(1)}, bf16[3,64,896]{2,1,0:T(8,128)(2,1)S(1)}, u32[]{:S(2)}, u32[]{:S(2)}) collective-permute-start(bf16[3,64,896]{2,1,0:T(8,128)(2,1)S(1)} %get-tuple-element.42), channel_id=1, source_target_pairs={{0,480},{32,64},{64,32},{96,128},{128,96},{160,192},{192,160},{224... | collective-permute-start | bytes 1032200 | tf_op jit(solution)/shard_map/ppermute | solution.py:197
  55.9 14.9 %collective-permute-start.7 = (bf16[64,896]{1,0:T(8,128)(2,1)}, bf16[64,896]{1,0:T(8,128)(2,1)S(1)}, u32[]{:S(2)}, u32[]{:S(2)}) collective-permute-start(bf16[64,896]{1,0:T(8,128)(2,1)} %fusion.8), channel_id=1, source_target_pairs={{0,96},{32,448},{64,160},{96,0},{128,224},{160,64},{192,288},{224,... | collective-permute-start | bytes 344072 | tf_op jit(solution)/shard_map/ppermute | solution.py:197
  59.5 11.3 %collective-permute-start.8 = (bf16[64,896]{1,0:T(8,128)(2,1)}, bf16[64,896]{1,0:T(8,128)(2,1)S(1)}, u32[]{:S(2)}, u32[]{:S(2)}) collective-permute-start(bf16[64,896]{1,0:T(8,128)(2,1)} %fusion.2), channel_id=1, source_target_pairs={{0,416},{32,128},{64,480},{96,192},{128,32},{160,256},{192,96},{22... | collective-permute-start | bytes 344072 | tf_op jit(solution)/shard_map/ppermute | solution.py:197
  64.0 6.7 %copy-start.3 = (bf16[8,2048]{1,0:T(8,128)(2,1)S(1)}, bf16[8,2048]{1,0:T(8,128)(2,1)}, u32[]{:S(2)}) copy-start(bf16[8,2048]{1,0:T(8,128)(2,1)} %param.5) | copy-start | bytes 98308
  65.3 21.6 %all-to-all-start.1 = ((bf16[16,8,2048]{2,1,0:T(8,128)(2,1)}), bf16[16,8,2048]{2,1,0:T(8,128)(2,1)S(1)}, u32[]{:S(2)}, u32[]{:S(2)}) async-start(bf16[16,8,2048]{2,1,0:T(8,128)(2,1)} %fusion.1), calls=%async_computation.1 | async-start | bytes 1048576 | tf_op jit(solution)/shard_map/all_to_all | solution.py:297
  71.0 9.7 %collective-permute-start.10 = (bf16[64,896]{1,0:T(8,128)(2,1)S(1)}, bf16[64,896]{1,0:T(8,128)(2,1)S(1)}, u32[]{:S(2)}, u32[]{:S(2)}) collective-permute-start(bf16[64,896]{1,0:T(8,128)(2,1)S(1)} %get-tuple-element.48), channel_id=1, source_target_pairs={{0,416},{32,128},{64,480},{96,192},{128,32},{160,256},{192,96},{22... | collective-permute-start | bytes 344072 | tf_op jit(solution)/shard_map/ppermute | solution.py:197
  76.2 9.9 %collective-permute-start.9 = (bf16[64,896]{1,0:T(8,128)(2,1)S(1)}, bf16[64,896]{1,0:T(8,128)(2,1)S(1)}, u32[]{:S(2)}, u32[]{:S(2)}) collective-permute-start(bf16[64,896]{1,0:T(8,128)(2,1)S(1)} %get-tuple-element.47), channel_id=1, source_target_pairs={{0,96},{32,448},{64,160},{96,0},{128,224},{160,64},{192,288},{224,... | collective-permute-start | bytes 344072 | tf_op jit(solution)/shard_map/ppermute | solution.py:197

commit v15 on v13

--- a/solution.py
+++ b/solution.py
@@ -274,6 +274,7 @@
     )(normed, grads, grads_own, gate_weight.T, up_weight.T)
 
     from_far = move(far, -2, nz).astype(f32)
+    base = lax.optimization_barrier(outer_hub[1].astype(f32) + from_far)
     outer_ahead, outer_behind = move(outer_ahead, 1, nz), move(outer_behind, -1, nz)
     inner_ahead, inner_behind = move(inner_ahead, 1, nz), move(inner_behind, -1, nz)
 
@@ -292,7 +293,10 @@
         )
 
     plus, minus = lax.optimization_barrier(
-        (outer(0).astype(bf16), (outer(1) + from_far).astype(bf16))
+        (
+            outer(0).astype(bf16),
+            (base + outer_ahead[1].astype(f32) + outer_behind[1].astype(f32)).astype(bf16),
+        )
     )
     part, first_sum = lax.optimization_barrier((part, plus))
     plus, minus = move(first_sum, 3, nz), move(minus, -3, nz)

time: 89.9 us -> 91.6 us (1.019)
  starting transfers between devices: 60.7 us -> 62.4 us
    ppermute x9, starting transfers between devices: 39.4 us -> 41.2 us  [move(): return lax.ppermute(value, 'z', pairs)]
where the time goes in v15:
time: 91.6 us; the launch traced here: 90.8 us
  starting transfers between devices  62.4 us (68%)
  waiting for transfers between devices  17.5 us (19%)
  Pallas kernels  5.98 us (7%)
  local copies, waits for them, and re-layouts  2.75 us (3%)
  other arithmetic  1.36 us (1%)
    ppermute x9, starting transfers between devices, move(): return lax.ppermute(value, 'z', pairs)  41.2 us
    ppermute x9, waiting for transfers between devices, move(): return lax.ppermute(value, 'z', pairs)  9.36 us
    all_to_all x1, starting transfers between devices, shards(): same = lax.all_to_all(copies, ('yh', 'x', 'yl'), 0, 0, tiled=True)  7.58 us
    ppermute x1, waiting for transfers between devices, shards(): other = lax.ppermute(own, 'yh', [(0, 1), (1, 0)])  7.39 us
    all_to_all x1, starting transfers between devices, shards(): moved = lax.all_to_all(blocks, TENSOR, 0, 0, tiled=True)  5.42 us
    ppermute x1, starting transfers between devices, shards(): other = lax.ppermute(own, 'yh', [(0, 1), (1, 0)])  4.78 us
    ppermute x1, starting transfers between devices, shards(): swapped = lax.ppermute(same, 'core', [(0, 1), (1, 0)])  3.44 us
    pallas_call x1, Pallas kernels, shards(): pl.pallas_call(functools.partial(rest_kernel, factor, nz), out_shape=[jax...  2.31 us
  transfers between devices with their start and end apart: 13, of which 4 were waited for; matrix products, arithmetic and copies ran while one was open for 2% of the time, Pallas kernels for 4%

profile of v15, /device:TPU:1, one launch (start us, length us, event | category | flops | bytes accessed | tf_op | source)
XLA Modules:
  0.0 90.8 jit_solution(4524791849575483376)
XLA Ops:
  0.6 0.0 copy-start
  0.6 0.0 copy-start.2
  0.7 1.7 %broadcast_in_dim.2 = bf16[16,8,2048]{2,1,0:T(8,128)(2,1)} broadcast(bf16[8,2048]{1,0:T(8,128)(2,1)} %param.5), dimensions={1,2} | broadcast | bytes 557056 | tf_op jit(solution)/shard_map/broadcast_in_dim | solution.py:218
  2.4 7.6 %all-to-all-start = ((bf16[16,8,2048]{2,1,0:T(8,128)(2,1)}), bf16[16,8,2048]{2,1,0:T(8,128)(2,1)S(1)}, u32[]{:S(2)}, u32[]{:S(2)}) async-start(bf16[16,8,2048]{2,1,0:T(8,128)(2,1)} %broadcast_in_dim.2), calls=%async_computation | async-start | bytes 1048576 | tf_op jit(solution)/shard_map/all_to_all | solution.py:219
  10.0 1.0 %copy.8.own_ref = bf16[128,448]{1,0:T(8,128)(2,1)S(1)} copy(bf16[128,448]{0,1:T(8,128)(2,1)} %param.9) | data formatting | bytes 229376 | tf_op args[4]
  11.0 4.8 %collective-permute-start = (bf16[128,448]{1,0:T(8,128)(2,1)S(1)}, bf16[128,448]{1,0:T(8,128)(2,1)S(1)}, u32[]{:S(2)}, u32[]{:S(2)}) collective-permute-start(bf16[128,448]{1,0:T(8,128)(2,1)S(1)} %copy.8.own_ref), channel_id=1, source_target_pairs={{0,16},{16,0},{1,17},{17,1},{2,18},{18,2},{3,19},{19,3},{4,20},{20... | collective-permute-start | bytes 344072 | tf_op jit(solution)/shard_map/ppermute | solution.py:216
  15.8 7.4 %collective-permute-done.other_ref = bf16[128,448]{1,0:T(8,128)(2,1)S(1)} collective-permute-done((bf16[128,448]{1,0:T(8,128)(2,1)S(1)}, bf16[128,448]{1,0:T(8,128)(2,1)S(1)}, u32[]{:S(2)}, u32[]{:S(2)}) %collective-permute-start) | collective-permute-done | bytes 114720 | tf_op jit(solution)/shard_map/ppermute | solution.py:216
  23.2 0.0 all-to-all-done
  23.2 0.0 copy-start.1
  23.2 3.4 %collective-permute-start.1 = (bf16[128,2048]{1,0:T(8,128)(2,1)S(1)}, bf16[128,2048]{1,0:T(8,128)(2,1)S(1)}, u32[]{:S(2)}, u32[]{:S(2)}) collective-permute-start(bf16[128,2048]{1,0:T(8,128)(2,1)S(1)} %bitcast.33), channel_id=1, source_target_pairs={{0,1},{1,0},{2,3},{3,2},{4,5},{5,4},{6,7},{7,6},{8,9},{9,8},{10,11... | collective-permute-start | bytes 1572872 | tf_op jit(solution)/shard_map/ppermute | solution.py:222
  26.6 0.0 copy-done
  26.6 0.0 copy-done.2
  26.6 0.8 norm.1
  27.4 0.7 collective-permute-done.1.swapped_ref
  28.1 0.0 copy-done.1
  28.1 2.1 %local.1 = (bf16[64,896]{1,0:T(8,128)(2,1)S(1)}, bf16[2,64,896]{2,1,0:T(8,128)(2,1)S(1)}, bf16[2,64,896]{2,1,0:T(8,128)(2,1)S(1)}, bf16[128,896]{1,0:T(8,128)(2,...) custom-call(bf16[128,2048]{1,0:T(8,128)(2,1)S(1)} %get-tuple-element.29.same_ref, ...), custom_call_target="tpu_custom_call" | custom-call | flops 1409286144 | bytes 7340032 | tf_op jit(solution)/shard_map/local/pallas_call | solution.py:239
  30.3 11.1 %collective-permute-start.4 = (bf16[64,896]{1,0:T(8,128)(2,1)S(1)}, bf16[64,896]{1,0:T(8,128)(2,1)S(1)}, u32[]{:S(2)}, u32[]{:S(2)}) collective-permute-start(bf16[64,896]{1,0:T(8,128)(2,1)S(1)} %get-tuple-element.39), channel_id=1, source_target_pairs={{0,448},{32,96},{64,0},{96,160},{128,64},{160,224},{192,128},{224,... | collective-permute-start | bytes 344072 | tf_op jit(solution)/shard_map/ppermute | solution.py:206
  41.4 1.9 %collective-permute-start.2 = (bf16[2,64,896]{2,1,0:T(8,128)(2,1)S(1)}, bf16[2,64,896]{2,1,0:T(8,128)(2,1)S(1)}, u32[]{:S(2)}, u32[]{:S(2)}) collective-permute-start(bf16[2,64,896]{2,1,0:T(8,128)(2,1)S(1)} %get-tuple-element.37), channel_id=1, source_target_pairs={{0,32},{32,0},{64,96},{96,64},{128,160},{160,128},{192,224},{224,1... | collective-permute-start | bytes 688136 | tf_op jit(solution)/shard_map/ppermute | solution.py:206
  43.3 3.3 %collective-permute-start.3 = (bf16[2,64,896]{2,1,0:T(8,128)(2,1)S(1)}, bf16[2,64,896]{2,1,0:T(8,128)(2,1)S(1)}, u32[]{:S(2)}, u32[]{:S(2)}) collective-permute-start(bf16[2,64,896]{2,1,0:T(8,128)(2,1)S(1)} %get-tuple-element.38), channel_id=1, source_target_pairs={{0,480},{32,64},{64,32},{96,128},{128,96},{160,192},{192,160},{224... | collective-permute-start | bytes 688136 | tf_op jit(solution)/shard_map/ppermute | solution.py:206
  46.6 2.3 %rest.1 = (bf16[3,64,896]{2,1,0:T(8,128)(2,1)S(1)}, bf16[3,64,896]{2,1,0:T(8,128)(2,1)S(1)}, bf16[2,64,896]{2,1,0:T(8,128)(2,1)S(1)}, bf16[3,64,896]{2,1,0:T(8,128)(2,1)S(1)}, bf16[128,2048]{1,0:T(8,128)(2,1)}) custom-call(bf16[256,2048]{1,0:T(8,128)(2,1)S(1)} %get-tuple-element.32.normed_ref, bf16[256,896]{1,0:T(8,128)(2,1)S(1)} %get-tuple-element.33.grads_ref, ...), custom_call_target="tpu_custom_call" | custom-call | flops 1409286144 | bytes 4194304 | tf_op jit(solution)/shard_map/rest/pallas_call | solution.py:260
  48.9 0.0 copy-start.3
  48.9 2.1 %collective-permute-start.5 = (bf16[3,64,896]{2,1,0:T(8,128)(2,1)S(1)}, bf16[3,64,896]{2,1,0:T(8,128)(2,1)S(1)}, u32[]{:S(2)}, u32[]{:S(2)}) collective-permute-start(bf16[3,64,896]{2,1,0:T(8,128)(2,1)S(1)} %get-tuple-element.43), channel_id=1, source_target_pairs={{0,32},{32,0},{64,96},{96,64},{128,160},{160,128},{192,224},{224,1... | collective-permute-start | bytes 1032200 | tf_op jit(solution)/shard_map/ppermute | solution.py:206
  51.0 4.5 %collective-permute-start.6 = (bf16[3,64,896]{2,1,0:T(8,128)(2,1)S(1)}, bf16[3,64,896]{2,1,0:T(8,128)(2,1)S(1)}, u32[]{:S(2)}, u32[]{:S(2)}) collective-permute-start(bf16[3,64,896]{2,1,0:T(8,128)(2,1)S(1)} %get-tuple-element.44), channel_id=1, source_target_pairs={{0,480},{32,64},{64,32},{96,128},{128,96},{160,192},{192,160},{224... | collective-permute-start | bytes 1032200 | tf_op jit(solution)/shard_map/ppermute | solution.py:206
  55.6 0.0 collective-permute-done.4
  55.6 0.0 collective-permute-done.2
  55.6 0.0 collective-permute-done.3
  55.7 0.1 fusion.3
  55.8 3.5 %collective-permute-start.7 = (bf16[64,896]{1,0:T(8,128)(2,1)S(1)}, bf16[64,896]{1,0:T(8,128)(2,1)S(1)}, u32[]{:S(2)}, u32[]{:S(2)}) collective-permute-start(bf16[64,896]{1,0:T(8,128)(2,1)S(1)} %fusion.3), channel_id=1, source_target_pairs={{0,96},{32,448},{64,160},{96,0},{128,224},{160,64},{192,288},{224,... | collective-permute-start | bytes 344072 | tf_op jit(solution)/shard_map/ppermute | solution.py:206
  59.3 4.0 %collective-permute-start.8 = (bf16[64,896]{1,0:T(8,128)(2,1)S(1)}, bf16[64,896]{1,0:T(8,128)(2,1)S(1)}, u32[]{:S(2)}, u32[]{:S(2)}) collective-permute-start(bf16[64,896]{1,0:T(8,128)(2,1)S(1)} %fusion), channel_id=1, source_target_pairs={{0,416},{32,128},{64,480},{96,192},{128,32},{160,256},{192,96},{22... | collective-permute-start | bytes 344072 | tf_op jit(solution)/shard_map/ppermute | solution.py:206
  63.3 5.4 %all-to-all-start.1 = ((bf16[16,8,2048]{2,1,0:T(8,128)(2,1)}), bf16[16,8,2048]{2,1,0:T(8,128)(2,1)S(1)}, u32[]{:S(2)}, u32[]{:S(2)}) async-start(bf16[16,8,2048]{2,1,0:T(8,128)(2,1)} %bitcast.8), calls=%async_computation.1 | async-start | bytes 1048576 | tf_op jit(solution)/shard_map/all_to_all | solution.py:305
  68.8 0.0 copy-done.3
  68.8 0.1 fusion.10
  68.9 0.0 collective-permute-done.7
  68.9 0.2 collective-permute-done.8
  69.1 0.0 collective-permute-done.5.ahead_ref
  69.1 0.0 collective-permute-done.6.behind_ref
  69.1 0.1 fusion.1
  69.2 7.0 %collective-permute-start.10 = (bf16[64,896]{1,0:T(8,128)(2,1)S(1)}, bf16[64,896]{1,0:T(8,128)(2,1)S(1)}, u32[]{:S(2)}, u32[]{:S(2)}) collective-permute-start(bf16[64,896]{1,0:T(8,128)(2,1)S(1)} %get-tuple-element.50), channel_id=1, source_target_pairs={{0,416},{32,128},{64,480},{96,192},{128,32},{160,256},{192,96},{22... | collective-permute-start | bytes 344072 | tf_op jit(solution)/shard_map/ppermute | solution.py:206
  76.2 3.7 %collective-permute-start.9 = (bf16[64,896]{1,0:T(8,128)(2,1)S(1)}, bf16[64,896]{1,0:T(8,128)(2,1)S(1)}, u32[]{:S(2)}, u32[]{:S(2)}) collective-permute-start(bf16[64,896]{1,0:T(8,128)(2,1)S(1)} %get-tuple-element.49), channel_id=1, source_target_pairs={{0,96},{32,448},{64,160},{96,0},{128,224},{160,64},{192,288},{224,... | collective-permute-start | bytes 344072 | tf_op jit(solution)/shard_map/ppermute | solution.py:206
  79.9 0.0 collective-permute-done.10.minus_ref
  79.9 9.2 %collective-permute-done.9.plus_ref = bf16[64,896]{1,0:T(8,128)(2,1)S(1)} collective-permute-done((bf16[64,896]{1,0:T(8,128)(2,1)S(1)}, bf16[64,896]{1,0:T(8,128)(2,1)S(1)}, u32[]{:S(2)}, u32[]{:S(2)}) %collective-permute-start.9) | collective-permute-done | bytes 114720 | tf_op jit(solution)/shard_map/ppermute | solution.py:206
  89.1 0.8 total.1
  89.9 0.0 all-to-all-done.1
  89.9 0.1 convert_reduce_fusion
  89.9 0.2 fusion.6
  90.1 0.7 fusion.9
  (4 shorter events, 0.1 us)
Async XLA Ops:
  0.6 26.0 %copy-start = (bf16[2048,448]{0,1:T(8,128)(2,1)S(1)}, bf16[2048,448]{0,1:T(8,128)(2,1)}, u32[]{:S(2)}) copy-start(bf16[2048,448]{0,1:T(8,128)(2,1)} %param.8) | copy-start | bytes 5505028
  0.6 26.0 %copy-start.2 = (f32[2048]{0:T(1024)S(1)}, f32[2048]{0:T(1024)}, u32[]{:S(2)}) copy-start(f32[2048]{0:T(1024)} %param.6) | copy-start | bytes 24580
  2.4 20.8 %all-to-all-start = ((bf16[16,8,2048]{2,1,0:T(8,128)(2,1)}), bf16[16,8,2048]{2,1,0:T(8,128)(2,1)S(1)}, u32[]{:S(2)}, u32[]{:S(2)}) async-start(bf16[16,8,2048]{2,1,0:T(8,128)(2,1)} %broadcast_in_dim.2), calls=%async_computation | async-start | bytes 1048576 | tf_op jit(solution)/shard_map/all_to_all | solution.py:219
  11.0 12.2 %collective-permute-start = (bf16[128,448]{1,0:T(8,128)(2,1)S(1)}, bf16[128,448]{1,0:T(8,128)(2,1)S(1)}, u32[]{:S(2)}, u32[]{:S(2)}) collective-permute-start(bf16[128,448]{1,0:T(8,128)(2,1)S(1)} %copy.8.own_ref), channel_id=1, source_target_pairs={{0,16},{16,0},{1,17},{17,1},{2,18},{18,2},{3,19},{19,3},{4,20},{20... | collective-permute-start | bytes 344072 | tf_op jit(solution)/shard_map/ppermute | solution.py:216
  23.2 5.0 %copy-start.1 = (bf16[2048,448]{0,1:T(8,128)(2,1)S(1)}, bf16[2048,448]{0,1:T(8,128)(2,1)}, u32[]{:S(2)}) copy-start(bf16[2048,448]{0,1:T(8,128)(2,1)} %param.7) | copy-start | bytes 5505028
  23.2 5.0 %collective-permute-start.1 = (bf16[128,2048]{1,0:T(8,128)(2,1)S(1)}, bf16[128,2048]{1,0:T(8,128)(2,1)S(1)}, u32[]{:S(2)}, u32[]{:S(2)}) collective-permute-start(bf16[128,2048]{1,0:T(8,128)(2,1)S(1)} %bitcast.33), channel_id=1, source_target_pairs={{0,1},{1,0},{2,3},{3,2},{4,5},{5,4},{6,7},{7,6},{8,9},{9,8},{10,11... | collective-permute-start | bytes 1572872 | tf_op jit(solution)/shard_map/ppermute | solution.py:222
  30.3 25.3 %collective-permute-start.4 = (bf16[64,896]{1,0:T(8,128)(2,1)S(1)}, bf16[64,896]{1,0:T(8,128)(2,1)S(1)}, u32[]{:S(2)}, u32[]{:S(2)}) collective-permute-start(bf16[64,896]{1,0:T(8,128)(2,1)S(1)} %get-tuple-element.39), channel_id=1, source_target_pairs={{0,448},{32,96},{64,0},{96,160},{128,64},{160,224},{192,128},{224,... | collective-permute-start | bytes 344072 | tf_op jit(solution)/shard_map/ppermute | solution.py:206
  41.4 14.3 %collective-permute-start.2 = (bf16[2,64,896]{2,1,0:T(8,128)(2,1)S(1)}, bf16[2,64,896]{2,1,0:T(8,128)(2,1)S(1)}, u32[]{:S(2)}, u32[]{:S(2)}) collective-permute-start(bf16[2,64,896]{2,1,0:T(8,128)(2,1)S(1)} %get-tuple-element.37), channel_id=1, source_target_pairs={{0,32},{32,0},{64,96},{96,64},{128,160},{160,128},{192,224},{224,1... | collective-permute-start | bytes 688136 | tf_op jit(solution)/shard_map/ppermute | solution.py:206
  43.3 12.4 %collective-permute-start.3 = (bf16[2,64,896]{2,1,0:T(8,128)(2,1)S(1)}, bf16[2,64,896]{2,1,0:T(8,128)(2,1)S(1)}, u32[]{:S(2)}, u32[]{:S(2)}) collective-permute-start(bf16[2,64,896]{2,1,0:T(8,128)(2,1)S(1)} %get-tuple-element.38), channel_id=1, source_target_pairs={{0,480},{32,64},{64,32},{96,128},{128,96},{160,192},{192,160},{224... | collective-permute-start | bytes 688136 | tf_op jit(solution)/shard_map/ppermute | solution.py:206
  48.9 19.8 %copy-start.3 = (bf16[8,2048]{1,0:T(8,128)(2,1)S(1)}, bf16[8,2048]{1,0:T(8,128)(2,1)}, u32[]{:S(2)}) copy-start(bf16[8,2048]{1,0:T(8,128)(2,1)} %param.5) | copy-start | bytes 98308
  48.9 20.1 %collective-permute-start.5 = (bf16[3,64,896]{2,1,0:T(8,128)(2,1)S(1)}, bf16[3,64,896]{2,1,0:T(8,128)(2,1)S(1)}, u32[]{:S(2)}, u32[]{:S(2)}) collective-permute-start(bf16[3,64,896]{2,1,0:T(8,128)(2,1)S(1)} %get-tuple-element.43), channel_id=1, source_target_pairs={{0,32},{32,0},{64,96},{96,64},{128,160},{160,128},{192,224},{224,1... | collective-permute-start | bytes 1032200 | tf_op jit(solution)/shard_map/ppermute | solution.py:206
  51.0 18.1 %collective-permute-start.6 = (bf16[3,64,896]{2,1,0:T(8,128)(2,1)S(1)}, bf16[3,64,896]{2,1,0:T(8,128)(2,1)S(1)}, u32[]{:S(2)}, u32[]{:S(2)}) collective-permute-start(bf16[3,64,896]{2,1,0:T(8,128)(2,1)S(1)} %get-tuple-element.44), channel_id=1, source_target_pairs={{0,480},{32,64},{64,32},{96,128},{128,96},{160,192},{192,160},{224... | collective-permute-start | bytes 1032200 | tf_op jit(solution)/shard_map/ppermute | solution.py:206
  55.8 13.1 %collective-permute-start.7 = (bf16[64,896]{1,0:T(8,128)(2,1)S(1)}, bf16[64,896]{1,0:T(8,128)(2,1)S(1)}, u32[]{:S(2)}, u32[]{:S(2)}) collective-permute-start(bf16[64,896]{1,0:T(8,128)(2,1)S(1)} %fusion.3), channel_id=1, source_target_pairs={{0,96},{32,448},{64,160},{96,0},{128,224},{160,64},{192,288},{224,... | collective-permute-start | bytes 344072 | tf_op jit(solution)/shard_map/ppermute | solution.py:206
  59.3 9.8 %collective-permute-start.8 = (bf16[64,896]{1,0:T(8,128)(2,1)S(1)}, bf16[64,896]{1,0:T(8,128)(2,1)S(1)}, u32[]{:S(2)}, u32[]{:S(2)}) collective-permute-start(bf16[64,896]{1,0:T(8,128)(2,1)S(1)} %fusion), channel_id=1, source_target_pairs={{0,416},{32,128},{64,480},{96,192},{128,32},{160,256},{192,96},{22... | collective-permute-start | bytes 344072 | tf_op jit(solution)/shard_map/ppermute | solution.py:206
  63.3 26.5 %all-to-all-start.1 = ((bf16[16,8,2048]{2,1,0:T(8,128)(2,1)}), bf16[16,8,2048]{2,1,0:T(8,128)(2,1)S(1)}, u32[]{:S(2)}, u32[]{:S(2)}) async-start(bf16[16,8,2048]{2,1,0:T(8,128)(2,1)} %bitcast.8), calls=%async_computation.1 | async-start | bytes 1048576 | tf_op jit(solution)/shard_map/all_to_all | solution.py:305
  69.2 10.7 %collective-permute-start.10 = (bf16[64,896]{1,0:T(8,128)(2,1)S(1)}, bf16[64,896]{1,0:T(8,128)(2,1)S(1)}, u32[]{:S(2)}, u32[]{:S(2)}) collective-permute-start(bf16[64,896]{1,0:T(8,128)(2,1)S(1)} %get-tuple-element.50), channel_id=1, source_target_pairs={{0,416},{32,128},{64,480},{96,192},{128,32},{160,256},{192,96},{22... | collective-permute-start | bytes 344072 | tf_op jit(solution)/shard_map/ppermute | solution.py:206
  76.2 12.9 %collective-permute-start.9 = (bf16[64,896]{1,0:T(8,128)(2,1)S(1)}, bf16[64,896]{1,0:T(8,128)(2,1)S(1)}, u32[]{:S(2)}, u32[]{:S(2)}) collective-permute-start(bf16[64,896]{1,0:T(8,128)(2,1)S(1)} %get-tuple-element.49), channel_id=1, source_target_pairs={{0,96},{32,448},{64,160},{96,0},{128,224},{160,64},{192,288},{224,... | collective-permute-start | bytes 344072 | tf_op jit(solution)/shard_map/ppermute | solution.py:206
